TPU v7x, 256 devices: a whole 4x4x8 slice. The times are simulated.
256 devices in a mesh: chart: 32 (over z, y), frame: 8 (over x, core).
Axes of the slice: x: 4, y: 4, z: 8, core: 2. Of those that a mesh axis runs over, the one named last changes fastest.
Arguments:
- features: bfloat16 [16, 512, 64, 128], P('frame', 'chart'), may hold values from -6 to 6
- spatial_a: bfloat16 [3, 3, 64, 64], replicated, may hold values from -0.25 to 0.25
- first_time_kernel: bfloat16 [3, 64, 64], replicated, may hold values from -0.4375 to 0.4375
- spatial_b: bfloat16 [3, 3, 64, 64], replicated, may hold values from -0.25 to 0.25
- second_time_kernel: bfloat16 [3, 64, 64], replicated, may hold values from -0.4375 to 0.4375
- seam_owner: int32 [32, 16], replicated, may hold values from -1 to 31, as said below
- seam_row: int32 [32, 16], replicated, may hold values from -1 to 15
- seam_to: int32 [32, 16], replicated, may hold values from -1 to 15
- grad_out: bfloat16 [16, 512, 64, 128], P('frame', 'chart'), may hold values from -6 to 6
Outputs:
- blended: bfloat16 [16, 512, 64, 128], P('frame', 'chart')
- grad_features: bfloat16 [16, 512, 64, 128], P('frame', 'chart')
- grad_spatial_a: float32 [3, 3, 64, 64], replicated
- grad_temporal_a: float32 [3, 64, 64], replicated
- grad_spatial_b: float32 [3, 3, 64, 64], replicated
- grad_temporal_b: float32 [3, 64, 64], replicated
Inputs may be any that keep to these rules, and one draw needn't show every extreme that they name: An entry is empty exactly where seam_owner is -1, and then seam_row and seam_to are -1 as well. A live entry's owner differs from its tile by 1 to 2. At most 4 live entries of one tile share an owner, and every tile has exactly 4 live entries from one owner. Live counts differ from tile to tile.
All inputs are finite; a program needn't handle non-finite values.
Results may differ from a plain program's by a relative error of at most 0.013.
Values may be sent and summed in bfloat16 or wider, within the bound.
A program may use at most 64 MiB of HBM per device.

v0:
```python
import jax
import jax.numpy as jnp
from jax import lax
from jax.sharding import PartitionSpec as P

NEAR_DILATION = 1
REACH = 2
SEAM_CAP = 4


def with_halo(cells, sides, width):
    for axis, dim in sides:
        count = lax.axis_size(axis)
        ends = count - 1
        head = lax.slice_in_dim(cells, 0, width, axis=dim)
        tail = lax.slice_in_dim(cells, cells.shape[dim] - width, cells.shape[dim], axis=dim)
        cells = jnp.concatenate(
            [
                lax.ppermute(tail, axis, [(i, (i + 1) % count) for i in range(ends)]),
                cells,
                lax.ppermute(head, axis, [((i + 1) % count, i) for i in range(ends)]),
            ],
            axis=dim,
        )
    return cells


def from_behind(array, axis, by):
    peers = lax.axis_size(axis)
    pairs = [(i, i + by) for i in range(peers) if 0 <= i + by < peers]
    return lax.ppermute(array, axis, pairs)


def silu_slope(values):
    logistic = jax.nn.sigmoid(values)
    return logistic * (1.0 + values * (1.0 - logistic))


def pad_columns(values):
    return jnp.pad(values, ((0, 0), (0, 0), (0, 0), (1, 1)))


def frames_padding(values, spacing):
    return jnp.pad(values, ((spacing, spacing), (0, 0), (0, 0), (0, 0)))


def chart_rim(values):
    return with_halo(values, (("chart", 1),), 1)


def to_tiles(values):
    return lax.all_to_all(values, "frame", split_axis=1, concat_axis=0, tiled=True)


def to_frames(values):
    return lax.all_to_all(values, "frame", split_axis=0, concat_axis=1, tiled=True)


def near_send(values, steps_by):
    return from_behind(values, "chart", steps_by)


def spatial_apply(padded, weight):
    strips = padded.shape[1] - 2
    pixels = padded.shape[3] - 2
    summed = None
    for row_tap in range(3):
        for col_tap in range(3):
            partial_sum = jnp.einsum(
                "oc,fscp->fsop",
                weight[row_tap, col_tap],
                padded[:, row_tap : row_tap + strips, :, col_tap : col_tap + pixels],
                preferred_element_type=jnp.float32,
            )
            summed = partial_sum if summed is None else summed + partial_sum
    return summed


def spatial_transpose(padded, weight):
    strips = padded.shape[1] - 2
    pixels = padded.shape[3] - 2
    summed = None
    for row_tap in range(3):
        for col_tap in range(3):
            partial_sum = jnp.einsum(
                "oc,fsop->fscp",
                weight[row_tap, col_tap],
                padded[
                    :, 2 - row_tap : 2 - row_tap + strips, :, 2 - col_tap : 2 - col_tap + pixels
                ],
                preferred_element_type=jnp.float32,
            )
            summed = partial_sum if summed is None else summed + partial_sum
    return summed


def spatial_weight(slopes, padded):
    strips = slopes.shape[1]
    pixels = slopes.shape[3]
    return jnp.stack(
        [
            jnp.stack(
                [
                    jnp.einsum(
                        "fsop,fscp->oc",
                        slopes,
                        padded[:, row_tap : row_tap + strips, :, col_tap : col_tap + pixels],
                        preferred_element_type=jnp.float32,
                    )
                    for col_tap in range(3)
                ]
            )
            for row_tap in range(3)
        ]
    )


def apply_time_kernel(padded, weight, spacing):
    frames = padded.shape[0] - 2 * spacing
    summed = None
    for kernel_tap in range(3):
        partial_sum = jnp.einsum(
            "oc,fscp->fsop",
            weight[kernel_tap],
            padded[kernel_tap * spacing : kernel_tap * spacing + frames],
            preferred_element_type=jnp.float32,
        )
        summed = partial_sum if summed is None else summed + partial_sum
    return summed


def time_kernel_transposed(padded, weight, spacing):
    frames = padded.shape[0] - 2 * spacing
    summed = None
    for kernel_tap in range(3):
        start_at = (2 - kernel_tap) * spacing
        partial_sum = jnp.einsum(
            "oc,fsop->fscp",
            weight[kernel_tap],
            padded[start_at : start_at + frames],
            preferred_element_type=jnp.float32,
        )
        summed = partial_sum if summed is None else summed + partial_sum
    return summed


def time_kernel_weight(slopes, padded, spacing):
    frames = slopes.shape[0]
    return jnp.stack(
        [
            jnp.einsum(
                "fsop,fscp->oc",
                slopes,
                padded[kernel_tap * spacing : kernel_tap * spacing + frames],
                preferred_element_type=jnp.float32,
            )
            for kernel_tap in range(3)
        ]
    )


def spatial_forward(inputs, weight, rim_fn):
    padded = pad_columns(rim_fn(inputs))
    before = spatial_apply(padded, weight)
    output = (inputs.astype(jnp.float32) + jax.nn.silu(before)).astype(jnp.bfloat16)
    return (output, before, padded)


def spatial_backward(upstream, before, padded, weight, rim_fn):
    slopes = (upstream.astype(jnp.float32) * silu_slope(before)).astype(jnp.bfloat16)
    grad_weight = spatial_weight(slopes, padded)
    spread = pad_columns(rim_fn(slopes))
    result = (upstream.astype(jnp.float32) + spatial_transpose(spread, weight)).astype(jnp.bfloat16)
    return (result, grad_weight)


def time_kernel_forward(inputs, weight, spacing, time_pad):
    padded = time_pad(inputs, spacing)
    before = apply_time_kernel(padded, weight, spacing)
    output = (inputs.astype(jnp.float32) + jax.nn.silu(before)).astype(jnp.bfloat16)
    return (output, before, padded)


def temporal_backward(upstream, before, padded, weight, spacing, time_pad):
    slopes = (upstream.astype(jnp.float32) * silu_slope(before)).astype(jnp.bfloat16)
    grad_weight = time_kernel_weight(slopes, padded, spacing)
    result = (
        upstream.astype(jnp.float32)
        + time_kernel_transposed(time_pad(slopes, spacing), weight, spacing)
    ).astype(jnp.bfloat16)
    return (result, grad_weight)


def seam_tables(seam_owner, seam_row, seam_to, strips):
    slot_count = seam_owner.shape[1]
    active = seam_owner >= 0
    earlier = jnp.arange(slot_count)[None, :] < jnp.arange(slot_count)[:, None]
    ordinal = jnp.sum((seam_owner[:, :, None] == seam_owner[:, None, :]) & earlier[None], axis=2)
    myself = lax.axis_index("chart")
    rank_hit = (ordinal[:, None, :] == jnp.arange(SEAM_CAP)[None, :, None]) & active[:, None, :]
    as_owner = rank_hit & (seam_owner[:, None, :] == myself)
    send_strip = jnp.sum(jnp.where(as_owner, seam_row[:, None, :], 0), axis=2)
    send_active = jnp.any(as_owner, axis=2)
    own_owner = lax.dynamic_index_in_dim(seam_owner, myself, 0, keepdims=False)
    own_to = lax.dynamic_index_in_dim(seam_to, myself, 0, keepdims=False)
    own_ordinal = lax.dynamic_index_in_dim(ordinal, myself, 0, keepdims=False)
    landing = (own_to[:, None] == jnp.arange(strips)[None, :]).astype(jnp.float32)
    return (send_strip, send_active, own_owner, own_to, own_ordinal, landing)


def receiver_side(tables, owner_ids):
    own_owner, own_to, own_ordinal, landing = (tables[2], tables[3], tables[4], tables[5])
    match_slot = (
        (own_owner[:, None, None] >= 0)
        & (own_owner[:, None, None] == owner_ids[None, :, None])
        & (own_ordinal[:, None, None] == jnp.arange(SEAM_CAP)[None, None, :])
    )
    matrix = jnp.einsum("kt,kqr->tqr", landing, match_slot.astype(jnp.float32))
    back_strip = jnp.sum(jnp.where(match_slot, own_to[:, None, None], 0), axis=0)
    return (matrix, back_strip)


def sender_side(tables, receiver_ids, strips):
    send_strip, send_active = (tables[0], tables[1])
    tile_count = send_strip.shape[0]
    inside_range = (receiver_ids >= 0) & (receiver_ids < tile_count)
    clipped = jnp.clip(receiver_ids, 0, tile_count - 1)
    strip_ids = jnp.take(send_strip, clipped, axis=0)
    live_ids = jnp.take(send_active, clipped, axis=0) & inside_range[:, None]
    matrix = ((strip_ids[None] == jnp.arange(strips)[:, None, None]) & live_ids[None]).astype(
        jnp.float32
    )
    return (strip_ids, matrix)


def pick_strips(values, strip_ids):
    gathered = jnp.take(values, strip_ids.reshape(-1), axis=1)
    return gathered.reshape(
        values.shape[0], strip_ids.shape[0], strip_ids.shape[1], values.shape[2], values.shape[3]
    )


def place_strips(received, matrix):
    return jnp.einsum(
        "tqr,fqrcp->ftcp", matrix.astype(jnp.bfloat16), received, preferred_element_type=jnp.float32
    )


def shards(
    features,
    spatial_a,
    first_time_kernel,
    spatial_b,
    second_time_kernel,
    seam_owner,
    seam_row,
    seam_to,
    grad_out,
):
    total_frames = features.shape[0] * lax.axis_size("frame")
    wide_dilation = min(8, total_frames // 4)
    strips = features.shape[1]
    first_layer, pre_one, padded_zero = spatial_forward(features, spatial_a, chart_rim)
    first_layer_tiles = to_tiles(first_layer)
    second_layer, second_preactivation, first_padded = time_kernel_forward(
        first_layer_tiles, first_time_kernel, NEAR_DILATION, frames_padding
    )
    frames_two = to_frames(second_layer)
    frames_three, pre_three, padded_two = spatial_forward(frames_two, spatial_b, chart_rim)
    third_layer = to_tiles(frames_three)
    layer_four, fourth_preactivation, third_padded = time_kernel_forward(
        third_layer, second_time_kernel, wide_dilation, frames_padding
    )
    frames_four = to_frames(layer_four)
    tables = seam_tables(seam_owner, seam_row, seam_to, strips)
    myself = lax.axis_index("chart")
    offsets = [offset for offset in range(-REACH, REACH + 1) if offset != 0]
    offset_array = jnp.array(offsets, dtype=jnp.int32)
    arrivals = []
    for offset in offsets:
        strip_ids, unused_matrix = sender_side(tables, jnp.reshape(myself - offset, (1,)), strips)
        arrivals.append(near_send(pick_strips(frames_four, strip_ids), -offset))
    receive_matrix, back_strip = receiver_side(tables, myself + offset_array)
    moved = place_strips(jnp.concatenate(arrivals, axis=1), receive_matrix)
    returns = []
    for position, offset in enumerate(offsets):
        returns.append(
            near_send(pick_strips(grad_out, back_strip[position : position + 1]), offset)
        )
    unused_ids, return_matrix = sender_side(tables, myself - offset_array, strips)
    moved_back = place_strips(jnp.concatenate(returns, axis=1), return_matrix)
    blended = (frames_four.astype(jnp.float32) + moved).astype(jnp.bfloat16)
    fourth_gradient = (grad_out.astype(jnp.float32) + moved_back).astype(jnp.bfloat16)
    fourth_gradient_tiles = to_tiles(fourth_gradient)
    third_gradient, gradient_kernel_second = temporal_backward(
        fourth_gradient_tiles,
        fourth_preactivation,
        third_padded,
        second_time_kernel,
        wide_dilation,
        frames_padding,
    )
    frames_grad_three = to_frames(third_gradient)
    frames_grad_two, grad_sb = spatial_backward(
        frames_grad_three, pre_three, padded_two, spatial_b, chart_rim
    )
    second_gradient = to_tiles(frames_grad_two)
    first_gradient, gradient_kernel_first = temporal_backward(
        second_gradient,
        second_preactivation,
        first_padded,
        first_time_kernel,
        NEAR_DILATION,
        frames_padding,
    )
    frames_grad_one = to_frames(first_gradient)
    grad_features, grad_sa = spatial_backward(
        frames_grad_one, pre_one, padded_zero, spatial_a, chart_rim
    )
    summed_sa, summed_ta, summed_sb, summed_tb = lax.psum(
        (grad_sa, gradient_kernel_first, grad_sb, gradient_kernel_second), ("chart", "frame")
    )
    pixel_frames = total_frames * strips * lax.axis_size("chart") * features.shape[3]
    grad_scale = float(pixel_frames) ** (-0.5)
    return (
        blended,
        grad_features,
        summed_sa * grad_scale,
        summed_ta * grad_scale,
        summed_sb * grad_scale,
        summed_tb * grad_scale,
    )


def solution(mesh):
    placed = (
        P("frame", "chart", None, None),
        P(),
        P(),
        P(),
        P(),
        P(),
        P(),
        P(),
        P("frame", "chart", None, None),
    )
    return jax.shard_map(
        shards,
        mesh=mesh,
        in_specs=placed,
        out_specs=(
            P("frame", "chart", None, None),
            P("frame", "chart", None, None),
            P(),
            P(),
            P(),
            P(),
        ),
        check_vma=False,
    )
```

profile of v0, /device:TPU:1, one launch (start us, length us, event | category | flops | bytes accessed | tf_op | source)
XLA Modules:
  0.0 771.0 jit_solution(17505815255640823043)
XLA Ops:
  8.1 4.0 collective-permute-start
  12.1 1.3 collective-permute-start.1
  17.7 1.6 gather_fusion.6
  19.4 1.3 collective-permute-start.8
  20.7 1.6 gather_fusion.9
  23.1 6.9 collective-permute-start.11
  31.4 3.9 collective-permute-start.10
  39.8 1.3 collective-permute-start.9
  44.3 1.5 add_convert_fusion.3
  46.6 6.5 all-to-all-start
  54.9 7.6 all-to-all-done
  63.3 1.6 add_convert_fusion.2
  64.9 4.4 all-to-all-start.1
  70.7 7.9 %all-to-all-done.1 = bf16[16,2,64,128]{3,2,1,0:T(8,128)(2,1)S(1)} async-done(((bf16[16,2,64,128]{3,2,1,0:T(8,128)(2,1)}), bf16[16,2,64,128]{3,2,1,0:T(8,128)(2,1)S(1)}, u32[]{:S(2)}, u32[]{:S(2)}) %all-to-all-start.1) | async-done | bytes 524320 | tf_op jit(solution)/shard_map/all_to_all | solution.py:56
  78.7 4.3 collective-permute-start.2
  83.0 1.8 fusion.21
  85.8 4.6 all-to-all-start.4
  90.4 1.3 collective-permute-start.3
  92.3 3.0 collective-permute-done.3
  95.4 1.4 select_maximum_fusion.4
  99.0 1.5 add_convert_fusion.1
  101.3 5.7 all-to-all-start.2
  107.0 1.2 pad_clamp_fusion.8
  108.9 1.4 fusion.208
  111.4 5.0 all-to-all-done.2
  119.8 1.5 fusion.26
  123.2 5.0 all-to-all-start.5
  128.2 1.4 convolution_bitcast_fusion.2
  129.6 1.3 convolution_bitcast_fusion.4
  131.8 5.8 all-to-all-done.5
  137.7 5.0 all-to-all-start.3
  142.6 1.2 copy.239
  152.1 1.6 copy.218
  155.4 2.4 gather_fusion.5
  157.8 2.4 gather_fusion.4
  160.2 2.4 gather_fusion.3
  162.6 2.4 gather_fusion.2
  164.9 1.7 fusion.105
  166.6 3.6 collective-permute-start.5
  170.2 1.7 fusion.106
  171.8 9.9 %collective-permute-start.4 = (bf16[2,1,4,64,128]{4,2,1,3,0:T(4,128)(2,1)}, bf16[2,1,4,64,128]{4,2,1,3,0:T(4,128)(2,1)}, u32[]{:S(2)}, u32[]{:S(2)}) collective-permute-start(bf16[2,1,4,64,128]{4,2,1,3,0:T(4,128)(2,1)} %fusion.106), channel_id=1, source_target_pairs={{0,16},{8,24},{16,32},{24,40},{32,48},{40,56},{48,64},{56,72},{64,... | collective-permute-start | bytes 393224 | tf_op jit(solution)/shard_map/ppermute | solution.py:31
  181.8 1.7 fusion.104
  183.4 1.3 collective-permute-start.6
  184.7 4.0 collective-permute-start.12
  188.7 1.3 collective-permute-start.13
  190.0 1.7 fusion.103
  191.7 1.7 convolution_bitcast_fusion.6
  194.9 1.3 collective-permute-start.7
  201.8 5.6 all-to-all-start.6
  209.4 7.5 all-to-all-done.6
  219.5 1.2 fusion.20
  220.9 4.4 all-to-all-start.7
  226.1 1.5 fusion.22
  228.6 264.3 %all-reduce.13.cloned.1.call-done = (f32[3,64,64]{2,1,0:T(8,128)}, f32[3,64,64]{2,1,0:T(8,128)}) async-done(((f32[3,64,64]{2,1,0:T(8,128)}, f32[3,64,64]{2,1,0:T(8,128)}), (f32[3,64,64]{2,1,0:T(8,128)}, f32[3,64,64]{2,1,0:T(8,128)})) %all-reduce.13.cloned.1.call-update) | async-done | bytes 98320 | tf_op jit(solution)/shard_map/psum | solution.py:320
  493.0 1.5 broadcast_multiply_fusion.3
  494.5 1.5 broadcast_multiply_fusion.2
  496.2 1.6 multiply_convert_fusion
  500.5 3.2 collective-permute-start.14
  503.7 1.3 collective-permute-start.15
  506.4 1.9 collective-permute-done.15
  512.0 1.1 fusion.24
  513.1 247.7 %all-reduce.15.cloned.1.call-done = (f32[3,3,64,64]{3,2,1,0:T(8,128)}, f32[3,3,64,64]{3,2,1,0:T(8,128)}) async-done(((f32[3,3,64,64]{3,2,1,0:T(8,128)}, f32[3,3,64,64]{3,2,1,0:T(8,128)}), (f32[3,3,64,64]{3,2,1,0:T(8,128)}, f32[3,3,64,64]{3,2,1,0:T(8,128)})) %all-reduce.15.cloned.1.call-update) | async-done | bytes 294928 | tf_op jit(solution)/shard_map/psum | solution.py:320
  760.8 1.7 broadcast_multiply_fusion.1
  762.5 1.7 broadcast_multiply_fusion
  (241 shorter events, 63.4 us)
Async XLA Ops:
  7.2 6.2 copy-start
  7.2 28.1 %copy-start.28 = (s32[32,16]{0,1:T(8,128)S(1)}, s32[32,16]{0,1:T(8,128)}, u32[]{:S(2)}) copy-start(s32[32,16]{0,1:T(8,128)} %param.19) | copy-start | bytes 6148
  7.2 22.8 %copy-start.18 = (bf16[2,16,64,128]{3,2,1,0:T(8,128)(2,1)S(1)}, bf16[2,16,64,128]{3,2,1,0:T(8,128)(2,1)}, u32[]{:S(2)}) copy-start(bf16[2,16,64,128]{3,2,1,0:T(8,128)(2,1)} %param.22) | copy-start | bytes 1572868
  7.2 28.1 %copy-start.36 = (s32[32,16]{0,1:T(8,128)S(1)}, s32[32,16]{0,1:T(8,128)}, u32[]{:S(2)}) copy-start(s32[32,16]{0,1:T(8,128)} %param.20) | copy-start | bytes 6148
  8.1 31.7 %collective-permute-start = (bf16[2,1,64,128]{3,2,1,0:T(8,128)(2,1)S(1)}, bf16[2,1,64,128]{3,2,1,0:T(8,128)(2,1)S(1)}, u32[]{:S(2)}, u32[]{:S(2)}) collective-permute-start(bf16[2,1,64,128]{3,2,1,0:T(8,128)(2,1)S(1)} %get-tuple-element.75), channel_id=1, source_target_pairs={{0,8},{8,16},{16,24},{24,32},{32,40},{40,48},{48,56},{56,64},{64,7... | collective-permute-start | bytes 98312 | tf_op jit(solution)/shard_map/ppermute | solution.py:19
  12.1 29.0 %collective-permute-start.1 = (bf16[2,1,64,128]{3,2,1,0:T(8,128)(2,1)S(1)}, bf16[2,1,64,128]{3,2,1,0:T(8,128)(2,1)S(1)}, u32[]{:S(2)}, u32[]{:S(2)}) collective-permute-start(bf16[2,1,64,128]{3,2,1,0:T(8,128)(2,1)S(1)} %get-tuple-element.76), channel_id=1, source_target_pairs={{8,0},{16,8},{24,16},{32,24},{40,32},{48,40},{56,48},{64,56},{72,6... | collective-permute-start | bytes 98312 | tf_op jit(solution)/shard_map/ppermute | solution.py:21
  13.6 2.7 copy-start.38
  16.0 25.0 %copy-start.4 = (bf16[2,16,64,128]{3,2,1,0:T(8,128)(2,1)S(1)}, bf16[2,16,64,128]{3,2,1,0:T(8,128)(2,1)}, u32[]{:S(2)}) copy-start(bf16[2,16,64,128]{3,2,1,0:T(8,128)(2,1)} %param.14) | copy-start | bytes 1572868
  16.8 18.4 %copy-start.37 = (pred[16,4]{0,1:T(4,128)(4,1)}, pred[16,4]{0,1:T(4,128)(4,1)S(1)}, u32[]{:S(2)}) copy-start(pred[16,4]{0,1:T(4,128)(4,1)S(1)} %compare_and_fusion.10) | copy-start | bytes 196
  19.4 63.6 %collective-permute-start.8 = (bf16[2,1,4,64,128]{4,2,1,3,0:T(4,128)(2,1)S(1)}, bf16[2,1,4,64,128]{4,2,1,3,0:T(4,128)(2,1)}, u32[]{:S(2)}, u32[]{:S(2)}) collective-permute-start(bf16[2,1,4,64,128]{4,2,1,3,0:T(4,128)(2,1)S(1)} %fusion.102), channel_id=1, source_target_pairs={{16,0},{24,8},{32,16},{40,24},{48,32},{56,40},{64,48},{72,56},{80,... | collective-permute-start | bytes 393224 | tf_op jit(solution)/shard_map/ppermute | solution.py:31
  23.1 59.9 %collective-permute-start.11 = (bf16[2,1,4,64,128]{4,2,1,3,0:T(4,128)(2,1)}, bf16[2,1,4,64,128]{4,2,1,3,0:T(4,128)(2,1)}, u32[]{:S(2)}, u32[]{:S(2)}) collective-permute-start(bf16[2,1,4,64,128]{4,2,1,3,0:T(4,128)(2,1)} %fusion.99), channel_id=1, source_target_pairs={{0,16},{8,24},{16,32},{24,40},{32,48},{40,56},{48,64},{56,72},{64,... | collective-permute-start | bytes 393224 | tf_op jit(solution)/shard_map/ppermute | solution.py:31
  31.4 51.6 %collective-permute-start.10 = (bf16[2,1,4,64,128]{4,2,1,3,0:T(4,128)(2,1)}, bf16[2,1,4,64,128]{4,2,1,3,0:T(4,128)(2,1)}, u32[]{:S(2)}, u32[]{:S(2)}) collective-permute-start(bf16[2,1,4,64,128]{4,2,1,3,0:T(4,128)(2,1)} %fusion.100), channel_id=1, source_target_pairs={{0,8},{8,16},{16,24},{24,32},{32,40},{40,48},{48,56},{56,64},{64,7... | collective-permute-start | bytes 393224 | tf_op jit(solution)/shard_map/ppermute | solution.py:31
  35.3 6.4 copy-start.16
  39.8 2.3 copy-start.23
  39.8 43.2 %collective-permute-start.9 = (bf16[2,1,4,64,128]{4,2,1,3,0:T(4,128)(2,1)}, bf16[2,1,4,64,128]{4,2,1,3,0:T(4,128)(2,1)}, u32[]{:S(2)}, u32[]{:S(2)}) collective-permute-start(bf16[2,1,4,64,128]{4,2,1,3,0:T(4,128)(2,1)} %fusion.101), channel_id=1, source_target_pairs={{8,0},{16,8},{24,16},{32,24},{40,32},{48,40},{56,48},{64,56},{72,6... | collective-permute-start | bytes 393224 | tf_op jit(solution)/shard_map/ppermute | solution.py:31
  41.1 3.2 copy-start.29
  46.6 15.9 %copy-start.21 = (bf16[3,64,64]{2,1,0:T(8,128)(2,1)S(1)}, bf16[3,64,64]{2,1,0:T(8,128)(2,1)}, u32[]{:S(2)}) copy-start(bf16[3,64,64]{2,1,0:T(8,128)(2,1)} %param.16) | copy-start | bytes 73732
  46.6 15.9 %all-to-all-start = ((bf16[2,16,64,128]{3,2,0,1:T(8,128)(2,1)}), bf16[2,16,64,128]{3,2,0,1:T(8,128)(2,1)S(1)}, u32[]{:S(2)}, u32[]{:S(2)}) async-start(bf16[2,16,64,128]{3,2,0,1:T(8,128)(2,1)} %copy.213), calls=%async_computation | async-start | bytes 1048576 | tf_op jit(solution)/shard_map/all_to_all | solution.py:52
  62.5 0.8 copy-start.6
  64.9 13.8 %all-to-all-start.1 = ((bf16[16,2,64,128]{3,2,1,0:T(8,128)(2,1)}), bf16[16,2,64,128]{3,2,1,0:T(8,128)(2,1)S(1)}, u32[]{:S(2)}, u32[]{:S(2)}) async-start(bf16[16,2,64,128]{3,2,1,0:T(8,128)(2,1)} %get-tuple-element.88), calls=%async_computation.1 | async-start | bytes 1048576 | tf_op jit(solution)/shard_map/all_to_all | solution.py:56
  78.7 13.0 %collective-permute-start.2 = (bf16[2,1,64,128]{3,2,1,0:T(8,128)(2,1)S(1)}, bf16[2,1,64,128]{3,2,1,0:T(8,128)(2,1)S(1)}, u32[]{:S(2)}, u32[]{:S(2)}) collective-permute-start(bf16[2,1,64,128]{3,2,1,0:T(8,128)(2,1)S(1)} %get-tuple-element.73), channel_id=1, source_target_pairs={{0,8},{8,16},{16,24},{24,32},{32,40},{40,48},{48,56},{56,64},{64,7... | collective-permute-start | bytes 98312 | tf_op jit(solution)/shard_map/ppermute | solution.py:19
  84.8 6.9 copy-start.15
  85.8 15.5 %all-to-all-start.4 = ((bf16[2,16,64,128]{3,2,0,1:T(8,128)(2,1)}), bf16[2,16,64,128]{3,2,0,1:T(8,128)(2,1)S(1)}, u32[]{:S(2)}, u32[]{:S(2)}) async-start(bf16[2,16,64,128]{3,2,0,1:T(8,128)(2,1)} %copy.234), calls=%async_computation.4 | async-start | bytes 1048576 | tf_op jit(solution)/shard_map/all_to_all | solution.py:52
  90.4 4.9 collective-permute-start.3
  95.4 3.6 copy-start.31
  101.3 15.1 %all-to-all-start.2 = ((bf16[2,16,64,128]{3,2,0,1:T(8,128)(2,1)}), bf16[2,16,64,128]{3,2,0,1:T(8,128)(2,1)}, u32[]{:S(2)}, u32[]{:S(2)}) async-start(bf16[2,16,64,128]{3,2,0,1:T(8,128)(2,1)} %copy.216), calls=%async_computation.2 | async-start | bytes 1048576 | tf_op jit(solution)/shard_map/all_to_all | solution.py:52
  116.5 2.1 copy-start.20
  118.5 1.2 copy-start.10
  123.2 14.5 %all-to-all-start.5 = ((bf16[16,2,64,128]{3,2,1,0:T(8,128)(2,1)}), bf16[16,2,64,128]{3,2,1,0:T(8,128)(2,1)}, u32[]{:S(2)}, u32[]{:S(2)}) async-start(bf16[16,2,64,128]{3,2,1,0:T(8,128)(2,1)} %fusion.19), calls=%async_computation.5 | async-start | bytes 1048576 | tf_op jit(solution)/shard_map/all_to_all | solution.py:56
  128.2 2.7 copy-start.9
  137.7 14.5 %all-to-all-start.3 = ((bf16[16,2,64,128]{3,2,1,0:T(8,128)(2,1)}), bf16[16,2,64,128]{3,2,1,0:T(8,128)(2,1)}, u32[]{:S(2)}, u32[]{:S(2)}) async-start(bf16[16,2,64,128]{3,2,1,0:T(8,128)(2,1)} %get-tuple-element.68), calls=%async_computation.3 | async-start | bytes 1048576 | tf_op jit(solution)/shard_map/all_to_all | solution.py:56
  142.6 1.4 copy-start.14
  143.9 1.0 copy-start.2
  153.7 0.8 copy-start.11
  164.9 28.4 %copy-start.26 = (bf16[2,1,64,128]{3,2,1,0:T(8,128)(2,1)S(1)}, bf16[2,1,64,128]{3,2,1,0:T(8,128)(2,1)}, u32[]{:S(2)}) copy-start(bf16[2,1,64,128]{3,2,1,0:T(8,128)(2,1)} %copy-done.25) | copy-start | bytes 98308
  166.6 59.5 %collective-permute-start.5 = (bf16[2,1,4,64,128]{4,2,1,3,0:T(4,128)(2,1)}, bf16[2,1,4,64,128]{4,2,1,3,0:T(4,128)(2,1)}, u32[]{:S(2)}, u32[]{:S(2)}) collective-permute-start(bf16[2,1,4,64,128]{4,2,1,3,0:T(4,128)(2,1)} %fusion.105), channel_id=1, source_target_pairs={{0,8},{8,16},{16,24},{24,32},{32,40},{40,48},{48,56},{56,64},{64,7... | collective-permute-start | bytes 393224 | tf_op jit(solution)/shard_map/ppermute | solution.py:31
  171.8 54.2 %collective-permute-start.4 = (bf16[2,1,4,64,128]{4,2,1,3,0:T(4,128)(2,1)}, bf16[2,1,4,64,128]{4,2,1,3,0:T(4,128)(2,1)}, u32[]{:S(2)}, u32[]{:S(2)}) collective-permute-start(bf16[2,1,4,64,128]{4,2,1,3,0:T(4,128)(2,1)} %fusion.106), channel_id=1, source_target_pairs={{0,16},{8,24},{16,32},{24,40},{32,48},{40,56},{48,64},{56,72},{64,... | collective-permute-start | bytes 393224 | tf_op jit(solution)/shard_map/ppermute | solution.py:31
  183.4 42.7 %collective-permute-start.6 = (bf16[2,1,4,64,128]{4,2,1,3,0:T(4,128)(2,1)}, bf16[2,1,4,64,128]{4,2,1,3,0:T(4,128)(2,1)}, u32[]{:S(2)}, u32[]{:S(2)}) collective-permute-start(bf16[2,1,4,64,128]{4,2,1,3,0:T(4,128)(2,1)} %fusion.104), channel_id=1, source_target_pairs={{8,0},{16,8},{24,16},{32,24},{40,32},{48,40},{56,48},{64,56},{72,6... | collective-permute-start | bytes 393224 | tf_op jit(solution)/shard_map/ppermute | solution.py:31
  184.7 10.2 %collective-permute-start.12 = (bf16[2,1,64,128]{3,2,1,0:T(8,128)(2,1)}, bf16[2,1,64,128]{3,2,1,0:T(8,128)(2,1)S(1)}, u32[]{:S(2)}, u32[]{:S(2)}) collective-permute-start(bf16[2,1,64,128]{3,2,1,0:T(8,128)(2,1)} %get-tuple-element.71), channel_id=1, source_target_pairs={{0,8},{8,16},{16,24},{24,32},{32,40},{40,48},{48,56},{56,64},{64,7... | collective-permute-start | bytes 98312 | tf_op jit(solution)/shard_map/ppermute | solution.py:19
  188.7 7.5 collective-permute-start.13
  191.7 2.6 copy-start.27
  191.7 2.6 copy-start.33
  191.7 2.6 copy-start.34
  194.9 31.2 %collective-permute-start.7 = (bf16[2,1,4,64,128]{4,2,1,3,0:T(4,128)(2,1)}, bf16[2,1,4,64,128]{4,2,1,3,0:T(4,128)(2,1)}, u32[]{:S(2)}, u32[]{:S(2)}) collective-permute-start(bf16[2,1,4,64,128]{4,2,1,3,0:T(4,128)(2,1)} %fusion.103), channel_id=1, source_target_pairs={{16,0},{24,8},{32,16},{40,24},{48,32},{56,40},{64,48},{72,56},{80,... | collective-permute-start | bytes 393224 | tf_op jit(solution)/shard_map/ppermute | solution.py:31
  199.4 1.2 copy-start.3
  201.8 6.7 copy-start.32
  201.8 6.8 copy-start.19
  201.8 15.0 %all-to-all-start.6 = ((bf16[2,16,64,128]{3,2,0,1:T(8,128)(2,1)}), bf16[2,16,64,128]{3,2,0,1:T(8,128)(2,1)S(1)}, u32[]{:S(2)}, u32[]{:S(2)}) async-start(bf16[2,16,64,128]{3,2,0,1:T(8,128)(2,1)} %copy.249), calls=%async_computation.6 | async-start | bytes 1048576 | tf_op jit(solution)/shard_map/all_to_all | solution.py:52
  207.5 1.1 copy-start.35
  208.6 8.4 %copy-start.13 = (f32[16,2,64,128]{3,2,1,0:T(8,128)S(1)}, f32[16,2,64,128]{3,2,1,0:T(8,128)}, u32[]{:S(2)}) copy-start(f32[16,2,64,128]{3,2,1,0:T(8,128)} %get-tuple-element.89) | copy-start | bytes 3145732
  217.0 1.0 copy-start.7
  218.0 0.8 copy-start.22
  220.7 5.5 copy-start.12
  220.7 5.5 copy-start.40
  220.9 275.1 %all-to-all-start.7 = ((bf16[16,2,64,128]{3,2,1,0:T(8,128)(2,1)}), bf16[16,2,64,128]{3,2,1,0:T(8,128)(2,1)S(1)}, u32[]{:S(2)}, u32[]{:S(2)}) async-start(bf16[16,2,64,128]{3,2,1,0:T(8,128)(2,1)} %fusion.20), calls=%async_computation.7 | async-start | bytes 1048576 | tf_op jit(solution)/shard_map/all_to_all | solution.py:56
  225.3 267.6 %all-reduce.13.cloned.1.call-start = ((), (), s32[]{:S(2)}) async-start(), calls=%async_computation.8 | async-start | bytes 393216 | tf_op jit(solution)/shard_map/psum | solution.py:320
  226.0 534.8 %all-reduce.15.cloned.1.call-start = ((), (), s32[]{:S(2)}) async-start(), calls=%async_computation.9 | async-start | bytes 1179648 | tf_op jit(solution)/shard_map/psum | solution.py:320
  497.8 1.0 copy-start.5
  499.8 5.2 copy-start.30
  500.5 4.9 copy-start.24
  500.5 6.0 collective-permute-start.14
  503.7 4.7 collective-permute-start.15
  506.4 2.6 copy-start.17
  511.9 252.3 %copy-start.1 = (s32[32,16]{0,1:T(8,128)S(1)}, s32[32,16]{0,1:T(8,128)}, u32[]{:S(2)}) copy-start(s32[32,16]{0,1:T(8,128)} %param.21) | copy-start | bytes 6148
  (3 other events, 2.0 us)
Sparse Core Ops, SparseCore 0:
  232.3 260.6 all-reduce.12
  506.6 254.2 all-reduce.14
where the time goes:
time: 774 us; the launch traced here: 771 us
  waiting for transfers between devices  552 us (71%)
  starting transfers between devices  91.2 us (12%)
  matrix products  43.5 us (6%)
  other arithmetic  35 us (5%)
  local copies, waits for them, and re-layouts  34.1 us (4%)
  between operations  15.3 us (2%)
    psum x2, waiting for transfers between devices, shards(): lax.psum((grad_sa, gradient_kernel_first, grad_sb, gradient_kernel_second...  512 us
    ppermute x8, starting transfers between devices, from_behind(): return lax.ppermute(array, axis, pairs)  29.4 us
    all_to_all x4, starting transfers between devices, to_tiles(): lax.all_to_all(values, 'frame', split_axis=1, concat_axis=0, tiled=True)  22.5 us
    all_to_all x4, waiting for transfers between devices, to_tiles(): lax.all_to_all(values, 'frame', split_axis=1, concat_axis=0, tiled=True)  20.1 us
    all_to_all x4, starting transfers between devices, to_frames(): lax.all_to_all(values, 'frame', split_axis=0, concat_axis=1, tiled=True)  18.7 us
  transfers between devices with their start and end apart: 26, of which 10 were waited for; matrix products, arithmetic and copies ran while one was open for 10% of the time, Pallas kernels for 0%

commit v1 on v0

--- a/solution.py
+++ b/solution.py
@@ -244,6 +244,23 @@
     return jnp.einsum(
         "tqr,fqrcp->ftcp", matrix.astype(jnp.bfloat16), received, preferred_element_type=jnp.float32
     )
+
+
+def exchange_sum(parts, axes):
+    flat = jnp.concatenate([part.reshape(-1) for part in parts])
+    sizes = [lax.axis_size(axis) for axis in axes]
+    for axis, size in zip(axes, sizes):
+        pieces = flat.reshape(size, -1)
+        flat = jnp.sum(lax.all_to_all(pieces, axis, 0, 0, tiled=True), axis=0)
+    for axis, size in reversed(list(zip(axes, sizes))):
+        copies = jnp.broadcast_to(flat[None], (size,) + flat.shape)
+        flat = lax.all_to_all(copies, axis, 0, 0, tiled=True).reshape(-1)
+    results = []
+    start = 0
+    for part in parts:
+        results.append(flat[start : start + part.size].reshape(part.shape))
+        start += part.size
+    return results
 
 
 def shards(
@@ -317,8 +334,8 @@
     grad_features, grad_sa = spatial_backward(
         frames_grad_one, pre_one, padded_zero, spatial_a, chart_rim
     )
-    summed_sa, summed_ta, summed_sb, summed_tb = lax.psum(
-        (grad_sa, gradient_kernel_first, grad_sb, gradient_kernel_second), ("chart", "frame")
+    summed_sa, summed_ta, summed_sb, summed_tb = exchange_sum(
+        (grad_sa, gradient_kernel_first, grad_sb, gradient_kernel_second), ("frame", "chart")
     )
     pixel_frames = total_frames * strips * lax.axis_size("chart") * features.shape[3]
     grad_scale = float(pixel_frames) ** (-0.5)

time: 774 us -> 308 us (0.40)
  waiting for transfers between devices: 552 us -> 63 us
  starting transfers between devices: 91.2 us -> 131 us
  between operations: 15.3 us -> 1.99 us
  other arithmetic: 35 us -> 26.2 us
    psum x2 -> x0, waiting for transfers between devices: 512 us -> none  [shards(): lax.psum((grad_sa, gradient_kernel_first, grad_sb, gradient_kernel_second...]
    all_to_all x0 -> x4, starting transfers between devices: none -> 37.5 us  [the longest x2 25.2 us: exchange_sum(): flat = jnp.sum(lax.all_to_all(pieces, axis, 0, 0, tiled=True), axis=0)]
    all_to_all x0 -> x4, waiting for transfers between devices: none -> 17.7 us  [the longest x2 11.5 us: exchange_sum(): flat = lax.all_to_all(copies, axis, 0, 0, tiled=True).reshape(-1)]
  transfers between devices with their start and end apart: 26 -> 28, of which waited for: 10 -> 12; matrix products, arithmetic and copies ran while one was open for 10% -> 25% of each run, Pallas kernels for 0% -> 0%
where the time goes in v1:
time: 308 us; the launch traced here: 305 us
  starting transfers between devices  131 us (43%)
  waiting for transfers between devices  63 us (20%)
  matrix products  48.2 us (16%)
  local copies, waits for them, and re-layouts  35 us (11%)
  other arithmetic  26.2 us (9%)
    ppermute x8, starting transfers between devices, from_behind(): return lax.ppermute(array, axis, pairs)  29.5 us
    all_to_all x2, starting transfers between devices, exchange_sum(): flat = jnp.sum(lax.all_to_all(pieces, axis, 0, 0, tiled=True), axis=0)  25.2 us
    all_to_all x4, starting transfers between devices, to_tiles(): lax.all_to_all(values, 'frame', split_axis=1, concat_axis=0, tiled=True)  22.7 us
    all_to_all x4, waiting for transfers between devices, to_frames(): lax.all_to_all(values, 'frame', split_axis=0, concat_axis=1, tiled=True)  22.3 us
    all_to_all x4, waiting for transfers between devices, to_tiles(): lax.all_to_all(values, 'frame', split_axis=1, concat_axis=0, tiled=True)  19.4 us
    all_to_all x4, starting transfers between devices, to_frames(): lax.all_to_all(values, 'frame', split_axis=0, concat_axis=1, tiled=True)  18.7 us
    ppermute x4, starting transfers between devices, with_halo(): lax.ppermute(tail, axis, [(i, (i + 1) % count) for i in range(ends)])  17.2 us
    dot_general x18, matrix products, spatial_transpose(): jnp.einsum('oc,fsop->fscp', weight[row_tap, col_tap], padded[:, 2 - row_t...  12.8 us
  transfers between devices with their start and end apart: 28, of which 12 were waited for; matrix products, arithmetic and copies ran while one was open for 25% of the time, Pallas kernels for 0%

profile of v1, /device:TPU:1, one launch (start us, length us, event | category | flops | bytes accessed | tf_op | source)
XLA Modules:
  0.0 305.2 jit_solution(5829720955614478728)
XLA Ops:
  1.5 4.0 %collective-permute-start = (bf16[2,1,64,128]{3,2,1,0:T(8,128)(2,1)S(1)}, bf16[2,1,64,128]{3,2,1,0:T(8,128)(2,1)S(1)}, u32[]{:S(2)}, u32[]{:S(2)}) collective-permute-start(bf16[2,1,64,128]{3,2,1,0:T(8,128)(2,1)S(1)} %get-tuple-element.81), channel_id=1, source_target_pairs={{0,8},{8,16},{16,24},{24,32},{32,40},{40,48},{48,56},{56,64},{64,7... | collective-permute-start | bytes 98312 | tf_op jit(solution)/shard_map/ppermute | solution.py:19
  5.5 1.3 collective-permute-start.1
  11.1 1.6 gather_fusion.6
  12.9 1.3 collective-permute-start.8
  14.2 1.6 gather_fusion.9
  15.9 6.9 %collective-permute-start.11 = (bf16[2,1,4,64,128]{4,2,1,3,0:T(4,128)(2,1)S(1)}, bf16[2,1,4,64,128]{4,2,1,3,0:T(4,128)(2,1)}, u32[]{:S(2)}, u32[]{:S(2)}) collective-permute-start(bf16[2,1,4,64,128]{4,2,1,3,0:T(4,128)(2,1)S(1)} %fusion.101), channel_id=1, source_target_pairs={{0,16},{8,24},{16,32},{24,40},{32,48},{40,56},{48,64},{56,72},{64,... | collective-permute-start | bytes 393224 | tf_op jit(solution)/shard_map/ppermute | solution.py:31
  23.5 3.9 %collective-permute-start.10 = (bf16[2,1,4,64,128]{4,2,1,3,0:T(4,128)(2,1)S(1)}, bf16[2,1,4,64,128]{4,2,1,3,0:T(4,128)(2,1)}, u32[]{:S(2)}, u32[]{:S(2)}) collective-permute-start(bf16[2,1,4,64,128]{4,2,1,3,0:T(4,128)(2,1)S(1)} %fusion.102), channel_id=1, source_target_pairs={{0,8},{8,16},{16,24},{24,32},{32,40},{40,48},{48,56},{56,64},{64,7... | collective-permute-start | bytes 393224 | tf_op jit(solution)/shard_map/ppermute | solution.py:31
  31.2 1.3 collective-permute-start.9
  35.7 1.5 add_convert_fusion.3
  38.0 6.5 %all-to-all-start = ((bf16[2,16,64,128]{3,2,0,1:T(8,128)(2,1)}), bf16[2,16,64,128]{3,2,0,1:T(8,128)(2,1)S(1)}, u32[]{:S(2)}, u32[]{:S(2)}) async-start(bf16[2,16,64,128]{3,2,0,1:T(8,128)(2,1)} %copy.265), calls=%async_computation | async-start | bytes 1048576 | tf_op jit(solution)/shard_map/all_to_all | solution.py:52
  46.1 7.7 %all-to-all-done = bf16[2,16,64,128]{3,2,0,1:T(8,128)(2,1)S(1)} async-done(((bf16[2,16,64,128]{3,2,0,1:T(8,128)(2,1)}), bf16[2,16,64,128]{3,2,0,1:T(8,128)(2,1)S(1)}, u32[]{:S(2)}, u32[]{:S(2)}) %all-to-all-start) | async-done | bytes 524320 | tf_op jit(solution)/shard_map/all_to_all | solution.py:52
  54.7 1.6 add_convert_fusion.2
  56.3 4.4 %all-to-all-start.1 = ((bf16[16,2,64,128]{3,2,1,0:T(8,128)(2,1)}), bf16[16,2,64,128]{3,2,1,0:T(8,128)(2,1)S(1)}, u32[]{:S(2)}, u32[]{:S(2)}) async-start(bf16[16,2,64,128]{3,2,1,0:T(8,128)(2,1)} %get-tuple-element.94), calls=%async_computation.1 | async-start | bytes 1048576 | tf_op jit(solution)/shard_map/all_to_all | solution.py:56
  62.2 7.9 %all-to-all-done.1 = bf16[16,2,64,128]{3,2,1,0:T(8,128)(2,1)S(1)} async-done(((bf16[16,2,64,128]{3,2,1,0:T(8,128)(2,1)}), bf16[16,2,64,128]{3,2,1,0:T(8,128)(2,1)S(1)}, u32[]{:S(2)}, u32[]{:S(2)}) %all-to-all-start.1) | async-done | bytes 524320 | tf_op jit(solution)/shard_map/all_to_all | solution.py:56
  70.7 4.3 %collective-permute-start.2 = (bf16[2,1,64,128]{3,2,1,0:T(8,128)(2,1)}, bf16[2,1,64,128]{3,2,1,0:T(8,128)(2,1)S(1)}, u32[]{:S(2)}, u32[]{:S(2)}) collective-permute-start(bf16[2,1,64,128]{3,2,1,0:T(8,128)(2,1)} %get-tuple-element.79), channel_id=1, source_target_pairs={{0,8},{8,16},{16,24},{24,32},{32,40},{40,48},{48,56},{56,64},{64,7... | collective-permute-start | bytes 98312 | tf_op jit(solution)/shard_map/ppermute | solution.py:19
  75.1 1.7 fusion.21
  77.8 4.6 %all-to-all-start.4 = ((bf16[2,16,64,128]{3,2,0,1:T(8,128)(2,1)}), bf16[2,16,64,128]{3,2,0,1:T(8,128)(2,1)S(1)}, u32[]{:S(2)}, u32[]{:S(2)}) async-start(bf16[2,16,64,128]{3,2,0,1:T(8,128)(2,1)} %copy.286), calls=%async_computation.4 | async-start | bytes 1048576 | tf_op jit(solution)/shard_map/all_to_all | solution.py:52
  82.4 1.3 collective-permute-start.3
  84.3 3.0 collective-permute-done.3
  87.3 1.4 select_maximum_fusion.4
  91.0 1.5 add_convert_fusion.1
  93.3 5.7 %all-to-all-start.2 = ((bf16[2,16,64,128]{3,2,0,1:T(8,128)(2,1)}), bf16[2,16,64,128]{3,2,0,1:T(8,128)(2,1)}, u32[]{:S(2)}, u32[]{:S(2)}) async-start(bf16[2,16,64,128]{3,2,0,1:T(8,128)(2,1)} %copy.268), calls=%async_computation.2 | async-start | bytes 1048576 | tf_op jit(solution)/shard_map/all_to_all | solution.py:52
  99.0 1.2 pad_clamp_fusion.8
  100.8 1.5 fusion.212
  103.4 5.1 %all-to-all-done.2 = bf16[2,16,64,128]{3,2,0,1:T(8,128)(2,1)} async-done(((bf16[2,16,64,128]{3,2,0,1:T(8,128)(2,1)}), bf16[2,16,64,128]{3,2,0,1:T(8,128)(2,1)}, u32[]{:S(2)}, u32[]{:S(2)}) %all-to-all-start.2) | async-done | bytes 524320 | tf_op jit(solution)/shard_map/all_to_all | solution.py:52
  111.8 1.5 fusion.26
  115.2 5.0 %all-to-all-start.5 = ((bf16[16,2,64,128]{3,2,1,0:T(8,128)(2,1)}), bf16[16,2,64,128]{3,2,1,0:T(8,128)(2,1)}, u32[]{:S(2)}, u32[]{:S(2)}) async-start(bf16[16,2,64,128]{3,2,1,0:T(8,128)(2,1)} %fusion.19), calls=%async_computation.5 | async-start | bytes 1048576 | tf_op jit(solution)/shard_map/all_to_all | solution.py:56
  120.2 1.4 convolution_bitcast_fusion.2
  121.6 1.3 convolution_bitcast_fusion.4
  123.9 5.8 %all-to-all-done.5 = bf16[16,2,64,128]{3,2,1,0:T(8,128)(2,1)} async-done(((bf16[16,2,64,128]{3,2,1,0:T(8,128)(2,1)}), bf16[16,2,64,128]{3,2,1,0:T(8,128)(2,1)}, u32[]{:S(2)}, u32[]{:S(2)}) %all-to-all-start.5) | async-done | bytes 524320 | tf_op jit(solution)/shard_map/all_to_all | solution.py:56
  129.7 5.0 %all-to-all-start.3 = ((bf16[16,2,64,128]{3,2,1,0:T(8,128)(2,1)}), bf16[16,2,64,128]{3,2,1,0:T(8,128)(2,1)}, u32[]{:S(2)}, u32[]{:S(2)}) async-start(bf16[16,2,64,128]{3,2,1,0:T(8,128)(2,1)} %get-tuple-element.74), calls=%async_computation.3 | async-start | bytes 1048576 | tf_op jit(solution)/shard_map/all_to_all | solution.py:56
  134.7 1.2 copy.291
  144.1 1.6 copy.270
  146.6 1.3 gather_fusion.4
  147.9 1.3 gather_fusion.3
  149.3 1.3 gather_fusion.2
  150.6 1.7 fusion.107
  152.3 3.7 %collective-permute-start.5 = (bf16[2,1,4,64,128]{4,2,1,3,0:T(4,128)(2,1)}, bf16[2,1,4,64,128]{4,2,1,3,0:T(4,128)(2,1)}, u32[]{:S(2)}, u32[]{:S(2)}) collective-permute-start(bf16[2,1,4,64,128]{4,2,1,3,0:T(4,128)(2,1)} %fusion.107), channel_id=1, source_target_pairs={{0,8},{8,16},{16,24},{24,32},{32,40},{40,48},{48,56},{56,64},{64,7... | collective-permute-start | bytes 393224 | tf_op jit(solution)/shard_map/ppermute | solution.py:31
  156.0 1.7 fusion.108
  157.6 9.9 %collective-permute-start.4 = (bf16[2,1,4,64,128]{4,2,1,3,0:T(4,128)(2,1)}, bf16[2,1,4,64,128]{4,2,1,3,0:T(4,128)(2,1)}, u32[]{:S(2)}, u32[]{:S(2)}) collective-permute-start(bf16[2,1,4,64,128]{4,2,1,3,0:T(4,128)(2,1)} %fusion.108), channel_id=1, source_target_pairs={{0,16},{8,24},{16,32},{24,40},{32,48},{40,56},{48,64},{56,72},{64,... | collective-permute-start | bytes 393224 | tf_op jit(solution)/shard_map/ppermute | solution.py:31
  167.6 1.7 fusion.106
  169.2 1.3 collective-permute-start.6
  170.5 4.0 %collective-permute-start.12 = (bf16[2,1,64,128]{3,2,1,0:T(8,128)(2,1)}, bf16[2,1,64,128]{3,2,1,0:T(8,128)(2,1)S(1)}, u32[]{:S(2)}, u32[]{:S(2)}) collective-permute-start(bf16[2,1,64,128]{3,2,1,0:T(8,128)(2,1)} %get-tuple-element.77), channel_id=1, source_target_pairs={{0,8},{8,16},{16,24},{24,32},{32,40},{40,48},{48,56},{56,64},{64,7... | collective-permute-start | bytes 98312 | tf_op jit(solution)/shard_map/ppermute | solution.py:19
  174.5 1.3 collective-permute-start.13
  175.8 1.4 fusion.105
  179.9 1.3 collective-permute-start.7
  186.8 5.9 %all-to-all-start.6 = ((bf16[2,16,64,128]{3,2,0,1:T(8,128)(2,1)}), bf16[2,16,64,128]{3,2,0,1:T(8,128)(2,1)S(1)}, u32[]{:S(2)}, u32[]{:S(2)}) async-start(bf16[2,16,64,128]{3,2,0,1:T(8,128)(2,1)} %copy.301), calls=%async_computation.6 | async-start | bytes 1048576 | tf_op jit(solution)/shard_map/all_to_all | solution.py:52
  193.0 1.5 fusion.22
  195.5 6.6 %all-to-all-done.6 = bf16[2,16,64,128]{3,2,0,1:T(8,128)(2,1)S(1)} async-done(((bf16[2,16,64,128]{3,2,0,1:T(8,128)(2,1)}), bf16[2,16,64,128]{3,2,0,1:T(8,128)(2,1)S(1)}, u32[]{:S(2)}, u32[]{:S(2)}) %all-to-all-start.6) | async-done | bytes 524320 | tf_op jit(solution)/shard_map/all_to_all | solution.py:52
  204.9 4.4 %all-to-all-start.7 = ((bf16[16,2,64,128]{3,2,1,0:T(8,128)(2,1)}), bf16[16,2,64,128]{3,2,1,0:T(8,128)(2,1)S(1)}, u32[]{:S(2)}, u32[]{:S(2)}) async-start(bf16[16,2,64,128]{3,2,1,0:T(8,128)(2,1)} %fusion.20), calls=%async_computation.7 | async-start | bytes 1048576 | tf_op jit(solution)/shard_map/all_to_all | solution.py:56
  210.2 8.4 %all-to-all-done.7 = bf16[16,2,64,128]{3,2,1,0:T(8,128)(2,1)S(1)} async-done(((bf16[16,2,64,128]{3,2,1,0:T(8,128)(2,1)}), bf16[16,2,64,128]{3,2,1,0:T(8,128)(2,1)S(1)}, u32[]{:S(2)}, u32[]{:S(2)}) %all-to-all-start.7) | async-done | bytes 524320 | tf_op jit(solution)/shard_map/all_to_all | solution.py:56
  218.8 1.6 multiply_convert_fusion
  224.3 1.3 collective-permute-start.15
  226.4 4.3 %all-to-all-start.8 = ((f32[8,1,12288]{2,1,0:T(1,128)}), f32[8,1,12288]{2,1,0:T(1,128)S(1)}, u32[]{:S(2)}, u32[]{:S(2)}) async-start(f32[8,1,12288]{2,1,0:T(1,128)} %bitcast.257), calls=%async_computation.8 | async-start | bytes 786432 | tf_op jit(solution)/shard_map/all_to_all | solution.py:254
  230.7 4.9 %collective-permute-start.14 = (bf16[2,1,64,128]{3,2,1,0:T(8,128)(2,1)S(1)}, bf16[2,1,64,128]{3,2,1,0:T(8,128)(2,1)S(1)}, u32[]{:S(2)}, u32[]{:S(2)}) collective-permute-start(bf16[2,1,64,128]{3,2,1,0:T(8,128)(2,1)S(1)} %get-tuple-element.75), channel_id=1, source_target_pairs={{0,8},{8,16},{16,24},{24,32},{32,40},{40,48},{48,56},{56,64},{64,7... | collective-permute-start | bytes 98312 | tf_op jit(solution)/shard_map/ppermute | solution.py:19
  238.4 1.4 convolution_add_fusion.26
  240.7 20.9 %all-to-all-start.9 = ((f32[32,1,384]{2,1,0:T(1,128)}), f32[32,1,384]{2,1,0:T(1,128)S(1)}, u32[]{:S(2)}, u32[]{:S(2)}) async-start(f32[32,1,384]{2,1,0:T(1,128)} %bitcast.258), calls=%async_computation.9 | async-start | bytes 98304 | tf_op jit(solution)/shard_map/all_to_all | solution.py:254
  261.6 2.6 convolution_add_fusion.25
  264.2 6.2 %all-to-all-done.9 = f32[32,1,384]{2,1,0:T(1,128)S(1)} async-done(((f32[32,1,384]{2,1,0:T(1,128)}), f32[32,1,384]{2,1,0:T(1,128)S(1)}, u32[]{:S(2)}, u32[]{:S(2)}) %all-to-all-start.9) | async-done | bytes 49184 | tf_op jit(solution)/shard_map/all_to_all | solution.py:254
  271.1 3.9 %all-to-all-start.10 = ((f32[32,1,384]{2,1,0:T(1,128)}), f32[32,1,384]{2,1,0:T(1,128)S(1)}, u32[]{:S(2)}, u32[]{:S(2)}) async-start(f32[32,1,384]{2,1,0:T(1,128)} %broadcast_in_dim.95), calls=%async_computation.10 | async-start | bytes 98304 | tf_op jit(solution)/shard_map/all_to_all | solution.py:257
  274.9 2.6 convolution_add_fusion.24
  277.5 6.1 %all-to-all-done.10 = f32[32,1,384]{2,1,0:T(1,128)S(1)} async-done(((f32[32,1,384]{2,1,0:T(1,128)}), f32[32,1,384]{2,1,0:T(1,128)S(1)}, u32[]{:S(2)}, u32[]{:S(2)}) %all-to-all-start.10) | async-done | bytes 49184 | tf_op jit(solution)/shard_map/all_to_all | solution.py:257
  284.6 8.4 %all-to-all-start.11 = ((f32[8,1,12288]{2,1,0:T(1,128)}), f32[8,1,12288]{2,1,0:T(1,128)S(1)}, u32[]{:S(2)}, u32[]{:S(2)}) async-start(f32[8,1,12288]{2,1,0:T(1,128)} %broadcast_in_dim.97), calls=%async_computation.11 | async-start | bytes 786432 | tf_op jit(solution)/shard_map/all_to_all | solution.py:257
  295.4 5.3 %all-to-all-done.11 = f32[8,1,12288]{2,1,0:T(1,128)S(1)} async-done(((f32[8,1,12288]{2,1,0:T(1,128)}), f32[8,1,12288]{2,1,0:T(1,128)S(1)}, u32[]{:S(2)}, u32[]{:S(2)}) %all-to-all-start.11) | async-done | bytes 393248 | tf_op jit(solution)/shard_map/all_to_all | solution.py:257
  (258 shorter events, 69.5 us)
Async XLA Ops:
  0.6 6.2 %copy-start = (s32[32,16]{0,1:T(8,128)S(1)}, s32[32,16]{0,1:T(8,128)}, u32[]{:S(2)}) copy-start(s32[32,16]{0,1:T(8,128)} %param.21) | copy-start | bytes 6148
  0.6 26.8 %copy-start.27 = (s32[32,16]{0,1:T(8,128)S(1)}, s32[32,16]{0,1:T(8,128)}, u32[]{:S(2)}) copy-start(s32[32,16]{0,1:T(8,128)} %param.19) | copy-start | bytes 6148
  0.7 22.1 %copy-start.17 = (bf16[2,16,64,128]{3,2,1,0:T(8,128)(2,1)S(1)}, bf16[2,16,64,128]{3,2,1,0:T(8,128)(2,1)}, u32[]{:S(2)}) copy-start(bf16[2,16,64,128]{3,2,1,0:T(8,128)(2,1)} %param.22) | copy-start | bytes 1572868
  0.7 26.8 %copy-start.38 = (s32[32,16]{0,1:T(8,128)S(1)}, s32[32,16]{0,1:T(8,128)}, u32[]{:S(2)}) copy-start(s32[32,16]{0,1:T(8,128)} %param.20) | copy-start | bytes 6148
  1.5 29.7 %collective-permute-start = (bf16[2,1,64,128]{3,2,1,0:T(8,128)(2,1)S(1)}, bf16[2,1,64,128]{3,2,1,0:T(8,128)(2,1)S(1)}, u32[]{:S(2)}, u32[]{:S(2)}) collective-permute-start(bf16[2,1,64,128]{3,2,1,0:T(8,128)(2,1)S(1)} %get-tuple-element.81), channel_id=1, source_target_pairs={{0,8},{8,16},{16,24},{24,32},{32,40},{40,48},{48,56},{56,64},{64,7... | collective-permute-start | bytes 98312 | tf_op jit(solution)/shard_map/ppermute | solution.py:19
  5.5 27.0 %collective-permute-start.1 = (bf16[2,1,64,128]{3,2,1,0:T(8,128)(2,1)S(1)}, bf16[2,1,64,128]{3,2,1,0:T(8,128)(2,1)S(1)}, u32[]{:S(2)}, u32[]{:S(2)}) collective-permute-start(bf16[2,1,64,128]{3,2,1,0:T(8,128)(2,1)S(1)} %get-tuple-element.82), channel_id=1, source_target_pairs={{8,0},{16,8},{24,16},{32,24},{40,32},{48,40},{56,48},{64,56},{72,6... | collective-permute-start | bytes 98312 | tf_op jit(solution)/shard_map/ppermute | solution.py:21
  7.1 2.7 copy-start.40
  9.5 23.0 %copy-start.4 = (bf16[2,16,64,128]{3,2,1,0:T(8,128)(2,1)S(1)}, bf16[2,16,64,128]{3,2,1,0:T(8,128)(2,1)}, u32[]{:S(2)}) copy-start(bf16[2,16,64,128]{3,2,1,0:T(8,128)(2,1)} %param.14) | copy-start | bytes 1572868
  10.2 0.8 copy-start.39
  12.9 62.2 %collective-permute-start.8 = (bf16[2,1,4,64,128]{4,2,1,3,0:T(4,128)(2,1)S(1)}, bf16[2,1,4,64,128]{4,2,1,3,0:T(4,128)(2,1)S(1)}, u32[]{:S(2)}, u32[]{:S(2)}) collective-permute-start(bf16[2,1,4,64,128]{4,2,1,3,0:T(4,128)(2,1)S(1)} %fusion.104), channel_id=1, source_target_pairs={{16,0},{24,8},{32,16},{40,24},{48,32},{56,40},{64,48},{72,56},{80,... | collective-permute-start | bytes 393224 | tf_op jit(solution)/shard_map/ppermute | solution.py:31
  15.9 59.1 %collective-permute-start.11 = (bf16[2,1,4,64,128]{4,2,1,3,0:T(4,128)(2,1)S(1)}, bf16[2,1,4,64,128]{4,2,1,3,0:T(4,128)(2,1)}, u32[]{:S(2)}, u32[]{:S(2)}) collective-permute-start(bf16[2,1,4,64,128]{4,2,1,3,0:T(4,128)(2,1)S(1)} %fusion.101), channel_id=1, source_target_pairs={{0,16},{8,24},{16,32},{24,40},{32,48},{40,56},{48,64},{56,72},{64,... | collective-permute-start | bytes 393224 | tf_op jit(solution)/shard_map/ppermute | solution.py:31
  23.5 51.5 %collective-permute-start.10 = (bf16[2,1,4,64,128]{4,2,1,3,0:T(4,128)(2,1)S(1)}, bf16[2,1,4,64,128]{4,2,1,3,0:T(4,128)(2,1)}, u32[]{:S(2)}, u32[]{:S(2)}) collective-permute-start(bf16[2,1,4,64,128]{4,2,1,3,0:T(4,128)(2,1)S(1)} %fusion.102), channel_id=1, source_target_pairs={{0,8},{8,16},{16,24},{24,32},{32,40},{40,48},{48,56},{56,64},{64,7... | collective-permute-start | bytes 393224 | tf_op jit(solution)/shard_map/ppermute | solution.py:31
  27.5 5.7 %copy-start.15 = (bf16[3,3,64,64]{3,2,1,0:T(8,128)(2,1)S(1)}, bf16[3,3,64,64]{3,2,1,0:T(8,128)(2,1)}, u32[]{:S(2)}) copy-start(bf16[3,3,64,64]{3,2,1,0:T(8,128)(2,1)} %param.15) | copy-start | bytes 221188
  31.2 2.3 copy-start.23
  31.2 43.8 %collective-permute-start.9 = (bf16[2,1,4,64,128]{4,2,1,3,0:T(4,128)(2,1)S(1)}, bf16[2,1,4,64,128]{4,2,1,3,0:T(4,128)(2,1)}, u32[]{:S(2)}, u32[]{:S(2)}) collective-permute-start(bf16[2,1,4,64,128]{4,2,1,3,0:T(4,128)(2,1)S(1)} %fusion.103), channel_id=1, source_target_pairs={{8,0},{16,8},{24,16},{32,24},{40,32},{48,40},{56,48},{64,56},{72,6... | collective-permute-start | bytes 393224 | tf_op jit(solution)/shard_map/ppermute | solution.py:31
  32.5 3.2 %copy-start.28 = (bf16[2,1,64,128]{3,2,1,0:T(8,128)(2,1)}, bf16[2,1,64,128]{3,2,1,0:T(8,128)(2,1)S(1)}, u32[]{:S(2)}) copy-start(bf16[2,1,64,128]{3,2,1,0:T(8,128)(2,1)S(1)} %collective-permute-done.1) | copy-start | bytes 98308
  38.0 15.9 %copy-start.21 = (bf16[3,64,64]{2,1,0:T(8,128)(2,1)S(1)}, bf16[3,64,64]{2,1,0:T(8,128)(2,1)}, u32[]{:S(2)}) copy-start(bf16[3,64,64]{2,1,0:T(8,128)(2,1)} %param.16) | copy-start | bytes 73732
  38.0 15.9 %all-to-all-start = ((bf16[2,16,64,128]{3,2,0,1:T(8,128)(2,1)}), bf16[2,16,64,128]{3,2,0,1:T(8,128)(2,1)S(1)}, u32[]{:S(2)}, u32[]{:S(2)}) async-start(bf16[2,16,64,128]{3,2,0,1:T(8,128)(2,1)} %copy.265), calls=%async_computation | async-start | bytes 1048576 | tf_op jit(solution)/shard_map/all_to_all | solution.py:52
  56.3 13.7 %all-to-all-start.1 = ((bf16[16,2,64,128]{3,2,1,0:T(8,128)(2,1)}), bf16[16,2,64,128]{3,2,1,0:T(8,128)(2,1)S(1)}, u32[]{:S(2)}, u32[]{:S(2)}) async-start(bf16[16,2,64,128]{3,2,1,0:T(8,128)(2,1)} %get-tuple-element.94), calls=%async_computation.1 | async-start | bytes 1048576 | tf_op jit(solution)/shard_map/all_to_all | solution.py:56
  70.7 12.9 %collective-permute-start.2 = (bf16[2,1,64,128]{3,2,1,0:T(8,128)(2,1)}, bf16[2,1,64,128]{3,2,1,0:T(8,128)(2,1)S(1)}, u32[]{:S(2)}, u32[]{:S(2)}) collective-permute-start(bf16[2,1,64,128]{3,2,1,0:T(8,128)(2,1)} %get-tuple-element.79), channel_id=1, source_target_pairs={{0,8},{8,16},{16,24},{24,32},{32,40},{40,48},{48,56},{56,64},{64,7... | collective-permute-start | bytes 98312 | tf_op jit(solution)/shard_map/ppermute | solution.py:19
  76.8 5.6 %copy-start.37 = (bf16[2,1,64,128]{3,2,1,0:T(8,128)(2,1)S(1)}, bf16[2,1,64,128]{3,2,1,0:T(8,128)(2,1)}, u32[]{:S(2)}) copy-start(bf16[2,1,64,128]{3,2,1,0:T(8,128)(2,1)} %get-tuple-element.80) | copy-start | bytes 98308
  76.8 6.9 %copy-start.14 = (bf16[3,3,64,64]{3,2,1,0:T(8,128)(2,1)S(1)}, bf16[3,3,64,64]{3,2,1,0:T(8,128)(2,1)}, u32[]{:S(2)}) copy-start(bf16[3,3,64,64]{3,2,1,0:T(8,128)(2,1)} %param.17) | copy-start | bytes 221188
  77.8 15.5 %all-to-all-start.4 = ((bf16[2,16,64,128]{3,2,0,1:T(8,128)(2,1)}), bf16[2,16,64,128]{3,2,0,1:T(8,128)(2,1)S(1)}, u32[]{:S(2)}, u32[]{:S(2)}) async-start(bf16[2,16,64,128]{3,2,0,1:T(8,128)(2,1)} %copy.286), calls=%async_computation.4 | async-start | bytes 1048576 | tf_op jit(solution)/shard_map/all_to_all | solution.py:52
  82.4 4.9 %collective-permute-start.3 = (bf16[2,1,64,128]{3,2,1,0:T(8,128)(2,1)S(1)}, bf16[2,1,64,128]{3,2,1,0:T(8,128)(2,1)S(1)}, u32[]{:S(2)}, u32[]{:S(2)}) collective-permute-start(bf16[2,1,64,128]{3,2,1,0:T(8,128)(2,1)S(1)} %copy-done.37), channel_id=1, source_target_pairs={{8,0},{16,8},{24,16},{32,24},{40,32},{48,40},{56,48},{64,56},{72,6... | collective-permute-start | bytes 98312 | tf_op jit(solution)/shard_map/ppermute | solution.py:21
  87.3 3.6 %copy-start.30 = (bf16[2,1,64,128]{3,2,1,0:T(8,128)(2,1)}, bf16[2,1,64,128]{3,2,1,0:T(8,128)(2,1)S(1)}, u32[]{:S(2)}) copy-start(bf16[2,1,64,128]{3,2,1,0:T(8,128)(2,1)S(1)} %collective-permute-done.3) | copy-start | bytes 98308
  93.3 15.1 %all-to-all-start.2 = ((bf16[2,16,64,128]{3,2,0,1:T(8,128)(2,1)}), bf16[2,16,64,128]{3,2,0,1:T(8,128)(2,1)}, u32[]{:S(2)}, u32[]{:S(2)}) async-start(bf16[2,16,64,128]{3,2,0,1:T(8,128)(2,1)} %copy.268), calls=%async_computation.2 | async-start | bytes 1048576 | tf_op jit(solution)/shard_map/all_to_all | solution.py:52
  108.4 2.1 copy-start.20
  110.5 1.2 copy-start.10
  115.2 14.5 %all-to-all-start.5 = ((bf16[16,2,64,128]{3,2,1,0:T(8,128)(2,1)}), bf16[16,2,64,128]{3,2,1,0:T(8,128)(2,1)}, u32[]{:S(2)}, u32[]{:S(2)}) async-start(bf16[16,2,64,128]{3,2,1,0:T(8,128)(2,1)} %fusion.19), calls=%async_computation.5 | async-start | bytes 1048576 | tf_op jit(solution)/shard_map/all_to_all | solution.py:56
  120.2 2.7 copy-start.9
  129.7 14.5 %all-to-all-start.3 = ((bf16[16,2,64,128]{3,2,1,0:T(8,128)(2,1)}), bf16[16,2,64,128]{3,2,1,0:T(8,128)(2,1)}, u32[]{:S(2)}, u32[]{:S(2)}) async-start(bf16[16,2,64,128]{3,2,1,0:T(8,128)(2,1)} %get-tuple-element.74), calls=%async_computation.3 | async-start | bytes 1048576 | tf_op jit(solution)/shard_map/all_to_all | solution.py:56
  134.7 1.4 copy-start.13
  135.9 1.0 copy-start.2
  150.6 27.4 %copy-start.31 = (bf16[2,1,64,128]{3,2,1,0:T(8,128)(2,1)S(1)}, bf16[2,1,64,128]{3,2,1,0:T(8,128)(2,1)}, u32[]{:S(2)}) copy-start(bf16[2,1,64,128]{3,2,1,0:T(8,128)(2,1)} %copy-done.30) | copy-start | bytes 98308
  152.3 26.0 %copy-start.26 = (bf16[2,1,64,128]{3,2,1,0:T(8,128)(2,1)S(1)}, bf16[2,1,64,128]{3,2,1,0:T(8,128)(2,1)}, u32[]{:S(2)}) copy-start(bf16[2,1,64,128]{3,2,1,0:T(8,128)(2,1)} %copy-done.25) | copy-start | bytes 98308
  152.3 40.6 %collective-permute-start.5 = (bf16[2,1,4,64,128]{4,2,1,3,0:T(4,128)(2,1)}, bf16[2,1,4,64,128]{4,2,1,3,0:T(4,128)(2,1)}, u32[]{:S(2)}, u32[]{:S(2)}) collective-permute-start(bf16[2,1,4,64,128]{4,2,1,3,0:T(4,128)(2,1)} %fusion.107), channel_id=1, source_target_pairs={{0,8},{8,16},{16,24},{24,32},{32,40},{40,48},{48,56},{56,64},{64,7... | collective-permute-start | bytes 393224 | tf_op jit(solution)/shard_map/ppermute | solution.py:31
  157.6 35.3 %collective-permute-start.4 = (bf16[2,1,4,64,128]{4,2,1,3,0:T(4,128)(2,1)}, bf16[2,1,4,64,128]{4,2,1,3,0:T(4,128)(2,1)}, u32[]{:S(2)}, u32[]{:S(2)}) collective-permute-start(bf16[2,1,4,64,128]{4,2,1,3,0:T(4,128)(2,1)} %fusion.108), channel_id=1, source_target_pairs={{0,16},{8,24},{16,32},{24,40},{32,48},{40,56},{48,64},{56,72},{64,... | collective-permute-start | bytes 393224 | tf_op jit(solution)/shard_map/ppermute | solution.py:31
  169.2 23.7 %collective-permute-start.6 = (bf16[2,1,4,64,128]{4,2,1,3,0:T(4,128)(2,1)}, bf16[2,1,4,64,128]{4,2,1,3,0:T(4,128)(2,1)}, u32[]{:S(2)}, u32[]{:S(2)}) collective-permute-start(bf16[2,1,4,64,128]{4,2,1,3,0:T(4,128)(2,1)} %fusion.106), channel_id=1, source_target_pairs={{8,0},{16,8},{24,16},{32,24},{40,32},{48,40},{56,48},{64,56},{72,6... | collective-permute-start | bytes 393224 | tf_op jit(solution)/shard_map/ppermute | solution.py:31
  170.5 9.4 %collective-permute-start.12 = (bf16[2,1,64,128]{3,2,1,0:T(8,128)(2,1)}, bf16[2,1,64,128]{3,2,1,0:T(8,128)(2,1)S(1)}, u32[]{:S(2)}, u32[]{:S(2)}) collective-permute-start(bf16[2,1,64,128]{3,2,1,0:T(8,128)(2,1)} %get-tuple-element.77), channel_id=1, source_target_pairs={{0,8},{8,16},{16,24},{24,32},{32,40},{40,48},{48,56},{56,64},{64,7... | collective-permute-start | bytes 98312 | tf_op jit(solution)/shard_map/ppermute | solution.py:19
  174.5 6.7 %collective-permute-start.13 = (bf16[2,1,64,128]{3,2,1,0:T(8,128)(2,1)}, bf16[2,1,64,128]{3,2,1,0:T(8,128)(2,1)S(1)}, u32[]{:S(2)}, u32[]{:S(2)}) collective-permute-start(bf16[2,1,64,128]{3,2,1,0:T(8,128)(2,1)} %get-tuple-element.78), channel_id=1, source_target_pairs={{8,0},{16,8},{24,16},{32,24},{40,32},{48,40},{56,48},{64,56},{72,6... | collective-permute-start | bytes 98312 | tf_op jit(solution)/shard_map/ppermute | solution.py:21
  178.0 1.2 copy-start.34
  178.0 1.2 copy-start.35
  179.9 13.1 %collective-permute-start.7 = (bf16[2,1,4,64,128]{4,2,1,3,0:T(4,128)(2,1)}, bf16[2,1,4,64,128]{4,2,1,3,0:T(4,128)(2,1)}, u32[]{:S(2)}, u32[]{:S(2)}) collective-permute-start(bf16[2,1,4,64,128]{4,2,1,3,0:T(4,128)(2,1)} %fusion.105), channel_id=1, source_target_pairs={{16,0},{24,8},{32,16},{40,24},{48,32},{56,40},{64,48},{72,56},{80,... | collective-permute-start | bytes 393224 | tf_op jit(solution)/shard_map/ppermute | solution.py:31
  184.4 1.2 copy-start.3
  186.0 6.8 %copy-start.32 = (f32[1,64,64]{2,1,0:T(8,128)S(1)}, f32[1,64,64]{2,1,0:T(8,128)}, u32[]{:S(2)}) copy-start(f32[1,64,64]{2,1,0:T(8,128)} %convolution_bitcast_fusion.11) | copy-start | bytes 49156
  186.0 6.8 %copy-start.33 = (f32[1,64,64]{2,1,0:T(8,128)S(1)}, f32[1,64,64]{2,1,0:T(8,128)}, u32[]{:S(2)}) copy-start(f32[1,64,64]{2,1,0:T(8,128)} %convolution_bitcast_fusion.13) | copy-start | bytes 49156
  186.0 6.8 %copy-start.36 = (f32[1,64,64]{2,1,0:T(8,128)S(1)}, f32[1,64,64]{2,1,0:T(8,128)}, u32[]{:S(2)}) copy-start(f32[1,64,64]{2,1,0:T(8,128)} %convolution_bitcast_fusion.12) | copy-start | bytes 49156
  186.0 6.8 %copy-start.18 = (f32[1,3,64,64]{3,2,1,0:T(8,128)S(1)}, f32[1,3,64,64]{3,2,1,0:T(8,128)}, u32[]{:S(2)}) copy-start(f32[1,3,64,64]{3,2,1,0:T(8,128)} %maximum_bitcast_fusion.5) | copy-start | bytes 147460
  186.8 6.1 %copy-start.42 = (f32[16,16]{0,1:S(1)}, f32[16,16]{0,1}, u32[]{:S(2)}) copy-start(f32[16,16]{0,1} %fusion.212) | copy-start | bytes 3076
  186.8 15.3 %all-to-all-start.6 = ((bf16[2,16,64,128]{3,2,0,1:T(8,128)(2,1)}), bf16[2,16,64,128]{3,2,0,1:T(8,128)(2,1)S(1)}, u32[]{:S(2)}, u32[]{:S(2)}) async-start(bf16[2,16,64,128]{3,2,0,1:T(8,128)(2,1)} %copy.301), calls=%async_computation.6 | async-start | bytes 1048576 | tf_op jit(solution)/shard_map/all_to_all | solution.py:52
  194.5 7.7 %copy-start.12 = (f32[16,2,64,128]{3,2,1,0:T(8,128)S(1)}, f32[16,2,64,128]{3,2,1,0:T(8,128)}, u32[]{:S(2)}) copy-start(f32[16,2,64,128]{3,2,1,0:T(8,128)} %get-tuple-element.95) | copy-start | bytes 3145732
  203.7 5.5 %copy-start.7 = (bf16[2,8,2,64,128]{4,3,2,0,1:T(8,128)(2,1)S(1)}, bf16[2,8,2,64,128]{4,3,2,0,1:T(8,128)(2,1)}, u32[]{:S(2)}) copy-start(bf16[2,8,2,64,128]{4,3,2,0,1:T(8,128)(2,1)} %copy-done.6) | copy-start | bytes 1572868
  204.9 13.8 %all-to-all-start.7 = ((bf16[16,2,64,128]{3,2,1,0:T(8,128)(2,1)}), bf16[16,2,64,128]{3,2,1,0:T(8,128)(2,1)S(1)}, u32[]{:S(2)}, u32[]{:S(2)}) async-start(bf16[16,2,64,128]{3,2,1,0:T(8,128)(2,1)} %fusion.20), calls=%async_computation.7 | async-start | bytes 1048576 | tf_op jit(solution)/shard_map/all_to_all | solution.py:56
  220.4 1.0 copy-start.5
  223.8 1.8 copy-start.19
  224.1 11.5 %copy-start.16 = (bf16[3,3,64,64]{3,2,1,0:T(8,128)(2,1)S(1)}, bf16[3,3,64,64]{3,2,1,0:T(8,128)(2,1)}, u32[]{:S(2)}) copy-start(bf16[3,3,64,64]{3,2,1,0:T(8,128)(2,1)} %param.15) | copy-start | bytes 221188
  224.3 11.3 %collective-permute-start.15 = (bf16[2,1,64,128]{3,2,1,0:T(8,128)(2,1)S(1)}, bf16[2,1,64,128]{3,2,1,0:T(8,128)(2,1)S(1)}, u32[]{:S(2)}, u32[]{:S(2)}) collective-permute-start(bf16[2,1,64,128]{3,2,1,0:T(8,128)(2,1)S(1)} %get-tuple-element.76), channel_id=1, source_target_pairs={{8,0},{16,8},{24,16},{32,24},{40,32},{48,40},{56,48},{64,56},{72,6... | collective-permute-start | bytes 98312 | tf_op jit(solution)/shard_map/ppermute | solution.py:21
  226.4 13.4 %all-to-all-start.8 = ((f32[8,1,12288]{2,1,0:T(1,128)}), f32[8,1,12288]{2,1,0:T(1,128)S(1)}, u32[]{:S(2)}, u32[]{:S(2)}) async-start(f32[8,1,12288]{2,1,0:T(1,128)} %bitcast.257), calls=%async_computation.8 | async-start | bytes 786432 | tf_op jit(solution)/shard_map/all_to_all | solution.py:254
  230.7 5.9 %collective-permute-start.14 = (bf16[2,1,64,128]{3,2,1,0:T(8,128)(2,1)S(1)}, bf16[2,1,64,128]{3,2,1,0:T(8,128)(2,1)S(1)}, u32[]{:S(2)}, u32[]{:S(2)}) collective-permute-start(bf16[2,1,64,128]{3,2,1,0:T(8,128)(2,1)S(1)} %get-tuple-element.75), channel_id=1, source_target_pairs={{0,8},{8,16},{16,24},{24,32},{32,40},{40,48},{48,56},{56,64},{64,7... | collective-permute-start | bytes 98312 | tf_op jit(solution)/shard_map/ppermute | solution.py:19
  240.7 29.7 %all-to-all-start.9 = ((f32[32,1,384]{2,1,0:T(1,128)}), f32[32,1,384]{2,1,0:T(1,128)S(1)}, u32[]{:S(2)}, u32[]{:S(2)}) async-start(f32[32,1,384]{2,1,0:T(1,128)} %bitcast.258), calls=%async_computation.9 | async-start | bytes 98304 | tf_op jit(solution)/shard_map/all_to_all | solution.py:254
  271.1 12.6 %all-to-all-start.10 = ((f32[32,1,384]{2,1,0:T(1,128)}), f32[32,1,384]{2,1,0:T(1,128)S(1)}, u32[]{:S(2)}, u32[]{:S(2)}) async-start(f32[32,1,384]{2,1,0:T(1,128)} %broadcast_in_dim.95), calls=%async_computation.10 | async-start | bytes 98304 | tf_op jit(solution)/shard_map/all_to_all | solution.py:257
  284.6 16.1 %all-to-all-start.11 = ((f32[8,1,12288]{2,1,0:T(1,128)}), f32[8,1,12288]{2,1,0:T(1,128)S(1)}, u32[]{:S(2)}, u32[]{:S(2)}) async-start(f32[8,1,12288]{2,1,0:T(1,128)} %broadcast_in_dim.97), calls=%async_computation.11 | async-start | bytes 786432 | tf_op jit(solution)/shard_map/all_to_all | solution.py:257
  293.1 1.2 copy-start.11
  294.3 10.9 %copy-start.1 = (s32[32,16]{0,1:T(8,128)S(1)}, s32[32,16]{0,1:T(8,128)}, u32[]{:S(2)}) copy-start(s32[32,16]{0,1:T(8,128)} %param.21) | copy-start | bytes 6148
  (7 other events, 5.1 us)

commit v2 on v1

--- a/solution.py
+++ b/solution.py
@@ -40,20 +40,8 @@
     return jnp.pad(values, ((0, 0), (0, 0), (0, 0), (1, 1)))
 
 
-def frames_padding(values, spacing):
-    return jnp.pad(values, ((spacing, spacing), (0, 0), (0, 0), (0, 0)))
-
-
 def chart_rim(values):
     return with_halo(values, (("chart", 1),), 1)
-
-
-def to_tiles(values):
-    return lax.all_to_all(values, "frame", split_axis=1, concat_axis=0, tiled=True)
-
-
-def to_frames(values):
-    return lax.all_to_all(values, "frame", split_axis=0, concat_axis=1, tiled=True)
 
 
 def near_send(values, steps_by):
@@ -115,50 +103,6 @@
     )
 
 
-def apply_time_kernel(padded, weight, spacing):
-    frames = padded.shape[0] - 2 * spacing
-    summed = None
-    for kernel_tap in range(3):
-        partial_sum = jnp.einsum(
-            "oc,fscp->fsop",
-            weight[kernel_tap],
-            padded[kernel_tap * spacing : kernel_tap * spacing + frames],
-            preferred_element_type=jnp.float32,
-        )
-        summed = partial_sum if summed is None else summed + partial_sum
-    return summed
-
-
-def time_kernel_transposed(padded, weight, spacing):
-    frames = padded.shape[0] - 2 * spacing
-    summed = None
-    for kernel_tap in range(3):
-        start_at = (2 - kernel_tap) * spacing
-        partial_sum = jnp.einsum(
-            "oc,fsop->fscp",
-            weight[kernel_tap],
-            padded[start_at : start_at + frames],
-            preferred_element_type=jnp.float32,
-        )
-        summed = partial_sum if summed is None else summed + partial_sum
-    return summed
-
-
-def time_kernel_weight(slopes, padded, spacing):
-    frames = slopes.shape[0]
-    return jnp.stack(
-        [
-            jnp.einsum(
-                "fsop,fscp->oc",
-                slopes,
-                padded[kernel_tap * spacing : kernel_tap * spacing + frames],
-                preferred_element_type=jnp.float32,
-            )
-            for kernel_tap in range(3)
-        ]
-    )
-
-
 def spatial_forward(inputs, weight, rim_fn):
     padded = pad_columns(rim_fn(inputs))
     before = spatial_apply(padded, weight)
@@ -174,21 +118,58 @@
     return (result, grad_weight)
 
 
-def time_kernel_forward(inputs, weight, spacing, time_pad):
-    padded = time_pad(inputs, spacing)
-    before = apply_time_kernel(padded, weight, spacing)
+def frame_shift(values, offset):
+    count = values.shape[0]
+    groups = []
+    for frame in range(count):
+        peer, row = divmod(frame + offset, count)
+        if groups and groups[-1][0] == peer:
+            groups[-1][2] = row + 1
+        else:
+            groups.append([peer, row, row + 1])
+    pieces = []
+    for peer, first, last in groups:
+        piece = values[first:last]
+        if peer != 0:
+            piece = from_behind(piece, "frame", -peer)
+        pieces.append(piece)
+    return pieces[0] if len(pieces) == 1 else jnp.concatenate(pieces, axis=0)
+
+
+def time_taps(values, spacing):
+    return (frame_shift(values, -spacing), values, frame_shift(values, spacing))
+
+
+def time_kernel_forward(inputs, weight, spacing):
+    taps = time_taps(inputs, spacing)
+    before = None
+    for kernel_tap in range(3):
+        partial_sum = jnp.einsum(
+            "oc,fscp->fsop", weight[kernel_tap], taps[kernel_tap], preferred_element_type=jnp.float32
+        )
+        before = partial_sum if before is None else before + partial_sum
     output = (inputs.astype(jnp.float32) + jax.nn.silu(before)).astype(jnp.bfloat16)
-    return (output, before, padded)
-
-
-def temporal_backward(upstream, before, padded, weight, spacing, time_pad):
+    return (output, before, taps)
+
+
+def temporal_backward(upstream, before, taps, weight, spacing):
     slopes = (upstream.astype(jnp.float32) * silu_slope(before)).astype(jnp.bfloat16)
-    grad_weight = time_kernel_weight(slopes, padded, spacing)
-    result = (
-        upstream.astype(jnp.float32)
-        + time_kernel_transposed(time_pad(slopes, spacing), weight, spacing)
-    ).astype(jnp.bfloat16)
-    return (result, grad_weight)
+    grad_weight = jnp.stack(
+        [
+            jnp.einsum("fsop,fscp->oc", slopes, taps[kernel_tap], preferred_element_type=jnp.float32)
+            for kernel_tap in range(3)
+        ]
+    )
+    spread = time_taps(slopes, spacing)
+    summed = upstream.astype(jnp.float32)
+    for kernel_tap in range(3):
+        summed = summed + jnp.einsum(
+            "oc,fsop->fscp",
+            weight[kernel_tap],
+            spread[2 - kernel_tap],
+            preferred_element_type=jnp.float32,
+        )
+    return (summed.astype(jnp.bfloat16), grad_weight)
 
 
 def seam_tables(seam_owner, seam_row, seam_to, strips):
@@ -278,17 +259,13 @@
     wide_dilation = min(8, total_frames // 4)
     strips = features.shape[1]
     first_layer, pre_one, padded_zero = spatial_forward(features, spatial_a, chart_rim)
-    first_layer_tiles = to_tiles(first_layer)
     second_layer, second_preactivation, first_padded = time_kernel_forward(
-        first_layer_tiles, first_time_kernel, NEAR_DILATION, frames_padding
-    )
-    frames_two = to_frames(second_layer)
-    frames_three, pre_three, padded_two = spatial_forward(frames_two, spatial_b, chart_rim)
-    third_layer = to_tiles(frames_three)
-    layer_four, fourth_preactivation, third_padded = time_kernel_forward(
-        third_layer, second_time_kernel, wide_dilation, frames_padding
-    )
-    frames_four = to_frames(layer_four)
+        first_layer, first_time_kernel, NEAR_DILATION
+    )
+    frames_three, pre_three, padded_two = spatial_forward(second_layer, spatial_b, chart_rim)
+    frames_four, fourth_preactivation, third_padded = time_kernel_forward(
+        frames_three, second_time_kernel, wide_dilation
+    )
     tables = seam_tables(seam_owner, seam_row, seam_to, strips)
     myself = lax.axis_index("chart")
     offsets = [offset for offset in range(-REACH, REACH + 1) if offset != 0]
@@ -308,31 +285,25 @@
     moved_back = place_strips(jnp.concatenate(returns, axis=1), return_matrix)
     blended = (frames_four.astype(jnp.float32) + moved).astype(jnp.bfloat16)
     fourth_gradient = (grad_out.astype(jnp.float32) + moved_back).astype(jnp.bfloat16)
-    fourth_gradient_tiles = to_tiles(fourth_gradient)
     third_gradient, gradient_kernel_second = temporal_backward(
-        fourth_gradient_tiles,
+        fourth_gradient,
         fourth_preactivation,
         third_padded,
         second_time_kernel,
         wide_dilation,
-        frames_padding,
-    )
-    frames_grad_three = to_frames(third_gradient)
+    )
     frames_grad_two, grad_sb = spatial_backward(
-        frames_grad_three, pre_three, padded_two, spatial_b, chart_rim
-    )
-    second_gradient = to_tiles(frames_grad_two)
+        third_gradient, pre_three, padded_two, spatial_b, chart_rim
+    )
     first_gradient, gradient_kernel_first = temporal_backward(
-        second_gradient,
+        frames_grad_two,
         second_preactivation,
         first_padded,
         first_time_kernel,
         NEAR_DILATION,
-        frames_padding,
-    )
-    frames_grad_one = to_frames(first_gradient)
+    )
     grad_features, grad_sa = spatial_backward(
-        frames_grad_one, pre_one, padded_zero, spatial_a, chart_rim
+        first_gradient, pre_one, padded_zero, spatial_a, chart_rim
     )
     summed_sa, summed_ta, summed_sb, summed_tb = exchange_sum(
         (grad_sa, gradient_kernel_first, grad_sb, gradient_kernel_second), ("frame", "chart")

time: 308 us -> 267 us (0.87)
  starting transfers between devices: 131 us -> 113 us
  waiting for transfers between devices: 63 us -> 51 us
  local copies, waits for them, and re-layouts: 35 us -> 26.4 us
  other arithmetic: 26.2 us -> 21.2 us
  matrix products: 48.2 us -> 51.4 us
    all_to_all x8 -> x0, waiting for transfers between devices: 41.7 us -> none  [the longest x4 22.3 us: to_frames(): lax.all_to_all(values, 'frame', split_axis=0, concat_axis=1, tiled=True)]
    all_to_all x8 -> x0, starting transfers between devices: 41.5 us -> none  [the longest x4 22.7 us: to_tiles(): lax.all_to_all(values, 'frame', split_axis=1, concat_axis=0, tiled=True)]
    ppermute x8 -> x16, waiting for transfers between devices: 0.02 us -> 26.5 us  [from_behind(): return lax.ppermute(array, axis, pairs)]
    ppermute x8 -> x16, starting transfers between devices: 29.5 us -> 53.4 us  [from_behind(): return lax.ppermute(array, axis, pairs)]
    dot_general x18, matrix products: 12.4 us -> 20.6 us  [the longest x6 10.5 us: temporal_backward(): jnp.einsum('oc,fsop->fscp', weight[kernel_tap], spread[2 - kernel_tap], p...]
    convert_element_type x8 -> x0, local copies, waits for them, and re-layouts: 5.99 us -> none  [the longest x2 1.67 us: spatial_forward(): (inputs.astype(jnp.float32) + jax.nn.silu(before)).astype(jnp.bfloat16)]
    dot_general x18, matrix products: 10.4 us -> 5.63 us  [spatial_weight(): jnp.einsum('fsop,fscp->oc', slopes, padded[:, row_tap:row_tap + strips, :...]
    gather x8, local copies, waits for them, and re-layouts: 9.08 us -> 12.8 us  [pick_strips(): gathered = jnp.take(values, strip_ids.reshape(-1), axis=1)]
where the time goes in v2:
time: 267 us; the launch traced here: 265 us
  starting transfers between devices  113 us (42%)
  matrix products  51.4 us (19%)
  waiting for transfers between devices  51 us (19%)
  local copies, waits for them, and re-layouts  26.4 us (10%)
  other arithmetic  21.2 us (8%)
    ppermute x16, starting transfers between devices, from_behind(): return lax.ppermute(array, axis, pairs)  53.4 us
    all_to_all x2, starting transfers between devices, exchange_sum(): flat = jnp.sum(lax.all_to_all(pieces, axis, 0, 0, tiled=True), axis=0)  27.6 us
    ppermute x16, waiting for transfers between devices, from_behind(): return lax.ppermute(array, axis, pairs)  26.5 us
    ppermute x4, starting transfers between devices, with_halo(): lax.ppermute(tail, axis, [(i, (i + 1) % count) for i in range(ends)])  15.4 us
    dot_general x18, matrix products, spatial_transpose(): jnp.einsum('oc,fsop->fscp', weight[row_tap, col_tap], padded[:, 2 - row_t...  13.6 us
    gather x8, local copies, waits for them, and re-layouts, pick_strips(): gathered = jnp.take(values, strip_ids.reshape(-1), axis=1)  12.8 us
    all_to_all x2, waiting for transfers between devices, exchange_sum(): flat = lax.all_to_all(copies, axis, 0, 0, tiled=True).reshape(-1)  12.6 us
    all_to_all x2, starting transfers between devices, exchange_sum(): flat = lax.all_to_all(copies, axis, 0, 0, tiled=True).reshape(-1)  11.4 us
  transfers between devices with their start and end apart: 28, of which 12 were waited for; matrix products, arithmetic and copies ran while one was open for 25% of the time, Pallas kernels for 0%

profile of v2, /device:TPU:1, one launch (start us, length us, event | category | flops | bytes accessed | tf_op | source)
XLA Modules:
  0.0 265.2 jit_solution(6126181137101957099)
XLA Ops:
  1.5 4.0 %collective-permute-start = (bf16[2,1,64,128]{3,2,1,0:T(8,128)(2,1)S(1)}, bf16[2,1,64,128]{3,2,1,0:T(8,128)(2,1)S(1)}, u32[]{:S(2)}, u32[]{:S(2)}) collective-permute-start(bf16[2,1,64,128]{3,2,1,0:T(8,128)(2,1)S(1)} %get-tuple-element.49), channel_id=1, source_target_pairs={{0,8},{8,16},{16,24},{24,32},{32,40},{40,48},{48,56},{56,64},{64,7... | collective-permute-start | bytes 98312 | tf_op jit(solution)/shard_map/ppermute | solution.py:19
  5.5 1.3 collective-permute-start.1
  10.6 1.7 gather_fusion.6
  12.4 1.3 collective-permute-start.12
  13.8 1.6 gather_fusion.9
  16.2 6.9 %collective-permute-start.15 = (bf16[2,1,4,64,128]{4,2,1,3,0:T(4,128)(2,1)}, bf16[2,1,4,64,128]{4,2,1,3,0:T(4,128)(2,1)}, u32[]{:S(2)}, u32[]{:S(2)}) collective-permute-start(bf16[2,1,4,64,128]{4,2,1,3,0:T(4,128)(2,1)} %fusion.104), channel_id=1, source_target_pairs={{0,16},{8,24},{16,32},{24,40},{32,48},{40,56},{48,64},{56,72},{64,... | collective-permute-start | bytes 393224 | tf_op jit(solution)/shard_map/ppermute | solution.py:31
  24.4 3.9 %collective-permute-start.14 = (bf16[2,1,4,64,128]{4,2,1,3,0:T(4,128)(2,1)}, bf16[2,1,4,64,128]{4,2,1,3,0:T(4,128)(2,1)}, u32[]{:S(2)}, u32[]{:S(2)}) collective-permute-start(bf16[2,1,4,64,128]{4,2,1,3,0:T(4,128)(2,1)} %fusion.105), channel_id=1, source_target_pairs={{0,8},{8,16},{16,24},{24,32},{32,40},{40,48},{48,56},{56,64},{64,7... | collective-permute-start | bytes 393224 | tf_op jit(solution)/shard_map/ppermute | solution.py:31
  37.7 1.5 add_convert_fusion.3
  39.2 5.1 %collective-permute-start.2 = (bf16[1,16,64,128]{3,2,1,0:T(8,128)(2,1)S(1)}, bf16[1,16,64,128]{3,2,1,0:T(8,128)(2,1)S(1)}, u32[]{:S(2)}, u32[]{:S(2)}) collective-permute-start(bf16[1,16,64,128]{3,2,1,0:T(8,128)(2,1)S(1)} %get-tuple-element.47), channel_id=1, source_target_pairs={{0,1},{1,2},{2,3},{3,4},{4,5},{5,6},{6,7},{8,9},{9,10},{10,11},{11... | collective-permute-start | bytes 786440 | tf_op jit(solution)/shard_map/ppermute | solution.py:31
  44.3 1.9 collective-permute-start.3
  46.6 5.5 %collective-permute-done.3 = bf16[1,16,64,128]{3,2,1,0:T(8,128)(2,1)S(1)} collective-permute-done((bf16[1,16,64,128]{3,2,1,0:T(8,128)(2,1)S(1)}, bf16[1,16,64,128]{3,2,1,0:T(8,128)(2,1)S(1)}, u32[]{:S(2)}, u32[]{:S(2)}) %collective-permute-start.3) | collective-permute-done | bytes 262176 | tf_op jit(solution)/shard_map/ppermute | solution.py:31
  53.5 1.5 add_convert_fusion.2
  55.0 3.0 %collective-permute-start.4 = (bf16[2,1,64,128]{3,2,1,0:T(8,128)(2,1)S(1)}, bf16[2,1,64,128]{3,2,1,0:T(8,128)(2,1)S(1)}, u32[]{:S(2)}, u32[]{:S(2)}) collective-permute-start(bf16[2,1,64,128]{3,2,1,0:T(8,128)(2,1)S(1)} %get-tuple-element.45), channel_id=1, source_target_pairs={{0,8},{8,16},{16,24},{24,32},{32,40},{40,48},{48,56},{56,64},{64,7... | collective-permute-start | bytes 98312 | tf_op jit(solution)/shard_map/ppermute | solution.py:19
  57.9 1.3 collective-permute-start.5
  59.3 1.3 collective-permute-start.13
  60.6 2.0 collective-permute-done.5
  65.8 1.5 add_convert_fusion.1
  67.3 1.3 collective-permute-start.7
  68.7 1.5 convolution_bitcast_fusion.6
  70.2 4.2 %collective-permute-start.6 = (bf16[2,16,64,128]{3,2,1,0:T(8,128)(2,1)S(1)}, bf16[2,16,64,128]{3,2,1,0:T(8,128)(2,1)S(1)}, u32[]{:S(2)}, u32[]{:S(2)}) collective-permute-start(bf16[2,16,64,128]{3,2,1,0:T(8,128)(2,1)S(1)} %get-tuple-element.64), channel_id=1, source_target_pairs={{0,2},{1,3},{2,4},{3,5},{4,6},{5,7},{8,10},{9,11},{10,12},{11,13},... | collective-permute-start | bytes 1572872 | tf_op jit(solution)/shard_map/ppermute | solution.py:31
  74.7 8.3 %collective-permute-done.7 = bf16[2,16,64,128]{3,2,1,0:T(8,128)(2,1)S(1)} collective-permute-done((bf16[2,16,64,128]{3,2,1,0:T(8,128)(2,1)S(1)}, bf16[2,16,64,128]{3,2,1,0:T(8,128)(2,1)S(1)}, u32[]{:S(2)}, u32[]{:S(2)}) %collective-permute-start.7) | collective-permute-done | bytes 524320 | tf_op jit(solution)/shard_map/ppermute | solution.py:31
  84.1 1.4 collective-permute-done.6
  85.5 1.9 fusion.25
  87.4 1.9 convolution_bitcast_fusion.9
  89.4 4.9 %collective-permute-start.17 = (bf16[2,16,64,128]{3,2,1,0:T(8,128)(2,1)}, bf16[2,16,64,128]{3,2,1,0:T(8,128)(2,1)}, u32[]{:S(2)}, u32[]{:S(2)}) collective-permute-start(bf16[2,16,64,128]{3,2,1,0:T(8,128)(2,1)} %get-tuple-element.37), channel_id=1, source_target_pairs={{0,2},{1,3},{2,4},{3,5},{4,6},{5,7},{8,10},{9,11},{10,12},{11,13},... | collective-permute-start | bytes 1572872 | tf_op jit(solution)/shard_map/ppermute | solution.py:31
  94.2 2.4 convolution_bitcast_fusion.4
  96.6 1.6 gather_fusion.5
  98.3 2.3 gather_fusion.4
  100.5 2.3 gather_fusion.3
  102.8 2.2 gather_fusion.2
  105.0 1.7 select_bitcast_fusion.3
  106.7 6.4 %collective-permute-start.8 = (bf16[2,1,4,64,128]{4,3,0,2,1:T(8,128)(2,1)}, bf16[2,1,4,64,128]{4,3,0,2,1:T(8,128)(2,1)}, u32[]{:S(2)}, u32[]{:S(2)}) collective-permute-start(bf16[2,1,4,64,128]{4,3,0,2,1:T(8,128)(2,1)} %select_bitcast_fusion.3), channel_id=1, source_target_pairs={{0,16},{8,24},{16,32},{24,40},{32,48},{40,56},{48,64},{56,72},{64,... | collective-permute-start | bytes 393224 | tf_op jit(solution)/shard_map/ppermute | solution.py:31
  113.1 1.6 select_bitcast_fusion.2
  114.8 4.3 %collective-permute-start.9 = (bf16[2,1,4,64,128]{4,3,0,2,1:T(8,128)(2,1)}, bf16[2,1,4,64,128]{4,3,0,2,1:T(8,128)(2,1)}, u32[]{:S(2)}, u32[]{:S(2)}) collective-permute-start(bf16[2,1,4,64,128]{4,3,0,2,1:T(8,128)(2,1)} %select_bitcast_fusion.2), channel_id=1, source_target_pairs={{0,8},{8,16},{16,24},{24,32},{32,40},{40,48},{48,56},{56,64},{64,7... | collective-permute-start | bytes 393224 | tf_op jit(solution)/shard_map/ppermute | solution.py:31
  119.0 1.7 select_bitcast_fusion.1
  120.7 1.4 collective-permute-start.10
  124.1 1.5 convolution_bitcast_fusion.8
  125.6 1.3 convolution_bitcast_fusion.10
  127.1 1.4 collective-permute-start.16
  128.6 1.8 collective-permute-done.11
  131.6 1.4 convolution_bitcast_fusion.7
  134.2 1.5 convolution_bitcast_fusion.3
  135.7 6.0 %collective-permute-done.16 = bf16[2,16,64,128]{3,2,1,0:T(8,128)(2,1)S(1)} collective-permute-done((bf16[2,16,64,128]{3,2,1,0:T(8,128)(2,1)}, bf16[2,16,64,128]{3,2,1,0:T(8,128)(2,1)S(1)}, u32[]{:S(2)}, u32[]{:S(2)}) %collective-permute-start.16) | collective-permute-done | bytes 524320 | tf_op jit(solution)/shard_map/ppermute | solution.py:31
  141.7 1.7 fusion.26
  145.7 3.7 %collective-permute-start.18 = (bf16[2,1,64,128]{3,2,1,0:T(8,128)(2,1)S(1)}, bf16[2,1,64,128]{3,2,1,0:T(8,128)(2,1)S(1)}, u32[]{:S(2)}, u32[]{:S(2)}) collective-permute-start(bf16[2,1,64,128]{3,2,1,0:T(8,128)(2,1)S(1)} %get-tuple-element.43), channel_id=1, source_target_pairs={{0,8},{8,16},{16,24},{24,32},{32,40},{40,48},{48,56},{56,64},{64,7... | collective-permute-start | bytes 98312 | tf_op jit(solution)/shard_map/ppermute | solution.py:19
  149.4 1.3 collective-permute-start.19
  151.6 2.5 collective-permute-done.19
  158.7 1.5 fusion.27
  162.3 5.5 %collective-permute-start.21 = (bf16[1,16,64,128]{3,2,1,0:T(8,128)(2,1)}, bf16[1,16,64,128]{3,2,1,0:T(8,128)(2,1)}, u32[]{:S(2)}, u32[]{:S(2)}) collective-permute-start(bf16[1,16,64,128]{3,2,1,0:T(8,128)(2,1)} %get-tuple-element.41), channel_id=1, source_target_pairs={{0,1},{1,2},{2,3},{3,4},{4,5},{5,6},{6,7},{8,9},{9,10},{10,11},{11... | collective-permute-start | bytes 786440 | tf_op jit(solution)/shard_map/ppermute | solution.py:31
  167.8 2.3 collective-permute-start.20
  171.4 1.3 convolution_bitcast_fusion
  172.7 2.9 %collective-permute-done.20 = bf16[1,16,64,128]{3,2,1,0:T(8,128)(2,1)} collective-permute-done((bf16[1,16,64,128]{3,2,1,0:T(8,128)(2,1)S(1)}, bf16[1,16,64,128]{3,2,1,0:T(8,128)(2,1)}, u32[]{:S(2)}, u32[]{:S(2)}) %collective-permute-start.20) | collective-permute-done | bytes 262176 | tf_op jit(solution)/shard_map/ppermute | solution.py:31
  175.6 2.5 fusion.28
  181.6 1.3 collective-permute-start.23
  183.7 3.4 %all-to-all-start = ((f32[8,1,12288]{2,1,0:T(1,128)}), f32[8,1,12288]{2,1,0:T(1,128)S(1)}, u32[]{:S(2)}, u32[]{:S(2)}) async-start(f32[8,1,12288]{2,1,0:T(1,128)} %bitcast.230), calls=%async_computation | async-start | bytes 786432 | tf_op jit(solution)/shard_map/all_to_all | solution.py:235
  187.1 4.7 %collective-permute-start.22 = (bf16[2,1,64,128]{3,2,1,0:T(8,128)(2,1)S(1)}, bf16[2,1,64,128]{3,2,1,0:T(8,128)(2,1)S(1)}, u32[]{:S(2)}, u32[]{:S(2)}) collective-permute-start(bf16[2,1,64,128]{3,2,1,0:T(8,128)(2,1)S(1)} %get-tuple-element.39), channel_id=1, source_target_pairs={{0,8},{8,16},{16,24},{24,32},{32,40},{40,48},{48,56},{56,64},{64,7... | collective-permute-start | bytes 98312 | tf_op jit(solution)/shard_map/ppermute | solution.py:19
  198.2 24.2 %all-to-all-start.1 = ((f32[32,1,384]{2,1,0:T(1,128)}), f32[32,1,384]{2,1,0:T(1,128)S(1)}, u32[]{:S(2)}, u32[]{:S(2)}) async-start(f32[32,1,384]{2,1,0:T(1,128)} %bitcast.231), calls=%async_computation.1 | async-start | bytes 98304 | tf_op jit(solution)/shard_map/all_to_all | solution.py:235
  222.4 1.3 convolution_add_fusion.19
  223.8 7.4 %all-to-all-done.1 = f32[32,1,384]{2,1,0:T(1,128)S(1)} async-done(((f32[32,1,384]{2,1,0:T(1,128)}), f32[32,1,384]{2,1,0:T(1,128)S(1)}, u32[]{:S(2)}, u32[]{:S(2)}) %all-to-all-start.1) | async-done | bytes 49184 | tf_op jit(solution)/shard_map/all_to_all | solution.py:235
  231.9 3.9 %all-to-all-start.2 = ((f32[32,1,384]{2,1,0:T(1,128)}), f32[32,1,384]{2,1,0:T(1,128)S(1)}, u32[]{:S(2)}, u32[]{:S(2)}) async-start(f32[32,1,384]{2,1,0:T(1,128)} %broadcast_in_dim.95), calls=%async_computation.2 | async-start | bytes 98304 | tf_op jit(solution)/shard_map/all_to_all | solution.py:238
  235.7 1.6 convolution_add_fusion.18
  237.4 7.1 %all-to-all-done.2 = f32[32,1,384]{2,1,0:T(1,128)S(1)} async-done(((f32[32,1,384]{2,1,0:T(1,128)}), f32[32,1,384]{2,1,0:T(1,128)S(1)}, u32[]{:S(2)}, u32[]{:S(2)}) %all-to-all-start.2) | async-done | bytes 49184 | tf_op jit(solution)/shard_map/all_to_all | solution.py:238
  245.4 7.6 %all-to-all-start.3 = ((f32[8,1,12288]{2,1,0:T(1,128)}), f32[8,1,12288]{2,1,0:T(1,128)S(1)}, u32[]{:S(2)}, u32[]{:S(2)}) async-start(f32[8,1,12288]{2,1,0:T(1,128)} %broadcast_in_dim.97), calls=%async_computation.3 | async-start | bytes 786432 | tf_op jit(solution)/shard_map/all_to_all | solution.py:238
  255.2 5.5 %all-to-all-done.3 = f32[8,1,12288]{2,1,0:T(1,128)S(1)} async-done(((f32[8,1,12288]{2,1,0:T(1,128)}), f32[8,1,12288]{2,1,0:T(1,128)S(1)}, u32[]{:S(2)}, u32[]{:S(2)}) %all-to-all-start.3) | async-done | bytes 393248 | tf_op jit(solution)/shard_map/all_to_all | solution.py:238
  (261 shorter events, 56.4 us)
Async XLA Ops:
  0.6 6.2 %copy-start = (s32[32,16]{0,1:T(8,128)S(1)}, s32[32,16]{0,1:T(8,128)}, u32[]{:S(2)}) copy-start(s32[32,16]{0,1:T(8,128)} %param.21) | copy-start | bytes 6148
  0.6 27.7 %copy-start.31 = (s32[32,16]{0,1:T(8,128)S(1)}, s32[32,16]{0,1:T(8,128)}, u32[]{:S(2)}) copy-start(s32[32,16]{0,1:T(8,128)} %param.19) | copy-start | bytes 6148
  0.7 22.4 %copy-start.15 = (bf16[2,16,64,128]{3,2,1,0:T(8,128)(2,1)S(1)}, bf16[2,16,64,128]{3,2,1,0:T(8,128)(2,1)}, u32[]{:S(2)}) copy-start(bf16[2,16,64,128]{3,2,1,0:T(8,128)(2,1)} %param.22) | copy-start | bytes 1572868
  0.7 27.7 %copy-start.39 = (s32[32,16]{0,1:T(8,128)S(1)}, s32[32,16]{0,1:T(8,128)}, u32[]{:S(2)}) copy-start(s32[32,16]{0,1:T(8,128)} %param.20) | copy-start | bytes 6148
  1.5 32.9 %collective-permute-start = (bf16[2,1,64,128]{3,2,1,0:T(8,128)(2,1)S(1)}, bf16[2,1,64,128]{3,2,1,0:T(8,128)(2,1)S(1)}, u32[]{:S(2)}, u32[]{:S(2)}) collective-permute-start(bf16[2,1,64,128]{3,2,1,0:T(8,128)(2,1)S(1)} %get-tuple-element.49), channel_id=1, source_target_pairs={{0,8},{8,16},{16,24},{24,32},{32,40},{40,48},{48,56},{56,64},{64,7... | collective-permute-start | bytes 98312 | tf_op jit(solution)/shard_map/ppermute | solution.py:19
  5.5 29.0 %collective-permute-start.1 = (bf16[2,1,64,128]{3,2,1,0:T(8,128)(2,1)S(1)}, bf16[2,1,64,128]{3,2,1,0:T(8,128)(2,1)S(1)}, u32[]{:S(2)}, u32[]{:S(2)}) collective-permute-start(bf16[2,1,64,128]{3,2,1,0:T(8,128)(2,1)S(1)} %get-tuple-element.50), channel_id=1, source_target_pairs={{8,0},{16,8},{24,16},{32,24},{40,32},{48,40},{56,48},{64,56},{72,6... | collective-permute-start | bytes 98312 | tf_op jit(solution)/shard_map/ppermute | solution.py:21
  10.6 23.9 %copy-start.2 = (bf16[2,16,64,128]{3,2,1,0:T(8,128)(2,1)S(1)}, bf16[2,16,64,128]{3,2,1,0:T(8,128)(2,1)}, u32[]{:S(2)}) copy-start(bf16[2,16,64,128]{3,2,1,0:T(8,128)(2,1)} %param.14) | copy-start | bytes 1572868
  12.4 56.2 %collective-permute-start.12 = (bf16[2,1,4,64,128]{4,2,1,3,0:T(4,128)(2,1)S(1)}, bf16[2,1,4,64,128]{4,2,1,3,0:T(4,128)(2,1)}, u32[]{:S(2)}, u32[]{:S(2)}) collective-permute-start(bf16[2,1,4,64,128]{4,2,1,3,0:T(4,128)(2,1)S(1)} %fusion.107), channel_id=1, source_target_pairs={{16,0},{24,8},{32,16},{40,24},{48,32},{56,40},{64,48},{72,56},{80,... | collective-permute-start | bytes 393224 | tf_op jit(solution)/shard_map/ppermute | solution.py:31
  16.2 52.5 %collective-permute-start.15 = (bf16[2,1,4,64,128]{4,2,1,3,0:T(4,128)(2,1)}, bf16[2,1,4,64,128]{4,2,1,3,0:T(4,128)(2,1)}, u32[]{:S(2)}, u32[]{:S(2)}) collective-permute-start(bf16[2,1,4,64,128]{4,2,1,3,0:T(4,128)(2,1)} %fusion.104), channel_id=1, source_target_pairs={{0,16},{8,24},{16,32},{24,40},{32,48},{40,56},{48,64},{56,72},{64,... | collective-permute-start | bytes 393224 | tf_op jit(solution)/shard_map/ppermute | solution.py:31
  24.4 44.2 %collective-permute-start.14 = (bf16[2,1,4,64,128]{4,2,1,3,0:T(4,128)(2,1)}, bf16[2,1,4,64,128]{4,2,1,3,0:T(4,128)(2,1)}, u32[]{:S(2)}, u32[]{:S(2)}) collective-permute-start(bf16[2,1,4,64,128]{4,2,1,3,0:T(4,128)(2,1)} %fusion.105), channel_id=1, source_target_pairs={{0,8},{8,16},{16,24},{24,32},{32,40},{40,48},{48,56},{56,64},{64,7... | collective-permute-start | bytes 393224 | tf_op jit(solution)/shard_map/ppermute | solution.py:31
  34.5 3.2 %copy-start.35 = (bf16[2,1,64,128]{3,2,1,0:T(8,128)(2,1)}, bf16[2,1,64,128]{3,2,1,0:T(8,128)(2,1)S(1)}, u32[]{:S(2)}) copy-start(bf16[2,1,64,128]{3,2,1,0:T(8,128)(2,1)S(1)} %collective-permute-done.1) | copy-start | bytes 98308
  37.7 8.6 %copy-start.34 = (bf16[3,64,64]{2,1,0:T(8,128)(2,1)S(1)}, bf16[3,64,64]{2,1,0:T(8,128)(2,1)}, u32[]{:S(2)}) copy-start(bf16[3,64,64]{2,1,0:T(8,128)(2,1)} %param.16) | copy-start | bytes 73732
  39.2 13.6 %copy-start.5 = (bf16[2,16,64,128]{3,2,1,0:T(8,128)(2,1)}, bf16[2,16,64,128]{3,2,1,0:T(8,128)(2,1)S(1)}, u32[]{:S(2)}) copy-start(bf16[2,16,64,128]{3,2,1,0:T(8,128)(2,1)S(1)} %get-tuple-element.60) | copy-start | bytes 1572868
  39.2 13.1 %copy-start.10 = (bf16[1,16,64,128]{3,2,1,0:T(8,128)(2,1)}, bf16[1,16,64,128]{3,2,1,0:T(8,128)(2,1)S(1)}, u32[]{:S(2)}) copy-start(bf16[1,16,64,128]{3,2,1,0:T(8,128)(2,1)S(1)} %get-tuple-element.47) | copy-start | bytes 786436
  39.2 13.5 %copy-start.24 = (bf16[1,16,64,128]{3,2,1,0:T(8,128)(2,1)}, bf16[1,16,64,128]{3,2,1,0:T(8,128)(2,1)S(1)}, u32[]{:S(2)}) copy-start(bf16[1,16,64,128]{3,2,1,0:T(8,128)(2,1)S(1)} %get-tuple-element.48) | copy-start | bytes 786436
  39.2 13.5 %collective-permute-start.2 = (bf16[1,16,64,128]{3,2,1,0:T(8,128)(2,1)S(1)}, bf16[1,16,64,128]{3,2,1,0:T(8,128)(2,1)S(1)}, u32[]{:S(2)}, u32[]{:S(2)}) collective-permute-start(bf16[1,16,64,128]{3,2,1,0:T(8,128)(2,1)S(1)} %get-tuple-element.47), channel_id=1, source_target_pairs={{0,1},{1,2},{2,3},{3,4},{4,5},{5,6},{6,7},{8,9},{9,10},{10,11},{11... | collective-permute-start | bytes 786440 | tf_op jit(solution)/shard_map/ppermute | solution.py:31
  44.3 7.7 %collective-permute-start.3 = (bf16[1,16,64,128]{3,2,1,0:T(8,128)(2,1)S(1)}, bf16[1,16,64,128]{3,2,1,0:T(8,128)(2,1)S(1)}, u32[]{:S(2)}, u32[]{:S(2)}) collective-permute-start(bf16[1,16,64,128]{3,2,1,0:T(8,128)(2,1)S(1)} %get-tuple-element.48), channel_id=1, source_target_pairs={{1,0},{2,1},{3,2},{4,3},{5,4},{6,5},{7,6},{9,8},{10,9},{11,10},{12... | collective-permute-start | bytes 786440 | tf_op jit(solution)/shard_map/ppermute | solution.py:31
  55.0 8.3 %copy-start.20 = (bf16[3,3,64,64]{3,2,1,0:T(8,128)(2,1)S(1)}, bf16[3,3,64,64]{3,2,1,0:T(8,128)(2,1)}, u32[]{:S(2)}) copy-start(bf16[3,3,64,64]{3,2,1,0:T(8,128)(2,1)} %param.17) | copy-start | bytes 221188
  55.0 4.3 %collective-permute-start.4 = (bf16[2,1,64,128]{3,2,1,0:T(8,128)(2,1)S(1)}, bf16[2,1,64,128]{3,2,1,0:T(8,128)(2,1)S(1)}, u32[]{:S(2)}, u32[]{:S(2)}) collective-permute-start(bf16[2,1,64,128]{3,2,1,0:T(8,128)(2,1)S(1)} %get-tuple-element.45), channel_id=1, source_target_pairs={{0,8},{8,16},{16,24},{24,32},{32,40},{40,48},{48,56},{56,64},{64,7... | collective-permute-start | bytes 98312 | tf_op jit(solution)/shard_map/ppermute | solution.py:19
  57.9 4.7 %collective-permute-start.5 = (bf16[2,1,64,128]{3,2,1,0:T(8,128)(2,1)S(1)}, bf16[2,1,64,128]{3,2,1,0:T(8,128)(2,1)S(1)}, u32[]{:S(2)}, u32[]{:S(2)}) collective-permute-start(bf16[2,1,64,128]{3,2,1,0:T(8,128)(2,1)S(1)} %get-tuple-element.46), channel_id=1, source_target_pairs={{8,0},{16,8},{24,16},{32,24},{40,32},{48,40},{56,48},{64,56},{72,6... | collective-permute-start | bytes 98312 | tf_op jit(solution)/shard_map/ppermute | solution.py:21
  59.3 4.3 %copy-start.28 = (bf16[2,1,64,128]{3,2,1,0:T(8,128)(2,1)}, bf16[2,1,64,128]{3,2,1,0:T(8,128)(2,1)S(1)}, u32[]{:S(2)}) copy-start(bf16[2,1,64,128]{3,2,1,0:T(8,128)(2,1)S(1)} %collective-permute-done.4) | copy-start | bytes 98308
  59.3 9.4 %collective-permute-start.13 = (bf16[2,1,4,64,128]{4,2,1,3,0:T(4,128)(2,1)S(1)}, bf16[2,1,4,64,128]{4,2,1,3,0:T(4,128)(2,1)S(1)}, u32[]{:S(2)}, u32[]{:S(2)}) collective-permute-start(bf16[2,1,4,64,128]{4,2,1,3,0:T(4,128)(2,1)S(1)} %fusion.106), channel_id=1, source_target_pairs={{8,0},{16,8},{24,16},{32,24},{40,32},{48,40},{56,48},{64,56},{72,6... | collective-permute-start | bytes 393224 | tf_op jit(solution)/shard_map/ppermute | solution.py:31
  62.6 3.2 %copy-start.37 = (bf16[2,1,64,128]{3,2,1,0:T(8,128)(2,1)}, bf16[2,1,64,128]{3,2,1,0:T(8,128)(2,1)S(1)}, u32[]{:S(2)}) copy-start(bf16[2,1,64,128]{3,2,1,0:T(8,128)(2,1)S(1)} %collective-permute-done.5) | copy-start | bytes 98308
  65.8 2.8 %copy-start.41 = (s32[4]{0:T(128)S(1)}, s32[4]{0:T(128)}, u32[]{:S(2)}) copy-start(s32[4]{0:T(128)} %compare_select_fusion.7) | copy-start | bytes 52
  67.3 15.7 %collective-permute-start.7 = (bf16[2,16,64,128]{3,2,1,0:T(8,128)(2,1)S(1)}, bf16[2,16,64,128]{3,2,1,0:T(8,128)(2,1)S(1)}, u32[]{:S(2)}, u32[]{:S(2)}) collective-permute-start(bf16[2,16,64,128]{3,2,1,0:T(8,128)(2,1)S(1)} %get-tuple-element.64), channel_id=1, source_target_pairs={{2,0},{3,1},{4,2},{5,3},{6,4},{7,5},{10,8},{11,9},{12,10},{13,11},... | collective-permute-start | bytes 1572872 | tf_op jit(solution)/shard_map/ppermute | solution.py:31
  68.6 5.8 %copy-start.32 = (bf16[3,64,64]{2,1,0:T(8,128)(2,1)S(1)}, bf16[3,64,64]{2,1,0:T(8,128)(2,1)}, u32[]{:S(2)}) copy-start(bf16[3,64,64]{2,1,0:T(8,128)(2,1)} %param.18) | copy-start | bytes 73732
  70.2 15.3 %copy-start.45 = (f32[2,64,128,16]{2,3,1,0:T(8,128)}, f32[2,64,128,16]{2,3,1,0:T(8,128)S(1)}, u32[]{:S(2)}) copy-start(f32[2,64,128,16]{2,3,1,0:T(8,128)S(1)} %convolution_bitcast_fusion.6) | copy-start | bytes 3145732
  70.2 15.3 %collective-permute-start.6 = (bf16[2,16,64,128]{3,2,1,0:T(8,128)(2,1)S(1)}, bf16[2,16,64,128]{3,2,1,0:T(8,128)(2,1)S(1)}, u32[]{:S(2)}, u32[]{:S(2)}) collective-permute-start(bf16[2,16,64,128]{3,2,1,0:T(8,128)(2,1)S(1)} %get-tuple-element.64), channel_id=1, source_target_pairs={{0,2},{1,3},{2,4},{3,5},{4,6},{5,7},{8,10},{9,11},{10,12},{11,13},... | collective-permute-start | bytes 1572872 | tf_op jit(solution)/shard_map/ppermute | solution.py:31
  74.7 10.8 %copy-start.16 = (bf16[2,16,64,128]{3,2,1,0:T(8,128)(2,1)S(1)}, bf16[2,16,64,128]{3,2,1,0:T(8,128)(2,1)}, u32[]{:S(2)}) copy-start(bf16[2,16,64,128]{3,2,1,0:T(8,128)(2,1)} %param.22) | copy-start | bytes 1572868
  89.4 44.8 %collective-permute-start.17 = (bf16[2,16,64,128]{3,2,1,0:T(8,128)(2,1)}, bf16[2,16,64,128]{3,2,1,0:T(8,128)(2,1)}, u32[]{:S(2)}, u32[]{:S(2)}) collective-permute-start(bf16[2,16,64,128]{3,2,1,0:T(8,128)(2,1)} %get-tuple-element.37), channel_id=1, source_target_pairs={{0,2},{1,3},{2,4},{3,5},{4,6},{5,7},{8,10},{9,11},{10,12},{11,13},... | collective-permute-start | bytes 1572872 | tf_op jit(solution)/shard_map/ppermute | solution.py:31
  98.2 23.9 %copy-start.40 = (pred[4]{0:T(512)(128)(4,1)S(1)}, pred[4]{0:T(512)(128)(4,1)}, u32[]{:S(2)}) copy-start(pred[4]{0:T(512)(128)(4,1)} %compare_and_fusion.4) | copy-start | bytes 16
  105.0 20.6 %copy-start.19 = (bf16[2,16,64,128]{3,2,1,0:T(8,128)(2,1)S(1)}, bf16[2,16,64,128]{3,2,1,0:T(8,128)(2,1)}, u32[]{:S(2)}) copy-start(bf16[2,16,64,128]{3,2,1,0:T(8,128)(2,1)} %copy-done.18) | copy-start | bytes 1572868
  106.7 20.4 %collective-permute-start.8 = (bf16[2,1,4,64,128]{4,3,0,2,1:T(8,128)(2,1)}, bf16[2,1,4,64,128]{4,3,0,2,1:T(8,128)(2,1)}, u32[]{:S(2)}, u32[]{:S(2)}) collective-permute-start(bf16[2,1,4,64,128]{4,3,0,2,1:T(8,128)(2,1)} %select_bitcast_fusion.3), channel_id=1, source_target_pairs={{0,16},{8,24},{16,32},{24,40},{32,48},{40,56},{48,64},{56,72},{64,... | collective-permute-start | bytes 393224 | tf_op jit(solution)/shard_map/ppermute | solution.py:31
  114.8 13.8 %collective-permute-start.9 = (bf16[2,1,4,64,128]{4,3,0,2,1:T(8,128)(2,1)}, bf16[2,1,4,64,128]{4,3,0,2,1:T(8,128)(2,1)}, u32[]{:S(2)}, u32[]{:S(2)}) collective-permute-start(bf16[2,1,4,64,128]{4,3,0,2,1:T(8,128)(2,1)} %select_bitcast_fusion.2), channel_id=1, source_target_pairs={{0,8},{8,16},{16,24},{24,32},{32,40},{40,48},{48,56},{56,64},{64,7... | collective-permute-start | bytes 393224 | tf_op jit(solution)/shard_map/ppermute | solution.py:31
  120.7 6.3 %copy-start.30 = (f32[1,64,64]{2,1,0:T(8,128)S(1)}, f32[1,64,64]{2,1,0:T(8,128)}, u32[]{:S(2)}) copy-start(f32[1,64,64]{2,1,0:T(8,128)} %convolution_bitcast_fusion.9) | copy-start | bytes 49156
  120.7 7.9 %collective-permute-start.10 = (bf16[2,1,4,64,128]{4,3,0,2,1:T(8,128)(2,1)}, bf16[2,1,4,64,128]{4,3,0,2,1:T(8,128)(2,1)}, u32[]{:S(2)}, u32[]{:S(2)}) collective-permute-start(bf16[2,1,4,64,128]{4,3,0,2,1:T(8,128)(2,1)} %select_bitcast_fusion.1), channel_id=1, source_target_pairs={{8,0},{16,8},{24,16},{32,24},{40,32},{48,40},{56,48},{64,56},{72,6... | collective-permute-start | bytes 393224 | tf_op jit(solution)/shard_map/ppermute | solution.py:31
  122.9 7.5 %collective-permute-start.11 = (bf16[2,1,4,64,128]{4,3,0,2,1:T(8,128)(2,1)}, bf16[2,1,4,64,128]{4,3,0,2,1:T(8,128)(2,1)}, u32[]{:S(2)}, u32[]{:S(2)}) collective-permute-start(bf16[2,1,4,64,128]{4,3,0,2,1:T(8,128)(2,1)} %select_bitcast_fusion), channel_id=1, source_target_pairs={{16,0},{24,8},{32,16},{40,24},{48,32},{56,40},{64,48},{72,56},{80,... | collective-permute-start | bytes 393224 | tf_op jit(solution)/shard_map/ppermute | solution.py:31
  127.1 5.9 %copy-start.8 = (bf16[2,16,64,128]{3,2,1,0:T(8,128)(2,1)S(1)}, bf16[2,16,64,128]{3,2,1,0:T(8,128)(2,1)}, u32[]{:S(2)}) copy-start(bf16[2,16,64,128]{3,2,1,0:T(8,128)(2,1)} %get-tuple-element.38) | copy-start | bytes 1572868
  127.1 14.6 %collective-permute-start.16 = (bf16[2,16,64,128]{3,2,1,0:T(8,128)(2,1)}, bf16[2,16,64,128]{3,2,1,0:T(8,128)(2,1)S(1)}, u32[]{:S(2)}, u32[]{:S(2)}) collective-permute-start(bf16[2,16,64,128]{3,2,1,0:T(8,128)(2,1)} %get-tuple-element.37), channel_id=1, source_target_pairs={{2,0},{3,1},{4,2},{5,3},{6,4},{7,5},{10,8},{11,9},{12,10},{13,11},... | collective-permute-start | bytes 1572872 | tf_op jit(solution)/shard_map/ppermute | solution.py:31
  131.5 10.1 %copy-start.46 = (f32[2,64,128,16]{2,3,1,0:T(8,128)S(1)}, f32[2,64,128,16]{2,3,1,0:T(8,128)}, u32[]{:S(2)}) copy-start(f32[2,64,128,16]{2,3,1,0:T(8,128)} %copy-done.45) | copy-start | bytes 3145732
  133.0 8.7 %copy-start.44 = (f32[2,16,64,128]{3,2,1,0:T(8,128)S(1)}, f32[2,16,64,128]{3,2,1,0:T(8,128)}, u32[]{:S(2)}) copy-start(f32[2,16,64,128]{3,2,1,0:T(8,128)} %get-tuple-element.65) | copy-start | bytes 3145732
  134.2 7.5 %copy-start.9 = (f32[2,16,64,128]{3,2,1,0:T(8,128)S(1)}, f32[2,16,64,128]{3,2,1,0:T(8,128)}, u32[]{:S(2)}) copy-start(f32[2,16,64,128]{3,2,1,0:T(8,128)} %convolution_bitcast_fusion.4) | copy-start | bytes 3145732
  134.2 7.5 %copy-start.17 = (bf16[2,16,64,128]{3,2,1,0:T(8,128)(2,1)S(1)}, bf16[2,16,64,128]{3,2,1,0:T(8,128)(2,1)}, u32[]{:S(2)}) copy-start(bf16[2,16,64,128]{3,2,1,0:T(8,128)(2,1)} %param.22) | copy-start | bytes 1572868
  143.4 7.7 %copy-start.3 = (bf16[2,16,64,128]{3,2,1,0:T(8,128)(2,1)}, bf16[2,16,64,128]{3,2,1,0:T(8,128)(2,1)S(1)}, u32[]{:S(2)}) copy-start(bf16[2,16,64,128]{3,2,1,0:T(8,128)(2,1)S(1)} %get-tuple-element.66) | copy-start | bytes 1572868
  145.0 5.7 %copy-start.38 = (bf16[2,1,64,128]{3,2,1,0:T(8,128)(2,1)S(1)}, bf16[2,1,64,128]{3,2,1,0:T(8,128)(2,1)}, u32[]{:S(2)}) copy-start(bf16[2,1,64,128]{3,2,1,0:T(8,128)(2,1)} %copy-done.37) | copy-start | bytes 98308
  145.7 5.4 %copy-start.29 = (bf16[2,1,64,128]{3,2,1,0:T(8,128)(2,1)S(1)}, bf16[2,1,64,128]{3,2,1,0:T(8,128)(2,1)}, u32[]{:S(2)}) copy-start(bf16[2,1,64,128]{3,2,1,0:T(8,128)(2,1)} %copy-done.28) | copy-start | bytes 98308
  145.7 5.9 %collective-permute-start.18 = (bf16[2,1,64,128]{3,2,1,0:T(8,128)(2,1)S(1)}, bf16[2,1,64,128]{3,2,1,0:T(8,128)(2,1)S(1)}, u32[]{:S(2)}, u32[]{:S(2)}) collective-permute-start(bf16[2,1,64,128]{3,2,1,0:T(8,128)(2,1)S(1)} %get-tuple-element.43), channel_id=1, source_target_pairs={{0,8},{8,16},{16,24},{24,32},{32,40},{40,48},{48,56},{56,64},{64,7... | collective-permute-start | bytes 98312 | tf_op jit(solution)/shard_map/ppermute | solution.py:19
  149.4 4.7 %collective-permute-start.19 = (bf16[2,1,64,128]{3,2,1,0:T(8,128)(2,1)S(1)}, bf16[2,1,64,128]{3,2,1,0:T(8,128)(2,1)S(1)}, u32[]{:S(2)}, u32[]{:S(2)}) collective-permute-start(bf16[2,1,64,128]{3,2,1,0:T(8,128)(2,1)S(1)} %get-tuple-element.44), channel_id=1, source_target_pairs={{8,0},{16,8},{24,16},{32,24},{40,32},{48,40},{56,48},{64,56},{72,6... | collective-permute-start | bytes 98312 | tf_op jit(solution)/shard_map/ppermute | solution.py:21
  151.5 3.3 %copy-start.21 = (bf16[3,3,64,64]{3,2,1,0:T(8,128)(2,1)S(1)}, bf16[3,3,64,64]{3,2,1,0:T(8,128)(2,1)}, u32[]{:S(2)}) copy-start(bf16[3,3,64,64]{3,2,1,0:T(8,128)(2,1)} %param.17) | copy-start | bytes 221188
  160.4 9.7 %copy-start.25 = (bf16[1,16,64,128]{3,2,1,0:T(8,128)(2,1)S(1)}, bf16[1,16,64,128]{3,2,1,0:T(8,128)(2,1)}, u32[]{:S(2)}) copy-start(bf16[1,16,64,128]{3,2,1,0:T(8,128)(2,1)} %copy-done.24) | copy-start | bytes 786436
  160.4 9.7 %copy-start.43 = (bf16[1,16,64,128]{3,2,1,0:T(8,128)(2,1)S(1)}, bf16[1,16,64,128]{3,2,1,0:T(8,128)(2,1)}, u32[]{:S(2)}) copy-start(bf16[1,16,64,128]{3,2,1,0:T(8,128)(2,1)} %copy-done.42) | copy-start | bytes 786436
  161.2 9.3 %copy-start.11 = (bf16[1,16,64,128]{3,2,1,0:T(8,128)(2,1)S(1)}, bf16[1,16,64,128]{3,2,1,0:T(8,128)(2,1)}, u32[]{:S(2)}) copy-start(bf16[1,16,64,128]{3,2,1,0:T(8,128)(2,1)} %copy-done.10) | copy-start | bytes 786436
  161.2 9.3 %copy-start.23 = (bf16[1,16,64,128]{3,2,1,0:T(8,128)(2,1)S(1)}, bf16[1,16,64,128]{3,2,1,0:T(8,128)(2,1)}, u32[]{:S(2)}) copy-start(bf16[1,16,64,128]{3,2,1,0:T(8,128)(2,1)} %copy-done.22) | copy-start | bytes 786436
  162.3 9.1 %collective-permute-start.21 = (bf16[1,16,64,128]{3,2,1,0:T(8,128)(2,1)}, bf16[1,16,64,128]{3,2,1,0:T(8,128)(2,1)}, u32[]{:S(2)}, u32[]{:S(2)}) collective-permute-start(bf16[1,16,64,128]{3,2,1,0:T(8,128)(2,1)} %get-tuple-element.41), channel_id=1, source_target_pairs={{0,1},{1,2},{2,3},{3,4},{4,5},{5,6},{6,7},{8,9},{9,10},{10,11},{11... | collective-permute-start | bytes 786440 | tf_op jit(solution)/shard_map/ppermute | solution.py:31
  167.8 7.8 %collective-permute-start.20 = (bf16[1,16,64,128]{3,2,1,0:T(8,128)(2,1)S(1)}, bf16[1,16,64,128]{3,2,1,0:T(8,128)(2,1)}, u32[]{:S(2)}, u32[]{:S(2)}) collective-permute-start(bf16[1,16,64,128]{3,2,1,0:T(8,128)(2,1)S(1)} %get-tuple-element.42), channel_id=1, source_target_pairs={{1,0},{2,1},{3,2},{4,3},{5,4},{6,5},{7,6},{9,8},{10,9},{11,10},{12... | collective-permute-start | bytes 786440 | tf_op jit(solution)/shard_map/ppermute | solution.py:31
  170.9 4.7 %copy-start.47 = (f32[2,16,64,128]{3,2,1,0:T(8,128)S(1)}, f32[2,16,64,128]{3,2,1,0:T(8,128)}, u32[]{:S(2)}) copy-start(f32[2,16,64,128]{3,2,1,0:T(8,128)} %get-tuple-element.61) | copy-start | bytes 3145732
  170.9 4.7 %copy-start.50 = (bf16[2,16,64,128]{3,2,1,0:T(8,128)(2,1)S(1)}, bf16[2,16,64,128]{3,2,1,0:T(8,128)(2,1)}, u32[]{:S(2)}) copy-start(bf16[2,16,64,128]{3,2,1,0:T(8,128)(2,1)} %get-tuple-element.69) | copy-start | bytes 1572868
  181.6 10.2 %collective-permute-start.23 = (bf16[2,1,64,128]{3,2,1,0:T(8,128)(2,1)S(1)}, bf16[2,1,64,128]{3,2,1,0:T(8,128)(2,1)S(1)}, u32[]{:S(2)}, u32[]{:S(2)}) collective-permute-start(bf16[2,1,64,128]{3,2,1,0:T(8,128)(2,1)S(1)} %get-tuple-element.40), channel_id=1, source_target_pairs={{8,0},{16,8},{24,16},{32,24},{40,32},{48,40},{56,48},{64,56},{72,6... | collective-permute-start | bytes 98312 | tf_op jit(solution)/shard_map/ppermute | solution.py:21
  183.7 13.6 %all-to-all-start = ((f32[8,1,12288]{2,1,0:T(1,128)}), f32[8,1,12288]{2,1,0:T(1,128)S(1)}, u32[]{:S(2)}, u32[]{:S(2)}) async-start(f32[8,1,12288]{2,1,0:T(1,128)} %bitcast.230), calls=%async_computation | async-start | bytes 786432 | tf_op jit(solution)/shard_map/all_to_all | solution.py:235
  187.1 5.8 %collective-permute-start.22 = (bf16[2,1,64,128]{3,2,1,0:T(8,128)(2,1)S(1)}, bf16[2,1,64,128]{3,2,1,0:T(8,128)(2,1)S(1)}, u32[]{:S(2)}, u32[]{:S(2)}) collective-permute-start(bf16[2,1,64,128]{3,2,1,0:T(8,128)(2,1)S(1)} %get-tuple-element.39), channel_id=1, source_target_pairs={{0,8},{8,16},{16,24},{24,32},{32,40},{40,48},{48,56},{56,64},{64,7... | collective-permute-start | bytes 98312 | tf_op jit(solution)/shard_map/ppermute | solution.py:19
  198.2 32.9 %all-to-all-start.1 = ((f32[32,1,384]{2,1,0:T(1,128)}), f32[32,1,384]{2,1,0:T(1,128)S(1)}, u32[]{:S(2)}, u32[]{:S(2)}) async-start(f32[32,1,384]{2,1,0:T(1,128)} %bitcast.231), calls=%async_computation.1 | async-start | bytes 98304 | tf_op jit(solution)/shard_map/all_to_all | solution.py:235
  231.9 12.6 %all-to-all-start.2 = ((f32[32,1,384]{2,1,0:T(1,128)}), f32[32,1,384]{2,1,0:T(1,128)S(1)}, u32[]{:S(2)}, u32[]{:S(2)}) async-start(f32[32,1,384]{2,1,0:T(1,128)} %broadcast_in_dim.95), calls=%async_computation.2 | async-start | bytes 98304 | tf_op jit(solution)/shard_map/all_to_all | solution.py:238
  245.4 15.3 %all-to-all-start.3 = ((f32[8,1,12288]{2,1,0:T(1,128)}), f32[8,1,12288]{2,1,0:T(1,128)S(1)}, u32[]{:S(2)}, u32[]{:S(2)}) async-start(f32[8,1,12288]{2,1,0:T(1,128)} %broadcast_in_dim.97), calls=%async_computation.3 | async-start | bytes 786432 | tf_op jit(solution)/shard_map/all_to_all | solution.py:238
  254.1 11.1 %copy-start.1 = (s32[32,16]{0,1:T(8,128)S(1)}, s32[32,16]{0,1:T(8,128)}, u32[]{:S(2)}) copy-start(s32[32,16]{0,1:T(8,128)} %param.21) | copy-start | bytes 6148
  (15 other events, 19.5 us)

commit v3 on v2

--- a/solution.py
+++ b/solution.py
@@ -229,13 +229,13 @@
 
 def exchange_sum(parts, axes):
     flat = jnp.concatenate([part.reshape(-1) for part in parts])
-    sizes = [lax.axis_size(axis) for axis in axes]
-    for axis, size in zip(axes, sizes):
-        pieces = flat.reshape(size, -1)
-        flat = jnp.sum(lax.all_to_all(pieces, axis, 0, 0, tiled=True), axis=0)
-    for axis, size in reversed(list(zip(axes, sizes))):
-        copies = jnp.broadcast_to(flat[None], (size,) + flat.shape)
-        flat = lax.all_to_all(copies, axis, 0, 0, tiled=True).reshape(-1)
+    size = 1
+    for axis in axes:
+        size *= lax.axis_size(axis)
+    pieces = flat.reshape(size, -1)
+    flat = jnp.sum(lax.all_to_all(pieces, axes, 0, 0, tiled=True), axis=0)
+    copies = jnp.broadcast_to(flat[None], (size,) + flat.shape)
+    flat = lax.all_to_all(copies, axes, 0, 0, tiled=True).reshape(-1)
     results = []
     start = 0
     for part in parts:

time: 267 us -> 257 us (0.963)
  starting transfers between devices: 113 us -> 103 us
  waiting for transfers between devices: 51 us -> 55.2 us
    all_to_all x4 -> x2, starting transfers between devices: 39 us -> 30.7 us  [the longest x1 23.3 us: exchange_sum(): flat = jnp.sum(lax.all_to_all(pieces, axes, 0, 0, tiled=True), axis=0)]
    all_to_all x4 -> x2, waiting for transfers between devices: 20 us -> 23.6 us  [the longest x1 13 us: exchange_sum(): flat = lax.all_to_all(copies, axes, 0, 0, tiled=True).reshape(-1)]
  transfers between devices with their start and end apart: 28 -> 26, of which waited for: 12 -> 12; matrix products, arithmetic and copies ran while one was open for 25% -> 25% of each run, Pallas kernels for 0% -> 0%
where the time goes in v3:
time: 257 us; the launch traced here: 255 us
  starting transfers between devices  103 us (40%)
  waiting for transfers between devices  55.2 us (21%)
  matrix products  49.2 us (19%)
  local copies, waits for them, and re-layouts  24.9 us (10%)
  other arithmetic  20.4 us (8%)
    ppermute x16, starting transfers between devices, from_behind(): return lax.ppermute(array, axis, pairs)  53.4 us
    ppermute x16, waiting for transfers between devices, from_behind(): return lax.ppermute(array, axis, pairs)  26.4 us
    all_to_all x1, starting transfers between devices, exchange_sum(): flat = jnp.sum(lax.all_to_all(pieces, axes, 0, 0, tiled=True), axis=0)  23.3 us
    ppermute x4, starting transfers between devices, with_halo(): lax.ppermute(tail, axis, [(i, (i + 1) % count) for i in range(ends)])  14 us
    all_to_all x1, waiting for transfers between devices, exchange_sum(): flat = lax.all_to_all(copies, axes, 0, 0, tiled=True).reshape(-1)  13 us
    gather x8, local copies, waits for them, and re-layouts, pick_strips(): gathered = jnp.take(values, strip_ids.reshape(-1), axis=1)  12.8 us
    dot_general x18, matrix products, spatial_transpose(): jnp.einsum('oc,fsop->fscp', weight[row_tap, col_tap], padded[:, 2 - row_t...  11.4 us
    all_to_all x1, waiting for transfers between devices, exchange_sum(): flat = jnp.sum(lax.all_to_all(pieces, axes, 0, 0, tiled=True), axis=0)  10.6 us
  transfers between devices with their start and end apart: 26, of which 12 were waited for; matrix products, arithmetic and copies ran while one was open for 25% of the time, Pallas kernels for 0%

profile of v3, /device:TPU:1, one launch (start us, length us, event | category | flops | bytes accessed | tf_op | source)
XLA Modules:
  0.0 255.0 jit_solution(9919394264828254350)
XLA Ops:
  1.5 4.0 %collective-permute-start = (bf16[2,1,64,128]{3,2,1,0:T(8,128)(2,1)S(1)}, bf16[2,1,64,128]{3,2,1,0:T(8,128)(2,1)S(1)}, u32[]{:S(2)}, u32[]{:S(2)}) collective-permute-start(bf16[2,1,64,128]{3,2,1,0:T(8,128)(2,1)S(1)} %get-tuple-element.49), channel_id=1, source_target_pairs={{0,8},{8,16},{16,24},{24,32},{32,40},{40,48},{48,56},{56,64},{64,7... | collective-permute-start | bytes 98312 | tf_op jit(solution)/shard_map/ppermute | solution.py:19
  5.5 1.3 collective-permute-start.1
  10.6 1.7 gather_fusion.6
  12.4 1.3 collective-permute-start.12
  13.8 1.6 gather_fusion.9
  16.2 6.9 %collective-permute-start.15 = (bf16[2,1,4,64,128]{4,2,1,3,0:T(4,128)(2,1)}, bf16[2,1,4,64,128]{4,2,1,3,0:T(4,128)(2,1)}, u32[]{:S(2)}, u32[]{:S(2)}) collective-permute-start(bf16[2,1,4,64,128]{4,2,1,3,0:T(4,128)(2,1)} %fusion.104), channel_id=1, source_target_pairs={{0,16},{8,24},{16,32},{24,40},{32,48},{40,56},{48,64},{56,72},{64,... | collective-permute-start | bytes 393224 | tf_op jit(solution)/shard_map/ppermute | solution.py:31
  24.4 3.9 %collective-permute-start.14 = (bf16[2,1,4,64,128]{4,2,1,3,0:T(4,128)(2,1)}, bf16[2,1,4,64,128]{4,2,1,3,0:T(4,128)(2,1)}, u32[]{:S(2)}, u32[]{:S(2)}) collective-permute-start(bf16[2,1,4,64,128]{4,2,1,3,0:T(4,128)(2,1)} %fusion.105), channel_id=1, source_target_pairs={{0,8},{8,16},{16,24},{24,32},{32,40},{40,48},{48,56},{56,64},{64,7... | collective-permute-start | bytes 393224 | tf_op jit(solution)/shard_map/ppermute | solution.py:31
  37.6 1.5 add_convert_fusion.3
  39.2 5.1 %collective-permute-start.2 = (bf16[1,16,64,128]{3,2,1,0:T(8,128)(2,1)S(1)}, bf16[1,16,64,128]{3,2,1,0:T(8,128)(2,1)S(1)}, u32[]{:S(2)}, u32[]{:S(2)}) collective-permute-start(bf16[1,16,64,128]{3,2,1,0:T(8,128)(2,1)S(1)} %get-tuple-element.47), channel_id=1, source_target_pairs={{0,1},{1,2},{2,3},{3,4},{4,5},{5,6},{6,7},{8,9},{9,10},{10,11},{11... | collective-permute-start | bytes 786440 | tf_op jit(solution)/shard_map/ppermute | solution.py:31
  44.3 1.9 collective-permute-start.3
  46.5 5.5 %collective-permute-done.3 = bf16[1,16,64,128]{3,2,1,0:T(8,128)(2,1)S(1)} collective-permute-done((bf16[1,16,64,128]{3,2,1,0:T(8,128)(2,1)S(1)}, bf16[1,16,64,128]{3,2,1,0:T(8,128)(2,1)S(1)}, u32[]{:S(2)}, u32[]{:S(2)}) %collective-permute-start.3) | collective-permute-done | bytes 262176 | tf_op jit(solution)/shard_map/ppermute | solution.py:31
  53.4 1.5 add_convert_fusion.2
  54.9 3.0 %collective-permute-start.4 = (bf16[2,1,64,128]{3,2,1,0:T(8,128)(2,1)S(1)}, bf16[2,1,64,128]{3,2,1,0:T(8,128)(2,1)S(1)}, u32[]{:S(2)}, u32[]{:S(2)}) collective-permute-start(bf16[2,1,64,128]{3,2,1,0:T(8,128)(2,1)S(1)} %get-tuple-element.45), channel_id=1, source_target_pairs={{0,8},{8,16},{16,24},{24,32},{32,40},{40,48},{48,56},{56,64},{64,7... | collective-permute-start | bytes 98312 | tf_op jit(solution)/shard_map/ppermute | solution.py:19
  57.9 1.3 collective-permute-start.5
  59.2 1.3 collective-permute-start.13
  60.5 2.0 collective-permute-done.5
  65.7 1.5 add_convert_fusion.1
  67.2 1.3 collective-permute-start.7
  68.6 1.5 convolution_bitcast_fusion.6
  70.1 4.2 %collective-permute-start.6 = (bf16[2,16,64,128]{3,2,1,0:T(8,128)(2,1)S(1)}, bf16[2,16,64,128]{3,2,1,0:T(8,128)(2,1)S(1)}, u32[]{:S(2)}, u32[]{:S(2)}) collective-permute-start(bf16[2,16,64,128]{3,2,1,0:T(8,128)(2,1)S(1)} %get-tuple-element.64), channel_id=1, source_target_pairs={{0,2},{1,3},{2,4},{3,5},{4,6},{5,7},{8,10},{9,11},{10,12},{11,13},... | collective-permute-start | bytes 1572872 | tf_op jit(solution)/shard_map/ppermute | solution.py:31
  74.6 8.3 %collective-permute-done.7 = bf16[2,16,64,128]{3,2,1,0:T(8,128)(2,1)S(1)} collective-permute-done((bf16[2,16,64,128]{3,2,1,0:T(8,128)(2,1)S(1)}, bf16[2,16,64,128]{3,2,1,0:T(8,128)(2,1)S(1)}, u32[]{:S(2)}, u32[]{:S(2)}) %collective-permute-start.7) | collective-permute-done | bytes 524320 | tf_op jit(solution)/shard_map/ppermute | solution.py:31
  84.0 1.4 collective-permute-done.6
  85.5 1.9 fusion.25
  87.3 2.0 convolution_bitcast_fusion.9
  89.3 4.9 %collective-permute-start.17 = (bf16[2,16,64,128]{3,2,1,0:T(8,128)(2,1)}, bf16[2,16,64,128]{3,2,1,0:T(8,128)(2,1)}, u32[]{:S(2)}, u32[]{:S(2)}) collective-permute-start(bf16[2,16,64,128]{3,2,1,0:T(8,128)(2,1)} %get-tuple-element.37), channel_id=1, source_target_pairs={{0,2},{1,3},{2,4},{3,5},{4,6},{5,7},{8,10},{9,11},{10,12},{11,13},... | collective-permute-start | bytes 1572872 | tf_op jit(solution)/shard_map/ppermute | solution.py:31
  94.2 2.4 convolution_bitcast_fusion.4
  96.6 1.6 gather_fusion.5
  98.2 2.3 gather_fusion.4
  100.5 2.3 gather_fusion.3
  102.7 2.3 gather_fusion.2
  105.0 1.7 select_bitcast_fusion.3
  106.7 6.4 %collective-permute-start.8 = (bf16[2,1,4,64,128]{4,3,0,2,1:T(8,128)(2,1)}, bf16[2,1,4,64,128]{4,3,0,2,1:T(8,128)(2,1)}, u32[]{:S(2)}, u32[]{:S(2)}) collective-permute-start(bf16[2,1,4,64,128]{4,3,0,2,1:T(8,128)(2,1)} %select_bitcast_fusion.3), channel_id=1, source_target_pairs={{0,16},{8,24},{16,32},{24,40},{32,48},{40,56},{48,64},{56,72},{64,... | collective-permute-start | bytes 393224 | tf_op jit(solution)/shard_map/ppermute | solution.py:31
  113.1 1.6 select_bitcast_fusion.2
  114.7 4.2 %collective-permute-start.9 = (bf16[2,1,4,64,128]{4,3,0,2,1:T(8,128)(2,1)}, bf16[2,1,4,64,128]{4,3,0,2,1:T(8,128)(2,1)}, u32[]{:S(2)}, u32[]{:S(2)}) collective-permute-start(bf16[2,1,4,64,128]{4,3,0,2,1:T(8,128)(2,1)} %select_bitcast_fusion.2), channel_id=1, source_target_pairs={{0,8},{8,16},{16,24},{24,32},{32,40},{40,48},{48,56},{56,64},{64,7... | collective-permute-start | bytes 393224 | tf_op jit(solution)/shard_map/ppermute | solution.py:31
  119.0 1.6 select_bitcast_fusion.1
  120.6 1.4 collective-permute-start.10
  122.8 1.3 collective-permute-start.11
  124.1 1.5 convolution_bitcast_fusion.8
  125.6 1.3 convolution_bitcast_fusion.10
  127.0 1.4 collective-permute-start.16
  128.5 1.8 collective-permute-done.11
  130.3 1.2 pad_maximum_fusion.6
  131.5 1.4 convolution_bitcast_fusion.7
  132.9 1.2 fusion.30
  134.1 1.5 convolution_bitcast_fusion.3
  135.6 6.0 %collective-permute-done.16 = bf16[2,16,64,128]{3,2,1,0:T(8,128)(2,1)S(1)} collective-permute-done((bf16[2,16,64,128]{3,2,1,0:T(8,128)(2,1)}, bf16[2,16,64,128]{3,2,1,0:T(8,128)(2,1)S(1)}, u32[]{:S(2)}, u32[]{:S(2)}) %collective-permute-start.16) | collective-permute-done | bytes 524320 | tf_op jit(solution)/shard_map/ppermute | solution.py:31
  141.6 1.7 fusion.26
  145.7 3.7 %collective-permute-start.18 = (bf16[2,1,64,128]{3,2,1,0:T(8,128)(2,1)S(1)}, bf16[2,1,64,128]{3,2,1,0:T(8,128)(2,1)S(1)}, u32[]{:S(2)}, u32[]{:S(2)}) collective-permute-start(bf16[2,1,64,128]{3,2,1,0:T(8,128)(2,1)S(1)} %get-tuple-element.43), channel_id=1, source_target_pairs={{0,8},{8,16},{16,24},{24,32},{32,40},{40,48},{48,56},{56,64},{64,7... | collective-permute-start | bytes 98312 | tf_op jit(solution)/shard_map/ppermute | solution.py:19
  149.4 1.3 collective-permute-start.19
  151.5 2.5 collective-permute-done.19
  158.6 1.5 fusion.27
  162.2 5.5 %collective-permute-start.21 = (bf16[1,16,64,128]{3,2,1,0:T(8,128)(2,1)}, bf16[1,16,64,128]{3,2,1,0:T(8,128)(2,1)}, u32[]{:S(2)}, u32[]{:S(2)}) collective-permute-start(bf16[1,16,64,128]{3,2,1,0:T(8,128)(2,1)} %get-tuple-element.41), channel_id=1, source_target_pairs={{0,1},{1,2},{2,3},{3,4},{4,5},{5,6},{6,7},{8,9},{9,10},{10,11},{11... | collective-permute-start | bytes 786440 | tf_op jit(solution)/shard_map/ppermute | solution.py:31
  167.7 2.4 collective-permute-start.20
  171.3 1.3 convolution_bitcast_fusion
  172.6 2.9 %collective-permute-done.20 = bf16[1,16,64,128]{3,2,1,0:T(8,128)(2,1)} collective-permute-done((bf16[1,16,64,128]{3,2,1,0:T(8,128)(2,1)S(1)}, bf16[1,16,64,128]{3,2,1,0:T(8,128)(2,1)}, u32[]{:S(2)}, u32[]{:S(2)}) %collective-permute-start.20) | collective-permute-done | bytes 262176 | tf_op jit(solution)/shard_map/ppermute | solution.py:31
  175.5 2.5 fusion.28
  181.5 1.3 collective-permute-start.23
  183.6 23.3 %all-to-all-start = ((f32[256,1,384]{2,1,0:T(1,128)}), f32[256,1,384]{2,1,0:T(1,128)S(1)}, u32[]{:S(2)}, u32[]{:S(2)}) async-start(f32[256,1,384]{2,1,0:T(1,128)} %bitcast.230), calls=%async_computation | async-start | bytes 786432 | tf_op jit(solution)/shard_map/all_to_all | solution.py:236
  206.9 3.3 %collective-permute-start.22 = (bf16[2,1,64,128]{3,2,1,0:T(8,128)(2,1)S(1)}, bf16[2,1,64,128]{3,2,1,0:T(8,128)(2,1)S(1)}, u32[]{:S(2)}, u32[]{:S(2)}) collective-permute-start(bf16[2,1,64,128]{3,2,1,0:T(8,128)(2,1)S(1)} %get-tuple-element.39), channel_id=1, source_target_pairs={{0,8},{8,16},{16,24},{24,32},{32,40},{40,48},{48,56},{56,64},{64,7... | collective-permute-start | bytes 98312 | tf_op jit(solution)/shard_map/ppermute | solution.py:19
  214.4 10.6 %all-to-all-done = f32[256,1,384]{2,1,0:T(1,128)S(1)} async-done(((f32[256,1,384]{2,1,0:T(1,128)}), f32[256,1,384]{2,1,0:T(1,128)S(1)}, u32[]{:S(2)}, u32[]{:S(2)}) %all-to-all-start) | async-done | bytes 393248 | tf_op jit(solution)/shard_map/all_to_all | solution.py:236
  226.2 7.4 %all-to-all-start.1 = ((f32[256,1,384]{2,1,0:T(1,128)}), f32[256,1,384]{2,1,0:T(1,128)S(1)}, u32[]{:S(2)}, u32[]{:S(2)}) async-start(f32[256,1,384]{2,1,0:T(1,128)} %broadcast_in_dim.88), calls=%async_computation.1 | async-start | bytes 786432 | tf_op jit(solution)/shard_map/all_to_all | solution.py:238
  234.7 1.2 convolution_add_fusion.18
  235.9 1.9 fusion.22
  237.8 13.0 %all-to-all-done.1 = f32[256,1,384]{2,1,0:T(1,128)S(1)} async-done(((f32[256,1,384]{2,1,0:T(1,128)}), f32[256,1,384]{2,1,0:T(1,128)S(1)}, u32[]{:S(2)}, u32[]{:S(2)}) %all-to-all-start.1) | async-done | bytes 393248 | tf_op jit(solution)/shard_map/all_to_all | solution.py:238
  (255 shorter events, 48.7 us)
Async XLA Ops:
  0.6 6.2 %copy-start = (s32[32,16]{0,1:T(8,128)S(1)}, s32[32,16]{0,1:T(8,128)}, u32[]{:S(2)}) copy-start(s32[32,16]{0,1:T(8,128)} %param.21) | copy-start | bytes 6148
  0.6 27.6 %copy-start.31 = (s32[32,16]{0,1:T(8,128)S(1)}, s32[32,16]{0,1:T(8,128)}, u32[]{:S(2)}) copy-start(s32[32,16]{0,1:T(8,128)} %param.19) | copy-start | bytes 6148
  0.7 22.4 %copy-start.15 = (bf16[2,16,64,128]{3,2,1,0:T(8,128)(2,1)S(1)}, bf16[2,16,64,128]{3,2,1,0:T(8,128)(2,1)}, u32[]{:S(2)}) copy-start(bf16[2,16,64,128]{3,2,1,0:T(8,128)(2,1)} %param.22) | copy-start | bytes 1572868
  0.7 27.7 %copy-start.39 = (s32[32,16]{0,1:T(8,128)S(1)}, s32[32,16]{0,1:T(8,128)}, u32[]{:S(2)}) copy-start(s32[32,16]{0,1:T(8,128)} %param.20) | copy-start | bytes 6148
  1.5 32.9 %collective-permute-start = (bf16[2,1,64,128]{3,2,1,0:T(8,128)(2,1)S(1)}, bf16[2,1,64,128]{3,2,1,0:T(8,128)(2,1)S(1)}, u32[]{:S(2)}, u32[]{:S(2)}) collective-permute-start(bf16[2,1,64,128]{3,2,1,0:T(8,128)(2,1)S(1)} %get-tuple-element.49), channel_id=1, source_target_pairs={{0,8},{8,16},{16,24},{24,32},{32,40},{40,48},{48,56},{56,64},{64,7... | collective-permute-start | bytes 98312 | tf_op jit(solution)/shard_map/ppermute | solution.py:19
  5.5 28.9 %collective-permute-start.1 = (bf16[2,1,64,128]{3,2,1,0:T(8,128)(2,1)S(1)}, bf16[2,1,64,128]{3,2,1,0:T(8,128)(2,1)S(1)}, u32[]{:S(2)}, u32[]{:S(2)}) collective-permute-start(bf16[2,1,64,128]{3,2,1,0:T(8,128)(2,1)S(1)} %get-tuple-element.50), channel_id=1, source_target_pairs={{8,0},{16,8},{24,16},{32,24},{40,32},{48,40},{56,48},{64,56},{72,6... | collective-permute-start | bytes 98312 | tf_op jit(solution)/shard_map/ppermute | solution.py:21
  10.6 23.8 %copy-start.2 = (bf16[2,16,64,128]{3,2,1,0:T(8,128)(2,1)S(1)}, bf16[2,16,64,128]{3,2,1,0:T(8,128)(2,1)}, u32[]{:S(2)}) copy-start(bf16[2,16,64,128]{3,2,1,0:T(8,128)(2,1)} %param.14) | copy-start | bytes 1572868
  12.4 56.1 %collective-permute-start.12 = (bf16[2,1,4,64,128]{4,2,1,3,0:T(4,128)(2,1)S(1)}, bf16[2,1,4,64,128]{4,2,1,3,0:T(4,128)(2,1)}, u32[]{:S(2)}, u32[]{:S(2)}) collective-permute-start(bf16[2,1,4,64,128]{4,2,1,3,0:T(4,128)(2,1)S(1)} %fusion.107), channel_id=1, source_target_pairs={{16,0},{24,8},{32,16},{40,24},{48,32},{56,40},{64,48},{72,56},{80,... | collective-permute-start | bytes 393224 | tf_op jit(solution)/shard_map/ppermute | solution.py:31
  16.2 52.4 %collective-permute-start.15 = (bf16[2,1,4,64,128]{4,2,1,3,0:T(4,128)(2,1)}, bf16[2,1,4,64,128]{4,2,1,3,0:T(4,128)(2,1)}, u32[]{:S(2)}, u32[]{:S(2)}) collective-permute-start(bf16[2,1,4,64,128]{4,2,1,3,0:T(4,128)(2,1)} %fusion.104), channel_id=1, source_target_pairs={{0,16},{8,24},{16,32},{24,40},{32,48},{40,56},{48,64},{56,72},{64,... | collective-permute-start | bytes 393224 | tf_op jit(solution)/shard_map/ppermute | solution.py:31
  24.4 44.2 %collective-permute-start.14 = (bf16[2,1,4,64,128]{4,2,1,3,0:T(4,128)(2,1)}, bf16[2,1,4,64,128]{4,2,1,3,0:T(4,128)(2,1)}, u32[]{:S(2)}, u32[]{:S(2)}) collective-permute-start(bf16[2,1,4,64,128]{4,2,1,3,0:T(4,128)(2,1)} %fusion.105), channel_id=1, source_target_pairs={{0,8},{8,16},{16,24},{24,32},{32,40},{40,48},{48,56},{56,64},{64,7... | collective-permute-start | bytes 393224 | tf_op jit(solution)/shard_map/ppermute | solution.py:31
  34.4 3.2 %copy-start.35 = (bf16[2,1,64,128]{3,2,1,0:T(8,128)(2,1)}, bf16[2,1,64,128]{3,2,1,0:T(8,128)(2,1)S(1)}, u32[]{:S(2)}) copy-start(bf16[2,1,64,128]{3,2,1,0:T(8,128)(2,1)S(1)} %collective-permute-done.1) | copy-start | bytes 98308
  37.6 8.6 %copy-start.34 = (bf16[3,64,64]{2,1,0:T(8,128)(2,1)S(1)}, bf16[3,64,64]{2,1,0:T(8,128)(2,1)}, u32[]{:S(2)}) copy-start(bf16[3,64,64]{2,1,0:T(8,128)(2,1)} %param.16) | copy-start | bytes 73732
  39.1 13.5 %copy-start.5 = (bf16[2,16,64,128]{3,2,1,0:T(8,128)(2,1)}, bf16[2,16,64,128]{3,2,1,0:T(8,128)(2,1)S(1)}, u32[]{:S(2)}) copy-start(bf16[2,16,64,128]{3,2,1,0:T(8,128)(2,1)S(1)} %get-tuple-element.60) | copy-start | bytes 1572868
  39.2 13.1 %copy-start.10 = (bf16[1,16,64,128]{3,2,1,0:T(8,128)(2,1)}, bf16[1,16,64,128]{3,2,1,0:T(8,128)(2,1)S(1)}, u32[]{:S(2)}) copy-start(bf16[1,16,64,128]{3,2,1,0:T(8,128)(2,1)S(1)} %get-tuple-element.47) | copy-start | bytes 786436
  39.2 13.5 %copy-start.24 = (bf16[1,16,64,128]{3,2,1,0:T(8,128)(2,1)}, bf16[1,16,64,128]{3,2,1,0:T(8,128)(2,1)S(1)}, u32[]{:S(2)}) copy-start(bf16[1,16,64,128]{3,2,1,0:T(8,128)(2,1)S(1)} %get-tuple-element.48) | copy-start | bytes 786436
  39.2 13.5 %collective-permute-start.2 = (bf16[1,16,64,128]{3,2,1,0:T(8,128)(2,1)S(1)}, bf16[1,16,64,128]{3,2,1,0:T(8,128)(2,1)S(1)}, u32[]{:S(2)}, u32[]{:S(2)}) collective-permute-start(bf16[1,16,64,128]{3,2,1,0:T(8,128)(2,1)S(1)} %get-tuple-element.47), channel_id=1, source_target_pairs={{0,1},{1,2},{2,3},{3,4},{4,5},{5,6},{6,7},{8,9},{9,10},{10,11},{11... | collective-permute-start | bytes 786440 | tf_op jit(solution)/shard_map/ppermute | solution.py:31
  44.3 7.7 %collective-permute-start.3 = (bf16[1,16,64,128]{3,2,1,0:T(8,128)(2,1)S(1)}, bf16[1,16,64,128]{3,2,1,0:T(8,128)(2,1)S(1)}, u32[]{:S(2)}, u32[]{:S(2)}) collective-permute-start(bf16[1,16,64,128]{3,2,1,0:T(8,128)(2,1)S(1)} %get-tuple-element.48), channel_id=1, source_target_pairs={{1,0},{2,1},{3,2},{4,3},{5,4},{6,5},{7,6},{9,8},{10,9},{11,10},{12... | collective-permute-start | bytes 786440 | tf_op jit(solution)/shard_map/ppermute | solution.py:31
  54.9 8.3 %copy-start.20 = (bf16[3,3,64,64]{3,2,1,0:T(8,128)(2,1)S(1)}, bf16[3,3,64,64]{3,2,1,0:T(8,128)(2,1)}, u32[]{:S(2)}) copy-start(bf16[3,3,64,64]{3,2,1,0:T(8,128)(2,1)} %param.17) | copy-start | bytes 221188
  54.9 4.3 %collective-permute-start.4 = (bf16[2,1,64,128]{3,2,1,0:T(8,128)(2,1)S(1)}, bf16[2,1,64,128]{3,2,1,0:T(8,128)(2,1)S(1)}, u32[]{:S(2)}, u32[]{:S(2)}) collective-permute-start(bf16[2,1,64,128]{3,2,1,0:T(8,128)(2,1)S(1)} %get-tuple-element.45), channel_id=1, source_target_pairs={{0,8},{8,16},{16,24},{24,32},{32,40},{40,48},{48,56},{56,64},{64,7... | collective-permute-start | bytes 98312 | tf_op jit(solution)/shard_map/ppermute | solution.py:19
  57.9 4.7 %collective-permute-start.5 = (bf16[2,1,64,128]{3,2,1,0:T(8,128)(2,1)S(1)}, bf16[2,1,64,128]{3,2,1,0:T(8,128)(2,1)S(1)}, u32[]{:S(2)}, u32[]{:S(2)}) collective-permute-start(bf16[2,1,64,128]{3,2,1,0:T(8,128)(2,1)S(1)} %get-tuple-element.46), channel_id=1, source_target_pairs={{8,0},{16,8},{24,16},{32,24},{40,32},{48,40},{56,48},{64,56},{72,6... | collective-permute-start | bytes 98312 | tf_op jit(solution)/shard_map/ppermute | solution.py:21
  59.2 4.3 %copy-start.28 = (bf16[2,1,64,128]{3,2,1,0:T(8,128)(2,1)}, bf16[2,1,64,128]{3,2,1,0:T(8,128)(2,1)S(1)}, u32[]{:S(2)}) copy-start(bf16[2,1,64,128]{3,2,1,0:T(8,128)(2,1)S(1)} %collective-permute-done.4) | copy-start | bytes 98308
  59.2 9.4 %collective-permute-start.13 = (bf16[2,1,4,64,128]{4,2,1,3,0:T(4,128)(2,1)S(1)}, bf16[2,1,4,64,128]{4,2,1,3,0:T(4,128)(2,1)S(1)}, u32[]{:S(2)}, u32[]{:S(2)}) collective-permute-start(bf16[2,1,4,64,128]{4,2,1,3,0:T(4,128)(2,1)S(1)} %fusion.106), channel_id=1, source_target_pairs={{8,0},{16,8},{24,16},{32,24},{40,32},{48,40},{56,48},{64,56},{72,6... | collective-permute-start | bytes 393224 | tf_op jit(solution)/shard_map/ppermute | solution.py:31
  62.5 3.2 %copy-start.37 = (bf16[2,1,64,128]{3,2,1,0:T(8,128)(2,1)}, bf16[2,1,64,128]{3,2,1,0:T(8,128)(2,1)S(1)}, u32[]{:S(2)}) copy-start(bf16[2,1,64,128]{3,2,1,0:T(8,128)(2,1)S(1)} %collective-permute-done.5) | copy-start | bytes 98308
  65.7 2.8 %copy-start.41 = (s32[4]{0:T(128)S(1)}, s32[4]{0:T(128)}, u32[]{:S(2)}) copy-start(s32[4]{0:T(128)} %compare_select_fusion.7) | copy-start | bytes 52
  67.2 15.7 %collective-permute-start.7 = (bf16[2,16,64,128]{3,2,1,0:T(8,128)(2,1)S(1)}, bf16[2,16,64,128]{3,2,1,0:T(8,128)(2,1)S(1)}, u32[]{:S(2)}, u32[]{:S(2)}) collective-permute-start(bf16[2,16,64,128]{3,2,1,0:T(8,128)(2,1)S(1)} %get-tuple-element.64), channel_id=1, source_target_pairs={{2,0},{3,1},{4,2},{5,3},{6,4},{7,5},{10,8},{11,9},{12,10},{13,11},... | collective-permute-start | bytes 1572872 | tf_op jit(solution)/shard_map/ppermute | solution.py:31
  68.5 5.8 %copy-start.32 = (bf16[3,64,64]{2,1,0:T(8,128)(2,1)S(1)}, bf16[3,64,64]{2,1,0:T(8,128)(2,1)}, u32[]{:S(2)}) copy-start(bf16[3,64,64]{2,1,0:T(8,128)(2,1)} %param.18) | copy-start | bytes 73732
  70.1 15.3 %copy-start.45 = (f32[2,64,128,16]{2,3,1,0:T(8,128)}, f32[2,64,128,16]{2,3,1,0:T(8,128)S(1)}, u32[]{:S(2)}) copy-start(f32[2,64,128,16]{2,3,1,0:T(8,128)S(1)} %convolution_bitcast_fusion.6) | copy-start | bytes 3145732
  70.1 15.3 %collective-permute-start.6 = (bf16[2,16,64,128]{3,2,1,0:T(8,128)(2,1)S(1)}, bf16[2,16,64,128]{3,2,1,0:T(8,128)(2,1)S(1)}, u32[]{:S(2)}, u32[]{:S(2)}) collective-permute-start(bf16[2,16,64,128]{3,2,1,0:T(8,128)(2,1)S(1)} %get-tuple-element.64), channel_id=1, source_target_pairs={{0,2},{1,3},{2,4},{3,5},{4,6},{5,7},{8,10},{9,11},{10,12},{11,13},... | collective-permute-start | bytes 1572872 | tf_op jit(solution)/shard_map/ppermute | solution.py:31
  74.6 10.8 %copy-start.16 = (bf16[2,16,64,128]{3,2,1,0:T(8,128)(2,1)S(1)}, bf16[2,16,64,128]{3,2,1,0:T(8,128)(2,1)}, u32[]{:S(2)}) copy-start(bf16[2,16,64,128]{3,2,1,0:T(8,128)(2,1)} %param.22) | copy-start | bytes 1572868
  89.3 44.8 %collective-permute-start.17 = (bf16[2,16,64,128]{3,2,1,0:T(8,128)(2,1)}, bf16[2,16,64,128]{3,2,1,0:T(8,128)(2,1)}, u32[]{:S(2)}, u32[]{:S(2)}) collective-permute-start(bf16[2,16,64,128]{3,2,1,0:T(8,128)(2,1)} %get-tuple-element.37), channel_id=1, source_target_pairs={{0,2},{1,3},{2,4},{3,5},{4,6},{5,7},{8,10},{9,11},{10,12},{11,13},... | collective-permute-start | bytes 1572872 | tf_op jit(solution)/shard_map/ppermute | solution.py:31
  98.2 23.9 %copy-start.40 = (pred[4]{0:T(512)(128)(4,1)S(1)}, pred[4]{0:T(512)(128)(4,1)}, u32[]{:S(2)}) copy-start(pred[4]{0:T(512)(128)(4,1)} %compare_and_fusion.4) | copy-start | bytes 16
  105.0 20.6 %copy-start.19 = (bf16[2,16,64,128]{3,2,1,0:T(8,128)(2,1)S(1)}, bf16[2,16,64,128]{3,2,1,0:T(8,128)(2,1)}, u32[]{:S(2)}) copy-start(bf16[2,16,64,128]{3,2,1,0:T(8,128)(2,1)} %copy-done.18) | copy-start | bytes 1572868
  106.7 20.3 %collective-permute-start.8 = (bf16[2,1,4,64,128]{4,3,0,2,1:T(8,128)(2,1)}, bf16[2,1,4,64,128]{4,3,0,2,1:T(8,128)(2,1)}, u32[]{:S(2)}, u32[]{:S(2)}) collective-permute-start(bf16[2,1,4,64,128]{4,3,0,2,1:T(8,128)(2,1)} %select_bitcast_fusion.3), channel_id=1, source_target_pairs={{0,16},{8,24},{16,32},{24,40},{32,48},{40,56},{48,64},{56,72},{64,... | collective-permute-start | bytes 393224 | tf_op jit(solution)/shard_map/ppermute | solution.py:31
  114.7 13.7 %collective-permute-start.9 = (bf16[2,1,4,64,128]{4,3,0,2,1:T(8,128)(2,1)}, bf16[2,1,4,64,128]{4,3,0,2,1:T(8,128)(2,1)}, u32[]{:S(2)}, u32[]{:S(2)}) collective-permute-start(bf16[2,1,4,64,128]{4,3,0,2,1:T(8,128)(2,1)} %select_bitcast_fusion.2), channel_id=1, source_target_pairs={{0,8},{8,16},{16,24},{24,32},{32,40},{40,48},{48,56},{56,64},{64,7... | collective-permute-start | bytes 393224 | tf_op jit(solution)/shard_map/ppermute | solution.py:31
  120.6 6.3 %copy-start.30 = (f32[1,64,64]{2,1,0:T(8,128)S(1)}, f32[1,64,64]{2,1,0:T(8,128)}, u32[]{:S(2)}) copy-start(f32[1,64,64]{2,1,0:T(8,128)} %convolution_bitcast_fusion.9) | copy-start | bytes 49156
  120.6 7.9 %collective-permute-start.10 = (bf16[2,1,4,64,128]{4,3,0,2,1:T(8,128)(2,1)}, bf16[2,1,4,64,128]{4,3,0,2,1:T(8,128)(2,1)}, u32[]{:S(2)}, u32[]{:S(2)}) collective-permute-start(bf16[2,1,4,64,128]{4,3,0,2,1:T(8,128)(2,1)} %select_bitcast_fusion.1), channel_id=1, source_target_pairs={{8,0},{16,8},{24,16},{32,24},{40,32},{48,40},{56,48},{64,56},{72,6... | collective-permute-start | bytes 393224 | tf_op jit(solution)/shard_map/ppermute | solution.py:31
  122.8 7.5 %collective-permute-start.11 = (bf16[2,1,4,64,128]{4,3,0,2,1:T(8,128)(2,1)}, bf16[2,1,4,64,128]{4,3,0,2,1:T(8,128)(2,1)}, u32[]{:S(2)}, u32[]{:S(2)}) collective-permute-start(bf16[2,1,4,64,128]{4,3,0,2,1:T(8,128)(2,1)} %select_bitcast_fusion), channel_id=1, source_target_pairs={{16,0},{24,8},{32,16},{40,24},{48,32},{56,40},{64,48},{72,56},{80,... | collective-permute-start | bytes 393224 | tf_op jit(solution)/shard_map/ppermute | solution.py:31
  127.0 5.9 %copy-start.8 = (bf16[2,16,64,128]{3,2,1,0:T(8,128)(2,1)S(1)}, bf16[2,16,64,128]{3,2,1,0:T(8,128)(2,1)}, u32[]{:S(2)}) copy-start(bf16[2,16,64,128]{3,2,1,0:T(8,128)(2,1)} %get-tuple-element.38) | copy-start | bytes 1572868
  127.0 14.6 %collective-permute-start.16 = (bf16[2,16,64,128]{3,2,1,0:T(8,128)(2,1)}, bf16[2,16,64,128]{3,2,1,0:T(8,128)(2,1)S(1)}, u32[]{:S(2)}, u32[]{:S(2)}) collective-permute-start(bf16[2,16,64,128]{3,2,1,0:T(8,128)(2,1)} %get-tuple-element.37), channel_id=1, source_target_pairs={{2,0},{3,1},{4,2},{5,3},{6,4},{7,5},{10,8},{11,9},{12,10},{13,11},... | collective-permute-start | bytes 1572872 | tf_op jit(solution)/shard_map/ppermute | solution.py:31
  131.5 10.1 %copy-start.46 = (f32[2,64,128,16]{2,3,1,0:T(8,128)S(1)}, f32[2,64,128,16]{2,3,1,0:T(8,128)}, u32[]{:S(2)}) copy-start(f32[2,64,128,16]{2,3,1,0:T(8,128)} %copy-done.45) | copy-start | bytes 3145732
  132.9 8.7 %copy-start.44 = (f32[2,16,64,128]{3,2,1,0:T(8,128)S(1)}, f32[2,16,64,128]{3,2,1,0:T(8,128)}, u32[]{:S(2)}) copy-start(f32[2,16,64,128]{3,2,1,0:T(8,128)} %get-tuple-element.65) | copy-start | bytes 3145732
  134.1 7.5 %copy-start.9 = (f32[2,16,64,128]{3,2,1,0:T(8,128)S(1)}, f32[2,16,64,128]{3,2,1,0:T(8,128)}, u32[]{:S(2)}) copy-start(f32[2,16,64,128]{3,2,1,0:T(8,128)} %convolution_bitcast_fusion.4) | copy-start | bytes 3145732
  134.1 7.5 %copy-start.17 = (bf16[2,16,64,128]{3,2,1,0:T(8,128)(2,1)S(1)}, bf16[2,16,64,128]{3,2,1,0:T(8,128)(2,1)}, u32[]{:S(2)}) copy-start(bf16[2,16,64,128]{3,2,1,0:T(8,128)(2,1)} %param.22) | copy-start | bytes 1572868
  143.3 7.7 %copy-start.3 = (bf16[2,16,64,128]{3,2,1,0:T(8,128)(2,1)}, bf16[2,16,64,128]{3,2,1,0:T(8,128)(2,1)S(1)}, u32[]{:S(2)}) copy-start(bf16[2,16,64,128]{3,2,1,0:T(8,128)(2,1)S(1)} %get-tuple-element.66) | copy-start | bytes 1572868
  144.9 5.7 %copy-start.38 = (bf16[2,1,64,128]{3,2,1,0:T(8,128)(2,1)S(1)}, bf16[2,1,64,128]{3,2,1,0:T(8,128)(2,1)}, u32[]{:S(2)}) copy-start(bf16[2,1,64,128]{3,2,1,0:T(8,128)(2,1)} %copy-done.37) | copy-start | bytes 98308
  145.6 5.4 %copy-start.29 = (bf16[2,1,64,128]{3,2,1,0:T(8,128)(2,1)S(1)}, bf16[2,1,64,128]{3,2,1,0:T(8,128)(2,1)}, u32[]{:S(2)}) copy-start(bf16[2,1,64,128]{3,2,1,0:T(8,128)(2,1)} %copy-done.28) | copy-start | bytes 98308
  145.7 5.9 %collective-permute-start.18 = (bf16[2,1,64,128]{3,2,1,0:T(8,128)(2,1)S(1)}, bf16[2,1,64,128]{3,2,1,0:T(8,128)(2,1)S(1)}, u32[]{:S(2)}, u32[]{:S(2)}) collective-permute-start(bf16[2,1,64,128]{3,2,1,0:T(8,128)(2,1)S(1)} %get-tuple-element.43), channel_id=1, source_target_pairs={{0,8},{8,16},{16,24},{24,32},{32,40},{40,48},{48,56},{56,64},{64,7... | collective-permute-start | bytes 98312 | tf_op jit(solution)/shard_map/ppermute | solution.py:19
  149.4 4.7 %collective-permute-start.19 = (bf16[2,1,64,128]{3,2,1,0:T(8,128)(2,1)S(1)}, bf16[2,1,64,128]{3,2,1,0:T(8,128)(2,1)S(1)}, u32[]{:S(2)}, u32[]{:S(2)}) collective-permute-start(bf16[2,1,64,128]{3,2,1,0:T(8,128)(2,1)S(1)} %get-tuple-element.44), channel_id=1, source_target_pairs={{8,0},{16,8},{24,16},{32,24},{40,32},{48,40},{56,48},{64,56},{72,6... | collective-permute-start | bytes 98312 | tf_op jit(solution)/shard_map/ppermute | solution.py:21
  151.3 2.7 %copy-start.4 = (bf16[2,16,64,128]{3,2,1,0:T(8,128)(2,1)S(1)}, bf16[2,16,64,128]{3,2,1,0:T(8,128)(2,1)}, u32[]{:S(2)}) copy-start(bf16[2,16,64,128]{3,2,1,0:T(8,128)(2,1)} %copy-done.3) | copy-start | bytes 1572868
  151.4 3.3 %copy-start.21 = (bf16[3,3,64,64]{3,2,1,0:T(8,128)(2,1)S(1)}, bf16[3,3,64,64]{3,2,1,0:T(8,128)(2,1)}, u32[]{:S(2)}) copy-start(bf16[3,3,64,64]{3,2,1,0:T(8,128)(2,1)} %param.17) | copy-start | bytes 221188
  160.3 9.8 %copy-start.25 = (bf16[1,16,64,128]{3,2,1,0:T(8,128)(2,1)S(1)}, bf16[1,16,64,128]{3,2,1,0:T(8,128)(2,1)}, u32[]{:S(2)}) copy-start(bf16[1,16,64,128]{3,2,1,0:T(8,128)(2,1)} %copy-done.24) | copy-start | bytes 786436
  160.3 9.8 %copy-start.43 = (bf16[1,16,64,128]{3,2,1,0:T(8,128)(2,1)S(1)}, bf16[1,16,64,128]{3,2,1,0:T(8,128)(2,1)}, u32[]{:S(2)}) copy-start(bf16[1,16,64,128]{3,2,1,0:T(8,128)(2,1)} %copy-done.42) | copy-start | bytes 786436
  161.1 9.3 %copy-start.11 = (bf16[1,16,64,128]{3,2,1,0:T(8,128)(2,1)S(1)}, bf16[1,16,64,128]{3,2,1,0:T(8,128)(2,1)}, u32[]{:S(2)}) copy-start(bf16[1,16,64,128]{3,2,1,0:T(8,128)(2,1)} %copy-done.10) | copy-start | bytes 786436
  161.1 9.3 %copy-start.23 = (bf16[1,16,64,128]{3,2,1,0:T(8,128)(2,1)S(1)}, bf16[1,16,64,128]{3,2,1,0:T(8,128)(2,1)}, u32[]{:S(2)}) copy-start(bf16[1,16,64,128]{3,2,1,0:T(8,128)(2,1)} %copy-done.22) | copy-start | bytes 786436
  162.2 9.1 %collective-permute-start.21 = (bf16[1,16,64,128]{3,2,1,0:T(8,128)(2,1)}, bf16[1,16,64,128]{3,2,1,0:T(8,128)(2,1)}, u32[]{:S(2)}, u32[]{:S(2)}) collective-permute-start(bf16[1,16,64,128]{3,2,1,0:T(8,128)(2,1)} %get-tuple-element.41), channel_id=1, source_target_pairs={{0,1},{1,2},{2,3},{3,4},{4,5},{5,6},{6,7},{8,9},{9,10},{10,11},{11... | collective-permute-start | bytes 786440 | tf_op jit(solution)/shard_map/ppermute | solution.py:31
  167.7 7.8 %collective-permute-start.20 = (bf16[1,16,64,128]{3,2,1,0:T(8,128)(2,1)S(1)}, bf16[1,16,64,128]{3,2,1,0:T(8,128)(2,1)}, u32[]{:S(2)}, u32[]{:S(2)}) collective-permute-start(bf16[1,16,64,128]{3,2,1,0:T(8,128)(2,1)S(1)} %get-tuple-element.42), channel_id=1, source_target_pairs={{1,0},{2,1},{3,2},{4,3},{5,4},{6,5},{7,6},{9,8},{10,9},{11,10},{12... | collective-permute-start | bytes 786440 | tf_op jit(solution)/shard_map/ppermute | solution.py:31
  170.8 4.7 %copy-start.47 = (f32[2,16,64,128]{3,2,1,0:T(8,128)S(1)}, f32[2,16,64,128]{3,2,1,0:T(8,128)}, u32[]{:S(2)}) copy-start(f32[2,16,64,128]{3,2,1,0:T(8,128)} %get-tuple-element.61) | copy-start | bytes 3145732
  170.8 4.7 %copy-start.50 = (bf16[2,16,64,128]{3,2,1,0:T(8,128)(2,1)S(1)}, bf16[2,16,64,128]{3,2,1,0:T(8,128)(2,1)}, u32[]{:S(2)}) copy-start(bf16[2,16,64,128]{3,2,1,0:T(8,128)(2,1)} %get-tuple-element.69) | copy-start | bytes 1572868
  181.4 28.8 %copy-start.13 = (bf16[3,3,64,64]{3,2,1,0:T(8,128)(2,1)S(1)}, bf16[3,3,64,64]{3,2,1,0:T(8,128)(2,1)}, u32[]{:S(2)}) copy-start(bf16[3,3,64,64]{3,2,1,0:T(8,128)(2,1)} %param.15) | copy-start | bytes 221188
  181.5 28.7 %collective-permute-start.23 = (bf16[2,1,64,128]{3,2,1,0:T(8,128)(2,1)S(1)}, bf16[2,1,64,128]{3,2,1,0:T(8,128)(2,1)S(1)}, u32[]{:S(2)}, u32[]{:S(2)}) collective-permute-start(bf16[2,1,64,128]{3,2,1,0:T(8,128)(2,1)S(1)} %get-tuple-element.40), channel_id=1, source_target_pairs={{8,0},{16,8},{24,16},{32,24},{40,32},{48,40},{56,48},{64,56},{72,6... | collective-permute-start | bytes 98312 | tf_op jit(solution)/shard_map/ppermute | solution.py:21
  183.6 41.4 %all-to-all-start = ((f32[256,1,384]{2,1,0:T(1,128)}), f32[256,1,384]{2,1,0:T(1,128)S(1)}, u32[]{:S(2)}, u32[]{:S(2)}) async-start(f32[256,1,384]{2,1,0:T(1,128)} %bitcast.230), calls=%async_computation | async-start | bytes 786432 | tf_op jit(solution)/shard_map/all_to_all | solution.py:236
  206.9 4.3 %collective-permute-start.22 = (bf16[2,1,64,128]{3,2,1,0:T(8,128)(2,1)S(1)}, bf16[2,1,64,128]{3,2,1,0:T(8,128)(2,1)S(1)}, u32[]{:S(2)}, u32[]{:S(2)}) collective-permute-start(bf16[2,1,64,128]{3,2,1,0:T(8,128)(2,1)S(1)} %get-tuple-element.39), channel_id=1, source_target_pairs={{0,8},{8,16},{16,24},{24,32},{32,40},{40,48},{48,56},{56,64},{64,7... | collective-permute-start | bytes 98312 | tf_op jit(solution)/shard_map/ppermute | solution.py:19
  226.2 24.6 %all-to-all-start.1 = ((f32[256,1,384]{2,1,0:T(1,128)}), f32[256,1,384]{2,1,0:T(1,128)S(1)}, u32[]{:S(2)}, u32[]{:S(2)}) async-start(f32[256,1,384]{2,1,0:T(1,128)} %broadcast_in_dim.88), calls=%async_computation.1 | async-start | bytes 786432 | tf_op jit(solution)/shard_map/all_to_all | solution.py:238
  235.9 19.1 %copy-start.1 = (s32[32,16]{0,1:T(8,128)S(1)}, s32[32,16]{0,1:T(8,128)}, u32[]{:S(2)}) copy-start(s32[32,16]{0,1:T(8,128)} %param.21) | copy-start | bytes 6148
  (13 other events, 15.7 us)

commit v4 on v3

--- a/solution.py
+++ b/solution.py
@@ -270,19 +270,26 @@
     myself = lax.axis_index("chart")
     offsets = [offset for offset in range(-REACH, REACH + 1) if offset != 0]
     offset_array = jnp.array(offsets, dtype=jnp.int32)
-    arrivals = []
-    for offset in offsets:
+    receive_matrix, back_strip = receiver_side(tables, myself + offset_array)
+    outgoing = {}
+    for position, offset in enumerate(offsets):
         strip_ids, unused_matrix = sender_side(tables, jnp.reshape(myself - offset, (1,)), strips)
-        arrivals.append(near_send(pick_strips(frames_four, strip_ids), -offset))
-    receive_matrix, back_strip = receiver_side(tables, myself + offset_array)
-    moved = place_strips(jnp.concatenate(arrivals, axis=1), receive_matrix)
-    returns = []
+        outgoing[offset] = pick_strips(frames_four, strip_ids)
+    arrivals = {}
+    returns = {}
     for position, offset in enumerate(offsets):
-        returns.append(
-            near_send(pick_strips(grad_out, back_strip[position : position + 1]), offset)
-        )
+        going_back = pick_strips(grad_out, back_strip[position : position + 1])
+        payload = jnp.concatenate([outgoing[-offset], going_back], axis=1)
+        landed = near_send(payload, offset)
+        arrivals[-offset] = landed[:, :1]
+        returns[offset] = landed[:, 1:]
+    moved = place_strips(
+        jnp.concatenate([arrivals[offset] for offset in offsets], axis=1), receive_matrix
+    )
     unused_ids, return_matrix = sender_side(tables, myself - offset_array, strips)
-    moved_back = place_strips(jnp.concatenate(returns, axis=1), return_matrix)
+    moved_back = place_strips(
+        jnp.concatenate([returns[offset] for offset in offsets], axis=1), return_matrix
+    )
     blended = (frames_four.astype(jnp.float32) + moved).astype(jnp.bfloat16)
     fourth_gradient = (grad_out.astype(jnp.float32) + moved_back).astype(jnp.bfloat16)
     third_gradient, gradient_kernel_second = temporal_backward(

time: 257 us -> 251 us (0.977)
  starting transfers between devices: 103 us -> 89.1 us
  other arithmetic: 20.4 us -> 25.2 us
  matrix products: 49.2 us -> 44.9 us
  waiting for transfers between devices: 55.2 us -> 58.9 us
  local copies, waits for them, and re-layouts: 24.9 us -> 28.2 us
    ppermute x16 -> x12, starting transfers between devices: 53.4 us -> 39.7 us  [from_behind(): return lax.ppermute(array, axis, pairs)]
    all_to_all x1, starting transfers between devices: 23.3 us -> 17.4 us  [exchange_sum(): flat = jnp.sum(lax.all_to_all(pieces, axes, 0, 0, tiled=True), axis=0)]
    ppermute x4, starting transfers between devices: 14 us -> 19.4 us  [with_halo(): lax.ppermute(tail, axis, [(i, (i + 1) % count) for i in range(ends)])]
    dot_general x6, matrix products: 5.63 us -> 2.81 us  [temporal_backward(): jnp.einsum('fsop,fscp->oc', slopes, taps[kernel_tap], preferred_element_t...]
    ppermute x16 -> x12, waiting for transfers between devices: 26.4 us -> 27.8 us  [from_behind(): return lax.ppermute(array, axis, pairs)]
  transfers between devices with their start and end apart: 26 -> 22, of which waited for: 12 -> 13; matrix products, arithmetic and copies ran while one was open for 25% -> 19% of each run, Pallas kernels for 0% -> 0%
where the time goes in v4:
time: 251 us; the launch traced here: 248 us
  starting transfers between devices  89.1 us (35%)
  waiting for transfers between devices  58.9 us (23%)
  matrix products  44.9 us (18%)
  local copies, waits for them, and re-layouts  28.2 us (11%)
  other arithmetic  25.2 us (10%)
    ppermute x12, starting transfers between devices, from_behind(): return lax.ppermute(array, axis, pairs)  39.7 us
    ppermute x12, waiting for transfers between devices, from_behind(): return lax.ppermute(array, axis, pairs)  27.8 us
    ppermute x4, starting transfers between devices, with_halo(): lax.ppermute(tail, axis, [(i, (i + 1) % count) for i in range(ends)])  19.4 us
    all_to_all x1, starting transfers between devices, exchange_sum(): flat = jnp.sum(lax.all_to_all(pieces, axes, 0, 0, tiled=True), axis=0)  17.4 us
    gather x8, local copies, waits for them, and re-layouts, pick_strips(): gathered = jnp.take(values, strip_ids.reshape(-1), axis=1)  13.4 us
    all_to_all x1, waiting for transfers between devices, exchange_sum(): flat = lax.all_to_all(copies, axes, 0, 0, tiled=True).reshape(-1)  13 us
    dot_general x18, matrix products, spatial_transpose(): jnp.einsum('oc,fsop->fscp', weight[row_tap, col_tap], padded[:, 2 - row_t...  11.4 us
    all_to_all x1, waiting for transfers between devices, exchange_sum(): flat = jnp.sum(lax.all_to_all(pieces, axes, 0, 0, tiled=True), axis=0)  10.6 us
  transfers between devices with their start and end apart: 22, of which 13 were waited for; matrix products, arithmetic and copies ran while one was open for 19% of the time, Pallas kernels for 0%

profile of v4, /device:TPU:1, one launch (start us, length us, event | category | flops | bytes accessed | tf_op | source)
XLA Modules:
  0.0 248.4 jit_solution(2666748287631604)
XLA Ops:
  1.5 4.0 %collective-permute-start = (bf16[2,1,64,128]{3,2,1,0:T(8,128)(2,1)S(1)}, bf16[2,1,64,128]{3,2,1,0:T(8,128)(2,1)S(1)}, u32[]{:S(2)}, u32[]{:S(2)}) collective-permute-start(bf16[2,1,64,128]{3,2,1,0:T(8,128)(2,1)S(1)} %get-tuple-element.47), channel_id=1, source_target_pairs={{0,8},{8,16},{16,24},{24,32},{32,40},{40,48},{48,56},{56,64},{64,7... | collective-permute-start | bytes 98312 | tf_op jit(solution)/shard_map/ppermute | solution.py:19
  5.5 1.3 collective-permute-start.1
  12.0 1.2 compare_and_fusion.9
  16.1 1.6 gather_fusion.5
  17.8 1.6 gather_fusion.7
  19.4 1.6 gather_fusion.9
  27.8 1.5 add_convert_fusion.3
  29.3 4.0 %collective-permute-start.2 = (bf16[1,16,64,128]{3,2,1,0:T(8,128)(2,1)S(1)}, bf16[1,16,64,128]{3,2,1,0:T(8,128)(2,1)S(1)}, u32[]{:S(2)}, u32[]{:S(2)}) collective-permute-start(bf16[1,16,64,128]{3,2,1,0:T(8,128)(2,1)S(1)} %get-tuple-element.45), channel_id=1, source_target_pairs={{0,1},{1,2},{2,3},{3,4},{4,5},{5,6},{6,7},{8,9},{9,10},{10,11},{11... | collective-permute-start | bytes 786440 | tf_op jit(solution)/shard_map/ppermute | solution.py:31
  33.3 1.9 collective-permute-start.3
  35.5 5.5 %collective-permute-done.3 = bf16[1,16,64,128]{3,2,1,0:T(8,128)(2,1)S(1)} collective-permute-done((bf16[1,16,64,128]{3,2,1,0:T(8,128)(2,1)S(1)}, bf16[1,16,64,128]{3,2,1,0:T(8,128)(2,1)S(1)}, u32[]{:S(2)}, u32[]{:S(2)}) %collective-permute-start.3) | collective-permute-done | bytes 262176 | tf_op jit(solution)/shard_map/ppermute | solution.py:31
  41.7 1.5 add_convert_fusion.2
  43.2 4.4 %collective-permute-start.4 = (bf16[2,1,64,128]{3,2,1,0:T(8,128)(2,1)S(1)}, bf16[2,1,64,128]{3,2,1,0:T(8,128)(2,1)S(1)}, u32[]{:S(2)}, u32[]{:S(2)}) collective-permute-start(bf16[2,1,64,128]{3,2,1,0:T(8,128)(2,1)S(1)} %get-tuple-element.43), channel_id=1, source_target_pairs={{0,8},{8,16},{16,24},{24,32},{32,40},{40,48},{48,56},{56,64},{64,7... | collective-permute-start | bytes 98312 | tf_op jit(solution)/shard_map/ppermute | solution.py:19
  47.6 1.3 collective-permute-start.5
  49.5 2.8 %collective-permute-done.5 = bf16[2,1,64,128]{3,2,1,0:T(8,128)(2,1)S(1)} collective-permute-done((bf16[2,1,64,128]{3,2,1,0:T(8,128)(2,1)S(1)}, bf16[2,1,64,128]{3,2,1,0:T(8,128)(2,1)S(1)}, u32[]{:S(2)}, u32[]{:S(2)}) %collective-permute-start.5) | collective-permute-done | bytes 32800 | tf_op jit(solution)/shard_map/ppermute | solution.py:21
  55.5 1.6 add_convert_fusion.1
  57.1 1.3 collective-permute-start.7
  59.0 1.7 gather_fusion.3
  60.7 1.3 select_bitcast_fusion.6
  62.1 4.0 %collective-permute-start.6 = (bf16[2,16,64,128]{3,2,1,0:T(8,128)(2,1)}, bf16[2,16,64,128]{3,2,1,0:T(8,128)(2,1)S(1)}, u32[]{:S(2)}, u32[]{:S(2)}) collective-permute-start(bf16[2,16,64,128]{3,2,1,0:T(8,128)(2,1)} %get-tuple-element.70), channel_id=1, source_target_pairs={{0,2},{1,3},{2,4},{3,5},{4,6},{5,7},{8,10},{9,11},{10,12},{11,13},... | collective-permute-start | bytes 1572872 | tf_op jit(solution)/shard_map/ppermute | solution.py:31
  66.1 1.3 fusion.107
  67.4 5.6 %collective-permute-done.7 = bf16[2,16,64,128]{3,2,1,0:T(8,128)(2,1)S(1)} collective-permute-done((bf16[2,16,64,128]{3,2,1,0:T(8,128)(2,1)}, bf16[2,16,64,128]{3,2,1,0:T(8,128)(2,1)S(1)}, u32[]{:S(2)}, u32[]{:S(2)}) %collective-permute-start.7) | collective-permute-done | bytes 524320 | tf_op jit(solution)/shard_map/ppermute | solution.py:31
  73.3 4.4 %collective-permute-done.6 = bf16[2,16,64,128]{3,2,1,0:T(8,128)(2,1)S(1)} collective-permute-done((bf16[2,16,64,128]{3,2,1,0:T(8,128)(2,1)}, bf16[2,16,64,128]{3,2,1,0:T(8,128)(2,1)S(1)}, u32[]{:S(2)}, u32[]{:S(2)}) %collective-permute-start.6) | collective-permute-done | bytes 524320 | tf_op jit(solution)/shard_map/ppermute | solution.py:31
  77.7 2.9 %add_convert_fusion = (bf16[2,16,64,128]{3,2,1,0:T(8,128)(2,1)}, f32[2,16,64,128]{3,2,1,0:T(8,128)}) fusion(bf16[2,16,64,128]{3,2,1,0:T(8,128)(2,1)} %get-tuple-element.70, f32[2,16,128,64]{2,3,1,0:T(8,128)S(1)} %fusion.104, f32[2,16,128,64]{2,3,1,0:T(8,128)S(1)} %fusion.107, bf16[2,16,64,128]{3,2,1,0:T(8,128)(2,1)S(1)} %collective-permute-done.6, ...), kind=kOutput, calls=%fused_computation.119 | convolution fusion | flops 35913728 | bytes 4734976 | tf_op jit(solution)/shard_map/oc,fscp->fsop/dot_general | solution.py:147
  80.6 1.7 gather_fusion.8
  82.3 1.7 gather_fusion.6
  84.1 1.6 gather_fusion.4
  85.7 1.7 gather_fusion.2
  88.2 1.0 pad_maximum_fusion.23
  89.2 6.8 %collective-permute-start.8 = (bf16[2,2,4,64,128]{4,3,0,2,1:T(8,128)(2,1)S(1)}, bf16[2,2,4,64,128]{4,3,0,2,1:T(8,128)(2,1)S(1)}, u32[]{:S(2)}, u32[]{:S(2)}) collective-permute-start(bf16[2,2,4,64,128]{4,3,0,2,1:T(8,128)(2,1)S(1)} %pad_maximum_fusion.23), channel_id=1, source_target_pairs={{0,16},{8,24},{16,32},{24,40},{32,48},{40,56},{48,64},{56,72},{64,... | collective-permute-start | bytes 786440 | tf_op jit(solution)/shard_map/ppermute | solution.py:31
  96.7 0.9 pad_maximum_fusion.24
  97.7 4.6 %collective-permute-start.9 = (bf16[2,2,4,64,128]{4,3,0,2,1:T(8,128)(2,1)S(1)}, bf16[2,2,4,64,128]{4,3,0,2,1:T(8,128)(2,1)S(1)}, u32[]{:S(2)}, u32[]{:S(2)}) collective-permute-start(bf16[2,2,4,64,128]{4,3,0,2,1:T(8,128)(2,1)S(1)} %pad_maximum_fusion.24), channel_id=1, source_target_pairs={{0,8},{8,16},{16,24},{24,32},{32,40},{40,48},{48,56},{56,64},{64,7... | collective-permute-start | bytes 786440 | tf_op jit(solution)/shard_map/ppermute | solution.py:31
  103.1 1.3 collective-permute-start.10
  104.5 1.5 collective-permute-start.11
  107.5 5.3 %collective-permute-done.10 = bf16[2,2,4,64,128]{4,3,0,2,1:T(8,128)(2,1)S(1)} collective-permute-done((bf16[2,2,4,64,128]{4,3,0,2,1:T(8,128)(2,1)S(1)}, bf16[2,2,4,64,128]{4,3,0,2,1:T(8,128)(2,1)S(1)}, u32[]{:S(2)}, u32[]{:S(2)}) %collective-permute-start.10) | collective-permute-done | bytes 262176 | tf_op jit(solution)/shard_map/ppermute | solution.py:31
  113.4 1.0 collective-permute-done.11
  117.0 1.4 convolution_bitcast_fusion.9
  118.4 4.8 %collective-permute-start.13 = (bf16[2,16,64,128]{3,2,1,0:T(8,128)(2,1)S(1)}, bf16[2,16,64,128]{3,2,1,0:T(8,128)(2,1)}, u32[]{:S(2)}, u32[]{:S(2)}) collective-permute-start(bf16[2,16,64,128]{3,2,1,0:T(8,128)(2,1)S(1)} %fusion.25), channel_id=1, source_target_pairs={{0,2},{1,3},{2,4},{3,5},{4,6},{5,7},{8,10},{9,11},{10,12},{11,13},... | collective-permute-start | bytes 1572872 | tf_op jit(solution)/shard_map/ppermute | solution.py:31
  123.3 1.3 collective-permute-start.12
  125.8 1.6 reshape.317
  127.4 1.2 pad_maximum_fusion.6
  129.2 1.2 fusion.30
  130.8 1.5 convolution_bitcast_fusion.3
  132.3 2.8 %collective-permute-done.12 = bf16[2,16,64,128]{3,2,1,0:T(8,128)(2,1)} collective-permute-done((bf16[2,16,64,128]{3,2,1,0:T(8,128)(2,1)S(1)}, bf16[2,16,64,128]{3,2,1,0:T(8,128)(2,1)}, u32[]{:S(2)}, u32[]{:S(2)}) %collective-permute-start.12) | collective-permute-done | bytes 524320 | tf_op jit(solution)/shard_map/ppermute | solution.py:31
  135.1 2.8 %fusion.26 = (bf16[2,16,64,128]{3,2,1,0:T(8,128)(2,1)S(1)}, bf16[2,16,64,128]{3,2,1,0:T(8,128)(2,1)}) fusion(f32[2,16,64,128]{3,2,1,0:T(8,128)S(1)} %copy-done.49, f32[2,16,64,128]{3,2,1,0:T(8,128)S(1)} %convolution_bitcast_fusion.3, f32[2,16,64,128]{3,2,1,0:T(8,128)S(1)} %convolution_bitcast_fusion.4, ...), kind=kOutput, calls=%fused_computation.112 | convolution fusion | flops 38273024 | bytes 6307840 | tf_op jit(solution)/shard_map/oc,fsop->fscp/dot_general | solution.py:166
  140.2 7.7 %collective-permute-start.14 = (bf16[2,1,64,128]{3,2,1,0:T(8,128)(2,1)S(1)}, bf16[2,1,64,128]{3,2,1,0:T(8,128)(2,1)S(1)}, u32[]{:S(2)}, u32[]{:S(2)}) collective-permute-start(bf16[2,1,64,128]{3,2,1,0:T(8,128)(2,1)S(1)} %get-tuple-element.41), channel_id=1, source_target_pairs={{0,8},{8,16},{16,24},{24,32},{32,40},{40,48},{48,56},{56,64},{64,7... | collective-permute-start | bytes 98312 | tf_op jit(solution)/shard_map/ppermute | solution.py:19
  148.0 1.3 collective-permute-start.15
  150.1 4.1 %collective-permute-done.15 = bf16[2,1,64,128]{3,2,1,0:T(8,128)(2,1)S(1)} collective-permute-done((bf16[2,1,64,128]{3,2,1,0:T(8,128)(2,1)S(1)}, bf16[2,1,64,128]{3,2,1,0:T(8,128)(2,1)S(1)}, u32[]{:S(2)}, u32[]{:S(2)}) %collective-permute-start.15) | collective-permute-done | bytes 32800 | tf_op jit(solution)/shard_map/ppermute | solution.py:21
  158.8 1.5 fusion.27
  161.7 5.2 %collective-permute-start.17 = (bf16[1,16,64,128]{3,2,1,0:T(8,128)(2,1)}, bf16[1,16,64,128]{3,2,1,0:T(8,128)(2,1)}, u32[]{:S(2)}, u32[]{:S(2)}) collective-permute-start(bf16[1,16,64,128]{3,2,1,0:T(8,128)(2,1)} %get-tuple-element.39), channel_id=1, source_target_pairs={{0,1},{1,2},{2,3},{3,4},{4,5},{5,6},{6,7},{8,9},{9,10},{10,11},{11... | collective-permute-start | bytes 786440 | tf_op jit(solution)/shard_map/ppermute | solution.py:31
  166.9 3.1 %collective-permute-start.16 = (bf16[1,16,64,128]{3,2,1,0:T(8,128)(2,1)S(1)}, bf16[1,16,64,128]{3,2,1,0:T(8,128)(2,1)}, u32[]{:S(2)}, u32[]{:S(2)}) collective-permute-start(bf16[1,16,64,128]{3,2,1,0:T(8,128)(2,1)S(1)} %get-tuple-element.40), channel_id=1, source_target_pairs={{1,0},{2,1},{3,2},{4,3},{5,4},{6,5},{7,6},{9,8},{10,9},{11,10},{12... | collective-permute-start | bytes 786440 | tf_op jit(solution)/shard_map/ppermute | solution.py:31
  170.8 1.4 convolution_bitcast_fusion
  172.2 2.5 %collective-permute-done.16 = bf16[1,16,64,128]{3,2,1,0:T(8,128)(2,1)} collective-permute-done((bf16[1,16,64,128]{3,2,1,0:T(8,128)(2,1)S(1)}, bf16[1,16,64,128]{3,2,1,0:T(8,128)(2,1)}, u32[]{:S(2)}, u32[]{:S(2)}) %collective-permute-start.16) | collective-permute-done | bytes 262176 | tf_op jit(solution)/shard_map/ppermute | solution.py:31
  174.7 2.5 %fusion.28 = (bf16[2,16,64,128]{3,2,1,0:T(8,128)(2,1)S(1)}, bf16[2,16,64,128]{3,2,1,0:T(8,128)(2,1)}) fusion(f32[2,16,64,128]{3,2,1,0:T(8,128)S(1)} %copy-done.50, f32[2,16,64,128]{3,2,1,0:T(8,128)S(1)} %convolution_bitcast_fusion, f32[2,16,64,128]{3,2,1,0:T(8,128)S(1)} %convolution_bitcast_fusion.1, bf16[3,64,64]{2,1,0:T(8,128)(2,1)S(1)} %copy-done.40, ...), kind=kOutput, calls=%fused_computation.114 | convolution fusion | flops 37748736 | bytes 5259264 | tf_op jit(solution)/shard_map/oc,fsop->fscp/dot_general | solution.py:166
  180.7 1.3 collective-permute-start.19
  182.8 17.4 %all-to-all-start = ((f32[256,1,384]{2,1,0:T(1,128)}), f32[256,1,384]{2,1,0:T(1,128)S(1)}, u32[]{:S(2)}, u32[]{:S(2)}) async-start(f32[256,1,384]{2,1,0:T(1,128)} %bitcast.230), calls=%async_computation | async-start | bytes 786432 | tf_op jit(solution)/shard_map/all_to_all | solution.py:236
  200.3 3.3 %collective-permute-start.18 = (bf16[2,1,64,128]{3,2,1,0:T(8,128)(2,1)S(1)}, bf16[2,1,64,128]{3,2,1,0:T(8,128)(2,1)S(1)}, u32[]{:S(2)}, u32[]{:S(2)}) collective-permute-start(bf16[2,1,64,128]{3,2,1,0:T(8,128)(2,1)S(1)} %get-tuple-element.37), channel_id=1, source_target_pairs={{0,8},{8,16},{16,24},{24,32},{32,40},{40,48},{48,56},{56,64},{64,7... | collective-permute-start | bytes 98312 | tf_op jit(solution)/shard_map/ppermute | solution.py:19
  206.7 1.1 convolution_add_fusion.19
  207.7 10.6 %all-to-all-done = f32[256,1,384]{2,1,0:T(1,128)S(1)} async-done(((f32[256,1,384]{2,1,0:T(1,128)}), f32[256,1,384]{2,1,0:T(1,128)S(1)}, u32[]{:S(2)}, u32[]{:S(2)}) %all-to-all-start) | async-done | bytes 393248 | tf_op jit(solution)/shard_map/all_to_all | solution.py:236
  218.6 1.0 broadcast_in_dim.91
  219.6 7.4 %all-to-all-start.1 = ((f32[256,1,384]{2,1,0:T(1,128)}), f32[256,1,384]{2,1,0:T(1,128)S(1)}, u32[]{:S(2)}, u32[]{:S(2)}) async-start(f32[256,1,384]{2,1,0:T(1,128)} %broadcast_in_dim.91), calls=%async_computation.1 | async-start | bytes 786432 | tf_op jit(solution)/shard_map/all_to_all | solution.py:238
  227.0 1.1 fusion.45
  228.1 1.2 convolution_add_fusion.18
  229.3 1.9 fusion.22
  231.2 13.0 %all-to-all-done.1 = f32[256,1,384]{2,1,0:T(1,128)S(1)} async-done(((f32[256,1,384]{2,1,0:T(1,128)}), f32[256,1,384]{2,1,0:T(1,128)S(1)}, u32[]{:S(2)}, u32[]{:S(2)}) %all-to-all-start.1) | async-done | bytes 393248 | tf_op jit(solution)/shard_map/all_to_all | solution.py:238
  (259 shorter events, 51.9 us)
Async XLA Ops:
  0.6 10.5 %copy-start = (s32[32,16]{0,1:T(8,128)S(1)}, s32[32,16]{0,1:T(8,128)}, u32[]{:S(2)}) copy-start(s32[32,16]{0,1:T(8,128)} %param.21) | copy-start | bytes 6148
  0.6 23.9 %copy-start.2 = (bf16[2,16,64,128]{3,2,1,0:T(8,128)(2,1)S(1)}, bf16[2,16,64,128]{3,2,1,0:T(8,128)(2,1)}, u32[]{:S(2)}) copy-start(bf16[2,16,64,128]{3,2,1,0:T(8,128)(2,1)} %param.14) | copy-start | bytes 1572868
  1.5 23.0 %collective-permute-start = (bf16[2,1,64,128]{3,2,1,0:T(8,128)(2,1)S(1)}, bf16[2,1,64,128]{3,2,1,0:T(8,128)(2,1)S(1)}, u32[]{:S(2)}, u32[]{:S(2)}) collective-permute-start(bf16[2,1,64,128]{3,2,1,0:T(8,128)(2,1)S(1)} %get-tuple-element.47), channel_id=1, source_target_pairs={{0,8},{8,16},{16,24},{24,32},{32,40},{40,48},{48,56},{56,64},{64,7... | collective-permute-start | bytes 98312 | tf_op jit(solution)/shard_map/ppermute | solution.py:19
  5.5 19.0 %collective-permute-start.1 = (bf16[2,1,64,128]{3,2,1,0:T(8,128)(2,1)S(1)}, bf16[2,1,64,128]{3,2,1,0:T(8,128)(2,1)S(1)}, u32[]{:S(2)}, u32[]{:S(2)}) collective-permute-start(bf16[2,1,64,128]{3,2,1,0:T(8,128)(2,1)S(1)} %get-tuple-element.48), channel_id=1, source_target_pairs={{8,0},{16,8},{24,16},{32,24},{40,32},{48,40},{56,48},{64,56},{72,6... | collective-permute-start | bytes 98312 | tf_op jit(solution)/shard_map/ppermute | solution.py:21
  22.5 2.7 %copy-start.19 = (bf16[3,3,64,64]{3,2,1,0:T(8,128)(2,1)S(1)}, bf16[3,3,64,64]{3,2,1,0:T(8,128)(2,1)}, u32[]{:S(2)}) copy-start(bf16[3,3,64,64]{3,2,1,0:T(8,128)(2,1)} %param.15) | copy-start | bytes 221188
  24.5 3.2 %copy-start.41 = (bf16[2,1,64,128]{3,2,1,0:T(8,128)(2,1)}, bf16[2,1,64,128]{3,2,1,0:T(8,128)(2,1)S(1)}, u32[]{:S(2)}) copy-start(bf16[2,1,64,128]{3,2,1,0:T(8,128)(2,1)S(1)} %collective-permute-done.1) | copy-start | bytes 98308
  27.7 7.5 %copy-start.39 = (bf16[3,64,64]{2,1,0:T(8,128)(2,1)S(1)}, bf16[3,64,64]{2,1,0:T(8,128)(2,1)}, u32[]{:S(2)}) copy-start(bf16[3,64,64]{2,1,0:T(8,128)(2,1)} %param.16) | copy-start | bytes 73732
  29.3 12.4 %copy-start.7 = (bf16[2,16,64,128]{3,2,1,0:T(8,128)(2,1)}, bf16[2,16,64,128]{3,2,1,0:T(8,128)(2,1)S(1)}, u32[]{:S(2)}) copy-start(bf16[2,16,64,128]{3,2,1,0:T(8,128)(2,1)S(1)} %get-tuple-element.66) | copy-start | bytes 1572868
  29.3 12.0 %copy-start.17 = (bf16[1,16,64,128]{3,2,1,0:T(8,128)(2,1)}, bf16[1,16,64,128]{3,2,1,0:T(8,128)(2,1)S(1)}, u32[]{:S(2)}) copy-start(bf16[1,16,64,128]{3,2,1,0:T(8,128)(2,1)S(1)} %get-tuple-element.45) | copy-start | bytes 786436
  29.3 12.4 %copy-start.30 = (bf16[1,16,64,128]{3,2,1,0:T(8,128)(2,1)}, bf16[1,16,64,128]{3,2,1,0:T(8,128)(2,1)S(1)}, u32[]{:S(2)}) copy-start(bf16[1,16,64,128]{3,2,1,0:T(8,128)(2,1)S(1)} %get-tuple-element.46) | copy-start | bytes 786436
  29.3 12.4 %collective-permute-start.2 = (bf16[1,16,64,128]{3,2,1,0:T(8,128)(2,1)S(1)}, bf16[1,16,64,128]{3,2,1,0:T(8,128)(2,1)S(1)}, u32[]{:S(2)}, u32[]{:S(2)}) collective-permute-start(bf16[1,16,64,128]{3,2,1,0:T(8,128)(2,1)S(1)} %get-tuple-element.45), channel_id=1, source_target_pairs={{0,1},{1,2},{2,3},{3,4},{4,5},{5,6},{6,7},{8,9},{9,10},{10,11},{11... | collective-permute-start | bytes 786440 | tf_op jit(solution)/shard_map/ppermute | solution.py:31
  33.3 7.7 %collective-permute-start.3 = (bf16[1,16,64,128]{3,2,1,0:T(8,128)(2,1)S(1)}, bf16[1,16,64,128]{3,2,1,0:T(8,128)(2,1)S(1)}, u32[]{:S(2)}, u32[]{:S(2)}) collective-permute-start(bf16[1,16,64,128]{3,2,1,0:T(8,128)(2,1)S(1)} %get-tuple-element.46), channel_id=1, source_target_pairs={{1,0},{2,1},{3,2},{4,3},{5,4},{6,5},{7,6},{9,8},{10,9},{11,10},{12... | collective-permute-start | bytes 786440 | tf_op jit(solution)/shard_map/ppermute | solution.py:31
  41.7 1.5 copy-start.47
  43.2 12.3 %copy-start.3 = (bf16[2,16,64,128]{3,2,1,0:T(8,128)(2,1)}, bf16[2,16,64,128]{3,2,1,0:T(8,128)(2,1)S(1)}, u32[]{:S(2)}) copy-start(bf16[2,16,64,128]{3,2,1,0:T(8,128)(2,1)S(1)} %get-tuple-element.68) | copy-start | bytes 1572868
  43.2 9.7 %copy-start.26 = (bf16[3,3,64,64]{3,2,1,0:T(8,128)(2,1)S(1)}, bf16[3,3,64,64]{3,2,1,0:T(8,128)(2,1)}, u32[]{:S(2)}) copy-start(bf16[3,3,64,64]{3,2,1,0:T(8,128)(2,1)} %param.17) | copy-start | bytes 221188
  43.2 6.3 %collective-permute-start.4 = (bf16[2,1,64,128]{3,2,1,0:T(8,128)(2,1)S(1)}, bf16[2,1,64,128]{3,2,1,0:T(8,128)(2,1)S(1)}, u32[]{:S(2)}, u32[]{:S(2)}) collective-permute-start(bf16[2,1,64,128]{3,2,1,0:T(8,128)(2,1)S(1)} %get-tuple-element.43), channel_id=1, source_target_pairs={{0,8},{8,16},{16,24},{24,32},{32,40},{40,48},{48,56},{56,64},{64,7... | collective-permute-start | bytes 98312 | tf_op jit(solution)/shard_map/ppermute | solution.py:19
  47.6 4.7 %collective-permute-start.5 = (bf16[2,1,64,128]{3,2,1,0:T(8,128)(2,1)S(1)}, bf16[2,1,64,128]{3,2,1,0:T(8,128)(2,1)S(1)}, u32[]{:S(2)}, u32[]{:S(2)}) collective-permute-start(bf16[2,1,64,128]{3,2,1,0:T(8,128)(2,1)S(1)} %get-tuple-element.44), channel_id=1, source_target_pairs={{8,0},{16,8},{24,16},{32,24},{40,32},{48,40},{56,48},{64,56},{72,6... | collective-permute-start | bytes 98312 | tf_op jit(solution)/shard_map/ppermute | solution.py:21
  49.5 3.8 %copy-start.35 = (bf16[2,1,64,128]{3,2,1,0:T(8,128)(2,1)}, bf16[2,1,64,128]{3,2,1,0:T(8,128)(2,1)S(1)}, u32[]{:S(2)}) copy-start(bf16[2,1,64,128]{3,2,1,0:T(8,128)(2,1)S(1)} %collective-permute-done.4) | copy-start | bytes 98308
  52.3 3.2 %copy-start.43 = (bf16[2,1,64,128]{3,2,1,0:T(8,128)(2,1)}, bf16[2,1,64,128]{3,2,1,0:T(8,128)(2,1)S(1)}, u32[]{:S(2)}) copy-start(bf16[2,1,64,128]{3,2,1,0:T(8,128)(2,1)S(1)} %collective-permute-done.5) | copy-start | bytes 98308
  57.1 15.9 %collective-permute-start.7 = (bf16[2,16,64,128]{3,2,1,0:T(8,128)(2,1)}, bf16[2,16,64,128]{3,2,1,0:T(8,128)(2,1)S(1)}, u32[]{:S(2)}, u32[]{:S(2)}) collective-permute-start(bf16[2,16,64,128]{3,2,1,0:T(8,128)(2,1)} %get-tuple-element.70), channel_id=1, source_target_pairs={{2,0},{3,1},{4,2},{5,3},{6,4},{7,5},{10,8},{11,9},{12,10},{13,11},... | collective-permute-start | bytes 1572872 | tf_op jit(solution)/shard_map/ppermute | solution.py:31
  60.7 12.3 %copy-start.37 = (bf16[3,64,64]{2,1,0:T(8,128)(2,1)S(1)}, bf16[3,64,64]{2,1,0:T(8,128)(2,1)}, u32[]{:S(2)}) copy-start(bf16[3,64,64]{2,1,0:T(8,128)(2,1)} %param.18) | copy-start | bytes 73732
  62.1 15.6 %collective-permute-start.6 = (bf16[2,16,64,128]{3,2,1,0:T(8,128)(2,1)}, bf16[2,16,64,128]{3,2,1,0:T(8,128)(2,1)S(1)}, u32[]{:S(2)}, u32[]{:S(2)}) collective-permute-start(bf16[2,16,64,128]{3,2,1,0:T(8,128)(2,1)} %get-tuple-element.70), channel_id=1, source_target_pairs={{0,2},{1,3},{2,4},{3,5},{4,6},{5,7},{8,10},{9,11},{10,12},{11,13},... | collective-permute-start | bytes 1572872 | tf_op jit(solution)/shard_map/ppermute | solution.py:31
  73.0 7.6 %copy-start.11 = (bf16[2,16,64,128]{3,2,1,0:T(8,128)(2,1)}, bf16[2,16,64,128]{3,2,1,0:T(8,128)(2,1)S(1)}, u32[]{:S(2)}) copy-start(bf16[2,16,64,128]{3,2,1,0:T(8,128)(2,1)S(1)} %collective-permute-done.7) | copy-start | bytes 1572868
  77.7 2.9 %copy-start.22 = (bf16[2,16,64,128]{3,2,1,0:T(8,128)(2,1)}, bf16[2,16,64,128]{3,2,1,0:T(8,128)(2,1)S(1)}, u32[]{:S(2)}) copy-start(bf16[2,16,64,128]{3,2,1,0:T(8,128)(2,1)S(1)} %collective-permute-done.6) | copy-start | bytes 1572868
  84.1 18.9 %copy-start.25 = (bf16[2,1,4,64,128]{4,3,0,2,1:T(8,128)(2,1)S(1)}, bf16[2,1,4,64,128]{4,3,0,2,1:T(8,128)(2,1)}, u32[]{:S(2)}) copy-start(bf16[2,1,4,64,128]{4,3,0,2,1:T(8,128)(2,1)} %select_bitcast_fusion.2) | copy-start | bytes 393220
  87.5 16.9 %copy-start.45 = (pred[4]{0:T(512)(128)(4,1)S(1)}, pred[4]{0:T(512)(128)(4,1)}, u32[]{:S(2)}) copy-start(pred[4]{0:T(512)(128)(4,1)} %get-tuple-element.84) | copy-start | bytes 16
  88.2 16.2 %copy-start.24 = (bf16[2,1,4,64,128]{4,3,0,2,1:T(8,128)(2,1)S(1)}, bf16[2,1,4,64,128]{4,3,0,2,1:T(8,128)(2,1)}, u32[]{:S(2)}) copy-start(bf16[2,1,4,64,128]{4,3,0,2,1:T(8,128)(2,1)} %select_bitcast_fusion) | copy-start | bytes 393220
  89.2 16.8 %collective-permute-start.8 = (bf16[2,2,4,64,128]{4,3,0,2,1:T(8,128)(2,1)S(1)}, bf16[2,2,4,64,128]{4,3,0,2,1:T(8,128)(2,1)S(1)}, u32[]{:S(2)}, u32[]{:S(2)}) collective-permute-start(bf16[2,2,4,64,128]{4,3,0,2,1:T(8,128)(2,1)S(1)} %pad_maximum_fusion.23), channel_id=1, source_target_pairs={{0,16},{8,24},{16,32},{24,40},{32,48},{40,56},{48,64},{56,72},{64,... | collective-permute-start | bytes 786440 | tf_op jit(solution)/shard_map/ppermute | solution.py:31
  97.7 9.1 %collective-permute-start.9 = (bf16[2,2,4,64,128]{4,3,0,2,1:T(8,128)(2,1)S(1)}, bf16[2,2,4,64,128]{4,3,0,2,1:T(8,128)(2,1)S(1)}, u32[]{:S(2)}, u32[]{:S(2)}) collective-permute-start(bf16[2,2,4,64,128]{4,3,0,2,1:T(8,128)(2,1)S(1)} %pad_maximum_fusion.24), channel_id=1, source_target_pairs={{0,8},{8,16},{16,24},{24,32},{32,40},{40,48},{48,56},{56,64},{64,7... | collective-permute-start | bytes 786440 | tf_op jit(solution)/shard_map/ppermute | solution.py:31
  103.1 9.7 %collective-permute-start.10 = (bf16[2,2,4,64,128]{4,3,0,2,1:T(8,128)(2,1)S(1)}, bf16[2,2,4,64,128]{4,3,0,2,1:T(8,128)(2,1)S(1)}, u32[]{:S(2)}, u32[]{:S(2)}) collective-permute-start(bf16[2,2,4,64,128]{4,3,0,2,1:T(8,128)(2,1)S(1)} %pad_maximum_fusion.25), channel_id=1, source_target_pairs={{8,0},{16,8},{24,16},{32,24},{40,32},{48,40},{56,48},{64,56},{72,6... | collective-permute-start | bytes 786440 | tf_op jit(solution)/shard_map/ppermute | solution.py:31
  104.5 9.9 %collective-permute-start.11 = (bf16[2,2,4,64,128]{4,3,0,2,1:T(8,128)(2,1)S(1)}, bf16[2,2,4,64,128]{4,3,0,2,1:T(8,128)(2,1)S(1)}, u32[]{:S(2)}, u32[]{:S(2)}) collective-permute-start(bf16[2,2,4,64,128]{4,3,0,2,1:T(8,128)(2,1)S(1)} %pad_maximum_fusion.26), channel_id=1, source_target_pairs={{16,0},{24,8},{32,16},{40,24},{48,32},{56,40},{64,48},{72,56},{80,... | collective-permute-start | bytes 786440 | tf_op jit(solution)/shard_map/ppermute | solution.py:31
  107.5 7.7 %copy-start.46 = (pred[4,4]{1,0:T(4,128)(4,1)S(1)}, pred[4,4]{1,0:T(4,128)(4,1)}, u32[]{:S(2)}) copy-start(pred[4,4]{1,0:T(4,128)(4,1)} %select_and_fusion) | copy-start | bytes 52
  116.5 8.1 %copy-start.12 = (bf16[2,16,64,128]{3,2,1,0:T(8,128)(2,1)S(1)}, bf16[2,16,64,128]{3,2,1,0:T(8,128)(2,1)}, u32[]{:S(2)}) copy-start(bf16[2,16,64,128]{3,2,1,0:T(8,128)(2,1)} %copy-done.11) | copy-start | bytes 1572868
  117.0 7.8 %copy-start.23 = (bf16[2,16,64,128]{3,2,1,0:T(8,128)(2,1)S(1)}, bf16[2,16,64,128]{3,2,1,0:T(8,128)(2,1)}, u32[]{:S(2)}) copy-start(bf16[2,16,64,128]{3,2,1,0:T(8,128)(2,1)} %copy-done.22) | copy-start | bytes 1572868
  118.4 12.3 %collective-permute-start.13 = (bf16[2,16,64,128]{3,2,1,0:T(8,128)(2,1)S(1)}, bf16[2,16,64,128]{3,2,1,0:T(8,128)(2,1)}, u32[]{:S(2)}, u32[]{:S(2)}) collective-permute-start(bf16[2,16,64,128]{3,2,1,0:T(8,128)(2,1)S(1)} %fusion.25), channel_id=1, source_target_pairs={{0,2},{1,3},{2,4},{3,5},{4,6},{5,7},{8,10},{9,11},{10,12},{11,13},... | collective-permute-start | bytes 1572872 | tf_op jit(solution)/shard_map/ppermute | solution.py:31
  123.3 11.8 %collective-permute-start.12 = (bf16[2,16,64,128]{3,2,1,0:T(8,128)(2,1)S(1)}, bf16[2,16,64,128]{3,2,1,0:T(8,128)(2,1)}, u32[]{:S(2)}, u32[]{:S(2)}) collective-permute-start(bf16[2,16,64,128]{3,2,1,0:T(8,128)(2,1)S(1)} %fusion.25), channel_id=1, source_target_pairs={{2,0},{3,1},{4,2},{5,3},{6,4},{7,5},{10,8},{11,9},{12,10},{13,11},... | collective-permute-start | bytes 1572872 | tf_op jit(solution)/shard_map/ppermute | solution.py:31
  127.4 1.8 copy-start.15
  130.4 4.7 %copy-start.49 = (f32[2,16,64,128]{3,2,1,0:T(8,128)S(1)}, f32[2,16,64,128]{3,2,1,0:T(8,128)}, u32[]{:S(2)}) copy-start(f32[2,16,64,128]{3,2,1,0:T(8,128)} %get-tuple-element.71) | copy-start | bytes 3145732
  130.8 4.3 %copy-start.10 = (f32[2,64,128,16]{2,3,1,0:T(8,128)S(1)}, f32[2,64,128,16]{2,3,1,0:T(8,128)}, u32[]{:S(2)}) copy-start(f32[2,64,128,16]{2,3,1,0:T(8,128)} %copy-done.9) | copy-start | bytes 3145732
  130.8 4.3 %copy-start.14 = (bf16[2,16,64,128]{3,2,1,0:T(8,128)(2,1)S(1)}, bf16[2,16,64,128]{3,2,1,0:T(8,128)(2,1)}, u32[]{:S(2)}) copy-start(bf16[2,16,64,128]{3,2,1,0:T(8,128)(2,1)} %param.22) | copy-start | bytes 1572868
  135.1 2.8 %copy-start.4 = (bf16[2,16,64,128]{3,2,1,0:T(8,128)(2,1)S(1)}, bf16[2,16,64,128]{3,2,1,0:T(8,128)(2,1)}, u32[]{:S(2)}) copy-start(bf16[2,16,64,128]{3,2,1,0:T(8,128)(2,1)} %copy-done.3) | copy-start | bytes 1572868
  137.9 11.7 %copy-start.5 = (bf16[2,16,64,128]{3,2,1,0:T(8,128)(2,1)}, bf16[2,16,64,128]{3,2,1,0:T(8,128)(2,1)S(1)}, u32[]{:S(2)}) copy-start(bf16[2,16,64,128]{3,2,1,0:T(8,128)(2,1)S(1)} %get-tuple-element.74) | copy-start | bytes 1572868
  139.5 9.8 %copy-start.44 = (bf16[2,1,64,128]{3,2,1,0:T(8,128)(2,1)S(1)}, bf16[2,1,64,128]{3,2,1,0:T(8,128)(2,1)}, u32[]{:S(2)}) copy-start(bf16[2,1,64,128]{3,2,1,0:T(8,128)(2,1)} %copy-done.43) | copy-start | bytes 98308
  140.2 9.4 %copy-start.36 = (bf16[2,1,64,128]{3,2,1,0:T(8,128)(2,1)S(1)}, bf16[2,1,64,128]{3,2,1,0:T(8,128)(2,1)}, u32[]{:S(2)}) copy-start(bf16[2,1,64,128]{3,2,1,0:T(8,128)(2,1)} %copy-done.35) | copy-start | bytes 98308
  140.2 9.9 %collective-permute-start.14 = (bf16[2,1,64,128]{3,2,1,0:T(8,128)(2,1)S(1)}, bf16[2,1,64,128]{3,2,1,0:T(8,128)(2,1)S(1)}, u32[]{:S(2)}, u32[]{:S(2)}) collective-permute-start(bf16[2,1,64,128]{3,2,1,0:T(8,128)(2,1)S(1)} %get-tuple-element.41), channel_id=1, source_target_pairs={{0,8},{8,16},{16,24},{24,32},{32,40},{40,48},{48,56},{56,64},{64,7... | collective-permute-start | bytes 98312 | tf_op jit(solution)/shard_map/ppermute | solution.py:19
  148.0 6.3 %collective-permute-start.15 = (bf16[2,1,64,128]{3,2,1,0:T(8,128)(2,1)S(1)}, bf16[2,1,64,128]{3,2,1,0:T(8,128)(2,1)S(1)}, u32[]{:S(2)}, u32[]{:S(2)}) collective-permute-start(bf16[2,1,64,128]{3,2,1,0:T(8,128)(2,1)S(1)} %get-tuple-element.42), channel_id=1, source_target_pairs={{8,0},{16,8},{24,16},{32,24},{40,32},{48,40},{56,48},{64,56},{72,6... | collective-permute-start | bytes 98312 | tf_op jit(solution)/shard_map/ppermute | solution.py:21
  149.9 4.3 %copy-start.6 = (bf16[2,16,64,128]{3,2,1,0:T(8,128)(2,1)S(1)}, bf16[2,16,64,128]{3,2,1,0:T(8,128)(2,1)}, u32[]{:S(2)}) copy-start(bf16[2,16,64,128]{3,2,1,0:T(8,128)(2,1)} %copy-done.5) | copy-start | bytes 1572868
  150.0 4.9 %copy-start.27 = (bf16[3,3,64,64]{3,2,1,0:T(8,128)(2,1)S(1)}, bf16[3,3,64,64]{3,2,1,0:T(8,128)(2,1)}, u32[]{:S(2)}) copy-start(bf16[3,3,64,64]{3,2,1,0:T(8,128)(2,1)} %param.17) | copy-start | bytes 221188
  158.8 1.5 copy-start.8
  160.5 9.5 %copy-start.31 = (bf16[1,16,64,128]{3,2,1,0:T(8,128)(2,1)S(1)}, bf16[1,16,64,128]{3,2,1,0:T(8,128)(2,1)}, u32[]{:S(2)}) copy-start(bf16[1,16,64,128]{3,2,1,0:T(8,128)(2,1)} %copy-done.30) | copy-start | bytes 786436
  160.6 9.5 %copy-start.48 = (bf16[1,16,64,128]{3,2,1,0:T(8,128)(2,1)S(1)}, bf16[1,16,64,128]{3,2,1,0:T(8,128)(2,1)}, u32[]{:S(2)}) copy-start(bf16[1,16,64,128]{3,2,1,0:T(8,128)(2,1)} %copy-done.47) | copy-start | bytes 786436
  161.3 9.0 %copy-start.18 = (bf16[1,16,64,128]{3,2,1,0:T(8,128)(2,1)S(1)}, bf16[1,16,64,128]{3,2,1,0:T(8,128)(2,1)}, u32[]{:S(2)}) copy-start(bf16[1,16,64,128]{3,2,1,0:T(8,128)(2,1)} %copy-done.17) | copy-start | bytes 786436
  161.3 9.0 %copy-start.29 = (bf16[1,16,64,128]{3,2,1,0:T(8,128)(2,1)S(1)}, bf16[1,16,64,128]{3,2,1,0:T(8,128)(2,1)}, u32[]{:S(2)}) copy-start(bf16[1,16,64,128]{3,2,1,0:T(8,128)(2,1)} %copy-done.28) | copy-start | bytes 786436
  161.7 9.1 %collective-permute-start.17 = (bf16[1,16,64,128]{3,2,1,0:T(8,128)(2,1)}, bf16[1,16,64,128]{3,2,1,0:T(8,128)(2,1)}, u32[]{:S(2)}, u32[]{:S(2)}) collective-permute-start(bf16[1,16,64,128]{3,2,1,0:T(8,128)(2,1)} %get-tuple-element.39), channel_id=1, source_target_pairs={{0,1},{1,2},{2,3},{3,4},{4,5},{5,6},{6,7},{8,9},{9,10},{10,11},{11... | collective-permute-start | bytes 786440 | tf_op jit(solution)/shard_map/ppermute | solution.py:31
  166.9 7.8 %collective-permute-start.16 = (bf16[1,16,64,128]{3,2,1,0:T(8,128)(2,1)S(1)}, bf16[1,16,64,128]{3,2,1,0:T(8,128)(2,1)}, u32[]{:S(2)}, u32[]{:S(2)}) collective-permute-start(bf16[1,16,64,128]{3,2,1,0:T(8,128)(2,1)S(1)} %get-tuple-element.40), channel_id=1, source_target_pairs={{1,0},{2,1},{3,2},{4,3},{5,4},{6,5},{7,6},{9,8},{10,9},{11,10},{12... | collective-permute-start | bytes 786440 | tf_op jit(solution)/shard_map/ppermute | solution.py:31
  170.7 4.0 %copy-start.50 = (f32[2,16,64,128]{3,2,1,0:T(8,128)S(1)}, f32[2,16,64,128]{3,2,1,0:T(8,128)}, u32[]{:S(2)}) copy-start(f32[2,16,64,128]{3,2,1,0:T(8,128)} %get-tuple-element.67) | copy-start | bytes 3145732
  170.7 4.0 %copy-start.53 = (bf16[2,16,64,128]{3,2,1,0:T(8,128)(2,1)S(1)}, bf16[2,16,64,128]{3,2,1,0:T(8,128)(2,1)}, u32[]{:S(2)}) copy-start(bf16[2,16,64,128]{3,2,1,0:T(8,128)(2,1)} %get-tuple-element.77) | copy-start | bytes 1572868
  180.3 1.8 copy-start.32
  180.6 23.0 %copy-start.20 = (bf16[3,3,64,64]{3,2,1,0:T(8,128)(2,1)S(1)}, bf16[3,3,64,64]{3,2,1,0:T(8,128)(2,1)}, u32[]{:S(2)}) copy-start(bf16[3,3,64,64]{3,2,1,0:T(8,128)(2,1)} %param.15) | copy-start | bytes 221188
  180.7 22.8 %collective-permute-start.19 = (bf16[2,1,64,128]{3,2,1,0:T(8,128)(2,1)S(1)}, bf16[2,1,64,128]{3,2,1,0:T(8,128)(2,1)S(1)}, u32[]{:S(2)}, u32[]{:S(2)}) collective-permute-start(bf16[2,1,64,128]{3,2,1,0:T(8,128)(2,1)S(1)} %get-tuple-element.38), channel_id=1, source_target_pairs={{8,0},{16,8},{24,16},{32,24},{40,32},{48,40},{56,48},{64,56},{72,6... | collective-permute-start | bytes 98312 | tf_op jit(solution)/shard_map/ppermute | solution.py:21
  182.8 35.5 %all-to-all-start = ((f32[256,1,384]{2,1,0:T(1,128)}), f32[256,1,384]{2,1,0:T(1,128)S(1)}, u32[]{:S(2)}, u32[]{:S(2)}) async-start(f32[256,1,384]{2,1,0:T(1,128)} %bitcast.230), calls=%async_computation | async-start | bytes 786432 | tf_op jit(solution)/shard_map/all_to_all | solution.py:236
  200.3 4.3 %collective-permute-start.18 = (bf16[2,1,64,128]{3,2,1,0:T(8,128)(2,1)S(1)}, bf16[2,1,64,128]{3,2,1,0:T(8,128)(2,1)S(1)}, u32[]{:S(2)}, u32[]{:S(2)}) collective-permute-start(bf16[2,1,64,128]{3,2,1,0:T(8,128)(2,1)S(1)} %get-tuple-element.37), channel_id=1, source_target_pairs={{0,8},{8,16},{16,24},{24,32},{32,40},{40,48},{48,56},{56,64},{64,7... | collective-permute-start | bytes 98312 | tf_op jit(solution)/shard_map/ppermute | solution.py:19
  219.6 24.6 %all-to-all-start.1 = ((f32[256,1,384]{2,1,0:T(1,128)}), f32[256,1,384]{2,1,0:T(1,128)S(1)}, u32[]{:S(2)}, u32[]{:S(2)}) async-start(f32[256,1,384]{2,1,0:T(1,128)} %broadcast_in_dim.91), calls=%async_computation.1 | async-start | bytes 786432 | tf_op jit(solution)/shard_map/all_to_all | solution.py:238
  229.3 19.1 %copy-start.1 = (s32[32,16]{0,1:T(8,128)S(1)}, s32[32,16]{0,1:T(8,128)}, u32[]{:S(2)}) copy-start(s32[32,16]{0,1:T(8,128)} %param.21) | copy-start | bytes 6148
  (12 other events, 12.9 us)

commit v5 on v4

--- a/solution.py
+++ b/solution.py
@@ -215,7 +215,12 @@
 
 
 def pick_strips(values, strip_ids):
-    gathered = jnp.take(values, strip_ids.reshape(-1), axis=1)
+    hot = (strip_ids.reshape(-1)[:, None] == jnp.arange(values.shape[1])[None, :]).astype(
+        values.dtype
+    )
+    gathered = jnp.einsum(
+        "qs,fscp->fqcp", hot, values, preferred_element_type=jnp.float32
+    ).astype(values.dtype)
     return gathered.reshape(
         values.shape[0], strip_ids.shape[0], strip_ids.shape[1], values.shape[2], values.shape[3]
     )

time: 251 us -> 237 us (0.944)
  other arithmetic: 25.2 us -> 14.7 us
  local copies, waits for them, and re-layouts: 28.2 us -> 17.9 us
  waiting for transfers between devices: 58.9 us -> 65.2 us
  matrix products: 44.9 us -> 48.4 us
    gather x8 -> x0, local copies, waits for them, and re-layouts: 13.4 us -> none  [pick_strips(): gathered = jnp.take(values, strip_ids.reshape(-1), axis=1)]
    dot_general x0 -> x8, matrix products: none -> 7.98 us  [pick_strips(): jnp.einsum('qs,fscp->fqcp', hot, values, preferred_element_type=jnp.float32)]
    ppermute x12, waiting for transfers between devices: 27.8 us -> 34.2 us  [from_behind(): return lax.ppermute(array, axis, pairs)]
    reshape x8 -> x0, other arithmetic: 5.83 us -> none  [pick_strips(): gathered.reshape(values.shape[0], strip_ids.shape[0], strip_ids.shape[1],...]
    ppermute x4, starting transfers between devices: 19.4 us -> 14.4 us  [with_halo(): lax.ppermute(tail, axis, [(i, (i + 1) % count) for i in range(ends)])]
    all_to_all x1, starting transfers between devices: 17.4 us -> 21.6 us  [exchange_sum(): flat = jnp.sum(lax.all_to_all(pieces, axes, 0, 0, tiled=True), axis=0)]
    dot_general x18, matrix products: 11.4 us -> 8.45 us  [spatial_transpose(): jnp.einsum('oc,fsop->fscp', weight[row_tap, col_tap], padded[:, 2 - row_t...]
  transfers between devices with their start and end apart: 22 -> 22, of which waited for: 13 -> 14; matrix products, arithmetic and copies ran while one was open for 19% -> 16% of each run, Pallas kernels for 0% -> 0%
where the time goes in v5:
time: 237 us; the launch traced here: 235 us
  starting transfers between devices  87.2 us (37%)
  waiting for transfers between devices  65.2 us (28%)
  matrix products  48.4 us (20%)
  local copies, waits for them, and re-layouts  17.9 us (8%)
  other arithmetic  14.7 us (6%)
    ppermute x12, starting transfers between devices, from_behind(): return lax.ppermute(array, axis, pairs)  39.1 us
    ppermute x12, waiting for transfers between devices, from_behind(): return lax.ppermute(array, axis, pairs)  34.2 us
    all_to_all x1, starting transfers between devices, exchange_sum(): flat = jnp.sum(lax.all_to_all(pieces, axes, 0, 0, tiled=True), axis=0)  21.6 us
    all_to_all x1, waiting for transfers between devices, exchange_sum(): flat = lax.all_to_all(copies, axes, 0, 0, tiled=True).reshape(-1)  14.6 us
    ppermute x4, starting transfers between devices, with_halo(): lax.ppermute(tail, axis, [(i, (i + 1) % count) for i in range(ends)])  14.4 us
    all_to_all x1, waiting for transfers between devices, exchange_sum(): flat = jnp.sum(lax.all_to_all(pieces, axes, 0, 0, tiled=True), axis=0)  11.4 us
    dot_general x18, matrix products, spatial_transpose(): jnp.einsum('oc,fsop->fscp', weight[row_tap, col_tap], padded[:, 2 - row_t...  8.45 us
    dot_general x18, matrix products, spatial_apply(): jnp.einsum('oc,fscp->fsop', weight[row_tap, col_tap], padded[:, row_tap:r...  8.04 us
  transfers between devices with their start and end apart: 22, of which 14 were waited for; matrix products, arithmetic and copies ran while one was open for 16% of the time, Pallas kernels for 0%

profile of v5, /device:TPU:1, one launch (start us, length us, event | category | flops | bytes accessed | tf_op | source)
XLA Modules:
  0.0 235.4 jit_solution(15461571313785119760)
XLA Ops:
  0.6 0.8 fusion.288
  1.5 4.0 %collective-permute-start = (bf16[2,1,64,128]{3,2,1,0:T(8,128)(2,1)S(1)}, bf16[2,1,64,128]{3,2,1,0:T(8,128)(2,1)S(1)}, u32[]{:S(2)}, u32[]{:S(2)}) collective-permute-start(bf16[2,1,64,128]{3,2,1,0:T(8,128)(2,1)S(1)} %get-tuple-element.38), channel_id=1, source_target_pairs={{0,8},{8,16},{16,24},{24,32},{32,40},{40,48},{48,56},{56,64},{64,7... | collective-permute-start | bytes 98312 | tf_op jit(solution)/shard_map/ppermute | solution.py:19
  5.5 1.3 collective-permute-start.1
  7.5 0.9 dynamic-slice_reduce_fusion.2
  9.8 0.9 convert_reduce_fusion
  11.4 0.9 dynamic-slice_reduce_fusion
  16.2 2.1 fusion.26
  18.3 2.1 fusion.32
  23.7 1.5 add_convert_fusion.3
  25.2 4.0 %collective-permute-start.2 = (bf16[1,16,64,128]{3,2,1,0:T(8,128)(2,1)S(1)}, bf16[1,16,64,128]{3,2,1,0:T(8,128)(2,1)S(1)}, u32[]{:S(2)}, u32[]{:S(2)}) collective-permute-start(bf16[1,16,64,128]{3,2,1,0:T(8,128)(2,1)S(1)} %get-tuple-element.36), channel_id=1, source_target_pairs={{0,1},{1,2},{2,3},{3,4},{4,5},{5,6},{6,7},{8,9},{9,10},{10,11},{11... | collective-permute-start | bytes 786440 | tf_op jit(solution)/shard_map/ppermute | solution.py:31
  29.2 1.9 collective-permute-start.3
  31.4 5.5 %collective-permute-done.3 = bf16[1,16,64,128]{3,2,1,0:T(8,128)(2,1)S(1)} collective-permute-done((bf16[1,16,64,128]{3,2,1,0:T(8,128)(2,1)S(1)}, bf16[1,16,64,128]{3,2,1,0:T(8,128)(2,1)S(1)}, u32[]{:S(2)}, u32[]{:S(2)}) %collective-permute-start.3) | collective-permute-done | bytes 262176 | tf_op jit(solution)/shard_map/ppermute | solution.py:31
  37.6 1.5 add_convert_fusion.2
  39.1 4.3 %collective-permute-start.4 = (bf16[2,1,64,128]{3,2,1,0:T(8,128)(2,1)S(1)}, bf16[2,1,64,128]{3,2,1,0:T(8,128)(2,1)S(1)}, u32[]{:S(2)}, u32[]{:S(2)}) collective-permute-start(bf16[2,1,64,128]{3,2,1,0:T(8,128)(2,1)S(1)} %get-tuple-element.34), channel_id=1, source_target_pairs={{0,8},{8,16},{16,24},{24,32},{32,40},{40,48},{48,56},{56,64},{64,7... | collective-permute-start | bytes 98312 | tf_op jit(solution)/shard_map/ppermute | solution.py:19
  43.3 1.3 collective-permute-start.5
  44.7 1.1 fusion.30
  45.7 2.3 collective-permute-done.5
  51.2 1.6 add_convert_fusion.1
  52.8 1.3 collective-permute-start.7
  54.1 1.0 fusion.28
  55.2 1.0 select_reduce_fusion.5
  56.2 1.5 fusion.230
  57.7 4.2 %collective-permute-start.6 = (bf16[2,16,64,128]{3,2,1,0:T(8,128)(2,1)}, bf16[2,16,64,128]{3,2,1,0:T(8,128)(2,1)S(1)}, u32[]{:S(2)}, u32[]{:S(2)}) collective-permute-start(bf16[2,16,64,128]{3,2,1,0:T(8,128)(2,1)} %get-tuple-element.59), channel_id=1, source_target_pairs={{0,2},{1,3},{2,4},{3,5},{4,6},{5,7},{8,10},{9,11},{10,12},{11,13},... | collective-permute-start | bytes 1572872 | tf_op jit(solution)/shard_map/ppermute | solution.py:31
  61.9 1.3 fusion.135
  63.2 5.5 %collective-permute-done.7 = bf16[2,16,64,128]{3,2,1,0:T(8,128)(2,1)S(1)} collective-permute-done((bf16[2,16,64,128]{3,2,1,0:T(8,128)(2,1)}, bf16[2,16,64,128]{3,2,1,0:T(8,128)(2,1)S(1)}, u32[]{:S(2)}, u32[]{:S(2)}) %collective-permute-start.7) | collective-permute-done | bytes 524320 | tf_op jit(solution)/shard_map/ppermute | solution.py:31
  69.6 3.8 %collective-permute-done.6 = bf16[2,16,64,128]{3,2,1,0:T(8,128)(2,1)S(1)} collective-permute-done((bf16[2,16,64,128]{3,2,1,0:T(8,128)(2,1)}, bf16[2,16,64,128]{3,2,1,0:T(8,128)(2,1)S(1)}, u32[]{:S(2)}, u32[]{:S(2)}) %collective-permute-start.6) | collective-permute-done | bytes 524320 | tf_op jit(solution)/shard_map/ppermute | solution.py:31
  73.4 1.6 add_convert_fusion
  76.4 6.8 %collective-permute-start.8 = (bf16[2,2,4,64,128]{4,2,3,0,1:T(4,128)(2,1)S(1)}, bf16[2,2,4,64,128]{4,2,3,0,1:T(4,128)(2,1)S(1)}, u32[]{:S(2)}, u32[]{:S(2)}) collective-permute-start(bf16[2,2,4,64,128]{4,2,3,0,1:T(4,128)(2,1)S(1)} %pad_maximum_fusion.21), channel_id=1, source_target_pairs={{0,16},{8,24},{16,32},{24,40},{32,48},{40,56},{48,64},{56,72},{64,... | collective-permute-start | bytes 786440 | tf_op jit(solution)/shard_map/ppermute | solution.py:31
  83.4 1.3 collective-permute-start.11
  84.9 1.3 collective-permute-start.10
  86.8 5.2 %collective-permute-start.9 = (bf16[2,2,4,64,128]{4,2,3,0,1:T(4,128)(2,1)S(1)}, bf16[2,2,4,64,128]{4,2,3,0,1:T(4,128)(2,1)S(1)}, u32[]{:S(2)}, u32[]{:S(2)}) collective-permute-start(bf16[2,2,4,64,128]{4,2,3,0,1:T(4,128)(2,1)S(1)} %pad_maximum_fusion.22), channel_id=1, source_target_pairs={{0,8},{8,16},{16,24},{24,32},{32,40},{40,48},{48,56},{56,64},{64,7... | collective-permute-start | bytes 786440 | tf_op jit(solution)/shard_map/ppermute | solution.py:31
  92.8 1.0 collective-permute-done.11
  94.6 8.7 %collective-permute-done.10 = bf16[2,2,4,64,128]{4,2,3,0,1:T(4,128)(2,1)S(1)} collective-permute-done((bf16[2,2,4,64,128]{4,2,3,0,1:T(4,128)(2,1)S(1)}, bf16[2,2,4,64,128]{4,2,3,0,1:T(4,128)(2,1)S(1)}, u32[]{:S(2)}, u32[]{:S(2)}) %collective-permute-start.10) | collective-permute-done | bytes 262176 | tf_op jit(solution)/shard_map/ppermute | solution.py:31
  106.3 1.3 convolution_bitcast_fusion.9
  107.6 4.8 %collective-permute-start.13 = (bf16[2,16,64,128]{3,2,1,0:T(8,128)(2,1)S(1)}, bf16[2,16,64,128]{3,2,1,0:T(8,128)(2,1)}, u32[]{:S(2)}, u32[]{:S(2)}) collective-permute-start(bf16[2,16,64,128]{3,2,1,0:T(8,128)(2,1)S(1)} %fusion.33), channel_id=1, source_target_pairs={{0,2},{1,3},{2,4},{3,5},{4,6},{5,7},{8,10},{9,11},{10,12},{11,13},... | collective-permute-start | bytes 1572872 | tf_op jit(solution)/shard_map/ppermute | solution.py:31
  112.4 1.3 collective-permute-start.12
  114.9 1.6 reshape.288
  116.5 1.5 convolution_bitcast_fusion.7
  118.1 1.2 fusion.38
  119.6 1.6 collective-permute-done.13
  121.2 1.4 convolution_bitcast_fusion.3
  122.6 3.3 %collective-permute-done.12 = bf16[2,16,64,128]{3,2,1,0:T(8,128)(2,1)} collective-permute-done((bf16[2,16,64,128]{3,2,1,0:T(8,128)(2,1)S(1)}, bf16[2,16,64,128]{3,2,1,0:T(8,128)(2,1)}, u32[]{:S(2)}, u32[]{:S(2)}) %collective-permute-start.12) | collective-permute-done | bytes 524320 | tf_op jit(solution)/shard_map/ppermute | solution.py:31
  126.0 2.0 fusion.34
  130.4 2.6 %collective-permute-start.14 = (bf16[2,1,64,128]{3,2,1,0:T(8,128)(2,1)S(1)}, bf16[2,1,64,128]{3,2,1,0:T(8,128)(2,1)S(1)}, u32[]{:S(2)}, u32[]{:S(2)}) collective-permute-start(bf16[2,1,64,128]{3,2,1,0:T(8,128)(2,1)S(1)} %get-tuple-element.32), channel_id=1, source_target_pairs={{0,8},{8,16},{16,24},{24,32},{32,40},{40,48},{48,56},{56,64},{64,7... | collective-permute-start | bytes 98312 | tf_op jit(solution)/shard_map/ppermute | solution.py:19
  133.0 1.5 collective-permute-start.15
  135.4 2.3 collective-permute-done.15
  141.3 0.8 copy-done.51
  142.1 1.5 fusion.35
  145.0 5.1 %collective-permute-start.17 = (bf16[1,16,64,128]{3,2,1,0:T(8,128)(2,1)}, bf16[1,16,64,128]{3,2,1,0:T(8,128)(2,1)S(1)}, u32[]{:S(2)}, u32[]{:S(2)}) collective-permute-start(bf16[1,16,64,128]{3,2,1,0:T(8,128)(2,1)} %get-tuple-element.30), channel_id=1, source_target_pairs={{0,1},{1,2},{2,3},{3,4},{4,5},{5,6},{6,7},{8,9},{9,10},{10,11},{11... | collective-permute-start | bytes 786440 | tf_op jit(solution)/shard_map/ppermute | solution.py:31
  150.1 1.9 collective-permute-start.16
  152.8 0.9 collective-permute-done.17
  154.1 3.8 %collective-permute-done.16 = bf16[1,16,64,128]{3,2,1,0:T(8,128)(2,1)} collective-permute-done((bf16[1,16,64,128]{3,2,1,0:T(8,128)(2,1)S(1)}, bf16[1,16,64,128]{3,2,1,0:T(8,128)(2,1)}, u32[]{:S(2)}, u32[]{:S(2)}) %collective-permute-start.16) | collective-permute-done | bytes 262176 | tf_op jit(solution)/shard_map/ppermute | solution.py:31
  157.9 2.5 %fusion.36 = (bf16[2,16,64,128]{3,2,1,0:T(8,128)(2,1)S(1)}, bf16[2,16,64,128]{3,2,1,0:T(8,128)(2,1)}) fusion(f32[2,16,64,128]{3,2,1,0:T(8,128)S(1)} %copy-done.50, f32[2,16,64,128]{3,2,1,0:T(8,128)S(1)} %convolution_bitcast_fusion, f32[2,16,64,128]{3,2,1,0:T(8,128)S(1)} %convolution_bitcast_fusion.1, bf16[3,64,64]{2,1,0:T(8,128)(2,1)S(1)} %copy-done.37, ...), kind=kOutput, calls=%fused_computation.122 | convolution fusion | flops 37748736 | bytes 5259264 | tf_op jit(solution)/shard_map/oc,fsop->fscp/dot_general | solution.py:166
  164.3 1.3 collective-permute-start.19
  166.4 21.6 %all-to-all-start = ((f32[256,1,384]{2,1,0:T(1,128)}), f32[256,1,384]{2,1,0:T(1,128)S(1)}, u32[]{:S(2)}, u32[]{:S(2)}) async-start(f32[256,1,384]{2,1,0:T(1,128)} %bitcast.244), calls=%async_computation | async-start | bytes 786432 | tf_op jit(solution)/shard_map/all_to_all | solution.py:241
  188.0 3.5 %collective-permute-start.18 = (bf16[2,1,64,128]{3,2,1,0:T(8,128)(2,1)S(1)}, bf16[2,1,64,128]{3,2,1,0:T(8,128)(2,1)S(1)}, u32[]{:S(2)}, u32[]{:S(2)}) collective-permute-start(bf16[2,1,64,128]{3,2,1,0:T(8,128)(2,1)S(1)} %get-tuple-element.28), channel_id=1, source_target_pairs={{0,8},{8,16},{16,24},{24,32},{32,40},{40,48},{48,56},{56,64},{64,7... | collective-permute-start | bytes 98312 | tf_op jit(solution)/shard_map/ppermute | solution.py:19
  194.8 11.4 %all-to-all-done = f32[256,1,384]{2,1,0:T(1,128)S(1)} async-done(((f32[256,1,384]{2,1,0:T(1,128)}), f32[256,1,384]{2,1,0:T(1,128)S(1)}, u32[]{:S(2)}, u32[]{:S(2)}) %all-to-all-start) | async-done | bytes 393248 | tf_op jit(solution)/shard_map/all_to_all | solution.py:241
  206.4 1.0 broadcast_in_dim.56
  207.4 6.7 %all-to-all-start.1 = ((f32[256,1,384]{2,1,0:T(1,128)}), f32[256,1,384]{2,1,0:T(1,128)S(1)}, u32[]{:S(2)}, u32[]{:S(2)}) async-start(f32[256,1,384]{2,1,0:T(1,128)} %broadcast_in_dim.56), calls=%async_computation.1 | async-start | bytes 786432 | tf_op jit(solution)/shard_map/all_to_all | solution.py:243
  215.4 1.2 fusion.22
  216.6 14.6 %all-to-all-done.1 = f32[256,1,384]{2,1,0:T(1,128)S(1)} async-done(((f32[256,1,384]{2,1,0:T(1,128)}), f32[256,1,384]{2,1,0:T(1,128)S(1)}, u32[]{:S(2)}, u32[]{:S(2)}) %all-to-all-start.1) | async-done | bytes 393248 | tf_op jit(solution)/shard_map/all_to_all | solution.py:243
  233.0 0.8 fusion.124
  233.8 0.8 mul.94
  234.6 0.8 mul.90
  (235 shorter events, 43.2 us)
Async XLA Ops:
  0.6 19.8 %copy-start.3 = (bf16[2,16,64,128]{3,2,1,0:T(8,128)(2,1)S(1)}, bf16[2,16,64,128]{3,2,1,0:T(8,128)(2,1)}, u32[]{:S(2)}) copy-start(bf16[2,16,64,128]{3,2,1,0:T(8,128)(2,1)} %param.12) | copy-start | bytes 1572868
  1.5 19.0 %collective-permute-start = (bf16[2,1,64,128]{3,2,1,0:T(8,128)(2,1)S(1)}, bf16[2,1,64,128]{3,2,1,0:T(8,128)(2,1)S(1)}, u32[]{:S(2)}, u32[]{:S(2)}) collective-permute-start(bf16[2,1,64,128]{3,2,1,0:T(8,128)(2,1)S(1)} %get-tuple-element.38), channel_id=1, source_target_pairs={{0,8},{8,16},{16,24},{24,32},{32,40},{40,48},{48,56},{56,64},{64,7... | collective-permute-start | bytes 98312 | tf_op jit(solution)/shard_map/ppermute | solution.py:19
  5.5 14.9 %collective-permute-start.1 = (bf16[2,1,64,128]{3,2,1,0:T(8,128)(2,1)S(1)}, bf16[2,1,64,128]{3,2,1,0:T(8,128)(2,1)S(1)}, u32[]{:S(2)}, u32[]{:S(2)}) collective-permute-start(bf16[2,1,64,128]{3,2,1,0:T(8,128)(2,1)S(1)} %get-tuple-element.39), channel_id=1, source_target_pairs={{8,0},{16,8},{24,16},{32,24},{40,32},{48,40},{56,48},{64,56},{72,6... | collective-permute-start | bytes 98312 | tf_op jit(solution)/shard_map/ppermute | solution.py:21
  11.4 6.9 %copy-start.38 = (s32[32,4]{0,1:T(4,128)}, s32[32,4]{0,1:T(4,128)S(1)}, u32[]{:S(2)}) copy-start(s32[32,4]{0,1:T(4,128)S(1)} %select_reduce_fusion) | copy-start | bytes 1540
  12.3 1.4 copy-start.43
  18.3 2.8 %copy-start.17 = (bf16[3,3,64,64]{3,2,1,0:T(8,128)(2,1)S(1)}, bf16[3,3,64,64]{3,2,1,0:T(8,128)(2,1)}, u32[]{:S(2)}) copy-start(bf16[3,3,64,64]{3,2,1,0:T(8,128)(2,1)} %param.13) | copy-start | bytes 221188
  20.5 3.2 %copy-start.39 = (bf16[2,1,64,128]{3,2,1,0:T(8,128)(2,1)}, bf16[2,1,64,128]{3,2,1,0:T(8,128)(2,1)S(1)}, u32[]{:S(2)}) copy-start(bf16[2,1,64,128]{3,2,1,0:T(8,128)(2,1)S(1)} %collective-permute-done.1) | copy-start | bytes 98308
  23.6 7.5 %copy-start.36 = (bf16[3,64,64]{2,1,0:T(8,128)(2,1)S(1)}, bf16[3,64,64]{2,1,0:T(8,128)(2,1)}, u32[]{:S(2)}) copy-start(bf16[3,64,64]{2,1,0:T(8,128)(2,1)} %param.14) | copy-start | bytes 73732
  25.1 12.4 %copy-start.9 = (bf16[2,16,64,128]{3,2,1,0:T(8,128)(2,1)}, bf16[2,16,64,128]{3,2,1,0:T(8,128)(2,1)S(1)}, u32[]{:S(2)}) copy-start(bf16[2,16,64,128]{3,2,1,0:T(8,128)(2,1)S(1)} %get-tuple-element.55) | copy-start | bytes 1572868
  25.2 12.0 %copy-start.15 = (bf16[1,16,64,128]{3,2,1,0:T(8,128)(2,1)}, bf16[1,16,64,128]{3,2,1,0:T(8,128)(2,1)S(1)}, u32[]{:S(2)}) copy-start(bf16[1,16,64,128]{3,2,1,0:T(8,128)(2,1)S(1)} %get-tuple-element.36) | copy-start | bytes 786436
  25.2 12.4 %copy-start.27 = (bf16[1,16,64,128]{3,2,1,0:T(8,128)(2,1)}, bf16[1,16,64,128]{3,2,1,0:T(8,128)(2,1)S(1)}, u32[]{:S(2)}) copy-start(bf16[1,16,64,128]{3,2,1,0:T(8,128)(2,1)S(1)} %get-tuple-element.37) | copy-start | bytes 786436
  25.2 12.4 %collective-permute-start.2 = (bf16[1,16,64,128]{3,2,1,0:T(8,128)(2,1)S(1)}, bf16[1,16,64,128]{3,2,1,0:T(8,128)(2,1)S(1)}, u32[]{:S(2)}, u32[]{:S(2)}) collective-permute-start(bf16[1,16,64,128]{3,2,1,0:T(8,128)(2,1)S(1)} %get-tuple-element.36), channel_id=1, source_target_pairs={{0,1},{1,2},{2,3},{3,4},{4,5},{5,6},{6,7},{8,9},{9,10},{10,11},{11... | collective-permute-start | bytes 786440 | tf_op jit(solution)/shard_map/ppermute | solution.py:31
  29.2 7.7 %collective-permute-start.3 = (bf16[1,16,64,128]{3,2,1,0:T(8,128)(2,1)S(1)}, bf16[1,16,64,128]{3,2,1,0:T(8,128)(2,1)S(1)}, u32[]{:S(2)}, u32[]{:S(2)}) collective-permute-start(bf16[1,16,64,128]{3,2,1,0:T(8,128)(2,1)S(1)} %get-tuple-element.37), channel_id=1, source_target_pairs={{1,0},{2,1},{3,2},{4,3},{5,4},{6,5},{7,6},{9,8},{10,9},{11,10},{12... | collective-permute-start | bytes 786440 | tf_op jit(solution)/shard_map/ppermute | solution.py:31
  37.6 7.1 %copy-start = (bf16[2,16,64,128]{3,2,1,0:T(8,128)(2,1)S(1)}, bf16[2,16,64,128]{3,2,1,0:T(8,128)(2,1)}, u32[]{:S(2)}) copy-start(bf16[2,16,64,128]{3,2,1,0:T(8,128)(2,1)} %param.20) | copy-start | bytes 1572868
  37.6 1.5 copy-start.47
  39.1 12.1 %copy-start.5 = (bf16[2,16,64,128]{3,2,1,0:T(8,128)(2,1)}, bf16[2,16,64,128]{3,2,1,0:T(8,128)(2,1)S(1)}, u32[]{:S(2)}) copy-start(bf16[2,16,64,128]{3,2,1,0:T(8,128)(2,1)S(1)} %get-tuple-element.57) | copy-start | bytes 1572868
  39.1 6.7 %collective-permute-start.4 = (bf16[2,1,64,128]{3,2,1,0:T(8,128)(2,1)S(1)}, bf16[2,1,64,128]{3,2,1,0:T(8,128)(2,1)S(1)}, u32[]{:S(2)}, u32[]{:S(2)}) collective-permute-start(bf16[2,1,64,128]{3,2,1,0:T(8,128)(2,1)S(1)} %get-tuple-element.34), channel_id=1, source_target_pairs={{0,8},{8,16},{16,24},{24,32},{32,40},{40,48},{48,56},{56,64},{64,7... | collective-permute-start | bytes 98312 | tf_op jit(solution)/shard_map/ppermute | solution.py:19
  43.3 4.7 %collective-permute-start.5 = (bf16[2,1,64,128]{3,2,1,0:T(8,128)(2,1)S(1)}, bf16[2,1,64,128]{3,2,1,0:T(8,128)(2,1)S(1)}, u32[]{:S(2)}, u32[]{:S(2)}) collective-permute-start(bf16[2,1,64,128]{3,2,1,0:T(8,128)(2,1)S(1)} %get-tuple-element.35), channel_id=1, source_target_pairs={{8,0},{16,8},{24,16},{32,24},{40,32},{48,40},{56,48},{64,56},{72,6... | collective-permute-start | bytes 98312 | tf_op jit(solution)/shard_map/ppermute | solution.py:21
  44.7 4.0 %copy-start.23 = (bf16[3,3,64,64]{3,2,1,0:T(8,128)(2,1)S(1)}, bf16[3,3,64,64]{3,2,1,0:T(8,128)(2,1)}, u32[]{:S(2)}) copy-start(bf16[3,3,64,64]{3,2,1,0:T(8,128)(2,1)} %param.15) | copy-start | bytes 221188
  45.7 3.3 %copy-start.32 = (bf16[2,1,64,128]{3,2,1,0:T(8,128)(2,1)}, bf16[2,1,64,128]{3,2,1,0:T(8,128)(2,1)S(1)}, u32[]{:S(2)}) copy-start(bf16[2,1,64,128]{3,2,1,0:T(8,128)(2,1)S(1)} %collective-permute-done.4) | copy-start | bytes 98308
  48.0 3.2 %copy-start.41 = (bf16[2,1,64,128]{3,2,1,0:T(8,128)(2,1)}, bf16[2,1,64,128]{3,2,1,0:T(8,128)(2,1)S(1)}, u32[]{:S(2)}) copy-start(bf16[2,1,64,128]{3,2,1,0:T(8,128)(2,1)S(1)} %collective-permute-done.5) | copy-start | bytes 98308
  51.2 2.9 %copy-start.45 = (s32[4]{0:T(128)S(1)}, s32[4]{0:T(128)}, u32[]{:S(2)}) copy-start(s32[4]{0:T(128)} %get-tuple-element.53) | copy-start | bytes 52
  52.8 15.9 %collective-permute-start.7 = (bf16[2,16,64,128]{3,2,1,0:T(8,128)(2,1)}, bf16[2,16,64,128]{3,2,1,0:T(8,128)(2,1)S(1)}, u32[]{:S(2)}, u32[]{:S(2)}) collective-permute-start(bf16[2,16,64,128]{3,2,1,0:T(8,128)(2,1)} %get-tuple-element.59), channel_id=1, source_target_pairs={{2,0},{3,1},{4,2},{5,3},{6,4},{7,5},{10,8},{11,9},{12,10},{13,11},... | collective-permute-start | bytes 1572872 | tf_op jit(solution)/shard_map/ppermute | solution.py:31
  55.2 13.6 %copy-start.34 = (bf16[3,64,64]{2,1,0:T(8,128)(2,1)S(1)}, bf16[3,64,64]{2,1,0:T(8,128)(2,1)}, u32[]{:S(2)}) copy-start(bf16[3,64,64]{2,1,0:T(8,128)(2,1)} %param.16) | copy-start | bytes 73732
  57.7 15.6 %collective-permute-start.6 = (bf16[2,16,64,128]{3,2,1,0:T(8,128)(2,1)}, bf16[2,16,64,128]{3,2,1,0:T(8,128)(2,1)S(1)}, u32[]{:S(2)}, u32[]{:S(2)}) collective-permute-start(bf16[2,16,64,128]{3,2,1,0:T(8,128)(2,1)} %get-tuple-element.59), channel_id=1, source_target_pairs={{0,2},{1,3},{2,4},{3,5},{4,6},{5,7},{8,10},{9,11},{10,12},{11,13},... | collective-permute-start | bytes 1572872 | tf_op jit(solution)/shard_map/ppermute | solution.py:31
  74.9 11.3 %copy-start.1 = (bf16[2,16,64,128]{3,2,1,0:T(8,128)(2,1)}, bf16[2,16,64,128]{3,2,1,0:T(8,128)(2,1)S(1)}, u32[]{:S(2)}) copy-start(bf16[2,16,64,128]{3,2,1,0:T(8,128)(2,1)S(1)} %get-tuple-element.61) | copy-start | bytes 1572868
  74.9 1.3 copy-start.20
  74.9 8.2 %copy-start.19 = (bf16[2,1,4,64,128]{4,2,3,0,1:T(4,128)(2,1)S(1)}, bf16[2,1,4,64,128]{4,2,3,0,1:T(4,128)(2,1)}, u32[]{:S(2)}) copy-start(bf16[2,1,4,64,128]{4,2,3,0,1:T(4,128)(2,1)} %fusion.32) | copy-start | bytes 393220
  75.4 9.3 %copy-start.21 = (bf16[2,1,4,64,128]{4,2,3,0,1:T(4,128)(2,1)S(1)}, bf16[2,1,4,64,128]{4,2,3,0,1:T(4,128)(2,1)}, u32[]{:S(2)}) copy-start(bf16[2,1,4,64,128]{4,2,3,0,1:T(4,128)(2,1)} %fusion.30) | copy-start | bytes 393220
  76.2 10.4 %copy-start.22 = (bf16[2,1,4,64,128]{4,2,3,0,1:T(4,128)(2,1)S(1)}, bf16[2,1,4,64,128]{4,2,3,0,1:T(4,128)(2,1)}, u32[]{:S(2)}) copy-start(bf16[2,1,4,64,128]{4,2,3,0,1:T(4,128)(2,1)} %fusion.28) | copy-start | bytes 393220
  76.4 15.7 %collective-permute-start.8 = (bf16[2,2,4,64,128]{4,2,3,0,1:T(4,128)(2,1)S(1)}, bf16[2,2,4,64,128]{4,2,3,0,1:T(4,128)(2,1)S(1)}, u32[]{:S(2)}, u32[]{:S(2)}) collective-permute-start(bf16[2,2,4,64,128]{4,2,3,0,1:T(4,128)(2,1)S(1)} %pad_maximum_fusion.21), channel_id=1, source_target_pairs={{0,16},{8,24},{16,32},{24,40},{32,48},{40,56},{48,64},{56,72},{64,... | collective-permute-start | bytes 786440 | tf_op jit(solution)/shard_map/ppermute | solution.py:31
  83.4 10.5 %collective-permute-start.11 = (bf16[2,2,4,64,128]{4,2,3,0,1:T(4,128)(2,1)S(1)}, bf16[2,2,4,64,128]{4,2,3,0,1:T(4,128)(2,1)S(1)}, u32[]{:S(2)}, u32[]{:S(2)}) collective-permute-start(bf16[2,2,4,64,128]{4,2,3,0,1:T(4,128)(2,1)S(1)} %pad_maximum_fusion.24), channel_id=1, source_target_pairs={{16,0},{24,8},{32,16},{40,24},{48,32},{56,40},{64,48},{72,56},{80,... | collective-permute-start | bytes 786440 | tf_op jit(solution)/shard_map/ppermute | solution.py:31
  84.9 18.4 %collective-permute-start.10 = (bf16[2,2,4,64,128]{4,2,3,0,1:T(4,128)(2,1)S(1)}, bf16[2,2,4,64,128]{4,2,3,0,1:T(4,128)(2,1)S(1)}, u32[]{:S(2)}, u32[]{:S(2)}) collective-permute-start(bf16[2,2,4,64,128]{4,2,3,0,1:T(4,128)(2,1)S(1)} %pad_maximum_fusion.23), channel_id=1, source_target_pairs={{8,0},{16,8},{24,16},{32,24},{40,32},{48,40},{56,48},{64,56},{72,6... | collective-permute-start | bytes 786440 | tf_op jit(solution)/shard_map/ppermute | solution.py:31
  86.8 18.0 %copy-start.44 = (s32[4,4]{1,0:T(4,128)S(1)}, s32[4,4]{1,0:T(4,128)}, u32[]{:S(2)}) copy-start(s32[4,4]{1,0:T(4,128)} %broadcast_select_fusion) | copy-start | bytes 196
  86.8 18.0 %copy-start.46 = (pred[4,4]{1,0:T(4,128)(4,1)S(1)}, pred[4,4]{1,0:T(4,128)(4,1)}, u32[]{:S(2)}) copy-start(pred[4,4]{1,0:T(4,128)(4,1)} %select_and_fusion) | copy-start | bytes 52
  86.8 17.2 %collective-permute-start.9 = (bf16[2,2,4,64,128]{4,2,3,0,1:T(4,128)(2,1)S(1)}, bf16[2,2,4,64,128]{4,2,3,0,1:T(4,128)(2,1)S(1)}, u32[]{:S(2)}, u32[]{:S(2)}) collective-permute-start(bf16[2,2,4,64,128]{4,2,3,0,1:T(4,128)(2,1)S(1)} %pad_maximum_fusion.22), channel_id=1, source_target_pairs={{0,8},{8,16},{16,24},{24,32},{32,40},{40,48},{48,56},{56,64},{64,7... | collective-permute-start | bytes 786440 | tf_op jit(solution)/shard_map/ppermute | solution.py:31
  105.3 8.4 %copy-start.12 = (bf16[2,16,64,128]{3,2,1,0:T(8,128)(2,1)S(1)}, bf16[2,16,64,128]{3,2,1,0:T(8,128)(2,1)}, u32[]{:S(2)}) copy-start(bf16[2,16,64,128]{3,2,1,0:T(8,128)(2,1)} %copy-done.11) | copy-start | bytes 1572868
  107.6 13.7 %collective-permute-start.13 = (bf16[2,16,64,128]{3,2,1,0:T(8,128)(2,1)S(1)}, bf16[2,16,64,128]{3,2,1,0:T(8,128)(2,1)}, u32[]{:S(2)}, u32[]{:S(2)}) collective-permute-start(bf16[2,16,64,128]{3,2,1,0:T(8,128)(2,1)S(1)} %fusion.33), channel_id=1, source_target_pairs={{0,2},{1,3},{2,4},{3,5},{4,6},{5,7},{8,10},{9,11},{10,12},{11,13},... | collective-permute-start | bytes 1572872 | tf_op jit(solution)/shard_map/ppermute | solution.py:31
  112.4 13.6 %collective-permute-start.12 = (bf16[2,16,64,128]{3,2,1,0:T(8,128)(2,1)S(1)}, bf16[2,16,64,128]{3,2,1,0:T(8,128)(2,1)}, u32[]{:S(2)}, u32[]{:S(2)}) collective-permute-start(bf16[2,16,64,128]{3,2,1,0:T(8,128)(2,1)S(1)} %fusion.33), channel_id=1, source_target_pairs={{2,0},{3,1},{4,2},{5,3},{6,4},{7,5},{10,8},{11,9},{12,10},{13,11},... | collective-permute-start | bytes 1572872 | tf_op jit(solution)/shard_map/ppermute | solution.py:31
  116.5 1.5 copy-start.2
  119.3 6.7 %copy-start.49 = (f32[2,16,64,128]{3,2,1,0:T(8,128)S(1)}, f32[2,16,64,128]{3,2,1,0:T(8,128)}, u32[]{:S(2)}) copy-start(f32[2,16,64,128]{3,2,1,0:T(8,128)} %get-tuple-element.60) | copy-start | bytes 3145732
  119.6 6.4 %copy-start.14 = (f32[2,64,128,16]{2,3,1,0:T(8,128)S(1)}, f32[2,64,128,16]{2,3,1,0:T(8,128)}, u32[]{:S(2)}) copy-start(f32[2,64,128,16]{2,3,1,0:T(8,128)} %copy-done.13) | copy-start | bytes 3145732
  126.0 2.0 copy-start.6
  128.0 6.9 %copy-start.7 = (bf16[2,16,64,128]{3,2,1,0:T(8,128)(2,1)}, bf16[2,16,64,128]{3,2,1,0:T(8,128)(2,1)S(1)}, u32[]{:S(2)}) copy-start(bf16[2,16,64,128]{3,2,1,0:T(8,128)(2,1)S(1)} %get-tuple-element.63) | copy-start | bytes 1572868
  129.7 4.9 %copy-start.42 = (bf16[2,1,64,128]{3,2,1,0:T(8,128)(2,1)S(1)}, bf16[2,1,64,128]{3,2,1,0:T(8,128)(2,1)}, u32[]{:S(2)}) copy-start(bf16[2,1,64,128]{3,2,1,0:T(8,128)(2,1)} %copy-done.41) | copy-start | bytes 98308
  130.3 4.5 %copy-start.33 = (bf16[2,1,64,128]{3,2,1,0:T(8,128)(2,1)S(1)}, bf16[2,1,64,128]{3,2,1,0:T(8,128)(2,1)}, u32[]{:S(2)}) copy-start(bf16[2,1,64,128]{3,2,1,0:T(8,128)(2,1)} %copy-done.32) | copy-start | bytes 98308
  130.4 5.0 %collective-permute-start.14 = (bf16[2,1,64,128]{3,2,1,0:T(8,128)(2,1)S(1)}, bf16[2,1,64,128]{3,2,1,0:T(8,128)(2,1)S(1)}, u32[]{:S(2)}, u32[]{:S(2)}) collective-permute-start(bf16[2,1,64,128]{3,2,1,0:T(8,128)(2,1)S(1)} %get-tuple-element.32), channel_id=1, source_target_pairs={{0,8},{8,16},{16,24},{24,32},{32,40},{40,48},{48,56},{56,64},{64,7... | collective-permute-start | bytes 98312 | tf_op jit(solution)/shard_map/ppermute | solution.py:19
  133.0 4.7 %collective-permute-start.15 = (bf16[2,1,64,128]{3,2,1,0:T(8,128)(2,1)S(1)}, bf16[2,1,64,128]{3,2,1,0:T(8,128)(2,1)S(1)}, u32[]{:S(2)}, u32[]{:S(2)}) collective-permute-start(bf16[2,1,64,128]{3,2,1,0:T(8,128)(2,1)S(1)} %get-tuple-element.33), channel_id=1, source_target_pairs={{8,0},{16,8},{24,16},{32,24},{40,32},{48,40},{56,48},{64,56},{72,6... | collective-permute-start | bytes 98312 | tf_op jit(solution)/shard_map/ppermute | solution.py:21
  135.2 2.5 %copy-start.8 = (bf16[2,16,64,128]{3,2,1,0:T(8,128)(2,1)S(1)}, bf16[2,16,64,128]{3,2,1,0:T(8,128)(2,1)}, u32[]{:S(2)}) copy-start(bf16[2,16,64,128]{3,2,1,0:T(8,128)(2,1)} %copy-done.7) | copy-start | bytes 1572868
  135.2 3.1 %copy-start.24 = (bf16[3,3,64,64]{3,2,1,0:T(8,128)(2,1)S(1)}, bf16[3,3,64,64]{3,2,1,0:T(8,128)(2,1)}, u32[]{:S(2)}) copy-start(bf16[3,3,64,64]{3,2,1,0:T(8,128)(2,1)} %param.15) | copy-start | bytes 221188
  142.1 1.5 copy-start.10
  143.9 8.2 %copy-start.28 = (bf16[1,16,64,128]{3,2,1,0:T(8,128)(2,1)S(1)}, bf16[1,16,64,128]{3,2,1,0:T(8,128)(2,1)}, u32[]{:S(2)}) copy-start(bf16[1,16,64,128]{3,2,1,0:T(8,128)(2,1)} %copy-done.27) | copy-start | bytes 786436
  143.9 8.2 %copy-start.48 = (bf16[1,16,64,128]{3,2,1,0:T(8,128)(2,1)S(1)}, bf16[1,16,64,128]{3,2,1,0:T(8,128)(2,1)}, u32[]{:S(2)}) copy-start(bf16[1,16,64,128]{3,2,1,0:T(8,128)(2,1)} %copy-done.47) | copy-start | bytes 786436
  144.6 7.7 %copy-start.16 = (bf16[1,16,64,128]{3,2,1,0:T(8,128)(2,1)S(1)}, bf16[1,16,64,128]{3,2,1,0:T(8,128)(2,1)}, u32[]{:S(2)}) copy-start(bf16[1,16,64,128]{3,2,1,0:T(8,128)(2,1)} %copy-done.15) | copy-start | bytes 786436
  144.6 7.8 %copy-start.26 = (bf16[1,16,64,128]{3,2,1,0:T(8,128)(2,1)S(1)}, bf16[1,16,64,128]{3,2,1,0:T(8,128)(2,1)}, u32[]{:S(2)}) copy-start(bf16[1,16,64,128]{3,2,1,0:T(8,128)(2,1)} %copy-done.25) | copy-start | bytes 786436
  145.0 8.8 %collective-permute-start.17 = (bf16[1,16,64,128]{3,2,1,0:T(8,128)(2,1)}, bf16[1,16,64,128]{3,2,1,0:T(8,128)(2,1)S(1)}, u32[]{:S(2)}, u32[]{:S(2)}) collective-permute-start(bf16[1,16,64,128]{3,2,1,0:T(8,128)(2,1)} %get-tuple-element.30), channel_id=1, source_target_pairs={{0,1},{1,2},{2,3},{3,4},{4,5},{5,6},{6,7},{8,9},{9,10},{10,11},{11... | collective-permute-start | bytes 786440 | tf_op jit(solution)/shard_map/ppermute | solution.py:31
  150.1 7.8 %collective-permute-start.16 = (bf16[1,16,64,128]{3,2,1,0:T(8,128)(2,1)S(1)}, bf16[1,16,64,128]{3,2,1,0:T(8,128)(2,1)}, u32[]{:S(2)}, u32[]{:S(2)}) collective-permute-start(bf16[1,16,64,128]{3,2,1,0:T(8,128)(2,1)S(1)} %get-tuple-element.31), channel_id=1, source_target_pairs={{1,0},{2,1},{3,2},{4,3},{5,4},{6,5},{7,6},{9,8},{10,9},{11,10},{12... | collective-permute-start | bytes 786440 | tf_op jit(solution)/shard_map/ppermute | solution.py:31
  152.8 5.1 %copy-start.50 = (f32[2,16,64,128]{3,2,1,0:T(8,128)S(1)}, f32[2,16,64,128]{3,2,1,0:T(8,128)}, u32[]{:S(2)}) copy-start(f32[2,16,64,128]{3,2,1,0:T(8,128)} %get-tuple-element.56) | copy-start | bytes 3145732
  152.8 5.1 %copy-start.52 = (bf16[2,16,64,128]{3,2,1,0:T(8,128)(2,1)S(1)}, bf16[2,16,64,128]{3,2,1,0:T(8,128)(2,1)}, u32[]{:S(2)}) copy-start(bf16[2,16,64,128]{3,2,1,0:T(8,128)(2,1)} %get-tuple-element.66) | copy-start | bytes 1572868
  163.9 1.8 copy-start.29
  164.3 27.2 %collective-permute-start.19 = (bf16[2,1,64,128]{3,2,1,0:T(8,128)(2,1)S(1)}, bf16[2,1,64,128]{3,2,1,0:T(8,128)(2,1)S(1)}, u32[]{:S(2)}, u32[]{:S(2)}) collective-permute-start(bf16[2,1,64,128]{3,2,1,0:T(8,128)(2,1)S(1)} %get-tuple-element.29), channel_id=1, source_target_pairs={{8,0},{16,8},{24,16},{32,24},{40,32},{48,40},{56,48},{64,56},{72,6... | collective-permute-start | bytes 98312 | tf_op jit(solution)/shard_map/ppermute | solution.py:21
  166.4 39.7 %all-to-all-start = ((f32[256,1,384]{2,1,0:T(1,128)}), f32[256,1,384]{2,1,0:T(1,128)S(1)}, u32[]{:S(2)}, u32[]{:S(2)}) async-start(f32[256,1,384]{2,1,0:T(1,128)} %bitcast.244), calls=%async_computation | async-start | bytes 786432 | tf_op jit(solution)/shard_map/all_to_all | solution.py:241
  188.0 4.3 %collective-permute-start.18 = (bf16[2,1,64,128]{3,2,1,0:T(8,128)(2,1)S(1)}, bf16[2,1,64,128]{3,2,1,0:T(8,128)(2,1)S(1)}, u32[]{:S(2)}, u32[]{:S(2)}) collective-permute-start(bf16[2,1,64,128]{3,2,1,0:T(8,128)(2,1)S(1)} %get-tuple-element.28), channel_id=1, source_target_pairs={{0,8},{8,16},{16,24},{24,32},{32,40},{40,48},{48,56},{56,64},{64,7... | collective-permute-start | bytes 98312 | tf_op jit(solution)/shard_map/ppermute | solution.py:19
  207.4 23.9 %all-to-all-start.1 = ((f32[256,1,384]{2,1,0:T(1,128)}), f32[256,1,384]{2,1,0:T(1,128)S(1)}, u32[]{:S(2)}, u32[]{:S(2)}) async-start(f32[256,1,384]{2,1,0:T(1,128)} %broadcast_in_dim.56), calls=%async_computation.1 | async-start | bytes 786432 | tf_op jit(solution)/shard_map/all_to_all | solution.py:243
  (11 other events, 10.6 us)

commit v6 on v5

--- a/solution.py
+++ b/solution.py
@@ -232,8 +232,8 @@
     )
 
 
-def exchange_sum(parts, axes):
-    flat = jnp.concatenate([part.reshape(-1) for part in parts])
+def exchange_sum(parts, axes, scale):
+    flat = jnp.concatenate([part.reshape(-1) for part in parts]) * scale
     size = 1
     for axis in axes:
         size *= lax.axis_size(axis)
@@ -317,18 +317,20 @@
     grad_features, grad_sa = spatial_backward(
         first_gradient, pre_one, padded_zero, spatial_a, chart_rim
     )
-    summed_sa, summed_ta, summed_sb, summed_tb = exchange_sum(
-        (grad_sa, gradient_kernel_first, grad_sb, gradient_kernel_second), ("frame", "chart")
-    )
     pixel_frames = total_frames * strips * lax.axis_size("chart") * features.shape[3]
     grad_scale = float(pixel_frames) ** (-0.5)
+    summed_sa, summed_ta, summed_sb, summed_tb = exchange_sum(
+        (grad_sa, gradient_kernel_first, grad_sb, gradient_kernel_second),
+        ("frame", "chart"),
+        grad_scale,
+    )
     return (
         blended,
         grad_features,
-        summed_sa * grad_scale,
-        summed_ta * grad_scale,
-        summed_sb * grad_scale,
-        summed_tb * grad_scale,
+        summed_sa,
+        summed_ta,
+        summed_sb,
+        summed_tb,
     )
 
 

time: 237 us -> 237 us (level)
    reshape x4 -> x8, local copies, waits for them, and re-layouts: 1.87 us -> 4.96 us  [the longest x4 3.09 us: exchange_sum(): results.append(flat[start:start + part.size].reshape(part.shape))]
    mul x4 -> x0, local copies, waits for them, and re-layouts: 3.09 us -> none  [the longest x1 0.82 us: shards(): summed_sb * grad_scale]
where the time goes in v6:
time: 237 us; the launch traced here: 235 us
  starting transfers between devices  87.2 us (37%)
  waiting for transfers between devices  65.2 us (28%)
  matrix products  48.4 us (20%)
  local copies, waits for them, and re-layouts  18.9 us (8%)
  other arithmetic  13.6 us (6%)
    ppermute x12, starting transfers between devices, from_behind(): return lax.ppermute(array, axis, pairs)  39.1 us
    ppermute x12, waiting for transfers between devices, from_behind(): return lax.ppermute(array, axis, pairs)  34.2 us
    all_to_all x1, starting transfers between devices, exchange_sum(): flat = jnp.sum(lax.all_to_all(pieces, axes, 0, 0, tiled=True), axis=0)  21.6 us
    all_to_all x1, waiting for transfers between devices, exchange_sum(): flat = lax.all_to_all(copies, axes, 0, 0, tiled=True).reshape(-1)  14.6 us
    ppermute x4, starting transfers between devices, with_halo(): lax.ppermute(tail, axis, [(i, (i + 1) % count) for i in range(ends)])  14.4 us
    all_to_all x1, waiting for transfers between devices, exchange_sum(): flat = jnp.sum(lax.all_to_all(pieces, axes, 0, 0, tiled=True), axis=0)  11.4 us
    dot_general x18, matrix products, spatial_transpose(): jnp.einsum('oc,fsop->fscp', weight[row_tap, col_tap], padded[:, 2 - row_t...  8.45 us
    dot_general x18, matrix products, spatial_apply(): jnp.einsum('oc,fscp->fsop', weight[row_tap, col_tap], padded[:, row_tap:r...  8.04 us
  transfers between devices with their start and end apart: 22, of which 14 were waited for; matrix products, arithmetic and copies ran while one was open for 16% of the time, Pallas kernels for 0%

profile of v6, /device:TPU:1, one launch (start us, length us, event | category | flops | bytes accessed | tf_op | source)
XLA Modules:
  0.0 235.3 jit_solution(7820356444705237596)
XLA Ops:
  0.6 0.8 fusion.284
  1.5 4.0 %collective-permute-start = (bf16[2,1,64,128]{3,2,1,0:T(8,128)(2,1)S(1)}, bf16[2,1,64,128]{3,2,1,0:T(8,128)(2,1)S(1)}, u32[]{:S(2)}, u32[]{:S(2)}) collective-permute-start(bf16[2,1,64,128]{3,2,1,0:T(8,128)(2,1)S(1)} %get-tuple-element.38), channel_id=1, source_target_pairs={{0,8},{8,16},{16,24},{24,32},{32,40},{40,48},{48,56},{56,64},{64,7... | collective-permute-start | bytes 98312 | tf_op jit(solution)/shard_map/ppermute | solution.py:19
  5.5 1.3 collective-permute-start.1
  7.5 0.9 dynamic-slice_reduce_fusion.2
  9.8 0.9 convert_reduce_fusion
  11.4 0.9 dynamic-slice_reduce_fusion
  16.2 2.1 fusion.26
  18.3 2.1 fusion.32
  23.7 1.5 add_convert_fusion.3
  25.2 4.0 %collective-permute-start.2 = (bf16[1,16,64,128]{3,2,1,0:T(8,128)(2,1)S(1)}, bf16[1,16,64,128]{3,2,1,0:T(8,128)(2,1)S(1)}, u32[]{:S(2)}, u32[]{:S(2)}) collective-permute-start(bf16[1,16,64,128]{3,2,1,0:T(8,128)(2,1)S(1)} %get-tuple-element.36), channel_id=1, source_target_pairs={{0,1},{1,2},{2,3},{3,4},{4,5},{5,6},{6,7},{8,9},{9,10},{10,11},{11... | collective-permute-start | bytes 786440 | tf_op jit(solution)/shard_map/ppermute | solution.py:31
  29.2 1.9 collective-permute-start.3
  31.4 5.5 %collective-permute-done.3 = bf16[1,16,64,128]{3,2,1,0:T(8,128)(2,1)S(1)} collective-permute-done((bf16[1,16,64,128]{3,2,1,0:T(8,128)(2,1)S(1)}, bf16[1,16,64,128]{3,2,1,0:T(8,128)(2,1)S(1)}, u32[]{:S(2)}, u32[]{:S(2)}) %collective-permute-start.3) | collective-permute-done | bytes 262176 | tf_op jit(solution)/shard_map/ppermute | solution.py:31
  37.6 1.5 add_convert_fusion.2
  39.1 4.3 %collective-permute-start.4 = (bf16[2,1,64,128]{3,2,1,0:T(8,128)(2,1)S(1)}, bf16[2,1,64,128]{3,2,1,0:T(8,128)(2,1)S(1)}, u32[]{:S(2)}, u32[]{:S(2)}) collective-permute-start(bf16[2,1,64,128]{3,2,1,0:T(8,128)(2,1)S(1)} %get-tuple-element.34), channel_id=1, source_target_pairs={{0,8},{8,16},{16,24},{24,32},{32,40},{40,48},{48,56},{56,64},{64,7... | collective-permute-start | bytes 98312 | tf_op jit(solution)/shard_map/ppermute | solution.py:19
  43.3 1.3 collective-permute-start.5
  44.7 1.1 fusion.30
  45.7 2.3 collective-permute-done.5
  51.2 1.6 add_convert_fusion.1
  52.8 1.3 collective-permute-start.7
  54.1 1.0 fusion.28
  55.2 1.0 select_reduce_fusion.5
  56.2 1.5 fusion.226
  57.7 4.2 %collective-permute-start.6 = (bf16[2,16,64,128]{3,2,1,0:T(8,128)(2,1)}, bf16[2,16,64,128]{3,2,1,0:T(8,128)(2,1)S(1)}, u32[]{:S(2)}, u32[]{:S(2)}) collective-permute-start(bf16[2,16,64,128]{3,2,1,0:T(8,128)(2,1)} %get-tuple-element.59), channel_id=1, source_target_pairs={{0,2},{1,3},{2,4},{3,5},{4,6},{5,7},{8,10},{9,11},{10,12},{11,13},... | collective-permute-start | bytes 1572872 | tf_op jit(solution)/shard_map/ppermute | solution.py:31
  61.9 1.3 fusion.131
  63.2 5.5 %collective-permute-done.7 = bf16[2,16,64,128]{3,2,1,0:T(8,128)(2,1)S(1)} collective-permute-done((bf16[2,16,64,128]{3,2,1,0:T(8,128)(2,1)}, bf16[2,16,64,128]{3,2,1,0:T(8,128)(2,1)S(1)}, u32[]{:S(2)}, u32[]{:S(2)}) %collective-permute-start.7) | collective-permute-done | bytes 524320 | tf_op jit(solution)/shard_map/ppermute | solution.py:31
  69.6 3.8 %collective-permute-done.6 = bf16[2,16,64,128]{3,2,1,0:T(8,128)(2,1)S(1)} collective-permute-done((bf16[2,16,64,128]{3,2,1,0:T(8,128)(2,1)}, bf16[2,16,64,128]{3,2,1,0:T(8,128)(2,1)S(1)}, u32[]{:S(2)}, u32[]{:S(2)}) %collective-permute-start.6) | collective-permute-done | bytes 524320 | tf_op jit(solution)/shard_map/ppermute | solution.py:31
  73.4 1.6 add_convert_fusion
  76.4 6.8 %collective-permute-start.8 = (bf16[2,2,4,64,128]{4,2,3,0,1:T(4,128)(2,1)S(1)}, bf16[2,2,4,64,128]{4,2,3,0,1:T(4,128)(2,1)S(1)}, u32[]{:S(2)}, u32[]{:S(2)}) collective-permute-start(bf16[2,2,4,64,128]{4,2,3,0,1:T(4,128)(2,1)S(1)} %pad_maximum_fusion.20), channel_id=1, source_target_pairs={{0,16},{8,24},{16,32},{24,40},{32,48},{40,56},{48,64},{56,72},{64,... | collective-permute-start | bytes 786440 | tf_op jit(solution)/shard_map/ppermute | solution.py:31
  83.4 1.3 collective-permute-start.11
  84.9 1.3 collective-permute-start.10
  86.8 5.2 %collective-permute-start.9 = (bf16[2,2,4,64,128]{4,2,3,0,1:T(4,128)(2,1)S(1)}, bf16[2,2,4,64,128]{4,2,3,0,1:T(4,128)(2,1)S(1)}, u32[]{:S(2)}, u32[]{:S(2)}) collective-permute-start(bf16[2,2,4,64,128]{4,2,3,0,1:T(4,128)(2,1)S(1)} %pad_maximum_fusion.21), channel_id=1, source_target_pairs={{0,8},{8,16},{16,24},{24,32},{32,40},{40,48},{48,56},{56,64},{64,7... | collective-permute-start | bytes 786440 | tf_op jit(solution)/shard_map/ppermute | solution.py:31
  92.8 1.0 collective-permute-done.11
  94.6 8.7 %collective-permute-done.10 = bf16[2,2,4,64,128]{4,2,3,0,1:T(4,128)(2,1)S(1)} collective-permute-done((bf16[2,2,4,64,128]{4,2,3,0,1:T(4,128)(2,1)S(1)}, bf16[2,2,4,64,128]{4,2,3,0,1:T(4,128)(2,1)S(1)}, u32[]{:S(2)}, u32[]{:S(2)}) %collective-permute-start.10) | collective-permute-done | bytes 262176 | tf_op jit(solution)/shard_map/ppermute | solution.py:31
  106.3 1.3 convolution_bitcast_fusion.9
  107.6 4.8 %collective-permute-start.13 = (bf16[2,16,64,128]{3,2,1,0:T(8,128)(2,1)S(1)}, bf16[2,16,64,128]{3,2,1,0:T(8,128)(2,1)}, u32[]{:S(2)}, u32[]{:S(2)}) collective-permute-start(bf16[2,16,64,128]{3,2,1,0:T(8,128)(2,1)S(1)} %fusion.33), channel_id=1, source_target_pairs={{0,2},{1,3},{2,4},{3,5},{4,6},{5,7},{8,10},{9,11},{10,12},{11,13},... | collective-permute-start | bytes 1572872 | tf_op jit(solution)/shard_map/ppermute | solution.py:31
  112.4 1.3 collective-permute-start.12
  114.9 1.6 reshape.300
  116.5 1.5 convolution_bitcast_fusion.7
  118.1 1.2 fusion.38
  119.6 1.6 collective-permute-done.13
  121.2 1.4 convolution_bitcast_fusion.3
  122.6 3.3 %collective-permute-done.12 = bf16[2,16,64,128]{3,2,1,0:T(8,128)(2,1)} collective-permute-done((bf16[2,16,64,128]{3,2,1,0:T(8,128)(2,1)S(1)}, bf16[2,16,64,128]{3,2,1,0:T(8,128)(2,1)}, u32[]{:S(2)}, u32[]{:S(2)}) %collective-permute-start.12) | collective-permute-done | bytes 524320 | tf_op jit(solution)/shard_map/ppermute | solution.py:31
  126.0 2.0 fusion.34
  130.4 2.6 %collective-permute-start.14 = (bf16[2,1,64,128]{3,2,1,0:T(8,128)(2,1)S(1)}, bf16[2,1,64,128]{3,2,1,0:T(8,128)(2,1)S(1)}, u32[]{:S(2)}, u32[]{:S(2)}) collective-permute-start(bf16[2,1,64,128]{3,2,1,0:T(8,128)(2,1)S(1)} %get-tuple-element.32), channel_id=1, source_target_pairs={{0,8},{8,16},{16,24},{24,32},{32,40},{40,48},{48,56},{56,64},{64,7... | collective-permute-start | bytes 98312 | tf_op jit(solution)/shard_map/ppermute | solution.py:19
  133.0 1.5 collective-permute-start.15
  135.4 2.3 collective-permute-done.15
  141.3 0.8 copy-done.51
  142.1 1.5 fusion.35
  145.0 5.1 %collective-permute-start.17 = (bf16[1,16,64,128]{3,2,1,0:T(8,128)(2,1)}, bf16[1,16,64,128]{3,2,1,0:T(8,128)(2,1)S(1)}, u32[]{:S(2)}, u32[]{:S(2)}) collective-permute-start(bf16[1,16,64,128]{3,2,1,0:T(8,128)(2,1)} %get-tuple-element.30), channel_id=1, source_target_pairs={{0,1},{1,2},{2,3},{3,4},{4,5},{5,6},{6,7},{8,9},{9,10},{10,11},{11... | collective-permute-start | bytes 786440 | tf_op jit(solution)/shard_map/ppermute | solution.py:31
  150.1 1.9 collective-permute-start.16
  152.8 0.9 collective-permute-done.17
  154.1 3.8 %collective-permute-done.16 = bf16[1,16,64,128]{3,2,1,0:T(8,128)(2,1)} collective-permute-done((bf16[1,16,64,128]{3,2,1,0:T(8,128)(2,1)S(1)}, bf16[1,16,64,128]{3,2,1,0:T(8,128)(2,1)}, u32[]{:S(2)}, u32[]{:S(2)}) %collective-permute-start.16) | collective-permute-done | bytes 262176 | tf_op jit(solution)/shard_map/ppermute | solution.py:31
  157.9 2.5 %fusion.36 = (bf16[2,16,64,128]{3,2,1,0:T(8,128)(2,1)S(1)}, bf16[2,16,64,128]{3,2,1,0:T(8,128)(2,1)}) fusion(f32[2,16,64,128]{3,2,1,0:T(8,128)S(1)} %copy-done.50, f32[2,16,64,128]{3,2,1,0:T(8,128)S(1)} %convolution_bitcast_fusion, f32[2,16,64,128]{3,2,1,0:T(8,128)S(1)} %convolution_bitcast_fusion.1, bf16[3,64,64]{2,1,0:T(8,128)(2,1)S(1)} %copy-done.37, ...), kind=kOutput, calls=%fused_computation.122 | convolution fusion | flops 37748736 | bytes 5259264 | tf_op jit(solution)/shard_map/oc,fsop->fscp/dot_general | solution.py:166
  164.3 1.3 collective-permute-start.19
  165.6 0.8 maximum_multiply_fusion
  166.4 21.6 %all-to-all-start = ((f32[256,1,384]{2,1,0:T(1,128)}), f32[256,1,384]{2,1,0:T(1,128)S(1)}, u32[]{:S(2)}, u32[]{:S(2)}) async-start(f32[256,1,384]{2,1,0:T(1,128)} %bitcast.244), calls=%async_computation | async-start | bytes 786432 | tf_op jit(solution)/shard_map/all_to_all | solution.py:241
  188.0 3.5 %collective-permute-start.18 = (bf16[2,1,64,128]{3,2,1,0:T(8,128)(2,1)S(1)}, bf16[2,1,64,128]{3,2,1,0:T(8,128)(2,1)S(1)}, u32[]{:S(2)}, u32[]{:S(2)}) collective-permute-start(bf16[2,1,64,128]{3,2,1,0:T(8,128)(2,1)S(1)} %get-tuple-element.28), channel_id=1, source_target_pairs={{0,8},{8,16},{16,24},{24,32},{32,40},{40,48},{48,56},{56,64},{64,7... | collective-permute-start | bytes 98312 | tf_op jit(solution)/shard_map/ppermute | solution.py:19
  194.8 11.4 %all-to-all-done = f32[256,1,384]{2,1,0:T(1,128)S(1)} async-done(((f32[256,1,384]{2,1,0:T(1,128)}), f32[256,1,384]{2,1,0:T(1,128)S(1)}, u32[]{:S(2)}, u32[]{:S(2)}) %all-to-all-start) | async-done | bytes 393248 | tf_op jit(solution)/shard_map/all_to_all | solution.py:241
  206.4 1.0 broadcast_in_dim.56
  207.4 6.7 %all-to-all-start.1 = ((f32[256,1,384]{2,1,0:T(1,128)}), f32[256,1,384]{2,1,0:T(1,128)S(1)}, u32[]{:S(2)}, u32[]{:S(2)}) async-start(f32[256,1,384]{2,1,0:T(1,128)} %broadcast_in_dim.56), calls=%async_computation.1 | async-start | bytes 786432 | tf_op jit(solution)/shard_map/all_to_all | solution.py:243
  215.4 1.2 fusion.22
  216.6 14.6 %all-to-all-done.1 = f32[256,1,384]{2,1,0:T(1,128)S(1)} async-done(((f32[256,1,384]{2,1,0:T(1,128)}), f32[256,1,384]{2,1,0:T(1,128)S(1)}, u32[]{:S(2)}, u32[]{:S(2)}) %all-to-all-start.1) | async-done | bytes 393248 | tf_op jit(solution)/shard_map/all_to_all | solution.py:243
  233.7 0.8 reshape.303
  234.5 0.8 reshape.301
  (235 shorter events, 43.1 us)
Async XLA Ops:
  0.6 19.8 %copy-start.3 = (bf16[2,16,64,128]{3,2,1,0:T(8,128)(2,1)S(1)}, bf16[2,16,64,128]{3,2,1,0:T(8,128)(2,1)}, u32[]{:S(2)}) copy-start(bf16[2,16,64,128]{3,2,1,0:T(8,128)(2,1)} %param.12) | copy-start | bytes 1572868
  1.5 19.0 %collective-permute-start = (bf16[2,1,64,128]{3,2,1,0:T(8,128)(2,1)S(1)}, bf16[2,1,64,128]{3,2,1,0:T(8,128)(2,1)S(1)}, u32[]{:S(2)}, u32[]{:S(2)}) collective-permute-start(bf16[2,1,64,128]{3,2,1,0:T(8,128)(2,1)S(1)} %get-tuple-element.38), channel_id=1, source_target_pairs={{0,8},{8,16},{16,24},{24,32},{32,40},{40,48},{48,56},{56,64},{64,7... | collective-permute-start | bytes 98312 | tf_op jit(solution)/shard_map/ppermute | solution.py:19
  5.5 14.9 %collective-permute-start.1 = (bf16[2,1,64,128]{3,2,1,0:T(8,128)(2,1)S(1)}, bf16[2,1,64,128]{3,2,1,0:T(8,128)(2,1)S(1)}, u32[]{:S(2)}, u32[]{:S(2)}) collective-permute-start(bf16[2,1,64,128]{3,2,1,0:T(8,128)(2,1)S(1)} %get-tuple-element.39), channel_id=1, source_target_pairs={{8,0},{16,8},{24,16},{32,24},{40,32},{48,40},{56,48},{64,56},{72,6... | collective-permute-start | bytes 98312 | tf_op jit(solution)/shard_map/ppermute | solution.py:21
  11.4 6.9 %copy-start.38 = (s32[32,4]{0,1:T(4,128)}, s32[32,4]{0,1:T(4,128)S(1)}, u32[]{:S(2)}) copy-start(s32[32,4]{0,1:T(4,128)S(1)} %select_reduce_fusion) | copy-start | bytes 1540
  12.3 1.4 copy-start.43
  18.3 2.8 %copy-start.17 = (bf16[3,3,64,64]{3,2,1,0:T(8,128)(2,1)S(1)}, bf16[3,3,64,64]{3,2,1,0:T(8,128)(2,1)}, u32[]{:S(2)}) copy-start(bf16[3,3,64,64]{3,2,1,0:T(8,128)(2,1)} %param.13) | copy-start | bytes 221188
  20.5 3.2 %copy-start.39 = (bf16[2,1,64,128]{3,2,1,0:T(8,128)(2,1)}, bf16[2,1,64,128]{3,2,1,0:T(8,128)(2,1)S(1)}, u32[]{:S(2)}) copy-start(bf16[2,1,64,128]{3,2,1,0:T(8,128)(2,1)S(1)} %collective-permute-done.1) | copy-start | bytes 98308
  23.6 7.5 %copy-start.36 = (bf16[3,64,64]{2,1,0:T(8,128)(2,1)S(1)}, bf16[3,64,64]{2,1,0:T(8,128)(2,1)}, u32[]{:S(2)}) copy-start(bf16[3,64,64]{2,1,0:T(8,128)(2,1)} %param.14) | copy-start | bytes 73732
  25.1 12.4 %copy-start.9 = (bf16[2,16,64,128]{3,2,1,0:T(8,128)(2,1)}, bf16[2,16,64,128]{3,2,1,0:T(8,128)(2,1)S(1)}, u32[]{:S(2)}) copy-start(bf16[2,16,64,128]{3,2,1,0:T(8,128)(2,1)S(1)} %get-tuple-element.55) | copy-start | bytes 1572868
  25.2 12.0 %copy-start.15 = (bf16[1,16,64,128]{3,2,1,0:T(8,128)(2,1)}, bf16[1,16,64,128]{3,2,1,0:T(8,128)(2,1)S(1)}, u32[]{:S(2)}) copy-start(bf16[1,16,64,128]{3,2,1,0:T(8,128)(2,1)S(1)} %get-tuple-element.36) | copy-start | bytes 786436
  25.2 12.4 %copy-start.27 = (bf16[1,16,64,128]{3,2,1,0:T(8,128)(2,1)}, bf16[1,16,64,128]{3,2,1,0:T(8,128)(2,1)S(1)}, u32[]{:S(2)}) copy-start(bf16[1,16,64,128]{3,2,1,0:T(8,128)(2,1)S(1)} %get-tuple-element.37) | copy-start | bytes 786436
  25.2 12.4 %collective-permute-start.2 = (bf16[1,16,64,128]{3,2,1,0:T(8,128)(2,1)S(1)}, bf16[1,16,64,128]{3,2,1,0:T(8,128)(2,1)S(1)}, u32[]{:S(2)}, u32[]{:S(2)}) collective-permute-start(bf16[1,16,64,128]{3,2,1,0:T(8,128)(2,1)S(1)} %get-tuple-element.36), channel_id=1, source_target_pairs={{0,1},{1,2},{2,3},{3,4},{4,5},{5,6},{6,7},{8,9},{9,10},{10,11},{11... | collective-permute-start | bytes 786440 | tf_op jit(solution)/shard_map/ppermute | solution.py:31
  29.2 7.7 %collective-permute-start.3 = (bf16[1,16,64,128]{3,2,1,0:T(8,128)(2,1)S(1)}, bf16[1,16,64,128]{3,2,1,0:T(8,128)(2,1)S(1)}, u32[]{:S(2)}, u32[]{:S(2)}) collective-permute-start(bf16[1,16,64,128]{3,2,1,0:T(8,128)(2,1)S(1)} %get-tuple-element.37), channel_id=1, source_target_pairs={{1,0},{2,1},{3,2},{4,3},{5,4},{6,5},{7,6},{9,8},{10,9},{11,10},{12... | collective-permute-start | bytes 786440 | tf_op jit(solution)/shard_map/ppermute | solution.py:31
  37.6 7.1 %copy-start = (bf16[2,16,64,128]{3,2,1,0:T(8,128)(2,1)S(1)}, bf16[2,16,64,128]{3,2,1,0:T(8,128)(2,1)}, u32[]{:S(2)}) copy-start(bf16[2,16,64,128]{3,2,1,0:T(8,128)(2,1)} %param.20) | copy-start | bytes 1572868
  37.6 1.5 copy-start.47
  39.1 12.1 %copy-start.5 = (bf16[2,16,64,128]{3,2,1,0:T(8,128)(2,1)}, bf16[2,16,64,128]{3,2,1,0:T(8,128)(2,1)S(1)}, u32[]{:S(2)}) copy-start(bf16[2,16,64,128]{3,2,1,0:T(8,128)(2,1)S(1)} %get-tuple-element.57) | copy-start | bytes 1572868
  39.1 6.7 %collective-permute-start.4 = (bf16[2,1,64,128]{3,2,1,0:T(8,128)(2,1)S(1)}, bf16[2,1,64,128]{3,2,1,0:T(8,128)(2,1)S(1)}, u32[]{:S(2)}, u32[]{:S(2)}) collective-permute-start(bf16[2,1,64,128]{3,2,1,0:T(8,128)(2,1)S(1)} %get-tuple-element.34), channel_id=1, source_target_pairs={{0,8},{8,16},{16,24},{24,32},{32,40},{40,48},{48,56},{56,64},{64,7... | collective-permute-start | bytes 98312 | tf_op jit(solution)/shard_map/ppermute | solution.py:19
  43.3 4.7 %collective-permute-start.5 = (bf16[2,1,64,128]{3,2,1,0:T(8,128)(2,1)S(1)}, bf16[2,1,64,128]{3,2,1,0:T(8,128)(2,1)S(1)}, u32[]{:S(2)}, u32[]{:S(2)}) collective-permute-start(bf16[2,1,64,128]{3,2,1,0:T(8,128)(2,1)S(1)} %get-tuple-element.35), channel_id=1, source_target_pairs={{8,0},{16,8},{24,16},{32,24},{40,32},{48,40},{56,48},{64,56},{72,6... | collective-permute-start | bytes 98312 | tf_op jit(solution)/shard_map/ppermute | solution.py:21
  44.7 4.0 %copy-start.23 = (bf16[3,3,64,64]{3,2,1,0:T(8,128)(2,1)S(1)}, bf16[3,3,64,64]{3,2,1,0:T(8,128)(2,1)}, u32[]{:S(2)}) copy-start(bf16[3,3,64,64]{3,2,1,0:T(8,128)(2,1)} %param.15) | copy-start | bytes 221188
  45.7 3.3 %copy-start.32 = (bf16[2,1,64,128]{3,2,1,0:T(8,128)(2,1)}, bf16[2,1,64,128]{3,2,1,0:T(8,128)(2,1)S(1)}, u32[]{:S(2)}) copy-start(bf16[2,1,64,128]{3,2,1,0:T(8,128)(2,1)S(1)} %collective-permute-done.4) | copy-start | bytes 98308
  48.0 3.2 %copy-start.41 = (bf16[2,1,64,128]{3,2,1,0:T(8,128)(2,1)}, bf16[2,1,64,128]{3,2,1,0:T(8,128)(2,1)S(1)}, u32[]{:S(2)}) copy-start(bf16[2,1,64,128]{3,2,1,0:T(8,128)(2,1)S(1)} %collective-permute-done.5) | copy-start | bytes 98308
  51.2 2.9 %copy-start.45 = (s32[4]{0:T(128)S(1)}, s32[4]{0:T(128)}, u32[]{:S(2)}) copy-start(s32[4]{0:T(128)} %get-tuple-element.53) | copy-start | bytes 52
  52.8 15.9 %collective-permute-start.7 = (bf16[2,16,64,128]{3,2,1,0:T(8,128)(2,1)}, bf16[2,16,64,128]{3,2,1,0:T(8,128)(2,1)S(1)}, u32[]{:S(2)}, u32[]{:S(2)}) collective-permute-start(bf16[2,16,64,128]{3,2,1,0:T(8,128)(2,1)} %get-tuple-element.59), channel_id=1, source_target_pairs={{2,0},{3,1},{4,2},{5,3},{6,4},{7,5},{10,8},{11,9},{12,10},{13,11},... | collective-permute-start | bytes 1572872 | tf_op jit(solution)/shard_map/ppermute | solution.py:31
  55.2 13.6 %copy-start.34 = (bf16[3,64,64]{2,1,0:T(8,128)(2,1)S(1)}, bf16[3,64,64]{2,1,0:T(8,128)(2,1)}, u32[]{:S(2)}) copy-start(bf16[3,64,64]{2,1,0:T(8,128)(2,1)} %param.16) | copy-start | bytes 73732
  57.7 15.6 %collective-permute-start.6 = (bf16[2,16,64,128]{3,2,1,0:T(8,128)(2,1)}, bf16[2,16,64,128]{3,2,1,0:T(8,128)(2,1)S(1)}, u32[]{:S(2)}, u32[]{:S(2)}) collective-permute-start(bf16[2,16,64,128]{3,2,1,0:T(8,128)(2,1)} %get-tuple-element.59), channel_id=1, source_target_pairs={{0,2},{1,3},{2,4},{3,5},{4,6},{5,7},{8,10},{9,11},{10,12},{11,13},... | collective-permute-start | bytes 1572872 | tf_op jit(solution)/shard_map/ppermute | solution.py:31
  74.9 11.3 %copy-start.1 = (bf16[2,16,64,128]{3,2,1,0:T(8,128)(2,1)}, bf16[2,16,64,128]{3,2,1,0:T(8,128)(2,1)S(1)}, u32[]{:S(2)}) copy-start(bf16[2,16,64,128]{3,2,1,0:T(8,128)(2,1)S(1)} %get-tuple-element.61) | copy-start | bytes 1572868
  74.9 1.3 copy-start.20
  74.9 8.2 %copy-start.19 = (bf16[2,1,4,64,128]{4,2,3,0,1:T(4,128)(2,1)S(1)}, bf16[2,1,4,64,128]{4,2,3,0,1:T(4,128)(2,1)}, u32[]{:S(2)}) copy-start(bf16[2,1,4,64,128]{4,2,3,0,1:T(4,128)(2,1)} %fusion.32) | copy-start | bytes 393220
  75.4 9.3 %copy-start.21 = (bf16[2,1,4,64,128]{4,2,3,0,1:T(4,128)(2,1)S(1)}, bf16[2,1,4,64,128]{4,2,3,0,1:T(4,128)(2,1)}, u32[]{:S(2)}) copy-start(bf16[2,1,4,64,128]{4,2,3,0,1:T(4,128)(2,1)} %fusion.30) | copy-start | bytes 393220
  76.2 10.4 %copy-start.22 = (bf16[2,1,4,64,128]{4,2,3,0,1:T(4,128)(2,1)S(1)}, bf16[2,1,4,64,128]{4,2,3,0,1:T(4,128)(2,1)}, u32[]{:S(2)}) copy-start(bf16[2,1,4,64,128]{4,2,3,0,1:T(4,128)(2,1)} %fusion.28) | copy-start | bytes 393220
  76.4 15.7 %collective-permute-start.8 = (bf16[2,2,4,64,128]{4,2,3,0,1:T(4,128)(2,1)S(1)}, bf16[2,2,4,64,128]{4,2,3,0,1:T(4,128)(2,1)S(1)}, u32[]{:S(2)}, u32[]{:S(2)}) collective-permute-start(bf16[2,2,4,64,128]{4,2,3,0,1:T(4,128)(2,1)S(1)} %pad_maximum_fusion.20), channel_id=1, source_target_pairs={{0,16},{8,24},{16,32},{24,40},{32,48},{40,56},{48,64},{56,72},{64,... | collective-permute-start | bytes 786440 | tf_op jit(solution)/shard_map/ppermute | solution.py:31
  83.4 10.5 %collective-permute-start.11 = (bf16[2,2,4,64,128]{4,2,3,0,1:T(4,128)(2,1)S(1)}, bf16[2,2,4,64,128]{4,2,3,0,1:T(4,128)(2,1)S(1)}, u32[]{:S(2)}, u32[]{:S(2)}) collective-permute-start(bf16[2,2,4,64,128]{4,2,3,0,1:T(4,128)(2,1)S(1)} %pad_maximum_fusion.23), channel_id=1, source_target_pairs={{16,0},{24,8},{32,16},{40,24},{48,32},{56,40},{64,48},{72,56},{80,... | collective-permute-start | bytes 786440 | tf_op jit(solution)/shard_map/ppermute | solution.py:31
  84.9 18.4 %collective-permute-start.10 = (bf16[2,2,4,64,128]{4,2,3,0,1:T(4,128)(2,1)S(1)}, bf16[2,2,4,64,128]{4,2,3,0,1:T(4,128)(2,1)S(1)}, u32[]{:S(2)}, u32[]{:S(2)}) collective-permute-start(bf16[2,2,4,64,128]{4,2,3,0,1:T(4,128)(2,1)S(1)} %pad_maximum_fusion.22), channel_id=1, source_target_pairs={{8,0},{16,8},{24,16},{32,24},{40,32},{48,40},{56,48},{64,56},{72,6... | collective-permute-start | bytes 786440 | tf_op jit(solution)/shard_map/ppermute | solution.py:31
  86.8 18.0 %copy-start.44 = (s32[4,4]{1,0:T(4,128)S(1)}, s32[4,4]{1,0:T(4,128)}, u32[]{:S(2)}) copy-start(s32[4,4]{1,0:T(4,128)} %broadcast_select_fusion) | copy-start | bytes 196
  86.8 18.0 %copy-start.46 = (pred[4,4]{1,0:T(4,128)(4,1)S(1)}, pred[4,4]{1,0:T(4,128)(4,1)}, u32[]{:S(2)}) copy-start(pred[4,4]{1,0:T(4,128)(4,1)} %select_and_fusion) | copy-start | bytes 52
  86.8 17.2 %collective-permute-start.9 = (bf16[2,2,4,64,128]{4,2,3,0,1:T(4,128)(2,1)S(1)}, bf16[2,2,4,64,128]{4,2,3,0,1:T(4,128)(2,1)S(1)}, u32[]{:S(2)}, u32[]{:S(2)}) collective-permute-start(bf16[2,2,4,64,128]{4,2,3,0,1:T(4,128)(2,1)S(1)} %pad_maximum_fusion.21), channel_id=1, source_target_pairs={{0,8},{8,16},{16,24},{24,32},{32,40},{40,48},{48,56},{56,64},{64,7... | collective-permute-start | bytes 786440 | tf_op jit(solution)/shard_map/ppermute | solution.py:31
  105.3 8.4 %copy-start.12 = (bf16[2,16,64,128]{3,2,1,0:T(8,128)(2,1)S(1)}, bf16[2,16,64,128]{3,2,1,0:T(8,128)(2,1)}, u32[]{:S(2)}) copy-start(bf16[2,16,64,128]{3,2,1,0:T(8,128)(2,1)} %copy-done.11) | copy-start | bytes 1572868
  107.6 13.7 %collective-permute-start.13 = (bf16[2,16,64,128]{3,2,1,0:T(8,128)(2,1)S(1)}, bf16[2,16,64,128]{3,2,1,0:T(8,128)(2,1)}, u32[]{:S(2)}, u32[]{:S(2)}) collective-permute-start(bf16[2,16,64,128]{3,2,1,0:T(8,128)(2,1)S(1)} %fusion.33), channel_id=1, source_target_pairs={{0,2},{1,3},{2,4},{3,5},{4,6},{5,7},{8,10},{9,11},{10,12},{11,13},... | collective-permute-start | bytes 1572872 | tf_op jit(solution)/shard_map/ppermute | solution.py:31
  112.4 13.6 %collective-permute-start.12 = (bf16[2,16,64,128]{3,2,1,0:T(8,128)(2,1)S(1)}, bf16[2,16,64,128]{3,2,1,0:T(8,128)(2,1)}, u32[]{:S(2)}, u32[]{:S(2)}) collective-permute-start(bf16[2,16,64,128]{3,2,1,0:T(8,128)(2,1)S(1)} %fusion.33), channel_id=1, source_target_pairs={{2,0},{3,1},{4,2},{5,3},{6,4},{7,5},{10,8},{11,9},{12,10},{13,11},... | collective-permute-start | bytes 1572872 | tf_op jit(solution)/shard_map/ppermute | solution.py:31
  116.5 1.5 copy-start.2
  119.3 6.7 %copy-start.49 = (f32[2,16,64,128]{3,2,1,0:T(8,128)S(1)}, f32[2,16,64,128]{3,2,1,0:T(8,128)}, u32[]{:S(2)}) copy-start(f32[2,16,64,128]{3,2,1,0:T(8,128)} %get-tuple-element.60) | copy-start | bytes 3145732
  119.6 6.4 %copy-start.14 = (f32[2,64,128,16]{2,3,1,0:T(8,128)S(1)}, f32[2,64,128,16]{2,3,1,0:T(8,128)}, u32[]{:S(2)}) copy-start(f32[2,64,128,16]{2,3,1,0:T(8,128)} %copy-done.13) | copy-start | bytes 3145732
  126.0 2.0 copy-start.6
  128.0 6.9 %copy-start.7 = (bf16[2,16,64,128]{3,2,1,0:T(8,128)(2,1)}, bf16[2,16,64,128]{3,2,1,0:T(8,128)(2,1)S(1)}, u32[]{:S(2)}) copy-start(bf16[2,16,64,128]{3,2,1,0:T(8,128)(2,1)S(1)} %get-tuple-element.63) | copy-start | bytes 1572868
  129.7 4.9 %copy-start.42 = (bf16[2,1,64,128]{3,2,1,0:T(8,128)(2,1)S(1)}, bf16[2,1,64,128]{3,2,1,0:T(8,128)(2,1)}, u32[]{:S(2)}) copy-start(bf16[2,1,64,128]{3,2,1,0:T(8,128)(2,1)} %copy-done.41) | copy-start | bytes 98308
  130.3 4.5 %copy-start.33 = (bf16[2,1,64,128]{3,2,1,0:T(8,128)(2,1)S(1)}, bf16[2,1,64,128]{3,2,1,0:T(8,128)(2,1)}, u32[]{:S(2)}) copy-start(bf16[2,1,64,128]{3,2,1,0:T(8,128)(2,1)} %copy-done.32) | copy-start | bytes 98308
  130.4 5.0 %collective-permute-start.14 = (bf16[2,1,64,128]{3,2,1,0:T(8,128)(2,1)S(1)}, bf16[2,1,64,128]{3,2,1,0:T(8,128)(2,1)S(1)}, u32[]{:S(2)}, u32[]{:S(2)}) collective-permute-start(bf16[2,1,64,128]{3,2,1,0:T(8,128)(2,1)S(1)} %get-tuple-element.32), channel_id=1, source_target_pairs={{0,8},{8,16},{16,24},{24,32},{32,40},{40,48},{48,56},{56,64},{64,7... | collective-permute-start | bytes 98312 | tf_op jit(solution)/shard_map/ppermute | solution.py:19
  133.0 4.7 %collective-permute-start.15 = (bf16[2,1,64,128]{3,2,1,0:T(8,128)(2,1)S(1)}, bf16[2,1,64,128]{3,2,1,0:T(8,128)(2,1)S(1)}, u32[]{:S(2)}, u32[]{:S(2)}) collective-permute-start(bf16[2,1,64,128]{3,2,1,0:T(8,128)(2,1)S(1)} %get-tuple-element.33), channel_id=1, source_target_pairs={{8,0},{16,8},{24,16},{32,24},{40,32},{48,40},{56,48},{64,56},{72,6... | collective-permute-start | bytes 98312 | tf_op jit(solution)/shard_map/ppermute | solution.py:21
  135.2 2.5 %copy-start.8 = (bf16[2,16,64,128]{3,2,1,0:T(8,128)(2,1)S(1)}, bf16[2,16,64,128]{3,2,1,0:T(8,128)(2,1)}, u32[]{:S(2)}) copy-start(bf16[2,16,64,128]{3,2,1,0:T(8,128)(2,1)} %copy-done.7) | copy-start | bytes 1572868
  135.2 3.1 %copy-start.24 = (bf16[3,3,64,64]{3,2,1,0:T(8,128)(2,1)S(1)}, bf16[3,3,64,64]{3,2,1,0:T(8,128)(2,1)}, u32[]{:S(2)}) copy-start(bf16[3,3,64,64]{3,2,1,0:T(8,128)(2,1)} %param.15) | copy-start | bytes 221188
  142.1 1.5 copy-start.10
  143.9 8.2 %copy-start.28 = (bf16[1,16,64,128]{3,2,1,0:T(8,128)(2,1)S(1)}, bf16[1,16,64,128]{3,2,1,0:T(8,128)(2,1)}, u32[]{:S(2)}) copy-start(bf16[1,16,64,128]{3,2,1,0:T(8,128)(2,1)} %copy-done.27) | copy-start | bytes 786436
  143.9 8.2 %copy-start.48 = (bf16[1,16,64,128]{3,2,1,0:T(8,128)(2,1)S(1)}, bf16[1,16,64,128]{3,2,1,0:T(8,128)(2,1)}, u32[]{:S(2)}) copy-start(bf16[1,16,64,128]{3,2,1,0:T(8,128)(2,1)} %copy-done.47) | copy-start | bytes 786436
  144.6 7.7 %copy-start.16 = (bf16[1,16,64,128]{3,2,1,0:T(8,128)(2,1)S(1)}, bf16[1,16,64,128]{3,2,1,0:T(8,128)(2,1)}, u32[]{:S(2)}) copy-start(bf16[1,16,64,128]{3,2,1,0:T(8,128)(2,1)} %copy-done.15) | copy-start | bytes 786436
  144.6 7.8 %copy-start.26 = (bf16[1,16,64,128]{3,2,1,0:T(8,128)(2,1)S(1)}, bf16[1,16,64,128]{3,2,1,0:T(8,128)(2,1)}, u32[]{:S(2)}) copy-start(bf16[1,16,64,128]{3,2,1,0:T(8,128)(2,1)} %copy-done.25) | copy-start | bytes 786436
  145.0 8.8 %collective-permute-start.17 = (bf16[1,16,64,128]{3,2,1,0:T(8,128)(2,1)}, bf16[1,16,64,128]{3,2,1,0:T(8,128)(2,1)S(1)}, u32[]{:S(2)}, u32[]{:S(2)}) collective-permute-start(bf16[1,16,64,128]{3,2,1,0:T(8,128)(2,1)} %get-tuple-element.30), channel_id=1, source_target_pairs={{0,1},{1,2},{2,3},{3,4},{4,5},{5,6},{6,7},{8,9},{9,10},{10,11},{11... | collective-permute-start | bytes 786440 | tf_op jit(solution)/shard_map/ppermute | solution.py:31
  150.1 7.8 %collective-permute-start.16 = (bf16[1,16,64,128]{3,2,1,0:T(8,128)(2,1)S(1)}, bf16[1,16,64,128]{3,2,1,0:T(8,128)(2,1)}, u32[]{:S(2)}, u32[]{:S(2)}) collective-permute-start(bf16[1,16,64,128]{3,2,1,0:T(8,128)(2,1)S(1)} %get-tuple-element.31), channel_id=1, source_target_pairs={{1,0},{2,1},{3,2},{4,3},{5,4},{6,5},{7,6},{9,8},{10,9},{11,10},{12... | collective-permute-start | bytes 786440 | tf_op jit(solution)/shard_map/ppermute | solution.py:31
  152.8 5.1 %copy-start.50 = (f32[2,16,64,128]{3,2,1,0:T(8,128)S(1)}, f32[2,16,64,128]{3,2,1,0:T(8,128)}, u32[]{:S(2)}) copy-start(f32[2,16,64,128]{3,2,1,0:T(8,128)} %get-tuple-element.56) | copy-start | bytes 3145732
  152.8 5.1 %copy-start.52 = (bf16[2,16,64,128]{3,2,1,0:T(8,128)(2,1)S(1)}, bf16[2,16,64,128]{3,2,1,0:T(8,128)(2,1)}, u32[]{:S(2)}) copy-start(bf16[2,16,64,128]{3,2,1,0:T(8,128)(2,1)} %get-tuple-element.66) | copy-start | bytes 1572868
  163.9 1.8 copy-start.29
  164.3 27.2 %collective-permute-start.19 = (bf16[2,1,64,128]{3,2,1,0:T(8,128)(2,1)S(1)}, bf16[2,1,64,128]{3,2,1,0:T(8,128)(2,1)S(1)}, u32[]{:S(2)}, u32[]{:S(2)}) collective-permute-start(bf16[2,1,64,128]{3,2,1,0:T(8,128)(2,1)S(1)} %get-tuple-element.29), channel_id=1, source_target_pairs={{8,0},{16,8},{24,16},{32,24},{40,32},{48,40},{56,48},{64,56},{72,6... | collective-permute-start | bytes 98312 | tf_op jit(solution)/shard_map/ppermute | solution.py:21
  166.4 39.7 %all-to-all-start = ((f32[256,1,384]{2,1,0:T(1,128)}), f32[256,1,384]{2,1,0:T(1,128)S(1)}, u32[]{:S(2)}, u32[]{:S(2)}) async-start(f32[256,1,384]{2,1,0:T(1,128)} %bitcast.244), calls=%async_computation | async-start | bytes 786432 | tf_op jit(solution)/shard_map/all_to_all | solution.py:241
  188.0 4.3 %collective-permute-start.18 = (bf16[2,1,64,128]{3,2,1,0:T(8,128)(2,1)S(1)}, bf16[2,1,64,128]{3,2,1,0:T(8,128)(2,1)S(1)}, u32[]{:S(2)}, u32[]{:S(2)}) collective-permute-start(bf16[2,1,64,128]{3,2,1,0:T(8,128)(2,1)S(1)} %get-tuple-element.28), channel_id=1, source_target_pairs={{0,8},{8,16},{16,24},{24,32},{32,40},{40,48},{48,56},{56,64},{64,7... | collective-permute-start | bytes 98312 | tf_op jit(solution)/shard_map/ppermute | solution.py:19
  207.4 23.9 %all-to-all-start.1 = ((f32[256,1,384]{2,1,0:T(1,128)}), f32[256,1,384]{2,1,0:T(1,128)S(1)}, u32[]{:S(2)}, u32[]{:S(2)}) async-start(f32[256,1,384]{2,1,0:T(1,128)} %broadcast_in_dim.56), calls=%async_computation.1 | async-start | bytes 786432 | tf_op jit(solution)/shard_map/all_to_all | solution.py:243
  (11 other events, 10.6 us)

commit v7 on v5

--- a/solution.py
+++ b/solution.py
@@ -318,7 +318,7 @@
         first_gradient, pre_one, padded_zero, spatial_a, chart_rim
     )
     summed_sa, summed_ta, summed_sb, summed_tb = exchange_sum(
-        (grad_sa, gradient_kernel_first, grad_sb, gradient_kernel_second), ("frame", "chart")
+        (grad_sa, gradient_kernel_first, grad_sb, gradient_kernel_second), ("chart", "frame")
     )
     pixel_frames = total_frames * strips * lax.axis_size("chart") * features.shape[3]
     grad_scale = float(pixel_frames) ** (-0.5)

time: 237 us -> 237 us (level)
  no operation moved by 1% of the time
where the time goes in v7:
time: 237 us; the launch traced here: 235 us
  starting transfers between devices  88.2 us (37%)
  waiting for transfers between devices  64.1 us (27%)
  matrix products  48.4 us (20%)
  local copies, waits for them, and re-layouts  17.9 us (8%)
  other arithmetic  14.7 us (6%)
    ppermute x12, starting transfers between devices, from_behind(): return lax.ppermute(array, axis, pairs)  39.1 us
    ppermute x12, waiting for transfers between devices, from_behind(): return lax.ppermute(array, axis, pairs)  34.2 us
    all_to_all x1, starting transfers between devices, exchange_sum(): flat = jnp.sum(lax.all_to_all(pieces, axes, 0, 0, tiled=True), axis=0)  21.6 us
    all_to_all x1, waiting for transfers between devices, exchange_sum(): flat = lax.all_to_all(copies, axes, 0, 0, tiled=True).reshape(-1)  14.5 us
    ppermute x4, starting transfers between devices, with_halo(): lax.ppermute(tail, axis, [(i, (i + 1) % count) for i in range(ends)])  14.4 us
    all_to_all x1, waiting for transfers between devices, exchange_sum(): flat = jnp.sum(lax.all_to_all(pieces, axes, 0, 0, tiled=True), axis=0)  10.3 us
    dot_general x18, matrix products, spatial_transpose(): jnp.einsum('oc,fsop->fscp', weight[row_tap, col_tap], padded[:, 2 - row_t...  8.45 us
    dot_general x18, matrix products, spatial_apply(): jnp.einsum('oc,fscp->fsop', weight[row_tap, col_tap], padded[:, row_tap:r...  8.04 us
  transfers between devices with their start and end apart: 22, of which 14 were waited for; matrix products, arithmetic and copies ran while one was open for 16% of the time, Pallas kernels for 0%

profile of v7, /device:TPU:1, one launch (start us, length us, event | category | flops | bytes accessed | tf_op | source)
XLA Modules:
  0.0 235.3 jit_solution(10487203026221177264)
XLA Ops:
  0.6 0.8 fusion.288
  1.5 4.0 %collective-permute-start = (bf16[2,1,64,128]{3,2,1,0:T(8,128)(2,1)S(1)}, bf16[2,1,64,128]{3,2,1,0:T(8,128)(2,1)S(1)}, u32[]{:S(2)}, u32[]{:S(2)}) collective-permute-start(bf16[2,1,64,128]{3,2,1,0:T(8,128)(2,1)S(1)} %get-tuple-element.38), channel_id=1, source_target_pairs={{0,8},{8,16},{16,24},{24,32},{32,40},{40,48},{48,56},{56,64},{64,7... | collective-permute-start | bytes 98312 | tf_op jit(solution)/shard_map/ppermute | solution.py:19
  5.5 1.3 collective-permute-start.1
  7.5 0.9 dynamic-slice_reduce_fusion.2
  9.8 0.9 convert_reduce_fusion
  11.4 0.9 dynamic-slice_reduce_fusion
  16.2 2.1 fusion.26
  18.3 2.1 fusion.32
  23.7 1.5 add_convert_fusion.3
  25.2 4.0 %collective-permute-start.2 = (bf16[1,16,64,128]{3,2,1,0:T(8,128)(2,1)S(1)}, bf16[1,16,64,128]{3,2,1,0:T(8,128)(2,1)S(1)}, u32[]{:S(2)}, u32[]{:S(2)}) collective-permute-start(bf16[1,16,64,128]{3,2,1,0:T(8,128)(2,1)S(1)} %get-tuple-element.36), channel_id=1, source_target_pairs={{0,1},{1,2},{2,3},{3,4},{4,5},{5,6},{6,7},{8,9},{9,10},{10,11},{11... | collective-permute-start | bytes 786440 | tf_op jit(solution)/shard_map/ppermute | solution.py:31
  29.2 1.9 collective-permute-start.3
  31.4 5.5 %collective-permute-done.3 = bf16[1,16,64,128]{3,2,1,0:T(8,128)(2,1)S(1)} collective-permute-done((bf16[1,16,64,128]{3,2,1,0:T(8,128)(2,1)S(1)}, bf16[1,16,64,128]{3,2,1,0:T(8,128)(2,1)S(1)}, u32[]{:S(2)}, u32[]{:S(2)}) %collective-permute-start.3) | collective-permute-done | bytes 262176 | tf_op jit(solution)/shard_map/ppermute | solution.py:31
  37.6 1.5 add_convert_fusion.2
  39.1 4.3 %collective-permute-start.4 = (bf16[2,1,64,128]{3,2,1,0:T(8,128)(2,1)S(1)}, bf16[2,1,64,128]{3,2,1,0:T(8,128)(2,1)S(1)}, u32[]{:S(2)}, u32[]{:S(2)}) collective-permute-start(bf16[2,1,64,128]{3,2,1,0:T(8,128)(2,1)S(1)} %get-tuple-element.34), channel_id=1, source_target_pairs={{0,8},{8,16},{16,24},{24,32},{32,40},{40,48},{48,56},{56,64},{64,7... | collective-permute-start | bytes 98312 | tf_op jit(solution)/shard_map/ppermute | solution.py:19
  43.3 1.3 collective-permute-start.5
  44.7 1.1 fusion.30
  45.7 2.3 collective-permute-done.5
  51.2 1.6 add_convert_fusion.1
  52.8 1.3 collective-permute-start.7
  54.1 1.0 fusion.28
  55.2 1.0 select_reduce_fusion.5
  56.2 1.5 fusion.230
  57.7 4.2 %collective-permute-start.6 = (bf16[2,16,64,128]{3,2,1,0:T(8,128)(2,1)}, bf16[2,16,64,128]{3,2,1,0:T(8,128)(2,1)S(1)}, u32[]{:S(2)}, u32[]{:S(2)}) collective-permute-start(bf16[2,16,64,128]{3,2,1,0:T(8,128)(2,1)} %get-tuple-element.59), channel_id=1, source_target_pairs={{0,2},{1,3},{2,4},{3,5},{4,6},{5,7},{8,10},{9,11},{10,12},{11,13},... | collective-permute-start | bytes 1572872 | tf_op jit(solution)/shard_map/ppermute | solution.py:31
  61.9 1.3 fusion.135
  63.2 5.5 %collective-permute-done.7 = bf16[2,16,64,128]{3,2,1,0:T(8,128)(2,1)S(1)} collective-permute-done((bf16[2,16,64,128]{3,2,1,0:T(8,128)(2,1)}, bf16[2,16,64,128]{3,2,1,0:T(8,128)(2,1)S(1)}, u32[]{:S(2)}, u32[]{:S(2)}) %collective-permute-start.7) | collective-permute-done | bytes 524320 | tf_op jit(solution)/shard_map/ppermute | solution.py:31
  69.6 3.8 %collective-permute-done.6 = bf16[2,16,64,128]{3,2,1,0:T(8,128)(2,1)S(1)} collective-permute-done((bf16[2,16,64,128]{3,2,1,0:T(8,128)(2,1)}, bf16[2,16,64,128]{3,2,1,0:T(8,128)(2,1)S(1)}, u32[]{:S(2)}, u32[]{:S(2)}) %collective-permute-start.6) | collective-permute-done | bytes 524320 | tf_op jit(solution)/shard_map/ppermute | solution.py:31
  73.4 1.6 add_convert_fusion
  76.4 6.8 %collective-permute-start.8 = (bf16[2,2,4,64,128]{4,2,3,0,1:T(4,128)(2,1)S(1)}, bf16[2,2,4,64,128]{4,2,3,0,1:T(4,128)(2,1)S(1)}, u32[]{:S(2)}, u32[]{:S(2)}) collective-permute-start(bf16[2,2,4,64,128]{4,2,3,0,1:T(4,128)(2,1)S(1)} %pad_maximum_fusion.21), channel_id=1, source_target_pairs={{0,16},{8,24},{16,32},{24,40},{32,48},{40,56},{48,64},{56,72},{64,... | collective-permute-start | bytes 786440 | tf_op jit(solution)/shard_map/ppermute | solution.py:31
  83.4 1.3 collective-permute-start.11
  84.9 1.3 collective-permute-start.10
  86.8 5.2 %collective-permute-start.9 = (bf16[2,2,4,64,128]{4,2,3,0,1:T(4,128)(2,1)S(1)}, bf16[2,2,4,64,128]{4,2,3,0,1:T(4,128)(2,1)S(1)}, u32[]{:S(2)}, u32[]{:S(2)}) collective-permute-start(bf16[2,2,4,64,128]{4,2,3,0,1:T(4,128)(2,1)S(1)} %pad_maximum_fusion.22), channel_id=1, source_target_pairs={{0,8},{8,16},{16,24},{24,32},{32,40},{40,48},{48,56},{56,64},{64,7... | collective-permute-start | bytes 786440 | tf_op jit(solution)/shard_map/ppermute | solution.py:31
  92.8 1.0 collective-permute-done.11
  94.6 8.7 %collective-permute-done.10 = bf16[2,2,4,64,128]{4,2,3,0,1:T(4,128)(2,1)S(1)} collective-permute-done((bf16[2,2,4,64,128]{4,2,3,0,1:T(4,128)(2,1)S(1)}, bf16[2,2,4,64,128]{4,2,3,0,1:T(4,128)(2,1)S(1)}, u32[]{:S(2)}, u32[]{:S(2)}) %collective-permute-start.10) | collective-permute-done | bytes 262176 | tf_op jit(solution)/shard_map/ppermute | solution.py:31
  106.3 1.3 convolution_bitcast_fusion.9
  107.6 4.8 %collective-permute-start.13 = (bf16[2,16,64,128]{3,2,1,0:T(8,128)(2,1)S(1)}, bf16[2,16,64,128]{3,2,1,0:T(8,128)(2,1)}, u32[]{:S(2)}, u32[]{:S(2)}) collective-permute-start(bf16[2,16,64,128]{3,2,1,0:T(8,128)(2,1)S(1)} %fusion.33), channel_id=1, source_target_pairs={{0,2},{1,3},{2,4},{3,5},{4,6},{5,7},{8,10},{9,11},{10,12},{11,13},... | collective-permute-start | bytes 1572872 | tf_op jit(solution)/shard_map/ppermute | solution.py:31
  112.4 1.3 collective-permute-start.12
  114.9 1.6 reshape.288
  116.5 1.5 convolution_bitcast_fusion.7
  118.1 1.2 fusion.38
  119.6 1.6 collective-permute-done.13
  121.2 1.4 convolution_bitcast_fusion.3
  122.6 3.3 %collective-permute-done.12 = bf16[2,16,64,128]{3,2,1,0:T(8,128)(2,1)} collective-permute-done((bf16[2,16,64,128]{3,2,1,0:T(8,128)(2,1)S(1)}, bf16[2,16,64,128]{3,2,1,0:T(8,128)(2,1)}, u32[]{:S(2)}, u32[]{:S(2)}) %collective-permute-start.12) | collective-permute-done | bytes 524320 | tf_op jit(solution)/shard_map/ppermute | solution.py:31
  126.0 2.0 fusion.34
  130.4 2.6 %collective-permute-start.14 = (bf16[2,1,64,128]{3,2,1,0:T(8,128)(2,1)S(1)}, bf16[2,1,64,128]{3,2,1,0:T(8,128)(2,1)S(1)}, u32[]{:S(2)}, u32[]{:S(2)}) collective-permute-start(bf16[2,1,64,128]{3,2,1,0:T(8,128)(2,1)S(1)} %get-tuple-element.32), channel_id=1, source_target_pairs={{0,8},{8,16},{16,24},{24,32},{32,40},{40,48},{48,56},{56,64},{64,7... | collective-permute-start | bytes 98312 | tf_op jit(solution)/shard_map/ppermute | solution.py:19
  133.0 1.5 collective-permute-start.15
  135.4 2.3 collective-permute-done.15
  141.3 0.8 copy-done.51
  142.1 1.5 fusion.35
  145.0 5.1 %collective-permute-start.17 = (bf16[1,16,64,128]{3,2,1,0:T(8,128)(2,1)}, bf16[1,16,64,128]{3,2,1,0:T(8,128)(2,1)S(1)}, u32[]{:S(2)}, u32[]{:S(2)}) collective-permute-start(bf16[1,16,64,128]{3,2,1,0:T(8,128)(2,1)} %get-tuple-element.30), channel_id=1, source_target_pairs={{0,1},{1,2},{2,3},{3,4},{4,5},{5,6},{6,7},{8,9},{9,10},{10,11},{11... | collective-permute-start | bytes 786440 | tf_op jit(solution)/shard_map/ppermute | solution.py:31
  150.1 1.9 collective-permute-start.16
  152.8 0.9 collective-permute-done.17
  154.1 3.8 %collective-permute-done.16 = bf16[1,16,64,128]{3,2,1,0:T(8,128)(2,1)} collective-permute-done((bf16[1,16,64,128]{3,2,1,0:T(8,128)(2,1)S(1)}, bf16[1,16,64,128]{3,2,1,0:T(8,128)(2,1)}, u32[]{:S(2)}, u32[]{:S(2)}) %collective-permute-start.16) | collective-permute-done | bytes 262176 | tf_op jit(solution)/shard_map/ppermute | solution.py:31
  157.9 2.5 %fusion.36 = (bf16[2,16,64,128]{3,2,1,0:T(8,128)(2,1)S(1)}, bf16[2,16,64,128]{3,2,1,0:T(8,128)(2,1)}) fusion(f32[2,16,64,128]{3,2,1,0:T(8,128)S(1)} %copy-done.50, f32[2,16,64,128]{3,2,1,0:T(8,128)S(1)} %convolution_bitcast_fusion, f32[2,16,64,128]{3,2,1,0:T(8,128)S(1)} %convolution_bitcast_fusion.1, bf16[3,64,64]{2,1,0:T(8,128)(2,1)S(1)} %copy-done.37, ...), kind=kOutput, calls=%fused_computation.122 | convolution fusion | flops 37748736 | bytes 5259264 | tf_op jit(solution)/shard_map/oc,fsop->fscp/dot_general | solution.py:166
  164.3 1.3 collective-permute-start.19
  166.4 21.6 %all-to-all-start = ((f32[256,1,384]{2,1,0:T(1,128)}), f32[256,1,384]{2,1,0:T(1,128)S(1)}, u32[]{:S(2)}, u32[]{:S(2)}) async-start(f32[256,1,384]{2,1,0:T(1,128)} %bitcast.244), calls=%async_computation | async-start | bytes 786432 | tf_op jit(solution)/shard_map/all_to_all | solution.py:241
  188.0 3.5 %collective-permute-start.18 = (bf16[2,1,64,128]{3,2,1,0:T(8,128)(2,1)S(1)}, bf16[2,1,64,128]{3,2,1,0:T(8,128)(2,1)S(1)}, u32[]{:S(2)}, u32[]{:S(2)}) collective-permute-start(bf16[2,1,64,128]{3,2,1,0:T(8,128)(2,1)S(1)} %get-tuple-element.28), channel_id=1, source_target_pairs={{0,8},{8,16},{16,24},{24,32},{32,40},{40,48},{48,56},{56,64},{64,7... | collective-permute-start | bytes 98312 | tf_op jit(solution)/shard_map/ppermute | solution.py:19
  194.8 10.3 %all-to-all-done = f32[256,1,384]{2,1,0:T(1,128)S(1)} async-done(((f32[256,1,384]{2,1,0:T(1,128)}), f32[256,1,384]{2,1,0:T(1,128)S(1)}, u32[]{:S(2)}, u32[]{:S(2)}) %all-to-all-start) | async-done | bytes 393248 | tf_op jit(solution)/shard_map/all_to_all | solution.py:241
  205.4 1.0 broadcast_in_dim.56
  206.3 7.7 %all-to-all-start.1 = ((f32[256,1,384]{2,1,0:T(1,128)}), f32[256,1,384]{2,1,0:T(1,128)S(1)}, u32[]{:S(2)}, u32[]{:S(2)}) async-start(f32[256,1,384]{2,1,0:T(1,128)} %broadcast_in_dim.56), calls=%async_computation.1 | async-start | bytes 786432 | tf_op jit(solution)/shard_map/all_to_all | solution.py:243
  215.5 1.2 fusion.22
  216.7 14.5 %all-to-all-done.1 = f32[256,1,384]{2,1,0:T(1,128)S(1)} async-done(((f32[256,1,384]{2,1,0:T(1,128)}), f32[256,1,384]{2,1,0:T(1,128)S(1)}, u32[]{:S(2)}, u32[]{:S(2)}) %all-to-all-start.1) | async-done | bytes 393248 | tf_op jit(solution)/shard_map/all_to_all | solution.py:243
  232.9 0.8 fusion.124
  233.7 0.8 mul.94
  234.5 0.8 mul.90
  (235 shorter events, 43.2 us)
Async XLA Ops:
  0.6 19.8 %copy-start.3 = (bf16[2,16,64,128]{3,2,1,0:T(8,128)(2,1)S(1)}, bf16[2,16,64,128]{3,2,1,0:T(8,128)(2,1)}, u32[]{:S(2)}) copy-start(bf16[2,16,64,128]{3,2,1,0:T(8,128)(2,1)} %param.12) | copy-start | bytes 1572868
  1.5 19.0 %collective-permute-start = (bf16[2,1,64,128]{3,2,1,0:T(8,128)(2,1)S(1)}, bf16[2,1,64,128]{3,2,1,0:T(8,128)(2,1)S(1)}, u32[]{:S(2)}, u32[]{:S(2)}) collective-permute-start(bf16[2,1,64,128]{3,2,1,0:T(8,128)(2,1)S(1)} %get-tuple-element.38), channel_id=1, source_target_pairs={{0,8},{8,16},{16,24},{24,32},{32,40},{40,48},{48,56},{56,64},{64,7... | collective-permute-start | bytes 98312 | tf_op jit(solution)/shard_map/ppermute | solution.py:19
  5.5 14.9 %collective-permute-start.1 = (bf16[2,1,64,128]{3,2,1,0:T(8,128)(2,1)S(1)}, bf16[2,1,64,128]{3,2,1,0:T(8,128)(2,1)S(1)}, u32[]{:S(2)}, u32[]{:S(2)}) collective-permute-start(bf16[2,1,64,128]{3,2,1,0:T(8,128)(2,1)S(1)} %get-tuple-element.39), channel_id=1, source_target_pairs={{8,0},{16,8},{24,16},{32,24},{40,32},{48,40},{56,48},{64,56},{72,6... | collective-permute-start | bytes 98312 | tf_op jit(solution)/shard_map/ppermute | solution.py:21
  11.4 6.9 %copy-start.38 = (s32[32,4]{0,1:T(4,128)}, s32[32,4]{0,1:T(4,128)S(1)}, u32[]{:S(2)}) copy-start(s32[32,4]{0,1:T(4,128)S(1)} %select_reduce_fusion) | copy-start | bytes 1540
  12.3 1.4 copy-start.43
  18.3 2.8 %copy-start.17 = (bf16[3,3,64,64]{3,2,1,0:T(8,128)(2,1)S(1)}, bf16[3,3,64,64]{3,2,1,0:T(8,128)(2,1)}, u32[]{:S(2)}) copy-start(bf16[3,3,64,64]{3,2,1,0:T(8,128)(2,1)} %param.13) | copy-start | bytes 221188
  20.5 3.2 %copy-start.39 = (bf16[2,1,64,128]{3,2,1,0:T(8,128)(2,1)}, bf16[2,1,64,128]{3,2,1,0:T(8,128)(2,1)S(1)}, u32[]{:S(2)}) copy-start(bf16[2,1,64,128]{3,2,1,0:T(8,128)(2,1)S(1)} %collective-permute-done.1) | copy-start | bytes 98308
  23.6 7.5 %copy-start.36 = (bf16[3,64,64]{2,1,0:T(8,128)(2,1)S(1)}, bf16[3,64,64]{2,1,0:T(8,128)(2,1)}, u32[]{:S(2)}) copy-start(bf16[3,64,64]{2,1,0:T(8,128)(2,1)} %param.14) | copy-start | bytes 73732
  25.1 12.4 %copy-start.9 = (bf16[2,16,64,128]{3,2,1,0:T(8,128)(2,1)}, bf16[2,16,64,128]{3,2,1,0:T(8,128)(2,1)S(1)}, u32[]{:S(2)}) copy-start(bf16[2,16,64,128]{3,2,1,0:T(8,128)(2,1)S(1)} %get-tuple-element.55) | copy-start | bytes 1572868
  25.2 12.0 %copy-start.15 = (bf16[1,16,64,128]{3,2,1,0:T(8,128)(2,1)}, bf16[1,16,64,128]{3,2,1,0:T(8,128)(2,1)S(1)}, u32[]{:S(2)}) copy-start(bf16[1,16,64,128]{3,2,1,0:T(8,128)(2,1)S(1)} %get-tuple-element.36) | copy-start | bytes 786436
  25.2 12.4 %copy-start.27 = (bf16[1,16,64,128]{3,2,1,0:T(8,128)(2,1)}, bf16[1,16,64,128]{3,2,1,0:T(8,128)(2,1)S(1)}, u32[]{:S(2)}) copy-start(bf16[1,16,64,128]{3,2,1,0:T(8,128)(2,1)S(1)} %get-tuple-element.37) | copy-start | bytes 786436
  25.2 12.4 %collective-permute-start.2 = (bf16[1,16,64,128]{3,2,1,0:T(8,128)(2,1)S(1)}, bf16[1,16,64,128]{3,2,1,0:T(8,128)(2,1)S(1)}, u32[]{:S(2)}, u32[]{:S(2)}) collective-permute-start(bf16[1,16,64,128]{3,2,1,0:T(8,128)(2,1)S(1)} %get-tuple-element.36), channel_id=1, source_target_pairs={{0,1},{1,2},{2,3},{3,4},{4,5},{5,6},{6,7},{8,9},{9,10},{10,11},{11... | collective-permute-start | bytes 786440 | tf_op jit(solution)/shard_map/ppermute | solution.py:31
  29.2 7.7 %collective-permute-start.3 = (bf16[1,16,64,128]{3,2,1,0:T(8,128)(2,1)S(1)}, bf16[1,16,64,128]{3,2,1,0:T(8,128)(2,1)S(1)}, u32[]{:S(2)}, u32[]{:S(2)}) collective-permute-start(bf16[1,16,64,128]{3,2,1,0:T(8,128)(2,1)S(1)} %get-tuple-element.37), channel_id=1, source_target_pairs={{1,0},{2,1},{3,2},{4,3},{5,4},{6,5},{7,6},{9,8},{10,9},{11,10},{12... | collective-permute-start | bytes 786440 | tf_op jit(solution)/shard_map/ppermute | solution.py:31
  37.6 7.1 %copy-start = (bf16[2,16,64,128]{3,2,1,0:T(8,128)(2,1)S(1)}, bf16[2,16,64,128]{3,2,1,0:T(8,128)(2,1)}, u32[]{:S(2)}) copy-start(bf16[2,16,64,128]{3,2,1,0:T(8,128)(2,1)} %param.20) | copy-start | bytes 1572868
  37.6 1.5 copy-start.47
  39.1 12.1 %copy-start.5 = (bf16[2,16,64,128]{3,2,1,0:T(8,128)(2,1)}, bf16[2,16,64,128]{3,2,1,0:T(8,128)(2,1)S(1)}, u32[]{:S(2)}) copy-start(bf16[2,16,64,128]{3,2,1,0:T(8,128)(2,1)S(1)} %get-tuple-element.57) | copy-start | bytes 1572868
  39.1 6.7 %collective-permute-start.4 = (bf16[2,1,64,128]{3,2,1,0:T(8,128)(2,1)S(1)}, bf16[2,1,64,128]{3,2,1,0:T(8,128)(2,1)S(1)}, u32[]{:S(2)}, u32[]{:S(2)}) collective-permute-start(bf16[2,1,64,128]{3,2,1,0:T(8,128)(2,1)S(1)} %get-tuple-element.34), channel_id=1, source_target_pairs={{0,8},{8,16},{16,24},{24,32},{32,40},{40,48},{48,56},{56,64},{64,7... | collective-permute-start | bytes 98312 | tf_op jit(solution)/shard_map/ppermute | solution.py:19
  43.3 4.7 %collective-permute-start.5 = (bf16[2,1,64,128]{3,2,1,0:T(8,128)(2,1)S(1)}, bf16[2,1,64,128]{3,2,1,0:T(8,128)(2,1)S(1)}, u32[]{:S(2)}, u32[]{:S(2)}) collective-permute-start(bf16[2,1,64,128]{3,2,1,0:T(8,128)(2,1)S(1)} %get-tuple-element.35), channel_id=1, source_target_pairs={{8,0},{16,8},{24,16},{32,24},{40,32},{48,40},{56,48},{64,56},{72,6... | collective-permute-start | bytes 98312 | tf_op jit(solution)/shard_map/ppermute | solution.py:21
  44.7 4.0 %copy-start.23 = (bf16[3,3,64,64]{3,2,1,0:T(8,128)(2,1)S(1)}, bf16[3,3,64,64]{3,2,1,0:T(8,128)(2,1)}, u32[]{:S(2)}) copy-start(bf16[3,3,64,64]{3,2,1,0:T(8,128)(2,1)} %param.15) | copy-start | bytes 221188
  45.7 3.3 %copy-start.32 = (bf16[2,1,64,128]{3,2,1,0:T(8,128)(2,1)}, bf16[2,1,64,128]{3,2,1,0:T(8,128)(2,1)S(1)}, u32[]{:S(2)}) copy-start(bf16[2,1,64,128]{3,2,1,0:T(8,128)(2,1)S(1)} %collective-permute-done.4) | copy-start | bytes 98308
  48.0 3.2 %copy-start.41 = (bf16[2,1,64,128]{3,2,1,0:T(8,128)(2,1)}, bf16[2,1,64,128]{3,2,1,0:T(8,128)(2,1)S(1)}, u32[]{:S(2)}) copy-start(bf16[2,1,64,128]{3,2,1,0:T(8,128)(2,1)S(1)} %collective-permute-done.5) | copy-start | bytes 98308
  51.2 2.9 %copy-start.45 = (s32[4]{0:T(128)S(1)}, s32[4]{0:T(128)}, u32[]{:S(2)}) copy-start(s32[4]{0:T(128)} %get-tuple-element.53) | copy-start | bytes 52
  52.8 15.9 %collective-permute-start.7 = (bf16[2,16,64,128]{3,2,1,0:T(8,128)(2,1)}, bf16[2,16,64,128]{3,2,1,0:T(8,128)(2,1)S(1)}, u32[]{:S(2)}, u32[]{:S(2)}) collective-permute-start(bf16[2,16,64,128]{3,2,1,0:T(8,128)(2,1)} %get-tuple-element.59), channel_id=1, source_target_pairs={{2,0},{3,1},{4,2},{5,3},{6,4},{7,5},{10,8},{11,9},{12,10},{13,11},... | collective-permute-start | bytes 1572872 | tf_op jit(solution)/shard_map/ppermute | solution.py:31
  55.2 13.6 %copy-start.34 = (bf16[3,64,64]{2,1,0:T(8,128)(2,1)S(1)}, bf16[3,64,64]{2,1,0:T(8,128)(2,1)}, u32[]{:S(2)}) copy-start(bf16[3,64,64]{2,1,0:T(8,128)(2,1)} %param.16) | copy-start | bytes 73732
  57.7 15.6 %collective-permute-start.6 = (bf16[2,16,64,128]{3,2,1,0:T(8,128)(2,1)}, bf16[2,16,64,128]{3,2,1,0:T(8,128)(2,1)S(1)}, u32[]{:S(2)}, u32[]{:S(2)}) collective-permute-start(bf16[2,16,64,128]{3,2,1,0:T(8,128)(2,1)} %get-tuple-element.59), channel_id=1, source_target_pairs={{0,2},{1,3},{2,4},{3,5},{4,6},{5,7},{8,10},{9,11},{10,12},{11,13},... | collective-permute-start | bytes 1572872 | tf_op jit(solution)/shard_map/ppermute | solution.py:31
  74.9 11.3 %copy-start.1 = (bf16[2,16,64,128]{3,2,1,0:T(8,128)(2,1)}, bf16[2,16,64,128]{3,2,1,0:T(8,128)(2,1)S(1)}, u32[]{:S(2)}) copy-start(bf16[2,16,64,128]{3,2,1,0:T(8,128)(2,1)S(1)} %get-tuple-element.61) | copy-start | bytes 1572868
  74.9 1.3 copy-start.20
  74.9 8.2 %copy-start.19 = (bf16[2,1,4,64,128]{4,2,3,0,1:T(4,128)(2,1)S(1)}, bf16[2,1,4,64,128]{4,2,3,0,1:T(4,128)(2,1)}, u32[]{:S(2)}) copy-start(bf16[2,1,4,64,128]{4,2,3,0,1:T(4,128)(2,1)} %fusion.32) | copy-start | bytes 393220
  75.4 9.3 %copy-start.21 = (bf16[2,1,4,64,128]{4,2,3,0,1:T(4,128)(2,1)S(1)}, bf16[2,1,4,64,128]{4,2,3,0,1:T(4,128)(2,1)}, u32[]{:S(2)}) copy-start(bf16[2,1,4,64,128]{4,2,3,0,1:T(4,128)(2,1)} %fusion.30) | copy-start | bytes 393220
  76.2 10.4 %copy-start.22 = (bf16[2,1,4,64,128]{4,2,3,0,1:T(4,128)(2,1)S(1)}, bf16[2,1,4,64,128]{4,2,3,0,1:T(4,128)(2,1)}, u32[]{:S(2)}) copy-start(bf16[2,1,4,64,128]{4,2,3,0,1:T(4,128)(2,1)} %fusion.28) | copy-start | bytes 393220
  76.4 15.7 %collective-permute-start.8 = (bf16[2,2,4,64,128]{4,2,3,0,1:T(4,128)(2,1)S(1)}, bf16[2,2,4,64,128]{4,2,3,0,1:T(4,128)(2,1)S(1)}, u32[]{:S(2)}, u32[]{:S(2)}) collective-permute-start(bf16[2,2,4,64,128]{4,2,3,0,1:T(4,128)(2,1)S(1)} %pad_maximum_fusion.21), channel_id=1, source_target_pairs={{0,16},{8,24},{16,32},{24,40},{32,48},{40,56},{48,64},{56,72},{64,... | collective-permute-start | bytes 786440 | tf_op jit(solution)/shard_map/ppermute | solution.py:31
  83.4 10.5 %collective-permute-start.11 = (bf16[2,2,4,64,128]{4,2,3,0,1:T(4,128)(2,1)S(1)}, bf16[2,2,4,64,128]{4,2,3,0,1:T(4,128)(2,1)S(1)}, u32[]{:S(2)}, u32[]{:S(2)}) collective-permute-start(bf16[2,2,4,64,128]{4,2,3,0,1:T(4,128)(2,1)S(1)} %pad_maximum_fusion.24), channel_id=1, source_target_pairs={{16,0},{24,8},{32,16},{40,24},{48,32},{56,40},{64,48},{72,56},{80,... | collective-permute-start | bytes 786440 | tf_op jit(solution)/shard_map/ppermute | solution.py:31
  84.9 18.4 %collective-permute-start.10 = (bf16[2,2,4,64,128]{4,2,3,0,1:T(4,128)(2,1)S(1)}, bf16[2,2,4,64,128]{4,2,3,0,1:T(4,128)(2,1)S(1)}, u32[]{:S(2)}, u32[]{:S(2)}) collective-permute-start(bf16[2,2,4,64,128]{4,2,3,0,1:T(4,128)(2,1)S(1)} %pad_maximum_fusion.23), channel_id=1, source_target_pairs={{8,0},{16,8},{24,16},{32,24},{40,32},{48,40},{56,48},{64,56},{72,6... | collective-permute-start | bytes 786440 | tf_op jit(solution)/shard_map/ppermute | solution.py:31
  86.8 18.0 %copy-start.44 = (s32[4,4]{1,0:T(4,128)S(1)}, s32[4,4]{1,0:T(4,128)}, u32[]{:S(2)}) copy-start(s32[4,4]{1,0:T(4,128)} %broadcast_select_fusion) | copy-start | bytes 196
  86.8 18.0 %copy-start.46 = (pred[4,4]{1,0:T(4,128)(4,1)S(1)}, pred[4,4]{1,0:T(4,128)(4,1)}, u32[]{:S(2)}) copy-start(pred[4,4]{1,0:T(4,128)(4,1)} %select_and_fusion) | copy-start | bytes 52
  86.8 17.2 %collective-permute-start.9 = (bf16[2,2,4,64,128]{4,2,3,0,1:T(4,128)(2,1)S(1)}, bf16[2,2,4,64,128]{4,2,3,0,1:T(4,128)(2,1)S(1)}, u32[]{:S(2)}, u32[]{:S(2)}) collective-permute-start(bf16[2,2,4,64,128]{4,2,3,0,1:T(4,128)(2,1)S(1)} %pad_maximum_fusion.22), channel_id=1, source_target_pairs={{0,8},{8,16},{16,24},{24,32},{32,40},{40,48},{48,56},{56,64},{64,7... | collective-permute-start | bytes 786440 | tf_op jit(solution)/shard_map/ppermute | solution.py:31
  105.3 8.4 %copy-start.12 = (bf16[2,16,64,128]{3,2,1,0:T(8,128)(2,1)S(1)}, bf16[2,16,64,128]{3,2,1,0:T(8,128)(2,1)}, u32[]{:S(2)}) copy-start(bf16[2,16,64,128]{3,2,1,0:T(8,128)(2,1)} %copy-done.11) | copy-start | bytes 1572868
  107.6 13.7 %collective-permute-start.13 = (bf16[2,16,64,128]{3,2,1,0:T(8,128)(2,1)S(1)}, bf16[2,16,64,128]{3,2,1,0:T(8,128)(2,1)}, u32[]{:S(2)}, u32[]{:S(2)}) collective-permute-start(bf16[2,16,64,128]{3,2,1,0:T(8,128)(2,1)S(1)} %fusion.33), channel_id=1, source_target_pairs={{0,2},{1,3},{2,4},{3,5},{4,6},{5,7},{8,10},{9,11},{10,12},{11,13},... | collective-permute-start | bytes 1572872 | tf_op jit(solution)/shard_map/ppermute | solution.py:31
  112.4 13.6 %collective-permute-start.12 = (bf16[2,16,64,128]{3,2,1,0:T(8,128)(2,1)S(1)}, bf16[2,16,64,128]{3,2,1,0:T(8,128)(2,1)}, u32[]{:S(2)}, u32[]{:S(2)}) collective-permute-start(bf16[2,16,64,128]{3,2,1,0:T(8,128)(2,1)S(1)} %fusion.33), channel_id=1, source_target_pairs={{2,0},{3,1},{4,2},{5,3},{6,4},{7,5},{10,8},{11,9},{12,10},{13,11},... | collective-permute-start | bytes 1572872 | tf_op jit(solution)/shard_map/ppermute | solution.py:31
  116.5 1.5 copy-start.2
  119.3 6.7 %copy-start.49 = (f32[2,16,64,128]{3,2,1,0:T(8,128)S(1)}, f32[2,16,64,128]{3,2,1,0:T(8,128)}, u32[]{:S(2)}) copy-start(f32[2,16,64,128]{3,2,1,0:T(8,128)} %get-tuple-element.60) | copy-start | bytes 3145732
  119.6 6.4 %copy-start.14 = (f32[2,64,128,16]{2,3,1,0:T(8,128)S(1)}, f32[2,64,128,16]{2,3,1,0:T(8,128)}, u32[]{:S(2)}) copy-start(f32[2,64,128,16]{2,3,1,0:T(8,128)} %copy-done.13) | copy-start | bytes 3145732
  126.0 2.0 copy-start.6
  128.0 6.9 %copy-start.7 = (bf16[2,16,64,128]{3,2,1,0:T(8,128)(2,1)}, bf16[2,16,64,128]{3,2,1,0:T(8,128)(2,1)S(1)}, u32[]{:S(2)}) copy-start(bf16[2,16,64,128]{3,2,1,0:T(8,128)(2,1)S(1)} %get-tuple-element.63) | copy-start | bytes 1572868
  129.7 4.9 %copy-start.42 = (bf16[2,1,64,128]{3,2,1,0:T(8,128)(2,1)S(1)}, bf16[2,1,64,128]{3,2,1,0:T(8,128)(2,1)}, u32[]{:S(2)}) copy-start(bf16[2,1,64,128]{3,2,1,0:T(8,128)(2,1)} %copy-done.41) | copy-start | bytes 98308
  130.3 4.5 %copy-start.33 = (bf16[2,1,64,128]{3,2,1,0:T(8,128)(2,1)S(1)}, bf16[2,1,64,128]{3,2,1,0:T(8,128)(2,1)}, u32[]{:S(2)}) copy-start(bf16[2,1,64,128]{3,2,1,0:T(8,128)(2,1)} %copy-done.32) | copy-start | bytes 98308
  130.4 5.0 %collective-permute-start.14 = (bf16[2,1,64,128]{3,2,1,0:T(8,128)(2,1)S(1)}, bf16[2,1,64,128]{3,2,1,0:T(8,128)(2,1)S(1)}, u32[]{:S(2)}, u32[]{:S(2)}) collective-permute-start(bf16[2,1,64,128]{3,2,1,0:T(8,128)(2,1)S(1)} %get-tuple-element.32), channel_id=1, source_target_pairs={{0,8},{8,16},{16,24},{24,32},{32,40},{40,48},{48,56},{56,64},{64,7... | collective-permute-start | bytes 98312 | tf_op jit(solution)/shard_map/ppermute | solution.py:19
  133.0 4.7 %collective-permute-start.15 = (bf16[2,1,64,128]{3,2,1,0:T(8,128)(2,1)S(1)}, bf16[2,1,64,128]{3,2,1,0:T(8,128)(2,1)S(1)}, u32[]{:S(2)}, u32[]{:S(2)}) collective-permute-start(bf16[2,1,64,128]{3,2,1,0:T(8,128)(2,1)S(1)} %get-tuple-element.33), channel_id=1, source_target_pairs={{8,0},{16,8},{24,16},{32,24},{40,32},{48,40},{56,48},{64,56},{72,6... | collective-permute-start | bytes 98312 | tf_op jit(solution)/shard_map/ppermute | solution.py:21
  135.2 2.5 %copy-start.8 = (bf16[2,16,64,128]{3,2,1,0:T(8,128)(2,1)S(1)}, bf16[2,16,64,128]{3,2,1,0:T(8,128)(2,1)}, u32[]{:S(2)}) copy-start(bf16[2,16,64,128]{3,2,1,0:T(8,128)(2,1)} %copy-done.7) | copy-start | bytes 1572868
  135.2 3.1 %copy-start.24 = (bf16[3,3,64,64]{3,2,1,0:T(8,128)(2,1)S(1)}, bf16[3,3,64,64]{3,2,1,0:T(8,128)(2,1)}, u32[]{:S(2)}) copy-start(bf16[3,3,64,64]{3,2,1,0:T(8,128)(2,1)} %param.15) | copy-start | bytes 221188
  142.1 1.5 copy-start.10
  143.9 8.2 %copy-start.28 = (bf16[1,16,64,128]{3,2,1,0:T(8,128)(2,1)S(1)}, bf16[1,16,64,128]{3,2,1,0:T(8,128)(2,1)}, u32[]{:S(2)}) copy-start(bf16[1,16,64,128]{3,2,1,0:T(8,128)(2,1)} %copy-done.27) | copy-start | bytes 786436
  143.9 8.2 %copy-start.48 = (bf16[1,16,64,128]{3,2,1,0:T(8,128)(2,1)S(1)}, bf16[1,16,64,128]{3,2,1,0:T(8,128)(2,1)}, u32[]{:S(2)}) copy-start(bf16[1,16,64,128]{3,2,1,0:T(8,128)(2,1)} %copy-done.47) | copy-start | bytes 786436
  144.6 7.7 %copy-start.16 = (bf16[1,16,64,128]{3,2,1,0:T(8,128)(2,1)S(1)}, bf16[1,16,64,128]{3,2,1,0:T(8,128)(2,1)}, u32[]{:S(2)}) copy-start(bf16[1,16,64,128]{3,2,1,0:T(8,128)(2,1)} %copy-done.15) | copy-start | bytes 786436
  144.6 7.8 %copy-start.26 = (bf16[1,16,64,128]{3,2,1,0:T(8,128)(2,1)S(1)}, bf16[1,16,64,128]{3,2,1,0:T(8,128)(2,1)}, u32[]{:S(2)}) copy-start(bf16[1,16,64,128]{3,2,1,0:T(8,128)(2,1)} %copy-done.25) | copy-start | bytes 786436
  145.0 8.8 %collective-permute-start.17 = (bf16[1,16,64,128]{3,2,1,0:T(8,128)(2,1)}, bf16[1,16,64,128]{3,2,1,0:T(8,128)(2,1)S(1)}, u32[]{:S(2)}, u32[]{:S(2)}) collective-permute-start(bf16[1,16,64,128]{3,2,1,0:T(8,128)(2,1)} %get-tuple-element.30), channel_id=1, source_target_pairs={{0,1},{1,2},{2,3},{3,4},{4,5},{5,6},{6,7},{8,9},{9,10},{10,11},{11... | collective-permute-start | bytes 786440 | tf_op jit(solution)/shard_map/ppermute | solution.py:31
  150.1 7.8 %collective-permute-start.16 = (bf16[1,16,64,128]{3,2,1,0:T(8,128)(2,1)S(1)}, bf16[1,16,64,128]{3,2,1,0:T(8,128)(2,1)}, u32[]{:S(2)}, u32[]{:S(2)}) collective-permute-start(bf16[1,16,64,128]{3,2,1,0:T(8,128)(2,1)S(1)} %get-tuple-element.31), channel_id=1, source_target_pairs={{1,0},{2,1},{3,2},{4,3},{5,4},{6,5},{7,6},{9,8},{10,9},{11,10},{12... | collective-permute-start | bytes 786440 | tf_op jit(solution)/shard_map/ppermute | solution.py:31
  152.8 5.1 %copy-start.50 = (f32[2,16,64,128]{3,2,1,0:T(8,128)S(1)}, f32[2,16,64,128]{3,2,1,0:T(8,128)}, u32[]{:S(2)}) copy-start(f32[2,16,64,128]{3,2,1,0:T(8,128)} %get-tuple-element.56) | copy-start | bytes 3145732
  152.8 5.1 %copy-start.52 = (bf16[2,16,64,128]{3,2,1,0:T(8,128)(2,1)S(1)}, bf16[2,16,64,128]{3,2,1,0:T(8,128)(2,1)}, u32[]{:S(2)}) copy-start(bf16[2,16,64,128]{3,2,1,0:T(8,128)(2,1)} %get-tuple-element.66) | copy-start | bytes 1572868
  163.9 1.8 copy-start.29
  164.3 27.2 %collective-permute-start.19 = (bf16[2,1,64,128]{3,2,1,0:T(8,128)(2,1)S(1)}, bf16[2,1,64,128]{3,2,1,0:T(8,128)(2,1)S(1)}, u32[]{:S(2)}, u32[]{:S(2)}) collective-permute-start(bf16[2,1,64,128]{3,2,1,0:T(8,128)(2,1)S(1)} %get-tuple-element.29), channel_id=1, source_target_pairs={{8,0},{16,8},{24,16},{32,24},{40,32},{48,40},{56,48},{64,56},{72,6... | collective-permute-start | bytes 98312 | tf_op jit(solution)/shard_map/ppermute | solution.py:21
  166.4 38.7 %all-to-all-start = ((f32[256,1,384]{2,1,0:T(1,128)}), f32[256,1,384]{2,1,0:T(1,128)S(1)}, u32[]{:S(2)}, u32[]{:S(2)}) async-start(f32[256,1,384]{2,1,0:T(1,128)} %bitcast.244), calls=%async_computation | async-start | bytes 786432 | tf_op jit(solution)/shard_map/all_to_all | solution.py:241
  188.0 4.3 %collective-permute-start.18 = (bf16[2,1,64,128]{3,2,1,0:T(8,128)(2,1)S(1)}, bf16[2,1,64,128]{3,2,1,0:T(8,128)(2,1)S(1)}, u32[]{:S(2)}, u32[]{:S(2)}) collective-permute-start(bf16[2,1,64,128]{3,2,1,0:T(8,128)(2,1)S(1)} %get-tuple-element.28), channel_id=1, source_target_pairs={{0,8},{8,16},{16,24},{24,32},{32,40},{40,48},{48,56},{56,64},{64,7... | collective-permute-start | bytes 98312 | tf_op jit(solution)/shard_map/ppermute | solution.py:19
  206.3 24.8 %all-to-all-start.1 = ((f32[256,1,384]{2,1,0:T(1,128)}), f32[256,1,384]{2,1,0:T(1,128)S(1)}, u32[]{:S(2)}, u32[]{:S(2)}) async-start(f32[256,1,384]{2,1,0:T(1,128)} %broadcast_in_dim.56), calls=%async_computation.1 | async-start | bytes 786432 | tf_op jit(solution)/shard_map/all_to_all | solution.py:243
  (11 other events, 10.6 us)

commit v8 on v5

--- a/solution.py
+++ b/solution.py
@@ -206,8 +206,9 @@
     tile_count = send_strip.shape[0]
     inside_range = (receiver_ids >= 0) & (receiver_ids < tile_count)
     clipped = jnp.clip(receiver_ids, 0, tile_count - 1)
-    strip_ids = jnp.take(send_strip, clipped, axis=0)
-    live_ids = jnp.take(send_active, clipped, axis=0) & inside_range[:, None]
+    hot = (clipped[:, None] == jnp.arange(tile_count)[None, :])[:, :, None]
+    strip_ids = jnp.sum(jnp.where(hot, send_strip[None], 0), axis=1)
+    live_ids = jnp.any(hot & send_active[None], axis=1) & inside_range[:, None]
     matrix = ((strip_ids[None] == jnp.arange(strips)[:, None, None]) & live_ids[None]).astype(
         jnp.float32
     )

time: 237 us -> 228 us (0.962)
  matrix products: 48.4 us -> 41.9 us
  local copies, waits for them, and re-layouts: 17.9 us -> 15.5 us
    dot_general x8, matrix products: 7.98 us -> 5.38 us  [pick_strips(): jnp.einsum('qs,fscp->fqcp', hot, values, preferred_element_type=jnp.float32)]
  transfers between devices with their start and end apart: 22 -> 22, of which waited for: 14 -> 14; matrix products, arithmetic and copies ran while one was open for 16% -> 13% of each run, Pallas kernels for 0% -> 0%
where the time goes in v8:
time: 228 us; the launch traced here: 227 us
  starting transfers between devices  87.3 us (38%)
  waiting for transfers between devices  67.4 us (30%)
  matrix products  41.9 us (18%)
  local copies, waits for them, and re-layouts  15.5 us (7%)
  other arithmetic  12.5 us (5%)
    ppermute x12, starting transfers between devices, from_behind(): return lax.ppermute(array, axis, pairs)  39.2 us
    ppermute x12, waiting for transfers between devices, from_behind(): return lax.ppermute(array, axis, pairs)  35.6 us
    all_to_all x1, starting transfers between devices, exchange_sum(): flat = jnp.sum(lax.all_to_all(pieces, axes, 0, 0, tiled=True), axis=0)  21.6 us
    all_to_all x1, waiting for transfers between devices, exchange_sum(): flat = lax.all_to_all(copies, axes, 0, 0, tiled=True).reshape(-1)  14.6 us
    ppermute x4, starting transfers between devices, with_halo(): lax.ppermute(tail, axis, [(i, (i + 1) % count) for i in range(ends)])  14.5 us
    all_to_all x1, waiting for transfers between devices, exchange_sum(): flat = jnp.sum(lax.all_to_all(pieces, axes, 0, 0, tiled=True), axis=0)  11.3 us
    dot_general x18, matrix products, spatial_transpose(): jnp.einsum('oc,fsop->fscp', weight[row_tap, col_tap], padded[:, 2 - row_t...  8.45 us
    dot_general x18, matrix products, spatial_apply(): jnp.einsum('oc,fscp->fsop', weight[row_tap, col_tap], padded[:, row_tap:r...  7.9 us
  transfers between devices with their start and end apart: 22, of which 14 were waited for; matrix products, arithmetic and copies ran while one was open for 13% of the time, Pallas kernels for 0%

profile of v8, /device:TPU:1, one launch (start us, length us, event | category | flops | bytes accessed | tf_op | source)
XLA Modules:
  0.0 226.6 jit_solution(12303254282965350195)
XLA Ops:
  0.6 0.8 fusion.292
  1.5 4.0 %collective-permute-start = (bf16[2,1,64,128]{3,2,1,0:T(8,128)(2,1)S(1)}, bf16[2,1,64,128]{3,2,1,0:T(8,128)(2,1)S(1)}, u32[]{:S(2)}, u32[]{:S(2)}) collective-permute-start(bf16[2,1,64,128]{3,2,1,0:T(8,128)(2,1)S(1)} %get-tuple-element.24), channel_id=1, source_target_pairs={{0,8},{8,16},{16,24},{24,32},{32,40},{40,48},{48,56},{56,64},{64,7... | collective-permute-start | bytes 98312 | tf_op jit(solution)/shard_map/ppermute | solution.py:19
  5.5 1.3 collective-permute-start.1
  7.5 0.9 dynamic-slice_reduce_fusion.2
  9.8 0.9 convert_reduce_fusion
  11.5 0.9 dynamic-slice_reduce_fusion
  12.6 1.5 fusion.26
  14.2 1.4 fusion.32
  19.9 1.5 add_convert_fusion.3
  21.4 4.0 %collective-permute-start.2 = (bf16[1,16,64,128]{3,2,1,0:T(8,128)(2,1)S(1)}, bf16[1,16,64,128]{3,2,1,0:T(8,128)(2,1)S(1)}, u32[]{:S(2)}, u32[]{:S(2)}) collective-permute-start(bf16[1,16,64,128]{3,2,1,0:T(8,128)(2,1)S(1)} %get-tuple-element.22), channel_id=1, source_target_pairs={{0,1},{1,2},{2,3},{3,4},{4,5},{5,6},{6,7},{8,9},{9,10},{10,11},{11... | collective-permute-start | bytes 786440 | tf_op jit(solution)/shard_map/ppermute | solution.py:31
  25.4 1.9 collective-permute-start.3
  27.6 5.5 %collective-permute-done.3 = bf16[1,16,64,128]{3,2,1,0:T(8,128)(2,1)S(1)} collective-permute-done((bf16[1,16,64,128]{3,2,1,0:T(8,128)(2,1)S(1)}, bf16[1,16,64,128]{3,2,1,0:T(8,128)(2,1)S(1)}, u32[]{:S(2)}, u32[]{:S(2)}) %collective-permute-start.3) | collective-permute-done | bytes 262176 | tf_op jit(solution)/shard_map/ppermute | solution.py:31
  33.8 1.5 add_convert_fusion.2
  35.3 4.4 %collective-permute-start.4 = (bf16[2,1,64,128]{3,2,1,0:T(8,128)(2,1)S(1)}, bf16[2,1,64,128]{3,2,1,0:T(8,128)(2,1)S(1)}, u32[]{:S(2)}, u32[]{:S(2)}) collective-permute-start(bf16[2,1,64,128]{3,2,1,0:T(8,128)(2,1)S(1)} %get-tuple-element.20), channel_id=1, source_target_pairs={{0,8},{8,16},{16,24},{24,32},{32,40},{40,48},{48,56},{56,64},{64,7... | collective-permute-start | bytes 98312 | tf_op jit(solution)/shard_map/ppermute | solution.py:19
  39.7 1.3 collective-permute-start.5
  41.2 3.2 %collective-permute-done.5 = bf16[2,1,64,128]{3,2,1,0:T(8,128)(2,1)S(1)} collective-permute-done((bf16[2,1,64,128]{3,2,1,0:T(8,128)(2,1)S(1)}, bf16[2,1,64,128]{3,2,1,0:T(8,128)(2,1)S(1)}, u32[]{:S(2)}, u32[]{:S(2)}) %collective-permute-start.5) | collective-permute-done | bytes 32800 | tf_op jit(solution)/shard_map/ppermute | solution.py:21
  47.6 1.5 add_convert_fusion.1
  49.1 1.3 collective-permute-start.7
  50.5 0.8 fusion.230
  51.3 4.2 %collective-permute-start.6 = (bf16[2,16,64,128]{3,2,1,0:T(8,128)(2,1)S(1)}, bf16[2,16,64,128]{3,2,1,0:T(8,128)(2,1)S(1)}, u32[]{:S(2)}, u32[]{:S(2)}) collective-permute-start(bf16[2,16,64,128]{3,2,1,0:T(8,128)(2,1)S(1)} %get-tuple-element.44), channel_id=1, source_target_pairs={{0,2},{1,3},{2,4},{3,5},{4,6},{5,7},{8,10},{9,11},{10,12},{11,13},... | collective-permute-start | bytes 1572872 | tf_op jit(solution)/shard_map/ppermute | solution.py:31
  55.8 9.0 %collective-permute-done.7 = bf16[2,16,64,128]{3,2,1,0:T(8,128)(2,1)S(1)} collective-permute-done((bf16[2,16,64,128]{3,2,1,0:T(8,128)(2,1)S(1)}, bf16[2,16,64,128]{3,2,1,0:T(8,128)(2,1)S(1)}, u32[]{:S(2)}, u32[]{:S(2)}) %collective-permute-start.7) | collective-permute-done | bytes 524320 | tf_op jit(solution)/shard_map/ppermute | solution.py:31
  65.1 1.5 collective-permute-done.6
  68.6 6.8 %collective-permute-start.8 = (bf16[2,2,4,64,128]{4,2,3,0,1:T(4,128)(2,1)S(1)}, bf16[2,2,4,64,128]{4,2,3,0,1:T(4,128)(2,1)S(1)}, u32[]{:S(2)}, u32[]{:S(2)}) collective-permute-start(bf16[2,2,4,64,128]{4,2,3,0,1:T(4,128)(2,1)S(1)} %pad_maximum_fusion.21), channel_id=1, source_target_pairs={{0,16},{8,24},{16,32},{24,40},{32,48},{40,56},{48,64},{56,72},{64,... | collective-permute-start | bytes 786440 | tf_op jit(solution)/shard_map/ppermute | solution.py:31
  75.6 1.3 collective-permute-start.11
  77.1 1.3 collective-permute-start.10
  79.0 5.2 %collective-permute-start.9 = (bf16[2,2,4,64,128]{4,2,3,0,1:T(4,128)(2,1)S(1)}, bf16[2,2,4,64,128]{4,2,3,0,1:T(4,128)(2,1)S(1)}, u32[]{:S(2)}, u32[]{:S(2)}) collective-permute-start(bf16[2,2,4,64,128]{4,2,3,0,1:T(4,128)(2,1)S(1)} %pad_maximum_fusion.22), channel_id=1, source_target_pairs={{0,8},{8,16},{16,24},{24,32},{32,40},{40,48},{48,56},{56,64},{64,7... | collective-permute-start | bytes 786440 | tf_op jit(solution)/shard_map/ppermute | solution.py:31
  84.2 0.7 fusion.296
  85.0 1.1 collective-permute-done.11
  86.0 0.7 fusion.293
  86.8 8.8 %collective-permute-done.10 = bf16[2,2,4,64,128]{4,2,3,0,1:T(4,128)(2,1)S(1)} collective-permute-done((bf16[2,2,4,64,128]{4,2,3,0,1:T(4,128)(2,1)S(1)}, bf16[2,2,4,64,128]{4,2,3,0,1:T(4,128)(2,1)S(1)}, u32[]{:S(2)}, u32[]{:S(2)}) %collective-permute-start.10) | collective-permute-done | bytes 262176 | tf_op jit(solution)/shard_map/ppermute | solution.py:31
  95.6 0.7 fusion.294
  96.4 0.7 fusion.295
  98.8 4.9 %collective-permute-start.13 = (bf16[2,16,64,128]{3,2,1,0:T(8,128)(2,1)S(1)}, bf16[2,16,64,128]{3,2,1,0:T(8,128)(2,1)}, u32[]{:S(2)}, u32[]{:S(2)}) collective-permute-start(bf16[2,16,64,128]{3,2,1,0:T(8,128)(2,1)S(1)} %fusion.33), channel_id=1, source_target_pairs={{0,2},{1,3},{2,4},{3,5},{4,6},{5,7},{8,10},{9,11},{10,12},{11,13},... | collective-permute-start | bytes 1572872 | tf_op jit(solution)/shard_map/ppermute | solution.py:31
  103.7 1.3 collective-permute-start.12
  106.2 1.6 reshape.437
  107.8 1.5 convolution_bitcast_fusion.7
  109.3 1.2 fusion.38
  110.9 1.6 collective-permute-done.13
  112.5 1.4 convolution_bitcast_fusion.3
  113.8 3.4 %collective-permute-done.12 = bf16[2,16,64,128]{3,2,1,0:T(8,128)(2,1)} collective-permute-done((bf16[2,16,64,128]{3,2,1,0:T(8,128)(2,1)S(1)}, bf16[2,16,64,128]{3,2,1,0:T(8,128)(2,1)}, u32[]{:S(2)}, u32[]{:S(2)}) %collective-permute-start.12) | collective-permute-done | bytes 524320 | tf_op jit(solution)/shard_map/ppermute | solution.py:31
  117.2 2.0 fusion.34
  121.6 2.5 %collective-permute-start.14 = (bf16[2,1,64,128]{3,2,1,0:T(8,128)(2,1)S(1)}, bf16[2,1,64,128]{3,2,1,0:T(8,128)(2,1)S(1)}, u32[]{:S(2)}, u32[]{:S(2)}) collective-permute-start(bf16[2,1,64,128]{3,2,1,0:T(8,128)(2,1)S(1)} %get-tuple-element.18), channel_id=1, source_target_pairs={{0,8},{8,16},{16,24},{24,32},{32,40},{40,48},{48,56},{56,64},{64,7... | collective-permute-start | bytes 98312 | tf_op jit(solution)/shard_map/ppermute | solution.py:19
  124.2 1.5 collective-permute-start.15
  126.5 2.3 %collective-permute-done.15 = bf16[2,1,64,128]{3,2,1,0:T(8,128)(2,1)S(1)} collective-permute-done((bf16[2,1,64,128]{3,2,1,0:T(8,128)(2,1)S(1)}, bf16[2,1,64,128]{3,2,1,0:T(8,128)(2,1)S(1)}, u32[]{:S(2)}, u32[]{:S(2)}) %collective-permute-start.15) | collective-permute-done | bytes 32800 | tf_op jit(solution)/shard_map/ppermute | solution.py:21
  132.4 0.8 copy-done.40
  133.2 1.5 fusion.35
  135.0 0.7 fusion.288
  136.1 5.2 %collective-permute-start.17 = (bf16[1,16,64,128]{3,2,1,0:T(8,128)(2,1)}, bf16[1,16,64,128]{3,2,1,0:T(8,128)(2,1)S(1)}, u32[]{:S(2)}, u32[]{:S(2)}) collective-permute-start(bf16[1,16,64,128]{3,2,1,0:T(8,128)(2,1)} %get-tuple-element.16), channel_id=1, source_target_pairs={{0,1},{1,2},{2,3},{3,4},{4,5},{5,6},{6,7},{8,9},{9,10},{10,11},{11... | collective-permute-start | bytes 786440 | tf_op jit(solution)/shard_map/ppermute | solution.py:31
  141.3 1.9 collective-permute-start.16
  144.0 0.9 collective-permute-done.17
  145.3 3.8 %collective-permute-done.16 = bf16[1,16,64,128]{3,2,1,0:T(8,128)(2,1)} collective-permute-done((bf16[1,16,64,128]{3,2,1,0:T(8,128)(2,1)S(1)}, bf16[1,16,64,128]{3,2,1,0:T(8,128)(2,1)}, u32[]{:S(2)}, u32[]{:S(2)}) %collective-permute-start.16) | collective-permute-done | bytes 262176 | tf_op jit(solution)/shard_map/ppermute | solution.py:31
  149.1 2.5 %fusion.36 = (bf16[2,16,64,128]{3,2,1,0:T(8,128)(2,1)S(1)}, bf16[2,16,64,128]{3,2,1,0:T(8,128)(2,1)}) fusion(f32[2,16,64,128]{3,2,1,0:T(8,128)S(1)} %copy-done.39, f32[2,16,64,128]{3,2,1,0:T(8,128)S(1)} %convolution_bitcast_fusion, f32[2,16,64,128]{3,2,1,0:T(8,128)S(1)} %convolution_bitcast_fusion.1, bf16[3,64,64]{2,1,0:T(8,128)(2,1)S(1)} %copy-done.31, ...), kind=kOutput, calls=%fused_computation.120 | convolution fusion | flops 37748736 | bytes 5259264 | tf_op jit(solution)/shard_map/oc,fsop->fscp/dot_general | solution.py:166
  155.5 1.3 collective-permute-start.19
  156.8 0.8 pad_maximum_fusion.6
  157.6 21.6 %all-to-all-start = ((f32[256,1,384]{2,1,0:T(1,128)}), f32[256,1,384]{2,1,0:T(1,128)S(1)}, u32[]{:S(2)}, u32[]{:S(2)}) async-start(f32[256,1,384]{2,1,0:T(1,128)} %bitcast.233), calls=%async_computation | async-start | bytes 786432 | tf_op jit(solution)/shard_map/all_to_all | solution.py:242
  179.2 3.5 %collective-permute-start.18 = (bf16[2,1,64,128]{3,2,1,0:T(8,128)(2,1)S(1)}, bf16[2,1,64,128]{3,2,1,0:T(8,128)(2,1)S(1)}, u32[]{:S(2)}, u32[]{:S(2)}) collective-permute-start(bf16[2,1,64,128]{3,2,1,0:T(8,128)(2,1)S(1)} %get-tuple-element.14), channel_id=1, source_target_pairs={{0,8},{8,16},{16,24},{24,32},{32,40},{40,48},{48,56},{56,64},{64,7... | collective-permute-start | bytes 98312 | tf_op jit(solution)/shard_map/ppermute | solution.py:19
  186.0 11.3 %all-to-all-done = f32[256,1,384]{2,1,0:T(1,128)S(1)} async-done(((f32[256,1,384]{2,1,0:T(1,128)}), f32[256,1,384]{2,1,0:T(1,128)S(1)}, u32[]{:S(2)}, u32[]{:S(2)}) %all-to-all-start) | async-done | bytes 393248 | tf_op jit(solution)/shard_map/all_to_all | solution.py:242
  197.6 1.0 broadcast_in_dim.149
  198.6 6.7 %all-to-all-start.1 = ((f32[256,1,384]{2,1,0:T(1,128)}), f32[256,1,384]{2,1,0:T(1,128)S(1)}, u32[]{:S(2)}, u32[]{:S(2)}) async-start(f32[256,1,384]{2,1,0:T(1,128)} %broadcast_in_dim.149), calls=%async_computation.1 | async-start | bytes 786432 | tf_op jit(solution)/shard_map/all_to_all | solution.py:244
  206.7 1.2 fusion.22
  207.8 14.6 %all-to-all-done.1 = f32[256,1,384]{2,1,0:T(1,128)S(1)} async-done(((f32[256,1,384]{2,1,0:T(1,128)}), f32[256,1,384]{2,1,0:T(1,128)S(1)}, u32[]{:S(2)}, u32[]{:S(2)}) %all-to-all-start.1) | async-done | bytes 393248 | tf_op jit(solution)/shard_map/all_to_all | solution.py:244
  224.2 0.8 fusion.124
  225.0 0.8 mul.94
  225.8 0.8 mul.90
  (212 shorter events, 37.0 us)
Async XLA Ops:
  0.6 15.0 %copy-start = (bf16[2,16,64,128]{3,2,1,0:T(8,128)(2,1)S(1)}, bf16[2,16,64,128]{3,2,1,0:T(8,128)(2,1)}, u32[]{:S(2)}) copy-start(bf16[2,16,64,128]{3,2,1,0:T(8,128)(2,1)} %param.18) | copy-start | bytes 1572868
  1.5 15.2 %collective-permute-start = (bf16[2,1,64,128]{3,2,1,0:T(8,128)(2,1)S(1)}, bf16[2,1,64,128]{3,2,1,0:T(8,128)(2,1)S(1)}, u32[]{:S(2)}, u32[]{:S(2)}) collective-permute-start(bf16[2,1,64,128]{3,2,1,0:T(8,128)(2,1)S(1)} %get-tuple-element.24), channel_id=1, source_target_pairs={{0,8},{8,16},{16,24},{24,32},{32,40},{40,48},{48,56},{56,64},{64,7... | collective-permute-start | bytes 98312 | tf_op jit(solution)/shard_map/ppermute | solution.py:19
  5.5 11.2 %collective-permute-start.1 = (bf16[2,1,64,128]{3,2,1,0:T(8,128)(2,1)S(1)}, bf16[2,1,64,128]{3,2,1,0:T(8,128)(2,1)S(1)}, u32[]{:S(2)}, u32[]{:S(2)}) collective-permute-start(bf16[2,1,64,128]{3,2,1,0:T(8,128)(2,1)S(1)} %get-tuple-element.25), channel_id=1, source_target_pairs={{8,0},{16,8},{24,16},{32,24},{40,32},{48,40},{56,48},{64,56},{72,6... | collective-permute-start | bytes 98312 | tf_op jit(solution)/shard_map/ppermute | solution.py:21
  12.6 4.1 %copy-start.3 = (bf16[2,16,64,128]{3,2,1,0:T(8,128)(2,1)S(1)}, bf16[2,16,64,128]{3,2,1,0:T(8,128)(2,1)}, u32[]{:S(2)}) copy-start(bf16[2,16,64,128]{3,2,1,0:T(8,128)(2,1)} %param.10) | copy-start | bytes 1572868
  16.0 1.3 copy-start.15
  16.7 1.0 copy-start.24
  16.7 3.2 %copy-start.32 = (bf16[2,1,64,128]{3,2,1,0:T(8,128)(2,1)}, bf16[2,1,64,128]{3,2,1,0:T(8,128)(2,1)S(1)}, u32[]{:S(2)}) copy-start(bf16[2,1,64,128]{3,2,1,0:T(8,128)(2,1)S(1)} %collective-permute-done.1) | copy-start | bytes 98308
  19.9 7.4 %copy-start.30 = (bf16[3,64,64]{2,1,0:T(8,128)(2,1)S(1)}, bf16[3,64,64]{2,1,0:T(8,128)(2,1)}, u32[]{:S(2)}) copy-start(bf16[3,64,64]{2,1,0:T(8,128)(2,1)} %param.12) | copy-start | bytes 73732
  21.4 12.4 %copy-start.9 = (bf16[2,16,64,128]{3,2,1,0:T(8,128)(2,1)}, bf16[2,16,64,128]{3,2,1,0:T(8,128)(2,1)S(1)}, u32[]{:S(2)}) copy-start(bf16[2,16,64,128]{3,2,1,0:T(8,128)(2,1)S(1)} %get-tuple-element.40) | copy-start | bytes 1572868
  21.4 12.0 %copy-start.13 = (bf16[1,16,64,128]{3,2,1,0:T(8,128)(2,1)}, bf16[1,16,64,128]{3,2,1,0:T(8,128)(2,1)S(1)}, u32[]{:S(2)}) copy-start(bf16[1,16,64,128]{3,2,1,0:T(8,128)(2,1)S(1)} %get-tuple-element.22) | copy-start | bytes 786436
  21.4 12.4 %copy-start.21 = (bf16[1,16,64,128]{3,2,1,0:T(8,128)(2,1)}, bf16[1,16,64,128]{3,2,1,0:T(8,128)(2,1)S(1)}, u32[]{:S(2)}) copy-start(bf16[1,16,64,128]{3,2,1,0:T(8,128)(2,1)S(1)} %get-tuple-element.23) | copy-start | bytes 786436
  21.4 12.4 %collective-permute-start.2 = (bf16[1,16,64,128]{3,2,1,0:T(8,128)(2,1)S(1)}, bf16[1,16,64,128]{3,2,1,0:T(8,128)(2,1)S(1)}, u32[]{:S(2)}, u32[]{:S(2)}) collective-permute-start(bf16[1,16,64,128]{3,2,1,0:T(8,128)(2,1)S(1)} %get-tuple-element.22), channel_id=1, source_target_pairs={{0,1},{1,2},{2,3},{3,4},{4,5},{5,6},{6,7},{8,9},{9,10},{10,11},{11... | collective-permute-start | bytes 786440 | tf_op jit(solution)/shard_map/ppermute | solution.py:31
  25.4 7.7 %collective-permute-start.3 = (bf16[1,16,64,128]{3,2,1,0:T(8,128)(2,1)S(1)}, bf16[1,16,64,128]{3,2,1,0:T(8,128)(2,1)S(1)}, u32[]{:S(2)}, u32[]{:S(2)}) collective-permute-start(bf16[1,16,64,128]{3,2,1,0:T(8,128)(2,1)S(1)} %get-tuple-element.23), channel_id=1, source_target_pairs={{1,0},{2,1},{3,2},{4,3},{5,4},{6,5},{7,6},{9,8},{10,9},{11,10},{12... | collective-permute-start | bytes 786440 | tf_op jit(solution)/shard_map/ppermute | solution.py:31
  33.1 0.7 copy-start.19
  33.8 1.5 copy-start.36
  35.3 12.2 %copy-start.5 = (bf16[2,16,64,128]{3,2,1,0:T(8,128)(2,1)}, bf16[2,16,64,128]{3,2,1,0:T(8,128)(2,1)S(1)}, u32[]{:S(2)}) copy-start(bf16[2,16,64,128]{3,2,1,0:T(8,128)(2,1)S(1)} %get-tuple-element.42) | copy-start | bytes 1572868
  35.3 9.7 %copy-start.17 = (bf16[3,3,64,64]{3,2,1,0:T(8,128)(2,1)S(1)}, bf16[3,3,64,64]{3,2,1,0:T(8,128)(2,1)}, u32[]{:S(2)}) copy-start(bf16[3,3,64,64]{3,2,1,0:T(8,128)(2,1)} %param.13) | copy-start | bytes 221188
  35.3 5.9 %collective-permute-start.4 = (bf16[2,1,64,128]{3,2,1,0:T(8,128)(2,1)S(1)}, bf16[2,1,64,128]{3,2,1,0:T(8,128)(2,1)S(1)}, u32[]{:S(2)}, u32[]{:S(2)}) collective-permute-start(bf16[2,1,64,128]{3,2,1,0:T(8,128)(2,1)S(1)} %get-tuple-element.20), channel_id=1, source_target_pairs={{0,8},{8,16},{16,24},{24,32},{32,40},{40,48},{48,56},{56,64},{64,7... | collective-permute-start | bytes 98312 | tf_op jit(solution)/shard_map/ppermute | solution.py:19
  39.7 4.7 %collective-permute-start.5 = (bf16[2,1,64,128]{3,2,1,0:T(8,128)(2,1)S(1)}, bf16[2,1,64,128]{3,2,1,0:T(8,128)(2,1)S(1)}, u32[]{:S(2)}, u32[]{:S(2)}) collective-permute-start(bf16[2,1,64,128]{3,2,1,0:T(8,128)(2,1)S(1)} %get-tuple-element.21), channel_id=1, source_target_pairs={{8,0},{16,8},{24,16},{32,24},{40,32},{48,40},{56,48},{64,56},{72,6... | collective-permute-start | bytes 98312 | tf_op jit(solution)/shard_map/ppermute | solution.py:21
  41.2 4.2 %copy-start.26 = (bf16[2,1,64,128]{3,2,1,0:T(8,128)(2,1)}, bf16[2,1,64,128]{3,2,1,0:T(8,128)(2,1)S(1)}, u32[]{:S(2)}) copy-start(bf16[2,1,64,128]{3,2,1,0:T(8,128)(2,1)S(1)} %collective-permute-done.4) | copy-start | bytes 98308
  44.4 3.2 %copy-start.34 = (bf16[2,1,64,128]{3,2,1,0:T(8,128)(2,1)}, bf16[2,1,64,128]{3,2,1,0:T(8,128)(2,1)S(1)}, u32[]{:S(2)}) copy-start(bf16[2,1,64,128]{3,2,1,0:T(8,128)(2,1)S(1)} %collective-permute-done.5) | copy-start | bytes 98308
  47.6 7.9 %copy-start.28 = (bf16[3,64,64]{2,1,0:T(8,128)(2,1)S(1)}, bf16[3,64,64]{2,1,0:T(8,128)(2,1)}, u32[]{:S(2)}) copy-start(bf16[3,64,64]{2,1,0:T(8,128)(2,1)} %param.14) | copy-start | bytes 73732
  49.1 15.7 %collective-permute-start.7 = (bf16[2,16,64,128]{3,2,1,0:T(8,128)(2,1)S(1)}, bf16[2,16,64,128]{3,2,1,0:T(8,128)(2,1)S(1)}, u32[]{:S(2)}, u32[]{:S(2)}) collective-permute-start(bf16[2,16,64,128]{3,2,1,0:T(8,128)(2,1)S(1)} %get-tuple-element.44), channel_id=1, source_target_pairs={{2,0},{3,1},{4,2},{5,3},{6,4},{7,5},{10,8},{11,9},{12,10},{13,11},... | collective-permute-start | bytes 1572872 | tf_op jit(solution)/shard_map/ppermute | solution.py:31
  51.3 15.3 %collective-permute-start.6 = (bf16[2,16,64,128]{3,2,1,0:T(8,128)(2,1)S(1)}, bf16[2,16,64,128]{3,2,1,0:T(8,128)(2,1)S(1)}, u32[]{:S(2)}, u32[]{:S(2)}) collective-permute-start(bf16[2,16,64,128]{3,2,1,0:T(8,128)(2,1)S(1)} %get-tuple-element.44), channel_id=1, source_target_pairs={{0,2},{1,3},{2,4},{3,5},{4,6},{5,7},{8,10},{9,11},{10,12},{11,13},... | collective-permute-start | bytes 1572872 | tf_op jit(solution)/shard_map/ppermute | solution.py:31
  67.2 11.2 %copy-start.1 = (bf16[2,16,64,128]{3,2,1,0:T(8,128)(2,1)}, bf16[2,16,64,128]{3,2,1,0:T(8,128)(2,1)S(1)}, u32[]{:S(2)}) copy-start(bf16[2,16,64,128]{3,2,1,0:T(8,128)(2,1)S(1)} %get-tuple-element.46) | copy-start | bytes 1572868
  68.6 15.6 %collective-permute-start.8 = (bf16[2,2,4,64,128]{4,2,3,0,1:T(4,128)(2,1)S(1)}, bf16[2,2,4,64,128]{4,2,3,0,1:T(4,128)(2,1)S(1)}, u32[]{:S(2)}, u32[]{:S(2)}) collective-permute-start(bf16[2,2,4,64,128]{4,2,3,0,1:T(4,128)(2,1)S(1)} %pad_maximum_fusion.21), channel_id=1, source_target_pairs={{0,16},{8,24},{16,32},{24,40},{32,48},{40,56},{48,64},{56,72},{64,... | collective-permute-start | bytes 786440 | tf_op jit(solution)/shard_map/ppermute | solution.py:31
  75.6 10.5 %collective-permute-start.11 = (bf16[2,2,4,64,128]{4,2,3,0,1:T(4,128)(2,1)S(1)}, bf16[2,2,4,64,128]{4,2,3,0,1:T(4,128)(2,1)S(1)}, u32[]{:S(2)}, u32[]{:S(2)}) collective-permute-start(bf16[2,2,4,64,128]{4,2,3,0,1:T(4,128)(2,1)S(1)} %pad_maximum_fusion.24), channel_id=1, source_target_pairs={{16,0},{24,8},{32,16},{40,24},{48,32},{56,40},{64,48},{72,56},{80,... | collective-permute-start | bytes 786440 | tf_op jit(solution)/shard_map/ppermute | solution.py:31
  77.1 18.5 %collective-permute-start.10 = (bf16[2,2,4,64,128]{4,2,3,0,1:T(4,128)(2,1)S(1)}, bf16[2,2,4,64,128]{4,2,3,0,1:T(4,128)(2,1)S(1)}, u32[]{:S(2)}, u32[]{:S(2)}) collective-permute-start(bf16[2,2,4,64,128]{4,2,3,0,1:T(4,128)(2,1)S(1)} %pad_maximum_fusion.23), channel_id=1, source_target_pairs={{8,0},{16,8},{24,16},{32,24},{40,32},{48,40},{56,48},{64,56},{72,6... | collective-permute-start | bytes 786440 | tf_op jit(solution)/shard_map/ppermute | solution.py:31
  79.0 17.4 %collective-permute-start.9 = (bf16[2,2,4,64,128]{4,2,3,0,1:T(4,128)(2,1)S(1)}, bf16[2,2,4,64,128]{4,2,3,0,1:T(4,128)(2,1)S(1)}, u32[]{:S(2)}, u32[]{:S(2)}) collective-permute-start(bf16[2,2,4,64,128]{4,2,3,0,1:T(4,128)(2,1)S(1)} %pad_maximum_fusion.22), channel_id=1, source_target_pairs={{0,8},{8,16},{16,24},{24,32},{32,40},{40,48},{48,56},{56,64},{64,7... | collective-permute-start | bytes 786440 | tf_op jit(solution)/shard_map/ppermute | solution.py:31
  97.6 1.0 copy-start.11
  98.8 13.6 %collective-permute-start.13 = (bf16[2,16,64,128]{3,2,1,0:T(8,128)(2,1)S(1)}, bf16[2,16,64,128]{3,2,1,0:T(8,128)(2,1)}, u32[]{:S(2)}, u32[]{:S(2)}) collective-permute-start(bf16[2,16,64,128]{3,2,1,0:T(8,128)(2,1)S(1)} %fusion.33), channel_id=1, source_target_pairs={{0,2},{1,3},{2,4},{3,5},{4,6},{5,7},{8,10},{9,11},{10,12},{11,13},... | collective-permute-start | bytes 1572872 | tf_op jit(solution)/shard_map/ppermute | solution.py:31
  103.7 13.5 %collective-permute-start.12 = (bf16[2,16,64,128]{3,2,1,0:T(8,128)(2,1)S(1)}, bf16[2,16,64,128]{3,2,1,0:T(8,128)(2,1)}, u32[]{:S(2)}, u32[]{:S(2)}) collective-permute-start(bf16[2,16,64,128]{3,2,1,0:T(8,128)(2,1)S(1)} %fusion.33), channel_id=1, source_target_pairs={{2,0},{3,1},{4,2},{5,3},{6,4},{7,5},{10,8},{11,9},{12,10},{13,11},... | collective-permute-start | bytes 1572872 | tf_op jit(solution)/shard_map/ppermute | solution.py:31
  107.8 1.5 copy-start.2
  109.3 1.2 copy-start.29
  110.5 6.7 %copy-start.38 = (f32[2,16,64,128]{3,2,1,0:T(8,128)S(1)}, f32[2,16,64,128]{3,2,1,0:T(8,128)}, u32[]{:S(2)}) copy-start(f32[2,16,64,128]{3,2,1,0:T(8,128)} %get-tuple-element.45) | copy-start | bytes 3145732
  110.9 6.3 %copy-start.12 = (f32[2,64,128,16]{2,3,1,0:T(8,128)S(1)}, f32[2,64,128,16]{2,3,1,0:T(8,128)}, u32[]{:S(2)}) copy-start(f32[2,64,128,16]{2,3,1,0:T(8,128)} %copy-done.11) | copy-start | bytes 3145732
  117.2 2.0 copy-start.6
  119.2 6.8 %copy-start.7 = (bf16[2,16,64,128]{3,2,1,0:T(8,128)(2,1)}, bf16[2,16,64,128]{3,2,1,0:T(8,128)(2,1)S(1)}, u32[]{:S(2)}) copy-start(bf16[2,16,64,128]{3,2,1,0:T(8,128)(2,1)S(1)} %get-tuple-element.48) | copy-start | bytes 1572868
  120.9 4.8 %copy-start.35 = (bf16[2,1,64,128]{3,2,1,0:T(8,128)(2,1)S(1)}, bf16[2,1,64,128]{3,2,1,0:T(8,128)(2,1)}, u32[]{:S(2)}) copy-start(bf16[2,1,64,128]{3,2,1,0:T(8,128)(2,1)} %copy-done.34) | copy-start | bytes 98308
  121.6 4.4 %copy-start.27 = (bf16[2,1,64,128]{3,2,1,0:T(8,128)(2,1)S(1)}, bf16[2,1,64,128]{3,2,1,0:T(8,128)(2,1)}, u32[]{:S(2)}) copy-start(bf16[2,1,64,128]{3,2,1,0:T(8,128)(2,1)} %copy-done.26) | copy-start | bytes 98308
  121.6 4.9 %collective-permute-start.14 = (bf16[2,1,64,128]{3,2,1,0:T(8,128)(2,1)S(1)}, bf16[2,1,64,128]{3,2,1,0:T(8,128)(2,1)S(1)}, u32[]{:S(2)}, u32[]{:S(2)}) collective-permute-start(bf16[2,1,64,128]{3,2,1,0:T(8,128)(2,1)S(1)} %get-tuple-element.18), channel_id=1, source_target_pairs={{0,8},{8,16},{16,24},{24,32},{32,40},{40,48},{48,56},{56,64},{64,7... | collective-permute-start | bytes 98312 | tf_op jit(solution)/shard_map/ppermute | solution.py:19
  124.2 4.7 %collective-permute-start.15 = (bf16[2,1,64,128]{3,2,1,0:T(8,128)(2,1)S(1)}, bf16[2,1,64,128]{3,2,1,0:T(8,128)(2,1)S(1)}, u32[]{:S(2)}, u32[]{:S(2)}) collective-permute-start(bf16[2,1,64,128]{3,2,1,0:T(8,128)(2,1)S(1)} %get-tuple-element.19), channel_id=1, source_target_pairs={{8,0},{16,8},{24,16},{32,24},{40,32},{48,40},{56,48},{64,56},{72,6... | collective-permute-start | bytes 98312 | tf_op jit(solution)/shard_map/ppermute | solution.py:21
  126.3 2.5 %copy-start.8 = (bf16[2,16,64,128]{3,2,1,0:T(8,128)(2,1)S(1)}, bf16[2,16,64,128]{3,2,1,0:T(8,128)(2,1)}, u32[]{:S(2)}) copy-start(bf16[2,16,64,128]{3,2,1,0:T(8,128)(2,1)} %copy-done.7) | copy-start | bytes 1572868
  126.4 3.1 %copy-start.18 = (bf16[3,3,64,64]{3,2,1,0:T(8,128)(2,1)S(1)}, bf16[3,3,64,64]{3,2,1,0:T(8,128)(2,1)}, u32[]{:S(2)}) copy-start(bf16[3,3,64,64]{3,2,1,0:T(8,128)(2,1)} %param.13) | copy-start | bytes 221188
  132.0 1.2 copy-start.40
  133.2 1.5 copy-start.10
  134.7 1.0 copy-start.31
  135.0 8.3 %copy-start.22 = (bf16[1,16,64,128]{3,2,1,0:T(8,128)(2,1)S(1)}, bf16[1,16,64,128]{3,2,1,0:T(8,128)(2,1)}, u32[]{:S(2)}) copy-start(bf16[1,16,64,128]{3,2,1,0:T(8,128)(2,1)} %copy-done.21) | copy-start | bytes 786436
  135.0 8.3 %copy-start.37 = (bf16[1,16,64,128]{3,2,1,0:T(8,128)(2,1)S(1)}, bf16[1,16,64,128]{3,2,1,0:T(8,128)(2,1)}, u32[]{:S(2)}) copy-start(bf16[1,16,64,128]{3,2,1,0:T(8,128)(2,1)} %copy-done.36) | copy-start | bytes 786436
  135.7 7.8 %copy-start.14 = (bf16[1,16,64,128]{3,2,1,0:T(8,128)(2,1)S(1)}, bf16[1,16,64,128]{3,2,1,0:T(8,128)(2,1)}, u32[]{:S(2)}) copy-start(bf16[1,16,64,128]{3,2,1,0:T(8,128)(2,1)} %copy-done.13) | copy-start | bytes 786436
  135.7 7.8 %copy-start.20 = (bf16[1,16,64,128]{3,2,1,0:T(8,128)(2,1)S(1)}, bf16[1,16,64,128]{3,2,1,0:T(8,128)(2,1)}, u32[]{:S(2)}) copy-start(bf16[1,16,64,128]{3,2,1,0:T(8,128)(2,1)} %copy-done.19) | copy-start | bytes 786436
  136.1 8.8 %collective-permute-start.17 = (bf16[1,16,64,128]{3,2,1,0:T(8,128)(2,1)}, bf16[1,16,64,128]{3,2,1,0:T(8,128)(2,1)S(1)}, u32[]{:S(2)}, u32[]{:S(2)}) collective-permute-start(bf16[1,16,64,128]{3,2,1,0:T(8,128)(2,1)} %get-tuple-element.16), channel_id=1, source_target_pairs={{0,1},{1,2},{2,3},{3,4},{4,5},{5,6},{6,7},{8,9},{9,10},{10,11},{11... | collective-permute-start | bytes 786440 | tf_op jit(solution)/shard_map/ppermute | solution.py:31
  141.3 7.8 %collective-permute-start.16 = (bf16[1,16,64,128]{3,2,1,0:T(8,128)(2,1)S(1)}, bf16[1,16,64,128]{3,2,1,0:T(8,128)(2,1)}, u32[]{:S(2)}, u32[]{:S(2)}) collective-permute-start(bf16[1,16,64,128]{3,2,1,0:T(8,128)(2,1)S(1)} %get-tuple-element.17), channel_id=1, source_target_pairs={{1,0},{2,1},{3,2},{4,3},{5,4},{6,5},{7,6},{9,8},{10,9},{11,10},{12... | collective-permute-start | bytes 786440 | tf_op jit(solution)/shard_map/ppermute | solution.py:31
  144.0 5.1 %copy-start.39 = (f32[2,16,64,128]{3,2,1,0:T(8,128)S(1)}, f32[2,16,64,128]{3,2,1,0:T(8,128)}, u32[]{:S(2)}) copy-start(f32[2,16,64,128]{3,2,1,0:T(8,128)} %get-tuple-element.41) | copy-start | bytes 3145732
  144.0 5.1 %copy-start.41 = (bf16[2,16,64,128]{3,2,1,0:T(8,128)(2,1)S(1)}, bf16[2,16,64,128]{3,2,1,0:T(8,128)(2,1)}, u32[]{:S(2)}) copy-start(bf16[2,16,64,128]{3,2,1,0:T(8,128)(2,1)} %get-tuple-element.51) | copy-start | bytes 1572868
  151.6 1.0 copy-start.4
  153.6 0.8 copy-start.33
  154.3 0.8 copy-start.25
  155.1 1.8 copy-start.23
  155.5 27.2 %collective-permute-start.19 = (bf16[2,1,64,128]{3,2,1,0:T(8,128)(2,1)S(1)}, bf16[2,1,64,128]{3,2,1,0:T(8,128)(2,1)S(1)}, u32[]{:S(2)}, u32[]{:S(2)}) collective-permute-start(bf16[2,1,64,128]{3,2,1,0:T(8,128)(2,1)S(1)} %get-tuple-element.15), channel_id=1, source_target_pairs={{8,0},{16,8},{24,16},{32,24},{40,32},{48,40},{56,48},{64,56},{72,6... | collective-permute-start | bytes 98312 | tf_op jit(solution)/shard_map/ppermute | solution.py:21
  157.6 39.7 %all-to-all-start = ((f32[256,1,384]{2,1,0:T(1,128)}), f32[256,1,384]{2,1,0:T(1,128)S(1)}, u32[]{:S(2)}, u32[]{:S(2)}) async-start(f32[256,1,384]{2,1,0:T(1,128)} %bitcast.233), calls=%async_computation | async-start | bytes 786432 | tf_op jit(solution)/shard_map/all_to_all | solution.py:242
  179.2 4.3 %collective-permute-start.18 = (bf16[2,1,64,128]{3,2,1,0:T(8,128)(2,1)S(1)}, bf16[2,1,64,128]{3,2,1,0:T(8,128)(2,1)S(1)}, u32[]{:S(2)}, u32[]{:S(2)}) collective-permute-start(bf16[2,1,64,128]{3,2,1,0:T(8,128)(2,1)S(1)} %get-tuple-element.14), channel_id=1, source_target_pairs={{0,8},{8,16},{16,24},{24,32},{32,40},{40,48},{48,56},{56,64},{64,7... | collective-permute-start | bytes 98312 | tf_op jit(solution)/shard_map/ppermute | solution.py:19
  198.6 23.9 %all-to-all-start.1 = ((f32[256,1,384]{2,1,0:T(1,128)}), f32[256,1,384]{2,1,0:T(1,128)S(1)}, u32[]{:S(2)}, u32[]{:S(2)}) async-start(f32[256,1,384]{2,1,0:T(1,128)} %broadcast_in_dim.149), calls=%async_computation.1 | async-start | bytes 786432 | tf_op jit(solution)/shard_map/all_to_all | solution.py:244
  205.6 1.0 copy-start.16
